TPU v7x, 32 devices: a whole 2x2x4 slice. The times are simulated.
32 devices in a mesh: dp: 8 (over z, x), tensor: 4 (over y, core).
Axes of the slice: x: 2, y: 2, z: 4, core: 2. Of those that a mesh axis runs over, the one named last changes fastest.
Arguments:
- tokens: bfloat16 [16384, 1024], P(('dp', 'tensor')), may hold values from -6 to 6
- memory: bfloat16 [16384, 1024], P(('dp', 'tensor')), may hold values from -6 to 6
- dec_lengths: int32 [8, 4], P('dp'), may hold values from 1 to 512, 1536 in all within a row
- mem_lengths: int32 [8, 4], P('dp'), may hold values from 1 to 512, 1536 in all within a row
- self_qkv: bfloat16 [3, 1024, 1024], P(None, None, 'tensor'), may hold values from -0.1875 to 0.1875
- self_out: bfloat16 [1024, 1024], P('tensor'), may hold values from -3 to 3
- cross_q: bfloat16 [1024, 1024], P(None, 'tensor'), may hold values from -0.1875 to 0.1875
- cross_kv: bfloat16 [2, 1024, 1024], P(None, None, 'tensor'), may hold values from -0.1875 to 0.1875
- cross_out: bfloat16 [1024, 1024], P('tensor'), may hold values from -3 to 3
- ffn_in: bfloat16 [1024, 4096], P(None, 'tensor'), may hold values from -0.1875 to 0.1875
- ffn_out: bfloat16 [4096, 1024], P('tensor'), may hold values from -0.375 to 0.375
- norm_gains: float32 [3, 1024], replicated, may hold values from 0.25 to 1.75
- norm_biases: float32 [3, 1024], replicated, may hold values from -3 to 3
- cotangent: bfloat16 [16384, 1024], P(('dp', 'tensor')), may hold values from -6 to 6
Outputs:
- out: bfloat16 [16384, 1024], P(('dp', 'tensor'))
- grad_tokens: float32 [16384, 1024], P(('dp', 'tensor'))
- grad_memory: float32 [16384, 1024], P(('dp', 'tensor'))
- grad_self_qkv: float32 [3, 1024, 1024], P(None, 'dp', 'tensor')
- grad_self_out: float32 [1024, 1024], P('tensor', 'dp')
- grad_cross_q: float32 [1024, 1024], P('dp', 'tensor')
- grad_cross_kv: float32 [2, 1024, 1024], P(None, 'dp', 'tensor')
- grad_cross_out: float32 [1024, 1024], P('tensor', 'dp')
- grad_ffn_in: float32 [1024, 4096], P('dp', 'tensor')
- grad_ffn_out: float32 [4096, 1024], P('tensor', 'dp')
- grad_gains: float32 [3, 1024], replicated
- grad_biases: float32 [3, 1024], replicated
Inputs may be any that keep to these rules, and one draw needn't show every extreme that they name: `dec_lengths`: each index of dp holds 4 decoder lengths summing to 1536, the longest exactly 512. `mem_lengths`: each index of dp holds 4 memory lengths summing to 1536, the longest exactly 512.
All inputs are finite; a program needn't handle non-finite values.
Results may differ from a plain program's by a relative error of at most 0.039.
Values may be sent and summed in bfloat16 or wider, within the bound.
No kernel may reach another device: no remote copies, remote signals or barrier semaphores. Data moves between devices by JAX's collectives and lax.ppermute only.
A program may use at most 256 MiB of HBM per device.

v0:
```python
import functools
import jax
import jax.numpy as jnp
from jax import lax
from jax.experimental import pallas as pl
from jax.experimental.pallas import tpu as pltpu
from jax.sharding import PartitionSpec as P

HEAD_DIM = 64
RESIDUAL_ALPHA = 4.16
NORM_EPSILON = 1e-05
MASKED_SCORE = -1000000000.0
SCORE_SCALE = HEAD_DIM ** (-0.5)
UNIT = 128
QUERY_BLOCK = 256
FFN_UNIT = 512
ROW_CHUNK = 64
BF16 = jnp.bfloat16
F32 = jnp.float32


def dot(left, right):
    return lax.dot_general(left, right, (((1,), (0,)), ((), ())), preferred_element_type=F32)


def dot_nt(left, right):
    return lax.dot_general(left, right, (((1,), (1,)), ((), ())), preferred_element_type=F32)


def shard_of(position):
    return ((position >> 2) & 1) | (position & 2) | ((position & 1) << 2)


def copy_of(source, target, sem):
    return pltpu.make_async_copy(source, target, sem)


def own_lanes(rows, head):
    lanes = lax.broadcasted_iota(jnp.int32, rows.shape, 1)
    return jnp.where((lanes >= HEAD_DIM) if head else (lanes < HEAD_DIM), rows, 0.0)


def extended_keys(keys, length):
    lanes = lax.broadcasted_iota(jnp.int32, keys.shape, 1)
    rows = lax.broadcasted_iota(jnp.int32, keys.shape, 0)
    mask = jnp.where((lanes == 0) & (rows >= length), MASKED_SCORE, 0.0).astype(BF16)
    keys = keys.astype(F32)
    return [jnp.concatenate([own_lanes(keys, head).astype(BF16), mask], axis=1) for head in (0, 1)]


def extended_query(query):
    lanes = lax.broadcasted_iota(jnp.int32, query.shape, 1)
    return jnp.concatenate([query, jnp.where(lanes == 0, 1.0, 0.0).astype(BF16)], axis=1)


def fill_diagonal(diagonal):
    keys = lax.broadcasted_iota(jnp.int32, diagonal.shape, 0)
    queries = lax.broadcasted_iota(jnp.int32, diagonal.shape, 1)
    diagonal[...] = jnp.where(keys <= queries, 0.0, MASKED_SCORE)


def key_ranges(block, keys, causal):
    if not causal:
        return [(0, keys)]
    return [(low, low + QUERY_BLOCK) for low in range(0, (block + 1) * QUERY_BLOCK, QUERY_BLOCK)]


def attend_unit(query, keys, values, length, causal, diagonal, lse_ref):
    rows, count = query.shape[0], keys.shape[0]
    values_t = jnp.transpose(values.astype(F32)).astype(BF16)
    wide_keys, wide_query = extended_keys(keys, length), extended_query(query)
    items = [(head, block) for block in range(rows // QUERY_BLOCK) for head in (0, 1)]
    scores, probs, totals, mixed = {}, {}, {}, {}
    for head, block in items:
        part = wide_query[block * QUERY_BLOCK : (block + 1) * QUERY_BLOCK]
        ranges = key_ranges(block, count, causal)
        scores[head, block] = [dot_nt(wide_keys[head][a:b], part) for a, b in ranges]
        if causal:
            scores[head, block][-1] = scores[head, block][-1] + diagonal[...]
    for head, block in items:
        pieces = scores[head, block]
        peak = functools.reduce(jnp.maximum, [jnp.max(p, axis=0, keepdims=True) for p in pieces])
        terms = [jnp.exp(p - peak) for p in pieces]
        total = sum(jnp.sum(t, axis=0, keepdims=True) for t in terms)
        at = slice(block * QUERY_BLOCK, (block + 1) * QUERY_BLOCK)
        lse_ref[head : head + 1, at] = peak + jnp.log(total)
        totals[head, block] = total
        probs[head, block] = jnp.concatenate([t.astype(BF16) for t in terms], axis=0)
    for head, block in items:
        own = values_t[head * HEAD_DIM : (head + 1) * HEAD_DIM, : probs[head, block].shape[0]]
        mixed[head, block] = dot(own, probs[head, block]) / totals[head, block]
    out = [
        jnp.transpose(jnp.concatenate([mixed[0, block], mixed[1, block]], axis=0))
        for block in range(rows // QUERY_BLOCK)
    ]
    return jnp.concatenate(out, axis=0).astype(BF16)


def attend_back_unit(query, keys, values, attended, grad, length, causal, diagonal, lse_ref):
    rows, count = query.shape[0], keys.shape[0]
    blocks = range(rows // QUERY_BLOCK)
    query_f, keys_f, grad_f = (a.astype(F32) for a in (query, keys, grad))
    wide_keys, wide_query = extended_keys(keys, length), extended_query(query)
    delta = jnp.transpose(grad_f * attended.astype(F32))
    deltas = [
        jnp.sum(delta[head * HEAD_DIM : (head + 1) * HEAD_DIM], axis=0, keepdims=True)
        for head in (0, 1)
    ]
    keys_t = jnp.transpose(keys_f).astype(BF16)
    query_own = [own_lanes(query_f, head).astype(BF16) for head in (0, 1)]
    grad_own = [own_lanes(grad_f, head).astype(BF16) for head in (0, 1)]
    items = [(head, block) for block in blocks for head in (0, 1)]
    scores, slopes, probs, back, grad_query = {}, {}, {}, {}, {}
    for head, block in items:
        at = slice(block * QUERY_BLOCK, (block + 1) * QUERY_BLOCK)
        for a, b in key_ranges(block, count, causal):
            scores[head, block, a] = dot_nt(wide_keys[head][a:b], wide_query[at])
            slopes[head, block, a] = dot_nt(values[a:b], grad_own[head][at])
    for head, block in items:
        at = slice(block * QUERY_BLOCK, (block + 1) * QUERY_BLOCK)
        ranges = key_ranges(block, count, causal)
        for a, b in ranges:
            score = scores[head, block, a]
            if causal and (a, b) == ranges[-1]:
                score = score + diagonal[...]
            prob = jnp.exp(score - lse_ref[head : head + 1, at])
            probs[head, block, a] = prob.astype(BF16)
            back[head, block, a] = (prob * (slopes[head, block, a] - deltas[head][:, at])).astype(BF16)
    for head, block in items:
        own = keys_t[head * HEAD_DIM : (head + 1) * HEAD_DIM]
        grad_query[head, block] = sum(
            dot(own[:, a:b], back[head, block, a]) for a, b in key_ranges(block, count, causal)
        )
    grad_keys, grad_values = [], []
    for low in sorted({key[2] for key in back}):
        live = [key for key in back if key[2] == low]
        at = [slice(block * QUERY_BLOCK, (block + 1) * QUERY_BLOCK) for _, block, _ in live]
        grad_values.append(
            dot(
                jnp.concatenate([probs[key] for key in live], axis=1),
                jnp.concatenate([grad_own[key[0]][a] for key, a in zip(live, at)], axis=0),
            )
        )
        grad_keys.append(
            dot(
                jnp.concatenate([back[key] for key in live], axis=1),
                jnp.concatenate([query_own[key[0]][a] for key, a in zip(live, at)], axis=0),
            )
        )
    grad_query = [
        jnp.transpose(jnp.concatenate([grad_query[0, block], grad_query[1, block]], axis=0)) * SCORE_SCALE
        for block in blocks
    ]
    return tuple(
        jnp.concatenate(parts, axis=0).astype(BF16) for parts in (grad_query, grad_keys, grad_values)
    )


def norm_chunk(hidden, gain, bias):
    center = hidden - jnp.mean(hidden, axis=-1, keepdims=True)
    inverse = lax.rsqrt(jnp.mean(center * center, axis=-1, keepdims=True) + NORM_EPSILON)
    normed = center * inverse
    return normed * gain + bias, normed, inverse


def norm_back_chunk(gradient, normed, inverse, gain):
    scaled = gradient * gain
    return inverse * (
        scaled
        - jnp.mean(scaled, axis=-1, keepdims=True)
        - normed * jnp.mean(scaled * normed, axis=-1, keepdims=True)
    )


def fold_rows(values):
    return jnp.sum(values.reshape(values.shape[0] // 8, 8, values.shape[1]), axis=0)


def each_chunk(rows, body):
    def step(index, carry):
        body(pl.ds(pl.multiple_of(index * ROW_CHUNK, ROW_CHUNK), ROW_CHUNK))
        return carry

    lax.fori_loop(0, rows // ROW_CHUNK, step, 0)


def natural_index(u, per_piece, split, swap):
    per_part = per_piece // split
    inner = lax.rem(u, per_piece)
    return (u - inner) + ((inner // per_part) ^ swap) * per_part + lax.rem(inner, per_part)


def transpose_shards(source, target, dp):
    for position in range(8):
        block = dp ^ shard_of(position)
        columns = source[:, pl.ds(pl.multiple_of(block * UNIT, UNIT), UNIT)]
        target[position * UNIT : (position + 1) * UNIT, :] = jnp.transpose(
            columns.astype(F32)
        ).astype(BF16)


SMEM = pl.BlockSpec(memory_space=pltpu.SMEM)
VMEM = pl.BlockSpec(memory_space=pltpu.VMEM)
ANY = pl.BlockSpec(memory_space=pl.ANY)


def params(limit=56):
    return pltpu.CompilerParams(vmem_limit_bytes=limit * 1024 * 1024)


def cost_of(microseconds):
    return pl.CostEstimate(flops=int(microseconds * 1.1e9), bytes_accessed=4 << 20, transcendentals=0)


def sds(shape, dtype):
    return jax.ShapeDtypeStruct(shape, dtype)


def attention_fwd_call(scalars, residual, others, weights, outs, plan, halved, partial, gain, bias):
    rows, depth = others[0].shape
    causal = len(others) == 1
    number = len(plan)
    last = gain is not None
    n_in, n_w, n_o = len(others), len(weights), len(outs)
    flat_w = [a for a in weights]
    has_partial = partial is not None

    def kernel(*refs):
        it = iter(refs)
        sc = next(it)
        in_refs = [next(it) for _ in range(n_in)]
        res_refs = [next(it) for _ in residual] if last else []
        w_refs = [[next(it) for _ in group] for group in flat_w]
        o_refs = [next(it) for _ in range(n_o)]
        part_ref = next(it) if has_partial else None
        gain_ref, bias_ref = (next(it), next(it)) if last else (None, None)
        q_ref, k_ref, v_ref, att_ref, lse_ref = (next(it) for _ in range(5))
        if last:
            low_ref, hat_ref, inv_ref = next(it), next(it), next(it)
        else:
            sum_ref = next(it)
        wbuf, obuf, att_all, diagonal, acc, wsem, osem = (next(it) for _ in range(7))
        length, swap = sc[0], sc[1]

        def offset(unit):
            array, half = unit
            if not halved[array]:
                return 0
            return pl.multiple_of((half ^ swap) * UNIT, UNIT)

        def w_copies():
            groups, column = [], 0
            for group in w_refs:
                stacked = len(group[0].shape) == 3
                for c in range(group[0].shape[0] if stacked else 1):
                    copies = []
                    for index, unit in enumerate(plan):
                        at = pl.ds(offset(unit), UNIT)
                        ref = group[unit[0]]
                        lanes = slice((column * number + index) * UNIT, (column * number + index + 1) * UNIT)
                        copies.append(copy_of(ref.at[c, :, at] if stacked else ref.at[:, at], wbuf.at[:, lanes], wsem.at[column, index]))
                    groups.append(copies)
                    column += 1
            return groups

        groups = w_copies()
        o_copies = [
            copy_of(o_refs[unit[0]].at[pl.ds(offset(unit), UNIT), :], obuf.at[index * UNIT : (index + 1) * UNIT, :], osem.at[index])
            for index, unit in enumerate(plan)
        ]
        for copies in groups:
            for copy in copies:
                copy.start()
        for copy in o_copies:
            copy.start()
        if causal:
            fill_diagonal(diagonal)
        for c, target in enumerate((q_ref, k_ref, v_ref)):
            for copy in groups[c]:
                copy.wait()
            rows_in = in_refs[0] if causal or c == 0 else in_refs[1]
            proj = dot(rows_in[...], wbuf[:, c * number * UNIT : (c + 1) * number * UNIT]).astype(BF16)
            if c == 0:
                proj = (proj.astype(F32) * SCORE_SCALE).astype(BF16)
            for index in range(number):
                target[index] = proj[:, index * UNIT : (index + 1) * UNIT]

        def step(u, carry):
            attended = attend_unit(q_ref[u], k_ref[u], v_ref[u], length, causal, diagonal, lse_ref.at[u])
            att_ref[u] = attended
            att_all[:, pl.ds(pl.multiple_of(u * UNIT, UNIT), UNIT)] = attended
            return carry

        lax.fori_loop(0, number, step, 0)
        for copy in o_copies:
            copy.wait()
        target = acc if last else sum_ref
        if has_partial:
            target[...] = part_ref[...] + dot(att_all[...], obuf[...])
        else:
            target[...] = dot(att_all[...], obuf[...])
        if last:
            def chunk(at):
                if len(res_refs) == 1:
                    old = res_refs[0][at, :].astype(F32)
                else:
                    old = res_refs[0][at, :] * res_refs[1][...] + res_refs[2][...]
                normed, hat, inverse = norm_chunk(RESIDUAL_ALPHA * old + acc[at, :], gain_ref[...], bias_ref[...])
                low_ref[at, :] = normed.astype(BF16)
                hat_ref[at, :] = hat
                inv_ref[at, :] = jnp.broadcast_to(inverse, (ROW_CHUNK, 128))

            each_chunk(rows, chunk)

    unit_rows = sds((number, rows, UNIT), BF16)
    shapes = [unit_rows] * 4 + [sds((number, 2, rows), F32)]
    if last:
        shapes += [sds((rows, depth), BF16), sds((rows, depth), F32), sds((rows, 128), F32)]
    else:
        shapes += [sds((rows, depth), F32)]
    args = [scalars, *others] + (list(residual) if last else [])
    specs = [SMEM] + [VMEM] * (len(args) - 1)
    for group in flat_w:
        args += group
        specs += [ANY] * len(group)
    args += outs
    specs += [ANY] * n_o
    if has_partial:
        args.append(partial)
        specs.append(VMEM)
    if last:
        args += [gain, bias]
        specs += [VMEM, VMEM]
    return pl.pallas_call(
        kernel,
        out_shape=shapes,
        in_specs=specs,
        out_specs=[VMEM] * len(shapes),
        scratch_shapes=[
            pltpu.VMEM((depth, 3 * number * UNIT), BF16),
            pltpu.VMEM((number * UNIT, depth), BF16),
            pltpu.VMEM((rows, number * UNIT), BF16),
            pltpu.VMEM((QUERY_BLOCK, QUERY_BLOCK), F32),
            pltpu.VMEM((rows, depth) if last else (8, 128), F32),
            pltpu.SemaphoreType.DMA((3, number)),
            pltpu.SemaphoreType.DMA((number,)),
        ],
        compiler_params=params(),
        cost_estimate=cost_of(number * 2.2),
        name="self_fwd" if causal else "cross_fwd",
    )(*args)


def attention_bwd_call(scalars, grad_low, others, weights, outs, saved, plan, halved, carried, norm):
    rows, depth = grad_low.shape
    causal = len(others) == 1
    number, n_in = len(plan), len(others)
    last = norm is not None

    def kernel(*refs):
        it = iter(refs)
        sc = next(it)
        h_ref = next(it)
        in_refs = [next(it) for _ in range(n_in)]
        acc_in = [next(it) for _ in carried]
        gain_ref = next(it) if last else None
        late_in = [next(it), next(it)] if last else []
        w_refs = [[next(it) for _ in group] for group in weights]
        o_refs = [next(it) for _ in outs]
        s_refs = [[next(it) for _ in call] for call in saved]
        sums = [next(it) for _ in range(n_in)] if not last else [None] + [next(it) for _ in range(n_in - 1)]
        if last:
            low_ref, scaled_ref, gsum_ref, bsum_ref = (next(it) for _ in range(4))
        g_ref = next(it)
        wbuf, obuf, sbuf, lbuf, att_all, grad_all, h_t = (next(it) for _ in range(7))
        in_t = [next(it) for _ in range(n_in)]
        dall, stage, diagonal = next(it), next(it), next(it)
        if last:
            acc, hat, inv = next(it), next(it), next(it)
            lsem = next(it)
        wsem, ssem, gsem = next(it), next(it), next(it)
        length, swap, dp = sc[0], sc[1], sc[2]
        if last:
            sums[0] = acc
        wide = number * UNIT

        def offset(unit):
            if not halved[unit[0]]:
                return 0
            return pl.multiple_of((unit[1] ^ swap) * UNIT, UNIT)

        o_copies, s_copies, w_copies = [], [], []
        for index, unit in enumerate(plan):
            at = pl.ds(offset(unit), UNIT)
            lanes = slice(index * UNIT, (index + 1) * UNIT)
            o_copies.append(copy_of(o_refs[unit[0]].at[at, :], obuf.at[lanes, :], wsem.at[3, index]))
            call = s_refs[unit[2]]
            for c in range(3):
                s_copies.append(copy_of(call[c].at[unit[3]], sbuf.at[index, c], ssem.at[c, index]))
            s_copies.append(copy_of(call[3].at[unit[3]], att_all.at[:, lanes], ssem.at[3, index]))
            s_copies.append(copy_of(call[4].at[unit[3]], lbuf.at[index], ssem.at[4, index]))
            column = 0
            for group in w_refs:
                ref = group[unit[0]]
                for source in [ref.at[:, at]] if len(ref.shape) == 2 else [ref.at[c, :, at] for c in range(ref.shape[0])]:
                    low = (column * number + index) * UNIT
                    w_copies.append(copy_of(source, wbuf.at[:, low : low + UNIT], wsem.at[column, index]))
                    column += 1
        for copy in o_copies + s_copies + w_copies:
            copy.start()
        if last:
            late = [copy_of(late_in[0], hat, lsem.at[0]), copy_of(late_in[1], inv, lsem.at[1])]
            for copy in late:
                copy.start()
        if causal:
            fill_diagonal(diagonal)
        transpose_shards(h_ref, h_t, dp)
        for ref, target in zip(in_refs, in_t):
            transpose_shards(ref, target, dp)
        for copy in o_copies:
            copy.wait()
        grad_att = dot_nt(h_ref[...], obuf[...]).astype(BF16)
        for index in range(number):
            grad_all[index] = grad_att[:, index * UNIT : (index + 1) * UNIT]
        for copy in s_copies:
            copy.wait()

        def step(u, carry):
            at = pl.ds(pl.multiple_of(u * UNIT, UNIT), UNIT)
            parts = attend_back_unit(
                sbuf[u, 0], sbuf[u, 1], sbuf[u, 2], att_all[:, at], grad_all[u], length, causal, diagonal, lbuf.at[u]
            )
            for c in range(3):
                dall[:, pl.ds(pl.multiple_of(c * wide + u * UNIT, UNIT), UNIT)] = parts[c]
            return carry

        lax.fori_loop(0, number, step, 0)

        def keep(weight, column):
            for index in range(number):
                part = weight[:, index * UNIT : (index + 1) * UNIT].astype(BF16)
                stage[index, :, :, column * UNIT : (column + 1) * UNIT] = part.reshape(8, UNIT, UNIT)

        for c in range(3):
            rows_t = in_t[0] if causal or c == 0 else in_t[1]
            keep(dot(rows_t[...], dall[:, c * wide : (c + 1) * wide]), c)
        keep(dot(h_t[...], att_all[...]), 3)
        g_copies = [
            copy_of(stage.at[index], g_ref.at[natural_index(index, 2, 2, swap)], gsem.at[index]) for index in range(number)
        ]
        for copy in g_copies:
            copy.start()
        for copy in w_copies:
            copy.wait()
        if causal:
            sums[0][...] = acc_in[0][...] + dot_nt(dall[...], wbuf[...])
        else:
            sums[0][...] = acc_in[0][...] + dot_nt(dall[:, :wide], wbuf[:, :wide])
            memory_sum = dot_nt(dall[:, wide:], wbuf[:, wide:])
            sums[1][...] = memory_sum + acc_in[1][...] if n_in == len(acc_in) else memory_sum
        if last:
            for copy in late:
                copy.wait()
            norm_back_rows(acc, hat, inv, gain_ref, low_ref, scaled_ref, gsum_ref, bsum_ref, rows)
        for copy in g_copies:
            copy.wait()

    big = sds((rows, depth), F32)
    sum_shapes = [big] * (n_in - 1 if last else n_in)
    shapes = list(sum_shapes)
    if last:
        shapes += [sds((rows, depth), BF16), big, sds((8, depth), F32), sds((8, depth), F32)]
    specs_out = [VMEM] * len(shapes) + [ANY]
    shapes.append(sds((number, 8, UNIT, 4 * UNIT), BF16))
    args = [scalars, grad_low, *others, *carried]
    if last:
        args.append(norm[2])
    specs = [SMEM] + [VMEM] * (len(args) - 1)
    tail = []
    if last:
        tail += [norm[0], norm[1]]
    for group in weights:
        tail += group
    tail += outs
    for call in saved:
        tail += call
    scratch = [
        pltpu.VMEM((depth, 3 * number * UNIT), BF16),
        pltpu.VMEM((number * UNIT, depth), BF16),
        pltpu.VMEM((number, 3, rows, UNIT), BF16),
        pltpu.VMEM((number, 2, rows), F32),
        pltpu.VMEM((rows, number * UNIT), BF16),
        pltpu.VMEM((number, rows, UNIT), BF16),
        pltpu.VMEM((depth, rows), BF16),
    ]
    scratch += [pltpu.VMEM((depth, rows), BF16)] * n_in
    scratch += [
        pltpu.VMEM((rows, 3 * number * UNIT), BF16),
        pltpu.VMEM((number, 8, UNIT, 4 * UNIT), BF16),
        pltpu.VMEM((QUERY_BLOCK, QUERY_BLOCK), F32),
    ]
    if last:
        scratch += [
            pltpu.VMEM((rows, depth), F32),
            pltpu.VMEM((rows, depth), F32),
            pltpu.VMEM((rows, 128), F32),
            pltpu.SemaphoreType.DMA((2,)),
        ]
    scratch += [
        pltpu.SemaphoreType.DMA((4, number)),
        pltpu.SemaphoreType.DMA((5, number)),
        pltpu.SemaphoreType.DMA((number,)),
    ]
    return pl.pallas_call(
        kernel,
        out_shape=shapes,
        in_specs=specs + [ANY] * len(tail),
        out_specs=specs_out,
        scratch_shapes=scratch,
        compiler_params=params(),
        cost_estimate=cost_of(number * 3.5),
        name="self_bwd" if causal else "cross_bwd",
    )(*args, *tail)


def norm_back_rows(acc, hat, inv, gain_ref, low_ref, scaled_ref, gsum_ref, bsum_ref, rows):
    gsum_ref[...] = jnp.zeros_like(gsum_ref)
    bsum_ref[...] = jnp.zeros_like(bsum_ref)

    def chunk(at):
        gradient, normed = acc[at, :], hat[at, :]
        grad_in = norm_back_chunk(gradient, normed, inv[at, :1], gain_ref[...])
        low_ref[at, :] = grad_in.astype(BF16)
        scaled_ref[at, :] = RESIDUAL_ALPHA * grad_in
        gsum_ref[...] += fold_rows(gradient * normed)
        bsum_ref[...] += fold_rows(gradient)

    each_chunk(rows, chunk)


GELU_SCALE = 0.7978845608028654
GELU_CUBE = 0.044715


def gelu_and_slope(pre):
    square = pre * pre
    inner = pre * (GELU_SCALE + (GELU_SCALE * GELU_CUBE) * square)
    curve = jnp.tanh(inner)
    half = 0.5 + 0.5 * curve
    slope = half * (1.0 + pre * (1.0 - curve) * (GELU_SCALE + (3.0 * GELU_SCALE * GELU_CUBE) * square))
    return pre * half, slope


def ffn_fwd_call(scalars, inputs, ups, downs, plan, halved, partial, final):
    rows, depth = inputs.shape
    number = len(plan)
    last, has_partial = final is not None, partial is not None

    def kernel(*refs):
        it = iter(refs)
        sc, x_ref = next(it), next(it)
        if last:
            gain_old, bias_old, gain_ref, bias_ref = (next(it) for _ in range(4))
            late_in = [next(it), next(it)]
        part_in = next(it) if has_partial else None
        up_refs = [next(it) for _ in ups]
        down_refs = [next(it) for _ in downs]
        if last:
            out_ref, low_ref, scaled_ref, gsum_ref, bsum_ref = (next(it) for _ in range(5))
        else:
            sum_ref = next(it)
        act_ref, slope_ref = next(it), next(it)
        ubuf, dbuf, abuf, sbuf, pbuf, psem = (next(it) for _ in range(6))
        if last:
            acc, hat, cot, lsem = (next(it) for _ in range(4))
        wsem, gsem = next(it), next(it)
        swap = sc[1]
        target = acc if last else sum_ref

        up_copies, down_copies = [], []
        for index, unit in enumerate(plan):
            low = pl.multiple_of((unit[1] ^ swap) * FFN_UNIT, FFN_UNIT) if halved[unit[0]] else 0
            at = pl.ds(low, FFN_UNIT)
            up_copies.append(copy_of(up_refs[unit[0]].at[:, at], ubuf.at[index], wsem.at[0, index]))
            down_copies.append(
                copy_of(down_refs[unit[0]].at[at, :], dbuf.at[index * FFN_UNIT : (index + 1) * FFN_UNIT, :], wsem.at[1, index])
            )
        for copy in up_copies + down_copies:
            copy.start()
        if has_partial:
            part_copy = copy_of(part_in, target, psem)
            part_copy.start()
        if last:
            late = [copy_of(late_in[0], hat, lsem.at[0]), copy_of(late_in[1], cot, lsem.at[1])]
            for copy in late:
                copy.start()
        saves = []

        def gate(pre, index):
            activated, slope = gelu_and_slope(pre)
            abuf[:, index * FFN_UNIT : (index + 1) * FFN_UNIT] = activated.astype(BF16)
            sbuf[:, index * FFN_UNIT : (index + 1) * FFN_UNIT] = slope.astype(BF16)

        for index in range(number):
            up_copies[index].wait()
            if index:
                gate(pbuf[(index - 1) % 2], index - 1)
            pbuf[index % 2] = dot(x_ref[...], ubuf[index])
        gate(pbuf[(number - 1) % 2], number - 1)
        for index in range(number):
            at = slice(index * FFN_UNIT, (index + 1) * FFN_UNIT)
            saves += [
                copy_of(abuf.at[:, at], act_ref.at[index], gsem.at[0, index]),
                copy_of(sbuf.at[:, at], slope_ref.at[index], gsem.at[1, index]),
            ]
        for copy in saves:
            copy.start()
        for copy in down_copies:
            copy.wait()
        if has_partial:
            part_copy.wait()
            target[...] += dot(abuf[...], dbuf[...])
        else:
            target[...] = dot(abuf[...], dbuf[...])
        if last:
            for copy in late:
                copy.wait()
            gsum_ref[...] = jnp.zeros_like(gsum_ref)
            bsum_ref[...] = jnp.zeros_like(bsum_ref)

            def chunk(at):
                old = hat[at, :] * gain_old[...] + bias_old[...]
                normed, xhat, inverse = norm_chunk(RESIDUAL_ALPHA * old + acc[at, :], gain_ref[...], bias_ref[...])
                out_ref[at, :] = normed.astype(BF16)
                gradient = cot[at, :].astype(F32)
                grad_in = norm_back_chunk(gradient, xhat, inverse, gain_ref[...])
                low_ref[at, :] = grad_in.astype(BF16)
                scaled_ref[at, :] = RESIDUAL_ALPHA * grad_in
                gsum_ref[...] += fold_rows(gradient * xhat)
                bsum_ref[...] += fold_rows(gradient)

            each_chunk(rows, chunk)
        for copy in saves:
            copy.wait()

    big, low = sds((rows, depth), F32), sds((rows, depth), BF16)
    if last:
        shapes = [low, low, big, sds((8, depth), F32), sds((8, depth), F32)]
    else:
        shapes = [big]
    specs_out = [VMEM] * len(shapes) + [ANY, ANY]
    shapes += [sds((number, rows, FFN_UNIT), BF16)] * 2
    args = [scalars, inputs]
    if last:
        args += [final[1], final[2], final[4], final[5]]
    specs = [SMEM] + [VMEM] * (len(args) - 1)
    tail = ([final[0], final[3]] if last else []) + ([partial] if has_partial else []) + list(ups) + list(downs)
    scratch = [
        pltpu.VMEM((number, depth, FFN_UNIT), BF16),
        pltpu.VMEM((number * FFN_UNIT, depth), BF16),
        pltpu.VMEM((rows, number * FFN_UNIT), BF16),
        pltpu.VMEM((rows, number * FFN_UNIT), BF16),
        pltpu.VMEM((2, rows, FFN_UNIT), F32),
        pltpu.SemaphoreType.DMA,
    ]
    if last:
        scratch += [
            pltpu.VMEM((rows, depth), F32),
            pltpu.VMEM((rows, depth), F32),
            pltpu.VMEM((rows, depth), BF16),
            pltpu.SemaphoreType.DMA((2,)),
        ]
    scratch += [pltpu.SemaphoreType.DMA((2, number)), pltpu.SemaphoreType.DMA((2, number))]
    return pl.pallas_call(
        kernel,
        out_shape=shapes,
        in_specs=specs + [ANY] * len(tail),
        out_specs=specs_out,
        scratch_shapes=scratch,
        compiler_params=params(),
        cost_estimate=cost_of(number * 2.2),
        name="ffn_fwd",
    )(*args, *tail)


def ffn_bwd_call(scalars, grad_low, inputs, ups, downs, saved, plan, halved, carried, norm):
    rows, depth = inputs.shape
    number = len(plan)
    last = norm is not None

    def kernel(*refs):
        it = iter(refs)
        sc, g_in, x_ref = (next(it) for _ in range(3))
        gain_ref = next(it) if last else None
        late_in = [next(it), next(it)] if last else []
        acc_in = next(it)
        up_refs = [next(it) for _ in ups]
        down_refs = [next(it) for _ in downs]
        s_refs = [[next(it) for _ in call] for call in saved]
        if last:
            low_ref, scaled_ref, gsum_ref, bsum_ref = (next(it) for _ in range(4))
        else:
            sum_ref = next(it)
        g_ref = next(it)
        ubuf, dbuf, abuf, sbuf, gbuf, x_t, g_t, stage, psem = (next(it) for _ in range(9))
        if last:
            acc, hat, inv, lsem = (next(it) for _ in range(4))
        wsem, gsem = next(it), next(it)
        swap, dp = sc[1], sc[2]
        target = acc if last else sum_ref

        copies = [[], [], [], []]
        for index, unit in enumerate(plan):
            low = pl.multiple_of((unit[1] ^ swap) * FFN_UNIT, FFN_UNIT) if halved[unit[0]] else 0
            at, lanes = pl.ds(low, FFN_UNIT), slice(index * FFN_UNIT, (index + 1) * FFN_UNIT)
            call = s_refs[unit[2]]
            copies[0].append(copy_of(down_refs[unit[0]].at[at, :], dbuf.at[lanes, :], wsem.at[0, index]))
            copies[1].append(copy_of(call[1].at[unit[3]], sbuf.at[index], wsem.at[1, index]))
            copies[2].append(copy_of(call[0].at[unit[3]], abuf.at[:, lanes], wsem.at[2, index]))
            copies[3].append(copy_of(up_refs[unit[0]].at[:, at], ubuf.at[:, lanes], wsem.at[3, index]))
        for group in copies:
            for copy in group:
                copy.start()
        part_copy = copy_of(acc_in, target, psem)
        part_copy.start()
        if last:
            late = [copy_of(late_in[0], hat, lsem.at[0]), copy_of(late_in[1], inv, lsem.at[1])]
            for copy in late:
                copy.start()
        transpose_shards(g_in, g_t, dp)
        transpose_shards(x_ref, x_t, dp)
        for index in range(number):
            copies[0][index].wait()
            copies[1][index].wait()
            grad_act = dot_nt(g_in[...], dbuf[index * FFN_UNIT : (index + 1) * FFN_UNIT, :]) * sbuf[index].astype(F32)
            gbuf[:, index * FFN_UNIT : (index + 1) * FFN_UNIT] = grad_act.astype(BF16)
        for copy in copies[2]:
            copy.wait()

        def keep(rows_t, source, column):
            for half in range(number // 2):
                wide = 2 * FFN_UNIT
                weight = dot(rows_t[...], source[:, half * wide : (half + 1) * wide]).astype(BF16)
                for inner in (0, 1):
                    part = weight[:, inner * FFN_UNIT : (inner + 1) * FFN_UNIT]
                    stage[2 * half + inner, :, :, column * FFN_UNIT : (column + 1) * FFN_UNIT] = part.reshape(8, UNIT, FFN_UNIT)

        keep(x_t, gbuf, 0)
        keep(g_t, abuf, 1)
        g_copies = [
            copy_of(stage.at[index], g_ref.at[natural_index(index, 2, 2, swap)], gsem.at[index]) for index in range(number)
        ]
        for copy in g_copies:
            copy.start()
        for copy in copies[3]:
            copy.wait()
        part_copy.wait()
        target[...] += dot_nt(gbuf[...], ubuf[...])
        if last:
            for copy in late:
                copy.wait()
            norm_back_rows(acc, hat, inv, gain_ref, low_ref, scaled_ref, gsum_ref, bsum_ref, rows)
        for copy in g_copies:
            copy.wait()

    big, low = sds((rows, depth), F32), sds((rows, depth), BF16)
    shapes = [low, big, sds((8, depth), F32), sds((8, depth), F32)] if last else [big]
    specs_out = [VMEM] * len(shapes) + [ANY]
    shapes.append(sds((number, 8, UNIT, 2 * FFN_UNIT), BF16))
    args = [scalars, grad_low, inputs] + ([norm[2]] if last else [])
    specs = [SMEM] + [VMEM] * (len(args) - 1)
    tail = ([norm[0], norm[1]] if last else []) + [carried] + list(ups) + list(downs)
    for call in saved:
        tail += call
    scratch = [
        pltpu.VMEM((depth, number * FFN_UNIT), BF16),
        pltpu.VMEM((number * FFN_UNIT, depth), BF16),
        pltpu.VMEM((rows, number * FFN_UNIT), BF16),
        pltpu.VMEM((number, rows, FFN_UNIT), BF16),
        pltpu.VMEM((rows, number * FFN_UNIT), BF16),
        pltpu.VMEM((depth, rows), BF16),
        pltpu.VMEM((depth, rows), BF16),
        pltpu.VMEM((number, 8, UNIT, 2 * FFN_UNIT), BF16),
        pltpu.SemaphoreType.DMA,
    ]
    if last:
        scratch += [
            pltpu.VMEM((rows, depth), F32),
            pltpu.VMEM((rows, depth), F32),
            pltpu.VMEM((rows, 128), F32),
            pltpu.SemaphoreType.DMA((2,)),
        ]
    scratch += [pltpu.SemaphoreType.DMA((4, number)), pltpu.SemaphoreType.DMA((number,))]
    return pl.pallas_call(
        kernel,
        out_shape=shapes,
        in_specs=specs + [ANY] * len(tail),
        out_specs=specs_out,
        scratch_shapes=scratch,
        compiler_params=params(),
        cost_estimate=cost_of(number * 3.6),
        name="ffn_bwd",
    )(*args, *tail)


def swap_pairs(count, mask):
    return [(i, i ^ mask) for i in range(count)]


def to_sibling(values):
    return lax.ppermute(values, "tensor", swap_pairs(4, 1))


def over_y(values):
    return lax.ppermute(values, "tensor", swap_pairs(4, 2))


def over_dp(values, mask):
    return lax.ppermute(values, "dp", swap_pairs(8, mask))


def over_x(values):
    return over_dp(values, 1)


def over_z_near(values):
    return over_dp(values, 2)


def over_z_far(values):
    return over_dp(values, 4)


def after(values, *earlier):
    return lax.optimization_barrier((values, *earlier))[0]


def add(*terms):
    total = terms[0].astype(F32)
    for term in terms[1:]:
        total = total + term.astype(F32)
    return total.astype(BF16)


class Reduction:
    def __init__(self, sent):
        self.sent = sent

    def first(self, kept):
        other = to_sibling(self.sent)
        units = kept.shape[0] // 2
        half = units // 2
        pair_kept = kept.reshape(2, units, *kept.shape[1:])[:, half:]
        pair_other = other.reshape(2, units, *other.shape[1:])[:, half:]
        self.left = (kept[:half], other[:half])
        self.right = (pair_kept[:, :, :4], pair_other[:, :, :4])
        self.sends = (
            add(kept[units : units + half], other[units : units + half]),
            add(pair_kept[:, :, 4:], pair_other[:, :, 4:]),
        )
        return self.sends

    def second(self):
        over = over_y(self.sends[0])
        cross = over_x(self.sends[1])
        left, right = self.left, self.right
        self.sends = (
            add(left[0][:, 4:], left[1][:, 4:], over[:, 4:]),
            add(right[0][1], right[1][1], cross[1]),
        )
        self.left = (left[0][:, :4], left[1][:, :4], over[:, :4])
        self.right = (right[0][0], right[1][0], cross[0])
        return self.sends

    def third(self):
        left, right = over_x(self.sends[0]), over_y(self.sends[1])
        self.low = jnp.concatenate([add(*self.left, left), add(*self.right, right)], axis=0)
        self.sends = self.low[:, 2:]
        return self.sends

    def fourth(self):
        low = add(self.low[:, :2], over_z_near(self.sends))
        self.low, self.sends = low[:, 0], low[:, 1]
        return self.sends

    def last(self):
        return add(self.low, over_z_far(self.sends)).astype(F32)


def sentence_body(
    tokens,
    memory,
    dec_lengths,
    mem_lengths,
    self_qkv,
    self_out,
    cross_q,
    cross_kv,
    cross_out,
    ffn_in,
    ffn_out,
    norm_gains,
    norm_biases,
    cotangent,
):
    dp = lax.axis_index("dp")
    mine = lax.axis_index("tensor")
    swap = dp & 1
    self_scalars = jnp.stack([dec_lengths[0, mine], swap, dp, mine]).astype(jnp.int32)
    cross_scalars = jnp.stack([mem_lengths[0, mine], swap, dp, mine]).astype(jnp.int32)
    gains = [norm_gains[i : i + 1] for i in range(3)]
    biases = [norm_biases[i : i + 1] for i in range(3)]

    def own_half(values, axis):
        half = values.shape[axis] // 2
        return lax.dynamic_slice_in_dim(values, swap * half, half, axis)

    def fetch(values, axis, *earlier):
        send = own_half(values, axis)
        if earlier:
            send = after(send, *earlier)
        near = over_y(send)
        far = over_dp(near, 1)
        return [values, to_sibling(values), near, far, to_sibling(near), to_sibling(far)]

    halves = [True, True]
    early = [(0, 0), (0, 1), (1, 0), (1, 1)]
    pair = [(0, 0), (1, 0)]

    qkv_sib, out_sib = to_sibling(self_qkv), to_sibling(self_out)
    qkv_near = over_y(own_half(self_qkv, 2))
    out_near = over_y(own_half(self_out, 0))
    self_a = attention_fwd_call(
        self_scalars, [], [tokens], [[self_qkv, qkv_sib]], [self_out, out_sib], early, halves, None, None, None
    )
    cq_near = over_y(after(own_half(cross_q, 1), out_near))
    ckv_near = over_y(after(own_half(cross_kv, 2), out_near))
    cout_near = over_y(after(own_half(cross_out, 0), out_near))
    qkv_gone, out_gone = after(qkv_near, self_a[5]), after(out_near, self_a[5])
    qkv_far, qkv_near3 = over_x(qkv_gone), to_sibling(qkv_gone)
    out_far, out_near3 = over_x(out_gone), to_sibling(out_gone)
    self_b = attention_fwd_call(
        self_scalars, [], [tokens], [[qkv_near, qkv_near3]], [out_near, out_near3], pair, [False] * 2,
        self_a[5], None, None,
    )
    qkv_far3, out_far3 = to_sibling(qkv_far), to_sibling(out_far)
    self_c = attention_fwd_call(
        self_scalars, [tokens], [tokens], [[qkv_far, qkv_far3]], [out_far, out_far3], pair, [False] * 2,
        self_b[5], gains[0], biases[0],
    )
    first_low, first_hat, first_inv = self_c[5:]
    w_qkv = [self_qkv, qkv_sib, qkv_near, qkv_far, qkv_near3, qkv_far3]
    w_self = [self_out, out_sib, out_near, out_far, out_near3, out_far3]

    cq_sib, ckv_sib, cout_sib = (
        to_sibling(after(w, out_near)) for w in (cross_q, cross_kv, cross_out)
    )
    cq_far, ckv_far, cout_far = (over_x(w) for w in (cq_near, ckv_near, cout_near))
    cq_near3, ckv_near3, cout_near3 = (to_sibling(w) for w in (cq_near, ckv_near, cout_near))
    cross_in = [first_low, memory]
    cross_a = attention_fwd_call(
        cross_scalars, [], cross_in, [[cross_q, cq_sib], [cross_kv, ckv_sib]], [cross_out, cout_sib], early,
        halves, None, None, None,
    )
    in_near = over_y(after(own_half(ffn_in, 1), cout_near))
    down_near = over_y(after(own_half(ffn_out, 0), cout_near))
    cross_b = attention_fwd_call(
        cross_scalars, [], cross_in, [[cq_near, cq_near3], [ckv_near, ckv_near3]], [cout_near, cout_near3],
        pair, [False] * 2, cross_a[5], None, None,
    )
    cq_far3, ckv_far3, cout_far3 = (to_sibling(w) for w in (cq_far, ckv_far, cout_far))
    cross_c = attention_fwd_call(
        cross_scalars, [first_hat, gains[0], biases[0]], cross_in, [[cq_far, cq_far3], [ckv_far, ckv_far3]],
        [cout_far, cout_far3], pair, [False] * 2, cross_b[5], gains[1], biases[1],
    )
    second_low, second_hat, second_inv = cross_c[5:]
    w_cq = [cross_q, cq_sib, cq_near, cq_far, cq_near3, cq_far3]
    w_ckv = [cross_kv, ckv_sib, ckv_near, ckv_far, ckv_near3, ckv_far3]
    w_cross = [cross_out, cout_sib, cout_near, cout_far, cout_near3, cout_far3]

    in_sib, down_sib = to_sibling(after(ffn_in, cout_near)), to_sibling(after(ffn_out, cout_near))
    in_far, down_far = over_x(in_near), over_x(down_near)
    in_near3, down_near3 = to_sibling(in_near), to_sibling(down_near)
    in_far3, down_far3 = to_sibling(in_far), to_sibling(down_far)
    w_in = [ffn_in, in_sib, in_near, in_far, in_near3, in_far3]
    w_down = [ffn_out, down_sib, down_near, down_far, down_near3, down_far3]
    ffn_a = ffn_fwd_call(
        cross_scalars, second_low, w_in[:2], w_down[:2], early, halves, None, None
    )
    ffn_b = ffn_fwd_call(
        cross_scalars, second_low, w_in[2::2], w_down[2::2], pair, [False] * 2, ffn_a[0], None
    )
    ffn_c = ffn_fwd_call(
        cross_scalars, second_low, w_in[3::2], w_down[3::2], pair, [False] * 2, ffn_b[0],
        (second_hat, gains[1], biases[1], cotangent, gains[2], biases[2]),
    )
    out_rows, third_low, third_scaled, third_gain, third_bias = ffn_c[:5]

    def plan_of(pieces):
        units = []
        for piece in pieces:
            for half in (0, 1):
                if piece < 2:
                    units.append((piece, half, 0, 2 * piece + half))
                else:
                    units.append((2 * piece - 2 + half, 0, 1 + half, piece - 2))
        return units

    halved = [True, True, False, False, False, False]
    ffn_saved = [ffn_a[1:3], ffn_b[1:3], ffn_c[5:7]]
    ffn_d = ffn_bwd_call(
        cross_scalars, third_low, second_low, w_in, w_down, ffn_saved, plan_of((1, 3)), halved,
        third_scaled, None,
    )
    ffn_sum = Reduction(ffn_d[1])
    ffn_e = ffn_bwd_call(
        cross_scalars, third_low, second_low, w_in, w_down, ffn_saved, plan_of((0, 2)), halved,
        ffn_d[0], (second_hat, second_inv, gains[1]),
    )
    second_back, second_scaled, second_gain, second_bias = ffn_e[:4]
    second_back = after(second_back, *ffn_sum.first(ffn_e[4]))

    cross_saved = [cross_a[:5], cross_b[:5], cross_c[:5]]
    cross_d = attention_bwd_call(
        cross_scalars, second_back, cross_in, [w_cq, w_ckv], w_cross, cross_saved, plan_of((1, 3)), halved,
        [second_scaled], None,
    )
    cross_sum = Reduction(cross_d[2])
    cross_e = attention_bwd_call(
        cross_scalars, second_back, cross_in, [w_cq, w_ckv], w_cross, cross_saved, plan_of((0, 2)), halved,
        cross_d[:2], (first_hat, first_inv, gains[0]),
    )
    grad_memory, first_back, first_scaled, first_gain, first_bias = cross_e[:5]
    norm_sums = jnp.stack([first_gain, second_gain, third_gain, first_bias, second_bias, third_bias])
    norm_total = jnp.sum(norm_sums, axis=1)
    first_back = after(first_back, *ffn_sum.second(), *cross_sum.first(cross_e[5]), norm_total)

    self_saved = [self_a[:5], self_b[:5], self_c[:5]]
    self_d = attention_bwd_call(
        self_scalars, first_back, [tokens], [w_qkv], w_self, self_saved, plan_of((1, 3)), halved,
        [first_scaled], None,
    )
    self_sum = Reduction(self_d[1])
    norm_total = norm_total + to_sibling(norm_total)
    gate = after(self_d[0], ffn_sum.third(), norm_total)
    self_e = attention_bwd_call(
        self_scalars, first_back, [tokens], [w_qkv], w_self, self_saved, plan_of((0, 2)), halved,
        [gate], None,
    )
    grad_tokens = self_e[0]
    own_sends = self_sum.first(self_e[1])
    cross_sum.second()
    ffn_sum.fourth()
    norm_total = norm_total + over_y(norm_total)
    self_sum.second()
    cross_sum.third()
    ffn_sum = ffn_sum.last()
    norm_total = norm_total + over_x(norm_total)
    self_sum.third()
    cross_sum.fourth()
    norm_total = norm_total + over_z_near(norm_total)
    self_sum.fourth()
    cross_sum = cross_sum.last()
    norm_total = norm_total + over_z_far(norm_total)
    self_sum = self_sum.last()

    def matrices(total):
        return total.reshape(2, UNIT, 4, UNIT).transpose(2, 1, 0, 3).reshape(4, UNIT, 2 * UNIT)

    self_grads, cross_grads = matrices(self_sum), matrices(cross_sum)
    ffn_grads = ffn_sum.transpose(1, 0, 2)
    return (
        out_rows,
        grad_tokens,
        grad_memory,
        self_grads[:3],
        self_grads[3].T,
        cross_grads[0],
        cross_grads[1:3],
        cross_grads[3].T,
        ffn_grads[:, :, :FFN_UNIT].reshape(UNIT, -1),
        ffn_grads[:, :, FFN_UNIT:].reshape(UNIT, -1).T,
        norm_total[:3],
        norm_total[3:],
    )


def sentence_fits(mesh, tokens, memory, dec_lengths):
    shape = dict(mesh.shape)
    rows = tokens.shape[0] // mesh.size
    sentences = dec_lengths.shape[1]
    return (
        shape["tensor"] == 4
        and shape["dp"] == 8
        and sentences == 4
        and rows == 512
        and memory.shape[0] // mesh.size == rows
        and tokens.shape[1] == 1024
    )


def smooth_gate(values):
    return jax.nn.gelu(values, approximate=True)


def norm_rows(hidden, norm_gain, norm_bias):
    center = hidden - jnp.mean(hidden, axis=-1, keepdims=True)
    inverse = lax.rsqrt(jnp.mean(center * center, axis=-1, keepdims=True) + NORM_EPSILON)
    normed = center * inverse
    return (normed * norm_gain + norm_bias, normed, inverse)


def norm_back(gradient, normed, inverse, norm_gain):
    scaled = gradient * norm_gain
    grad_in = inverse * (
        scaled
        - jnp.mean(scaled, axis=-1, keepdims=True)
        - normed * jnp.mean(scaled * normed, axis=-1, keepdims=True)
    )
    return (grad_in, jnp.sum(gradient * normed, axis=0), jnp.sum(gradient, axis=0))


def head_view(values, sentences):
    return values.reshape(sentences, -1, values.shape[1] // HEAD_DIM, HEAD_DIM)


def masked_scores(query_heads, key_heads, key_mask):
    scores = jnp.einsum(
        "sqhe,skhe->shqk", query_heads, key_heads, preferred_element_type=jnp.float32
    ) * HEAD_DIM ** (-0.5)
    return jnp.where(key_mask, scores, MASKED_SCORE)


def attention_forward(query_rows, key_rows, value_rows, key_mask, sentences):
    scores = masked_scores(
        head_view(query_rows, sentences), head_view(key_rows, sentences), key_mask
    )
    row_peak = jnp.max(scores, axis=-1, keepdims=True)
    exponent_terms = jnp.exp(scores - row_peak)
    row_sum = jnp.sum(exponent_terms, axis=-1, keepdims=True)
    softmax_probs = exponent_terms / row_sum
    attended = jnp.einsum(
        "shqk,skhe->sqhe",
        softmax_probs.astype(jnp.bfloat16),
        head_view(value_rows, sentences),
        preferred_element_type=jnp.float32,
    ).astype(jnp.bfloat16)
    return (attended.reshape(query_rows.shape), row_peak + jnp.log(row_sum))


def attention_backward(query_rows, key_rows, value_rows, key_mask, log_total, grad_rows, sentences):
    query_heads = head_view(query_rows, sentences)
    key_heads = head_view(key_rows, sentences)
    value_heads = head_view(value_rows, sentences)
    grad_heads = head_view(grad_rows, sentences)
    softmax_probs = jnp.exp(masked_scores(query_heads, key_heads, key_mask) - log_total)
    grad_probs = jnp.einsum(
        "sqhe,skhe->shqk", grad_heads, value_heads, preferred_element_type=jnp.float32
    )
    row_delta = jnp.sum(softmax_probs * grad_probs, axis=-1, keepdims=True)
    grad_scores = (softmax_probs * (grad_probs - row_delta)).astype(jnp.bfloat16)
    score_scale = HEAD_DIM ** (-0.5)
    grad_query = (
        jnp.einsum("shqk,skhe->sqhe", grad_scores, key_heads, preferred_element_type=jnp.float32)
        * score_scale
    ).astype(jnp.bfloat16)
    grad_key = (
        jnp.einsum("shqk,sqhe->skhe", grad_scores, query_heads, preferred_element_type=jnp.float32)
        * score_scale
    ).astype(jnp.bfloat16)
    grad_value = jnp.einsum(
        "shqk,sqhe->skhe",
        softmax_probs.astype(jnp.bfloat16),
        grad_heads,
        preferred_element_type=jnp.float32,
    ).astype(jnp.bfloat16)
    return (
        grad_query.reshape(query_rows.shape),
        grad_key.reshape(key_rows.shape),
        grad_value.reshape(value_rows.shape),
    )


def body(
    tokens,
    memory,
    dec_lengths,
    mem_lengths,
    self_qkv,
    self_out,
    cross_q,
    cross_kv,
    cross_out,
    ffn_in,
    ffn_out,
    norm_gains,
    norm_biases,
    cotangent,
):
    row_share = tokens.shape[0]
    sentences = dec_lengths.shape[1]
    all_tokens, all_memory = (
        lax.all_gather(tokens, "tensor", axis=0, tiled=True),
        lax.all_gather(memory, "tensor", axis=0, tiled=True),
    )
    sentence_len = all_tokens.shape[0] // sentences
    memory_len = all_memory.shape[0] // sentences
    positions = jnp.arange(sentence_len, dtype=jnp.int32)
    self_mask = (
        (positions[None, :] <= positions[:, None])[None]
        & (positions[None, None, :] < dec_lengths[0][:, None, None])
    )[:, None]
    memory_positions = jnp.arange(memory_len, dtype=jnp.int32)
    cross_mask = (memory_positions[None, :] < mem_lengths[0][:, None])[:, None, None, :]

    def branch_rows(attended, weight):
        return lax.psum_scatter(
            jnp.dot(attended, weight, preferred_element_type=jnp.float32).astype(jnp.bfloat16),
            "tensor",
            scatter_dimension=0,
            tiled=True,
        ).astype(jnp.float32)

    def branch_grad(grad_rows, attended, weight):
        grad_low = grad_rows.astype(jnp.bfloat16)
        grad_all = lax.all_gather(grad_low, "tensor", axis=0, tiled=True)
        grad_attended = jnp.dot(grad_all, weight.T, preferred_element_type=jnp.float32).astype(
            jnp.bfloat16
        )
        weight_part = jnp.dot(attended.T, grad_all, preferred_element_type=jnp.float32)
        return (grad_attended, weight_part)

    def gather_normed(values):
        return lax.all_gather(values, "tensor", axis=0, tiled=True)

    def head_input_sum(term):
        return lax.psum_scatter(
            term(jnp.int32(0), row_share * lax.axis_size("tensor")).astype(jnp.bfloat16),
            "tensor",
            scatter_dimension=0,
            tiled=True,
        ).astype(jnp.float32)

    self_proj = jnp.einsum(
        "td,cde->cte", all_tokens, self_qkv, preferred_element_type=jnp.float32
    ).astype(jnp.bfloat16)
    self_att, self_lse = attention_forward(
        self_proj[0], self_proj[1], self_proj[2], self_mask, sentences
    )
    self_branch = branch_rows(self_att, self_out)
    first_norm, first_hat, first_inv = norm_rows(
        RESIDUAL_ALPHA * tokens.astype(jnp.float32) + self_branch, norm_gains[0], norm_biases[0]
    )
    first_all = gather_normed(first_norm.astype(jnp.bfloat16))
    cross_query = jnp.dot(first_all, cross_q, preferred_element_type=jnp.float32).astype(
        jnp.bfloat16
    )
    cross_proj = jnp.einsum(
        "td,cde->cte", all_memory, cross_kv, preferred_element_type=jnp.float32
    ).astype(jnp.bfloat16)
    cross_att, cross_lse = attention_forward(
        cross_query, cross_proj[0], cross_proj[1], cross_mask, sentences
    )
    cross_branch = branch_rows(cross_att, cross_out)
    second_norm, second_hat, second_inv = norm_rows(
        RESIDUAL_ALPHA * first_norm + cross_branch, norm_gains[1], norm_biases[1]
    )
    second_all = gather_normed(second_norm.astype(jnp.bfloat16))
    pre_gate = jnp.dot(second_all, ffn_in, preferred_element_type=jnp.float32)
    activated = smooth_gate(pre_gate).astype(jnp.bfloat16)
    ffn_branch = lax.psum_scatter(
        jnp.dot(activated, ffn_out, preferred_element_type=jnp.float32).astype(jnp.bfloat16),
        "tensor",
        scatter_dimension=0,
        tiled=True,
    ).astype(jnp.float32)
    out_rows, third_hat, third_inv = norm_rows(
        RESIDUAL_ALPHA * second_norm + ffn_branch, norm_gains[2], norm_biases[2]
    )
    grad_third, third_gain, third_bias = norm_back(
        cotangent.astype(jnp.float32), third_hat, third_inv, norm_gains[2]
    )
    grad_ffn_all = lax.all_gather(grad_third.astype(jnp.bfloat16), "tensor", axis=0, tiled=True)
    unused_gate, gate_pull = jax.vjp(smooth_gate, pre_gate)
    grad_act = gate_pull(jnp.dot(grad_ffn_all, ffn_out.T, preferred_element_type=jnp.float32))[
        0
    ].astype(jnp.bfloat16)
    grad_ffn_out = jnp.dot(activated.T, grad_ffn_all, preferred_element_type=jnp.float32)
    grad_ffn_in = jnp.dot(second_all.T, grad_act, preferred_element_type=jnp.float32)
    grad_second = RESIDUAL_ALPHA * grad_third + lax.psum_scatter(
        jnp.dot(grad_act, ffn_in.T, preferred_element_type=jnp.float32).astype(jnp.bfloat16),
        "tensor",
        scatter_dimension=0,
        tiled=True,
    ).astype(jnp.float32)
    grad_second_in, second_gain, second_bias = norm_back(
        grad_second, second_hat, second_inv, norm_gains[1]
    )
    grad_cross_att, cross_out_part = branch_grad(grad_second_in, cross_att, cross_out)
    grad_cq, grad_ck, grad_cv = attention_backward(
        cross_query, cross_proj[0], cross_proj[1], cross_mask, cross_lse, grad_cross_att, sentences
    )
    grad_cross_q = jnp.dot(first_all.T, grad_cq, preferred_element_type=jnp.float32)
    cross_grads = jnp.stack([grad_ck, grad_cv])
    grad_cross_kv = jnp.einsum(
        "td,cte->cde", all_memory, cross_grads, preferred_element_type=jnp.float32
    )
    grad_memory = lax.psum_scatter(
        jnp.einsum("cte,cde->td", cross_grads, cross_kv, preferred_element_type=jnp.float32).astype(
            jnp.bfloat16
        ),
        "tensor",
        scatter_dimension=0,
        tiled=True,
    ).astype(jnp.float32)

    def cross_input_term(first_row, row_total):
        return jnp.dot(grad_cq, cross_q.T, preferred_element_type=jnp.float32)

    cross_input = head_input_sum(cross_input_term)
    grad_first = RESIDUAL_ALPHA * grad_second_in + cross_input
    grad_first_in, first_gain, first_bias = norm_back(
        grad_first, first_hat, first_inv, norm_gains[0]
    )
    grad_self_att, self_out_part = branch_grad(grad_first_in, self_att, self_out)
    grad_sq, grad_sk, grad_sv = attention_backward(
        self_proj[0], self_proj[1], self_proj[2], self_mask, self_lse, grad_self_att, sentences
    )
    self_grads = jnp.stack([grad_sq, grad_sk, grad_sv])
    grad_self_qkv = jnp.einsum(
        "td,cte->cde", all_tokens, self_grads, preferred_element_type=jnp.float32
    )

    def self_input_term(first_row, row_total):
        return jnp.einsum("cte,cde->td", self_grads, self_qkv, preferred_element_type=jnp.float32)

    self_input = head_input_sum(self_input_term)
    grad_tokens = RESIDUAL_ALPHA * grad_first_in + self_input
    summed = (
        lax.psum_scatter(
            grad_self_qkv.astype(jnp.bfloat16), "dp", scatter_dimension=1, tiled=True
        ).astype(jnp.float32),
        lax.psum_scatter(
            self_out_part.astype(jnp.bfloat16), "dp", scatter_dimension=1, tiled=True
        ).astype(jnp.float32),
        lax.psum_scatter(
            grad_cross_q.astype(jnp.bfloat16), "dp", scatter_dimension=0, tiled=True
        ).astype(jnp.float32),
        lax.psum_scatter(
            grad_cross_kv.astype(jnp.bfloat16), "dp", scatter_dimension=1, tiled=True
        ).astype(jnp.float32),
        lax.psum_scatter(
            cross_out_part.astype(jnp.bfloat16), "dp", scatter_dimension=1, tiled=True
        ).astype(jnp.float32),
        lax.psum_scatter(
            grad_ffn_in.astype(jnp.bfloat16), "dp", scatter_dimension=0, tiled=True
        ).astype(jnp.float32),
        lax.psum_scatter(
            grad_ffn_out.astype(jnp.bfloat16), "dp", scatter_dimension=1, tiled=True
        ).astype(jnp.float32),
    )
    gain_total, bias_total = lax.psum(
        (
            jnp.stack([first_gain, second_gain, third_gain]),
            jnp.stack([first_bias, second_bias, third_bias]),
        ),
        ("dp", "tensor"),
    )
    return (
        out_rows.astype(jnp.bfloat16),
        grad_tokens,
        grad_memory,
        summed[0],
        summed[1],
        summed[2],
        summed[3],
        summed[4],
        summed[5],
        summed[6],
        gain_total,
        bias_total,
    )


def solution(mesh):
    in_specs = (
        P(("dp", "tensor"), None),
        P(("dp", "tensor"), None),
        P("dp", None),
        P("dp", None),
        P(None, None, "tensor"),
        P("tensor", None),
        P(None, "tensor"),
        P(None, None, "tensor"),
        P("tensor", None),
        P(None, "tensor"),
        P("tensor", None),
        P(),
        P(),
        P(("dp", "tensor"), None),
    )
    out_specs = (
        P(("dp", "tensor"), None),
        P(("dp", "tensor"), None),
        P(("dp", "tensor"), None),
        P(None, "dp", "tensor"),
        P("tensor", "dp"),
        P("dp", "tensor"),
        P(None, "dp", "tensor"),
        P("tensor", "dp"),
        P("dp", "tensor"),
        P("tensor", "dp"),
        P(),
        P(),
    )

    def step(*args):
        chosen = sentence_body if sentence_fits(mesh, args[0], args[1], args[2]) else body
        return jax.shard_map(
            chosen, mesh=mesh, in_specs=in_specs, out_specs=out_specs, check_vma=False
        )(*args)

    return step
```

profile of v0, /device:TPU:0, one launch (start us, length us, event | category | flops | bytes accessed | tf_op | source)
XLA Modules:
  0.0 508.4 jit_solution(15183743176867948160)
XLA Ops:
  6.0 5.7 %collective-permute-done.5.refs_4_.refs_12_ = bf16[128,1024]{1,0:T(8,128)(2,1)S(1)} collective-permute-done((bf16[128,1024]{1,0:T(8,128)(2,1)S(1)}, bf16[128,1024]{1,0:T(8,128)(2,1)S(1)}, u32[]{:S(2)}, u32[]{:S(2)}) %collective-permute-start.5) | collective-permute-done | bytes 262176 | tf_op jit(solution)/shard_map/ppermute | solution.py:815
  23.6 20.6 %collective-permute-done.16.refs_7_.refs_19_.refs_23_ = bf16[128,1024]{1,0:T(8,128)(2,1)S(1)} collective-permute-done((bf16[128,1024]{1,0:T(8,128)(2,1)S(1)}, bf16[128,1024]{1,0:T(8,128)(2,1)S(1)}, u32[]{:S(2)}, u32[]{:S(2)}) %collective-permute-start.16) | collective-permute-done | bytes 262176 | tf_op jit(solution)/shard_map/ppermute | solution.py:815
  56.1 10.6 %self_fwd.3 = (bf16[4,512,128]{2,1,0:T(8,128)(2,1)}, bf16[4,512,128]{2,1,0:T(8,128)(2,1)}, bf16[4,512,128]{2,1,0:T(8,128)(2,1)}, bf16[4,512,128]{2,1,0:T(8,128)(...) custom-call(s32[4]{0:T(128)} %add_add_fusion.1.refs_0_, bf16[512,1024]{1,0:T(8,128)(2,1)} %refs_2_.15, ...), custom_call_target="tpu_custom_call" | custom-call | flops 9680000000 | bytes 4194304 | tf_op jit(solution)/shard_map/self_fwd/pallas_call | solution.py:334
  72.9 25.8 %collective-permute-done.14.refs_8_.refs_14_.refs_18_ = bf16[2,1024,128]{2,1,0:T(8,128)(2,1)} collective-permute-done((bf16[2,1024,128]{2,1,0:T(8,128)(2,1)}, bf16[2,1024,128]{2,1,0:T(8,128)(2,1)}, u32[]{:S(2)}, u32[]{:S(2)}) %collective-permute-start.14) | collective-permute-done | bytes 524320 | tf_op jit(solution)/shard_map/ppermute | solution.py:819
  107.5 8.5 %self_fwd.4 = (bf16[2,512,128]{2,1,0:T(8,128)(2,1)}, bf16[2,512,128]{2,1,0:T(8,128)(2,1)}, bf16[2,512,128]{2,1,0:T(8,128)(2,1)}, bf16[2,512,128]{2,1,0:T(8,128)(...) custom-call(s32[4]{0:T(128)} %add_add_fusion.1.refs_0_, bf16[512,1024]{1,0:T(8,128)(2,1)} %refs_2_.15, ...), custom_call_target="tpu_custom_call" | custom-call | flops 4840000000 | bytes 4194304 | tf_op jit(solution)/shard_map/self_fwd/pallas_call | solution.py:334
  116.7 11.1 %self_fwd.5 = (bf16[2,512,128]{2,1,0:T(8,128)(2,1)}, bf16[2,512,128]{2,1,0:T(8,128)(2,1)}, bf16[2,512,128]{2,1,0:T(8,128)(2,1)}, bf16[2,512,128]{2,1,0:T(8,128)(...) custom-call(s32[4]{0:T(128)} %add_add_fusion.1.refs_0_, ...), custom_call_target="tpu_custom_call" | custom-call | flops 4840000000 | bytes 4194304 | tf_op jit(solution)/shard_map/self_fwd/pallas_call | solution.py:334
  128.5 18.4 %collective-permute-done.27.refs_3_.refs_6_.refs_9_ = bf16[1024,512]{1,0:T(8,128)(2,1)} collective-permute-done((bf16[1024,512]{1,0:T(8,128)(2,1)S(1)}, bf16[1024,512]{1,0:T(8,128)(2,1)}, u32[]{:S(2)}, u32[]{:S(2)}) %collective-permute-start.27) | collective-permute-done | bytes 1048608 | tf_op jit(solution)/shard_map/ppermute | solution.py:815
  147.4 11.4 %cross_fwd.3 = (bf16[4,512,128]{2,1,0:T(8,128)(2,1)}, bf16[4,512,128]{2,1,0:T(8,128)(2,1)}, bf16[4,512,128]{2,1,0:T(8,128)(2,1)}, bf16[4,512,128]{2,1,0:T(8,128)...) custom-call(s32[4]{0:T(128)} %add_add_fusion.refs_0_, bf16[512,1024]{1,0:T(8,128)(2,1)} %get-tuple-element.104.refs_1_.refs_2_, ...), custom_call_target="tpu_custom_call" | custom-call | flops 9680000000 | bytes 4194304 | tf_op jit(solution)/shard_map/cross_fwd/pallas_call | solution.py:334
  158.8 9.5 %cross_fwd.4 = (bf16[2,512,128]{2,1,0:T(8,128)(2,1)}, bf16[2,512,128]{2,1,0:T(8,128)(2,1)}, bf16[2,512,128]{2,1,0:T(8,128)(2,1)}, bf16[2,512,128]{2,1,0:T(8,128)...) custom-call(s32[4]{0:T(128)} %add_add_fusion.refs_0_, bf16[512,1024]{1,0:T(8,128)(2,1)} %get-tuple-element.104.refs_1_.refs_2_, ...), custom_call_target="tpu_custom_call" | custom-call | flops 4840000000 | bytes 4194304 | tf_op jit(solution)/shard_map/cross_fwd/pallas_call | solution.py:334
  169.2 12.1 %cross_fwd.5 = (bf16[2,512,128]{2,1,0:T(8,128)(2,1)}, bf16[2,512,128]{2,1,0:T(8,128)(2,1)}, bf16[2,512,128]{2,1,0:T(8,128)(2,1)}, bf16[2,512,128]{2,1,0:T(8,128)...) custom-call(s32[4]{0:T(128)} %add_add_fusion.refs_0_, ...), custom_call_target="tpu_custom_call" | custom-call | flops 4840000000 | bytes 4194304 | tf_op jit(solution)/shard_map/cross_fwd/pallas_call | solution.py:334
  182.0 12.6 %ffn_fwd.3 = (f32[512,1024]{1,0:T(8,128)}, bf16[4,512,512]{2,1,0:T(8,128)(2,1)}, bf16[4,512,512]{2,1,0:T(8,128)(2,1)}) custom-call(s32[4]{0:T(128)} %add_add_fusion.refs_0_, bf16[512,1024]{1,0:T(8,128)(2,1)} %get-tuple-element.114.refs_1_.refs_2_, bf16[1024,1024]{1,0:T(8,128)(2,1)} %refs_7_.5, ...), custom_call_target="tpu_custom_call" | custom-call | flops 9680000000 | bytes 4194304 | tf_op jit(solution)/shard_map/ffn_fwd/pallas_call | solution.py:674
  195.6 8.1 %ffn_fwd.4 = (f32[512,1024]{1,0:T(8,128)}, bf16[2,512,512]{2,1,0:T(8,128)(2,1)}, bf16[2,512,512]{2,1,0:T(8,128)(2,1)}) custom-call(s32[4]{0:T(128)} %add_add_fusion.refs_0_, bf16[512,1024]{1,0:T(8,128)(2,1)} %get-tuple-element.114.refs_1_.refs_2_, f32[512,1024]{1,0:T(8,128)} %get-tuple-element.118.refs_2_, ...), custom_call_target="tpu_custom_call" | custom-call | flops 4840000000 | bytes 4194304 | tf_op jit(solution)/shard_map/ffn_fwd/pallas_call | solution.py:674
  204.7 11.7 %ffn_fwd.5 = (bf16[512,1024]{1,0:T(8,128)(2,1)}, bf16[512,1024]{1,0:T(8,128)(2,1)}, f32[512,1024]{1,0:T(8,128)}, f32[8,1024]{1,0:T(8,128)}, f32[8,1024]{1,0:T(8,...) custom-call(s32[4]{0:T(128)} %add_add_fusion.refs_0_, ...), custom_call_target="tpu_custom_call" | custom-call | flops 4840000000 | bytes 4194304 | tf_op jit(solution)/shard_map/ffn_fwd/pallas_call | solution.py:674
  216.4 16.5 %ffn_bwd.2 = (f32[512,1024]{1,0:T(8,128)}, bf16[4,8,128,1024]{3,2,1,0:T(8,128)(2,1)}) custom-call(s32[4]{0:T(128)} %add_add_fusion.refs_0_, bf16[512,1024]{1,0:T(8,128)(2,1)} %get-tuple-element.123.refs_1_, bf16[512,1024]{1,0:T(8,128)(2,1)} %get-tuple-element.114.refs_1_.refs_2_, f32[512,1024]{1,0:T(8,128)} %get-tuple-element.125.refs_3_, ...), custom_call_target="tpu_custom_call" | custom-call | flops 15840000000 | bytes 4194304 | tf_op jit(solution)/shard_map/ffn_bwd/pallas_call | solution.py:794
  233.2 17.7 %ffn_bwd.3 = (bf16[512,1024]{1,0:T(8,128)(2,1)}, f32[512,1024]{1,0:T(8,128)}, f32[8,1024]{1,0:T(8,128)}, f32[8,1024]{1,0:T(8,128)}, bf16[4,8,128,1024]{3,2,1,0:T(8,128)(2,1)}) custom-call(s32[4]{0:T(128)} %add_add_fusion.refs_0_, bf16[512,1024]{1,0:T(8,128)(2,1)} %get-tuple-element.123.refs_1_, bf16[512,1024]{1,0:T(8,128)(2,1)} %get-tuple-element.114.refs_1_.refs_2_, ...), custom_call_target="tpu_custom_call" | custom-call | flops 15840000000 | bytes 4194304 | tf_op jit(solution)/shard_map/ffn_bwd/pallas_call | solution.py:794
  258.8 19.0 %cross_bwd.2 = (f32[512,1024]{1,0:T(8,128)}, f32[512,1024]{1,0:T(8,128)}, bf16[4,8,128,512]{3,2,1,0:T(8,128)(2,1)}) custom-call(s32[4]{0:T(128)} %add_add_fusion.refs_0_, bf16[512,1024]{1,0:T(8,128)(2,1)} %get-tuple-element.136.refs_1_, bf16[512,1024]{1,0:T(8,128)(2,1)} %get-tuple-element.104.refs_1_.refs_2_, bf16[512,1024]{1,0:T(8,128)(2,1)} %refs_3_.5, ...), custom_call_target="tpu_custom_call" | custom-call | flops 15399999488 | bytes 4194304 | tf_op jit(solution)/shard_map/cross_bwd/pallas_call | solution.py:514
  281.2 21.7 %cross_bwd.3 = (f32[512,1024]{1,0:T(8,128)}, bf16[512,1024]{1,0:T(8,128)(2,1)}, f32[512,1024]{1,0:T(8,128)}, f32[8,1024]{1,0:T(8,128)}, f32[8,1024]{1,0:T(8,128)}, /*index=5*/bf16[4,8,128,512]{3,2,1,0:T(8,128)(2,1)}) custom-call(s32[4]{0:T(128)} %add_add_fusion.refs_0_, bf16[512,1024]{1,0:T(8,128)(2,1)} %get-tuple-element.136.refs_1_, ...), custom_call_target="tpu_custom_call" | custom-call | flops 15399999488 | bytes 4194304 | tf_op jit(solution)/shard_map/cross_bwd/pallas_call | solution.py:514
  304.5 21.4 %collective-permute-done.36 = bf16[1,8,128,1024]{3,2,1,0:T(8,128)(2,1)} collective-permute-done((bf16[1,8,128,1024]{3,2,1,0:T(8,128)(2,1)S(1)}, bf16[1,8,128,1024]{3,2,1,0:T(8,128)(2,1)}, u32[]{:S(2)}, u32[]{:S(2)}) %collective-permute-start.36) | collective-permute-done | bytes 2097184 | tf_op jit(solution)/shard_map/ppermute | solution.py:815
  336.2 16.5 %self_bwd.2 = (f32[512,1024]{1,0:T(8,128)}, bf16[4,8,128,512]{3,2,1,0:T(8,128)(2,1)}) custom-call(s32[4]{0:T(128)} %add_add_fusion.1.refs_0_, bf16[512,1024]{1,0:T(8,128)(2,1)} %get-tuple-element.165.refs_1_, bf16[512,1024]{1,0:T(8,128)(2,1)} %refs_2_.15, f32[512,1024]{1,0:T(8,128)} %get-tuple-element.166.refs_3_, bf16[3,1024,256]{2,1,0:T(8,128)(2,1)} %refs_4_.9, ...), custom_call_target="tpu_custom_call" | custom-call | flops 15399999488 | bytes 4194304 | tf_op jit(solution)/shard_map/self_bwd/pallas_call | solution.py:514
  361.6 18.9 %collective-permute-done.57 = f32[6,1024]{1,0:T(8,128)S(1)} collective-permute-done((f32[6,1024]{1,0:T(8,128)S(1)}, f32[6,1024]{1,0:T(8,128)S(1)}, u32[]{:S(2)}, u32[]{:S(2)}) %collective-permute-start.57) | collective-permute-done | bytes 24608 | tf_op jit(solution)/shard_map/ppermute | solution.py:815
  404.1 16.9 %self_bwd.3 = (f32[512,1024]{1,0:T(8,128)}, bf16[4,8,128,512]{3,2,1,0:T(8,128)(2,1)}) custom-call(s32[4]{0:T(128)} %add_add_fusion.1.refs_0_, bf16[512,1024]{1,0:T(8,128)(2,1)} %get-tuple-element.165.refs_1_, bf16[512,1024]{1,0:T(8,128)(2,1)} %refs_2_.15, f32[512,1024]{1,0:T(8,128)} %get-tuple-element.183.refs_3_, bf16[3,1024,256]{2,1,0:T(8,128)(2,1)} %refs_4_.9, ...), custom_call_target="tpu_custom_call" | custom-call | flops 15399999488 | bytes 4194304 | tf_op jit(solution)/shard_map/self_bwd/pallas_call | solution.py:514
  434.6 10.0 %collective-permute-done.56 = bf16[2,128,1024]{2,1,0:T(8,128)(2,1)S(1)} collective-permute-done((bf16[2,128,1024]{2,1,0:T(8,128)(2,1)S(1)}, bf16[2,128,1024]{2,1,0:T(8,128)(2,1)S(1)}, u32[]{:S(2)}, u32[]{:S(2)}) %collective-permute-start.56) | collective-permute-done | bytes 524320 | tf_op jit(solution)/shard_map/ppermute | solution.py:819
  453.9 10.1 %collective-permute-done.45 = bf16[2,1,4,128,512]{4,3,2,1,0:T(8,128)(2,1)S(1)} collective-permute-done((bf16[2,1,4,128,512]{4,3,2,1,0:T(8,128)(2,1)S(1)}, bf16[2,1,4,128,512]{4,3,2,1,0:T(8,128)(2,1)S(1)}, u32[]{:S(2)}, u32[]{:S(2)}) %collective-permute-start.45) | collective-permute-done | bytes 1048608 | tf_op jit(solution)/shard_map/ppermute | solution.py:819
  487.1 6.5 %collective-permute-done.47 = bf16[2,2,128,512]{3,2,1,0:T(8,128)(2,1)} collective-permute-done((bf16[2,2,128,512]{3,2,1,0:T(8,128)(2,1)}, bf16[2,2,128,512]{3,2,1,0:T(8,128)(2,1)}, u32[]{:S(2)}, u32[]{:S(2)}) %collective-permute-start.47) | collective-permute-done | bytes 524320 | tf_op jit(solution)/shard_map/ppermute | solution.py:819
  (243 shorter events, 165.2 us)
Async XLA Ops:
  0.7 55.2 %collective-permute-start.1 = (bf16[3,1024,256]{2,1,0:T(8,128)(2,1)}, bf16[3,1024,256]{2,1,0:T(8,128)(2,1)}, u32[]{:S(2)}, u32[]{:S(2)}) collective-permute-start(bf16[3,1024,256]{2,1,0:T(8,128)(2,1)} %refs_4_.9), channel_id=1, source_target_pairs={{0,1},{1,0},{2,3},{3,2},{4,5},{5,4},{6,7},{7,6},{8,9},{9,8},{10,11... | collective-permute-start | bytes 4718600 | tf_op jit(solution)/shard_map/ppermute | solution.py:811
  4.9 39.2 %collective-permute-start.2 = (bf16[256,1024]{1,0:T(8,128)(2,1)}, bf16[256,1024]{1,0:T(8,128)(2,1)}, u32[]{:S(2)}, u32[]{:S(2)}) collective-permute-start(bf16[256,1024]{1,0:T(8,128)(2,1)} %refs_10_.5), channel_id=1, source_target_pairs={{0,1},{1,0},{2,3},{3,2},{4,5},{5,4},{6,7},{7,6},{8,9},{9,8},{10,11... | collective-permute-start | bytes 1572872 | tf_op jit(solution)/shard_map/ppermute | solution.py:811
  15.4 38.9 %collective-permute-start = (bf16[3,1024,128]{2,1,0:T(8,128)(2,1)S(1)}, bf16[3,1024,128]{2,1,0:T(8,128)(2,1)}, u32[]{:S(2)}, u32[]{:S(2)}) collective-permute-start(bf16[3,1024,128]{2,1,0:T(8,128)(2,1)S(1)} %constant_dynamic-slice_fusion.6), channel_id=1, source_target_pairs={{0,2},{1,3},{2,0},{3,1},{4,6},{5,7},{6,4},{7,5},{8,10},{9,11},{10,... | collective-permute-start | bytes 2359304 | tf_op jit(solution)/shard_map/ppermute | solution.py:815
  21.8 32.5 %collective-permute-start.13 = (bf16[2,1024,128]{2,1,0:T(8,128)(2,1)S(1)}, bf16[2,1024,128]{2,1,0:T(8,128)(2,1)}, u32[]{:S(2)}, u32[]{:S(2)}) collective-permute-start(bf16[2,1024,128]{2,1,0:T(8,128)(2,1)S(1)} %constant_dynamic-slice_fusion.3), channel_id=1, source_target_pairs={{0,2},{1,3},{2,0},{3,1},{4,6},{5,7},{6,4},{7,5},{8,10},{9,11},{10,... | collective-permute-start | bytes 1572872 | tf_op jit(solution)/shard_map/ppermute | solution.py:815
  66.8 38.4 %collective-permute-start.3 = (bf16[3,1024,128]{2,1,0:T(8,128)(2,1)}, bf16[3,1024,128]{2,1,0:T(8,128)(2,1)}, u32[]{:S(2)}, u32[]{:S(2)}) collective-permute-start(bf16[3,1024,128]{2,1,0:T(8,128)(2,1)} %collective-permute-done.refs_2_.refs_6_), channel_id=1, source_target_pairs={{0,4},{4,0},{8,12},{12,8},{16,20},{20,16},{24,28},{28,24},{1,5},{5... | collective-permute-start | bytes 2359304 | tf_op jit(solution)/shard_map/ppermute | solution.py:819
  67.8 30.9 %collective-permute-start.14 = (bf16[2,1024,128]{2,1,0:T(8,128)(2,1)}, bf16[2,1024,128]{2,1,0:T(8,128)(2,1)}, u32[]{:S(2)}, u32[]{:S(2)}) collective-permute-start(bf16[2,1024,128]{2,1,0:T(8,128)(2,1)} %collective-permute-done.13.refs_5_.refs_13_.refs_17_), channel_id=1, source_target_pairs={{0,4},{4,0},{8,12},{12,8},{16,20},{20,16},{24,28},{28,24},{1,5},{5... | collective-permute-start | bytes 1572872 | tf_op jit(solution)/shard_map/ppermute | solution.py:819
  69.4 37.6 %collective-permute-start.8 = (bf16[3,1024,128]{2,1,0:T(8,128)(2,1)}, bf16[3,1024,128]{2,1,0:T(8,128)(2,1)}, u32[]{:S(2)}, u32[]{:S(2)}) collective-permute-start(bf16[3,1024,128]{2,1,0:T(8,128)(2,1)} %collective-permute-done.refs_2_.refs_6_), channel_id=1, source_target_pairs={{0,1},{1,0},{2,3},{3,2},{4,5},{5,4},{6,7},{7,6},{8,9},{9,8},{10,11... | collective-permute-start | bytes 2359304 | tf_op jit(solution)/shard_map/ppermute | solution.py:811
  69.6 29.1 %collective-permute-start.9 = (bf16[128,1024]{1,0:T(8,128)(2,1)S(1)}, bf16[128,1024]{1,0:T(8,128)(2,1)S(1)}, u32[]{:S(2)}, u32[]{:S(2)}) collective-permute-start(bf16[128,1024]{1,0:T(8,128)(2,1)S(1)} %copy-done.22), channel_id=1, source_target_pairs={{0,1},{1,0},{2,3},{3,2},{4,5},{5,4},{6,7},{7,6},{8,9},{9,8},{10,11... | collective-permute-start | bytes 786440 | tf_op jit(solution)/shard_map/ppermute | solution.py:811
  71.0 32.6 %collective-permute-start.6 = (bf16[128,1024]{1,0:T(8,128)(2,1)S(1)}, bf16[128,1024]{1,0:T(8,128)(2,1)S(1)}, u32[]{:S(2)}, u32[]{:S(2)}) collective-permute-start(bf16[128,1024]{1,0:T(8,128)(2,1)S(1)} %copy-done.22), channel_id=1, source_target_pairs={{0,4},{4,0},{8,12},{12,8},{16,20},{20,16},{24,28},{28,24},{1,5},{5... | collective-permute-start | bytes 786440 | tf_op jit(solution)/shard_map/ppermute | solution.py:819
  98.8 29.2 %collective-permute-start.29 = (bf16[512,1024]{1,0:T(8,128)(2,1)S(1)}, bf16[512,1024]{1,0:T(8,128)(2,1)}, u32[]{:S(2)}, u32[]{:S(2)}) collective-permute-start(bf16[512,1024]{1,0:T(8,128)(2,1)S(1)} %constant_dynamic-slice_fusion), channel_id=1, source_target_pairs={{0,2},{1,3},{2,0},{3,1},{4,6},{5,7},{6,4},{7,5},{8,10},{9,11},{10,... | collective-permute-start | bytes 3145736 | tf_op jit(solution)/shard_map/ppermute | solution.py:815
  103.6 43.3 %collective-permute-start.27 = (bf16[1024,512]{1,0:T(8,128)(2,1)S(1)}, bf16[1024,512]{1,0:T(8,128)(2,1)}, u32[]{:S(2)}, u32[]{:S(2)}) collective-permute-start(bf16[1024,512]{1,0:T(8,128)(2,1)S(1)} %constant_dynamic-slice_fusion.1), channel_id=1, source_target_pairs={{0,2},{1,3},{2,0},{3,1},{4,6},{5,7},{6,4},{7,5},{8,10},{9,11},{10,... | collective-permute-start | bytes 3145736 | tf_op jit(solution)/shard_map/ppermute | solution.py:815
  116.0 65.5 %collective-permute-start.25 = (bf16[1024,1024]{1,0:T(8,128)(2,1)S(1)}, bf16[1024,1024]{1,0:T(8,128)(2,1)}, u32[]{:S(2)}, u32[]{:S(2)}) collective-permute-start(bf16[1024,1024]{1,0:T(8,128)(2,1)S(1)} %copy-done.2), channel_id=1, source_target_pairs={{0,1},{1,0},{2,3},{3,2},{4,5},{5,4},{6,7},{7,6},{8,9},{9,8},{10,11... | collective-permute-start | bytes 6291464 | tf_op jit(solution)/shard_map/ppermute | solution.py:811
  116.1 65.8 %collective-permute-start.26 = (bf16[1024,1024]{1,0:T(8,128)(2,1)S(1)}, bf16[1024,1024]{1,0:T(8,128)(2,1)}, u32[]{:S(2)}, u32[]{:S(2)}) collective-permute-start(bf16[1024,1024]{1,0:T(8,128)(2,1)S(1)} %copy-done.3), channel_id=1, source_target_pairs={{0,1},{1,0},{2,3},{3,2},{4,5},{5,4},{6,7},{7,6},{8,9},{9,8},{10,11... | collective-permute-start | bytes 6291464 | tf_op jit(solution)/shard_map/ppermute | solution.py:811
  127.8 40.5 %collective-permute-start.15 = (bf16[2,1024,128]{2,1,0:T(8,128)(2,1)}, bf16[2,1024,128]{2,1,0:T(8,128)(2,1)S(1)}, u32[]{:S(2)}, u32[]{:S(2)}) collective-permute-start(bf16[2,1024,128]{2,1,0:T(8,128)(2,1)} %collective-permute-done.14.refs_8_.refs_14_.refs_18_), channel_id=1, source_target_pairs={{0,1},{1,0},{2,3},{3,2},{4,5},{5,4},{6,7},{7,6},{8,9},{9,8},{10,11... | collective-permute-start | bytes 1572872 | tf_op jit(solution)/shard_map/ppermute | solution.py:811
  127.9 40.5 %collective-permute-start.33 = (bf16[512,1024]{1,0:T(8,128)(2,1)}, bf16[512,1024]{1,0:T(8,128)(2,1)S(1)}, u32[]{:S(2)}, u32[]{:S(2)}) collective-permute-start(bf16[512,1024]{1,0:T(8,128)(2,1)} %collective-permute-done.29.refs_5_.refs_12_.refs_15_), channel_id=1, source_target_pairs={{0,4},{4,0},{8,12},{12,8},{16,20},{20,16},{24,28},{28,24},{1,5},{5... | collective-permute-start | bytes 3145736 | tf_op jit(solution)/shard_map/ppermute | solution.py:819
  146.9 34.4 %collective-permute-start.31 = (bf16[1024,512]{1,0:T(8,128)(2,1)}, bf16[1024,512]{1,0:T(8,128)(2,1)S(1)}, u32[]{:S(2)}, u32[]{:S(2)}) collective-permute-start(bf16[1024,512]{1,0:T(8,128)(2,1)} %collective-permute-done.27.refs_3_.refs_6_.refs_9_), channel_id=1, source_target_pairs={{0,4},{4,0},{8,12},{12,8},{16,20},{20,16},{24,28},{28,24},{1,5},{5... | collective-permute-start | bytes 3145736 | tf_op jit(solution)/shard_map/ppermute | solution.py:819
  277.7 54.4 %collective-permute-start.38 = (bf16[4,8,128,512]{3,2,1,0:T(8,128)(2,1)}, bf16[4,8,128,512]{3,2,1,0:T(8,128)(2,1)}, u32[]{:S(2)}, u32[]{:S(2)}) collective-permute-start(bf16[4,8,128,512]{3,2,1,0:T(8,128)(2,1)} %get-tuple-element.158), channel_id=1, source_target_pairs={{0,1},{1,0},{2,3},{3,2},{4,5},{5,4},{6,7},{7,6},{8,9},{9,8},{10,11... | collective-permute-start | bytes 12582920 | tf_op jit(solution)/shard_map/ppermute | solution.py:811
  278.2 47.8 %collective-permute-start.36 = (bf16[1,8,128,1024]{3,2,1,0:T(8,128)(2,1)S(1)}, bf16[1,8,128,1024]{3,2,1,0:T(8,128)(2,1)}, u32[]{:S(2)}, u32[]{:S(2)}) collective-permute-start(bf16[1,8,128,1024]{3,2,1,0:T(8,128)(2,1)S(1)} %add_convert_fusion.1), channel_id=1, source_target_pairs={{0,2},{1,3},{2,0},{3,1},{4,6},{5,7},{6,4},{7,5},{8,10},{9,11},{10,... | collective-permute-start | bytes 6291464 | tf_op jit(solution)/shard_map/ppermute | solution.py:815
  279.8 48.7 %collective-permute-start.37 = (bf16[2,1,4,128,1024]{4,3,2,1,0:T(8,128)(2,1)}, bf16[2,1,4,128,1024]{4,3,2,1,0:T(8,128)(2,1)}, u32[]{:S(2)}, u32[]{:S(2)}) collective-permute-start(bf16[2,1,4,128,1024]{4,3,2,1,0:T(8,128)(2,1)} %add_convert_fusion), channel_id=1, source_target_pairs={{0,4},{4,0},{8,12},{12,8},{16,20},{20,16},{24,28},{28,24},{1,5},{5... | collective-permute-start | bytes 6291464 | tf_op jit(solution)/shard_map/ppermute | solution.py:819
  352.7 75.9 %collective-permute-start.42 = (bf16[4,8,128,512]{3,2,1,0:T(8,128)(2,1)}, bf16[4,8,128,512]{3,2,1,0:T(8,128)(2,1)}, u32[]{:S(2)}, u32[]{:S(2)}) collective-permute-start(bf16[4,8,128,512]{3,2,1,0:T(8,128)(2,1)} %get-tuple-element.187), channel_id=1, source_target_pairs={{0,1},{1,0},{2,3},{3,2},{4,5},{5,4},{6,7},{7,6},{8,9},{9,8},{10,11... | collective-permute-start | bytes 12582920 | tf_op jit(solution)/shard_map/ppermute | solution.py:811
  352.8 41.0 %collective-permute-start.39 = (bf16[1,4,128,1024]{3,2,1,0:T(8,128)(2,1)S(1)}, bf16[1,4,128,1024]{3,2,1,0:T(8,128)(2,1)S(1)}, u32[]{:S(2)}, u32[]{:S(2)}) collective-permute-start(bf16[1,4,128,1024]{3,2,1,0:T(8,128)(2,1)S(1)} %add_convert_fusion.9), channel_id=1, source_target_pairs={{0,4},{4,0},{8,12},{12,8},{16,20},{20,16},{24,28},{28,24},{1,5},{5... | collective-permute-start | bytes 3145736 | tf_op jit(solution)/shard_map/ppermute | solution.py:819
  354.3 42.2 %collective-permute-start.40 = (bf16[1,4,128,1024]{3,2,1,0:T(8,128)(2,1)}, bf16[1,4,128,1024]{3,2,1,0:T(8,128)(2,1)S(1)}, u32[]{:S(2)}, u32[]{:S(2)}) collective-permute-start(bf16[1,4,128,1024]{3,2,1,0:T(8,128)(2,1)} %fusion.1), channel_id=1, source_target_pairs={{0,2},{1,3},{2,0},{3,1},{4,6},{5,7},{6,4},{7,5},{8,10},{9,11},{10,... | collective-permute-start | bytes 3145736 | tf_op jit(solution)/shard_map/ppermute | solution.py:815
  403.5 41.4 %collective-permute-start.51 = (bf16[2,1,4,128,512]{4,3,2,1,0:T(8,128)(2,1)S(1)}, bf16[2,1,4,128,512]{4,3,2,1,0:T(8,128)(2,1)}, u32[]{:S(2)}, u32[]{:S(2)}) collective-permute-start(bf16[2,1,4,128,512]{4,3,2,1,0:T(8,128)(2,1)S(1)} %add_convert_fusion.6), channel_id=1, source_target_pairs={{0,4},{4,0},{8,12},{12,8},{16,20},{20,16},{24,28},{28,24},{1,5},{5... | collective-permute-start | bytes 3145736 | tf_op jit(solution)/shard_map/ppermute | solution.py:819
  433.1 30.9 %collective-permute-start.45 = (bf16[2,1,4,128,512]{4,3,2,1,0:T(8,128)(2,1)S(1)}, bf16[2,1,4,128,512]{4,3,2,1,0:T(8,128)(2,1)S(1)}, u32[]{:S(2)}, u32[]{:S(2)}) collective-permute-start(bf16[2,1,4,128,512]{4,3,2,1,0:T(8,128)(2,1)S(1)} %add_convert_fusion.3), channel_id=1, source_target_pairs={{0,4},{4,0},{8,12},{12,8},{16,20},{20,16},{24,28},{28,24},{1,5},{5... | collective-permute-start | bytes 3145736 | tf_op jit(solution)/shard_map/ppermute | solution.py:819
  (66 other events, 943.6 us)
where the time goes:
time: 512 us; the launch traced here: 508 us
  Pallas kernels  204 us (40%)
  waiting for transfers between devices  179 us (35%)
  starting transfers between devices  57.3 us (11%)
  other arithmetic  47.7 us (9%)
  local copies, waits for them, and re-layouts  19.2 us (4%)
    ppermute x14, waiting for transfers between devices, over_y(): return lax.ppermute(values, 'tensor', swap_pairs(4, 2))  94.7 us
    ppermute x22, waiting for transfers between devices, over_dp(): return lax.ppermute(values, 'dp', swap_pairs(8, mask))  79.7 us
    pallas_call x4, Pallas kernels, attention_bwd_call(): pl.pallas_call(kernel, out_shape=shapes, in_specs=specs + [ANY] * len(tai...  74 us
    pallas_call x6, Pallas kernels, attention_fwd_call(): pl.pallas_call(kernel, out_shape=shapes, in_specs=specs, out_specs=[VMEM]...  63.3 us
    convert_element_type x21, other arithmetic, add(): return total.astype(BF16)  41.9 us
    pallas_call x2, Pallas kernels, ffn_bwd_call(): pl.pallas_call(kernel, out_shape=shapes, in_specs=specs + [ANY] * len(tai...  34.3 us
    pallas_call x3, Pallas kernels, ffn_fwd_call(): pl.pallas_call(kernel, out_shape=shapes, in_specs=specs + [ANY] * len(tai...  32.4 us
    ppermute x22, starting transfers between devices, over_dp(): return lax.ppermute(values, 'dp', swap_pairs(8, mask))  29.9 us
  transfers between devices with their start and end apart: 61, of which 23 were waited for; matrix products, arithmetic and copies ran while one was open for 10% of the time, Pallas kernels for 28%

commit v1 on v0

--- a/solution.py
+++ b/solution.py
@@ -184,12 +184,6 @@
     lax.fori_loop(0, rows // ROW_CHUNK, step, 0)
 
 
-def natural_index(u, per_piece, split, swap):
-    per_part = per_piece // split
-    inner = lax.rem(u, per_piece)
-    return (u - inner) + ((inner // per_part) ^ swap) * per_part + lax.rem(inner, per_part)
-
-
 def transpose_shards(source, target, dp):
     for position in range(8):
         block = dp ^ shard_of(position)
@@ -216,74 +210,69 @@
     return jax.ShapeDtypeStruct(shape, dtype)
 
 
-def attention_fwd_call(scalars, residual, others, weights, outs, plan, halved, partial, gain, bias):
+def pack_copies(packs, plan, number, order, buffer, sems):
+    groups = []
+    for matrix in range(4):
+        copies = []
+        for index, (array, half, relative) in enumerate(plan):
+            quarter = half + 2 * (matrix // 2)
+            if relative:
+                quarter = quarter ^ order
+            low = (matrix * number + index) * UNIT
+            copies.append(
+                copy_of(packs[array].at[quarter, matrix % 2], buffer.at[:, low : low + UNIT], sems.at[matrix, index])
+            )
+        groups.append(copies)
+    return groups
+
+
+def attention_fwd_call(scalars, residual, others, packs, plan, partial, norm):
     rows, depth = others[0].shape
     causal = len(others) == 1
-    number = len(plan)
-    last = gain is not None
-    n_in, n_w, n_o = len(others), len(weights), len(outs)
-    flat_w = [a for a in weights]
-    has_partial = partial is not None
+    number, wide = len(plan), len(plan) * UNIT
+    last, has_partial = norm is not None, partial is not None
 
     def kernel(*refs):
         it = iter(refs)
         sc = next(it)
-        in_refs = [next(it) for _ in range(n_in)]
-        res_refs = [next(it) for _ in residual] if last else []
-        w_refs = [[next(it) for _ in group] for group in flat_w]
-        o_refs = [next(it) for _ in range(n_o)]
-        part_ref = next(it) if has_partial else None
+        in_refs = [next(it) for _ in others]
         gain_ref, bias_ref = (next(it), next(it)) if last else (None, None)
+        old_rows = [next(it) for _ in residual[1:]] if last else []
+        res_in = next(it) if last else None
+        part_in = next(it) if has_partial else None
+        w_refs = [next(it) for _ in packs]
         q_ref, k_ref, v_ref, att_ref, lse_ref = (next(it) for _ in range(5))
         if last:
             low_ref, hat_ref, inv_ref = next(it), next(it), next(it)
         else:
             sum_ref = next(it)
-        wbuf, obuf, att_all, diagonal, acc, wsem, osem = (next(it) for _ in range(7))
-        length, swap = sc[0], sc[1]
-
-        def offset(unit):
-            array, half = unit
-            if not halved[array]:
-                return 0
-            return pl.multiple_of((half ^ swap) * UNIT, UNIT)
-
-        def w_copies():
-            groups, column = [], 0
-            for group in w_refs:
-                stacked = len(group[0].shape) == 3
-                for c in range(group[0].shape[0] if stacked else 1):
-                    copies = []
-                    for index, unit in enumerate(plan):
-                        at = pl.ds(offset(unit), UNIT)
-                        ref = group[unit[0]]
-                        lanes = slice((column * number + index) * UNIT, (column * number + index + 1) * UNIT)
-                        copies.append(copy_of(ref.at[c, :, at] if stacked else ref.at[:, at], wbuf.at[:, lanes], wsem.at[column, index]))
-                    groups.append(copies)
-                    column += 1
-            return groups
-
-        groups = w_copies()
-        o_copies = [
-            copy_of(o_refs[unit[0]].at[pl.ds(offset(unit), UNIT), :], obuf.at[index * UNIT : (index + 1) * UNIT, :], osem.at[index])
-            for index, unit in enumerate(plan)
-        ]
+        wbuf, att_all, diagonal, wsem, lsem = (next(it) for _ in range(5))
+        if last:
+            acc, old = next(it), next(it)
+        length, order = sc[0], sc[1]
+        groups = pack_copies(w_refs, plan, number, order, wbuf, wsem)
         for copies in groups:
             for copy in copies:
                 copy.start()
-        for copy in o_copies:
+        target = acc if last else sum_ref
+        late = []
+        if has_partial:
+            late.append(copy_of(part_in, target, lsem.at[0]))
+        if last:
+            late.append(copy_of(res_in, old, lsem.at[1]))
+        for copy in late:
             copy.start()
         if causal:
             fill_diagonal(diagonal)
-        for c, target in enumerate((q_ref, k_ref, v_ref)):
+        for c, result in enumerate((q_ref, k_ref, v_ref)):
             for copy in groups[c]:
                 copy.wait()
             rows_in = in_refs[0] if causal or c == 0 else in_refs[1]
-            proj = dot(rows_in[...], wbuf[:, c * number * UNIT : (c + 1) * number * UNIT]).astype(BF16)
+            proj = dot(rows_in[...], wbuf[:, c * wide : (c + 1) * wide]).astype(BF16)
             if c == 0:
                 proj = (proj.astype(F32) * SCORE_SCALE).astype(BF16)
             for index in range(number):
-                target[index] = proj[:, index * UNIT : (index + 1) * UNIT]
+                result[index] = proj[:, index * UNIT : (index + 1) * UNIT]
 
         def step(u, carry):
             attended = attend_unit(q_ref[u], k_ref[u], v_ref[u], length, causal, diagonal, lse_ref.at[u])
@@ -292,20 +281,18 @@
             return carry
 
         lax.fori_loop(0, number, step, 0)
-        for copy in o_copies:
+        for copy in groups[3] + late:
             copy.wait()
-        target = acc if last else sum_ref
         if has_partial:
-            target[...] = part_ref[...] + dot(att_all[...], obuf[...])
+            target[...] += dot_nt(att_all[...], wbuf[:, 3 * wide :])
         else:
-            target[...] = dot(att_all[...], obuf[...])
+            target[...] = dot_nt(att_all[...], wbuf[:, 3 * wide :])
         if last:
             def chunk(at):
-                if len(res_refs) == 1:
-                    old = res_refs[0][at, :].astype(F32)
-                else:
-                    old = res_refs[0][at, :] * res_refs[1][...] + res_refs[2][...]
-                normed, hat, inverse = norm_chunk(RESIDUAL_ALPHA * old + acc[at, :], gain_ref[...], bias_ref[...])
+                before = old[at, :].astype(F32)
+                if old_rows:
+                    before = before * old_rows[0][...] + old_rows[1][...]
+                normed, hat, inverse = norm_chunk(RESIDUAL_ALPHA * before + acc[at, :], gain_ref[...], bias_ref[...])
                 low_ref[at, :] = normed.astype(BF16)
                 hat_ref[at, :] = hat
                 inv_ref[at, :] = jnp.broadcast_to(inverse, (ROW_CHUNK, 128))
@@ -318,43 +305,35 @@
         shapes += [sds((rows, depth), BF16), sds((rows, depth), F32), sds((rows, 128), F32)]
     else:
         shapes += [sds((rows, depth), F32)]
-    args = [scalars, *others] + (list(residual) if last else [])
-    specs = [SMEM] + [VMEM] * (len(args) - 1)
-    for group in flat_w:
-        args += group
-        specs += [ANY] * len(group)
-    args += outs
-    specs += [ANY] * n_o
-    if has_partial:
-        args.append(partial)
-        specs.append(VMEM)
+    args = [scalars, *others]
     if last:
-        args += [gain, bias]
-        specs += [VMEM, VMEM]
+        args += [*norm, *residual[1:]]
+    tail = ([residual[0]] if last else []) + ([partial] if has_partial else []) + list(packs)
+    scratch = [
+        pltpu.VMEM((depth, 4 * wide), BF16),
+        pltpu.VMEM((rows, wide), BF16),
+        pltpu.VMEM((QUERY_BLOCK, QUERY_BLOCK), F32),
+        pltpu.SemaphoreType.DMA((4, number)),
+        pltpu.SemaphoreType.DMA((2,)),
+    ]
+    if last:
+        scratch += [pltpu.VMEM((rows, depth), F32), pltpu.VMEM((rows, depth), residual[0].dtype)]
     return pl.pallas_call(
         kernel,
         out_shape=shapes,
-        in_specs=specs,
+        in_specs=[SMEM] + [VMEM] * (len(args) - 1) + [ANY] * len(tail),
         out_specs=[VMEM] * len(shapes),
-        scratch_shapes=[
-            pltpu.VMEM((depth, 3 * number * UNIT), BF16),
-            pltpu.VMEM((number * UNIT, depth), BF16),
-            pltpu.VMEM((rows, number * UNIT), BF16),
-            pltpu.VMEM((QUERY_BLOCK, QUERY_BLOCK), F32),
-            pltpu.VMEM((rows, depth) if last else (8, 128), F32),
-            pltpu.SemaphoreType.DMA((3, number)),
-            pltpu.SemaphoreType.DMA((number,)),
-        ],
+        scratch_shapes=scratch,
         compiler_params=params(),
-        cost_estimate=cost_of(number * 2.2),
+        cost_estimate=cost_of(2.7 * number),
         name="self_fwd" if causal else "cross_fwd",
-    )(*args)
-
-
-def attention_bwd_call(scalars, grad_low, others, weights, outs, saved, plan, halved, carried, norm):
+    )(*args, *tail)
+
+
+def attention_bwd_call(scalars, grad_low, others, packs, saved, plan, carried, norm, results=1):
     rows, depth = grad_low.shape
     causal = len(others) == 1
-    number, n_in = len(plan), len(others)
+    number, n_in, wide = len(plan), len(others), len(plan) * UNIT
     last = norm is not None
 
     def kernel(*refs):
@@ -362,64 +341,49 @@
         sc = next(it)
         h_ref = next(it)
         in_refs = [next(it) for _ in range(n_in)]
-        acc_in = [next(it) for _ in carried]
         gain_ref = next(it) if last else None
         late_in = [next(it), next(it)] if last else []
-        w_refs = [[next(it) for _ in group] for group in weights]
-        o_refs = [next(it) for _ in outs]
+        acc_in = [next(it) for _ in carried]
+        w_refs = [next(it) for _ in packs]
         s_refs = [[next(it) for _ in call] for call in saved]
-        sums = [next(it) for _ in range(n_in)] if not last else [None] + [next(it) for _ in range(n_in - 1)]
+        sums = [None if last and not index else next(it) for index in range(n_in)]
         if last:
             low_ref, scaled_ref, gsum_ref, bsum_ref = (next(it) for _ in range(4))
-        g_ref = next(it)
-        wbuf, obuf, sbuf, lbuf, att_all, grad_all, h_t = (next(it) for _ in range(7))
+        g_refs = [next(it) for _ in range(results)]
+        wbuf, sbuf, lbuf, att_all, grad_all, h_t = (next(it) for _ in range(6))
         in_t = [next(it) for _ in range(n_in)]
         dall, stage, diagonal = next(it), next(it), next(it)
         if last:
             acc, hat, inv = next(it), next(it), next(it)
-            lsem = next(it)
-        wsem, ssem, gsem = next(it), next(it), next(it)
-        length, swap, dp = sc[0], sc[1], sc[2]
-        if last:
             sums[0] = acc
-        wide = number * UNIT
-
-        def offset(unit):
-            if not halved[unit[0]]:
-                return 0
-            return pl.multiple_of((unit[1] ^ swap) * UNIT, UNIT)
-
-        o_copies, s_copies, w_copies = [], [], []
+        wsem, ssem, gsem, lsem = (next(it) for _ in range(4))
+        length, order, dp = sc[0], sc[1], sc[2]
+
+        groups = pack_copies(w_refs, [unit[:3] for unit in plan], number, order, wbuf, wsem)
+        for copy in groups[3]:
+            copy.start()
+        s_copies = []
         for index, unit in enumerate(plan):
-            at = pl.ds(offset(unit), UNIT)
             lanes = slice(index * UNIT, (index + 1) * UNIT)
-            o_copies.append(copy_of(o_refs[unit[0]].at[at, :], obuf.at[lanes, :], wsem.at[3, index]))
-            call = s_refs[unit[2]]
+            call = s_refs[unit[3]]
             for c in range(3):
-                s_copies.append(copy_of(call[c].at[unit[3]], sbuf.at[index, c], ssem.at[c, index]))
-            s_copies.append(copy_of(call[3].at[unit[3]], att_all.at[:, lanes], ssem.at[3, index]))
-            s_copies.append(copy_of(call[4].at[unit[3]], lbuf.at[index], ssem.at[4, index]))
-            column = 0
-            for group in w_refs:
-                ref = group[unit[0]]
-                for source in [ref.at[:, at]] if len(ref.shape) == 2 else [ref.at[c, :, at] for c in range(ref.shape[0])]:
-                    low = (column * number + index) * UNIT
-                    w_copies.append(copy_of(source, wbuf.at[:, low : low + UNIT], wsem.at[column, index]))
-                    column += 1
-        for copy in o_copies + s_copies + w_copies:
+                s_copies.append(copy_of(call[c].at[unit[4]], sbuf.at[index, c], ssem.at[c, index]))
+            s_copies.append(copy_of(call[3].at[unit[4]], att_all.at[:, lanes], ssem.at[3, index]))
+            s_copies.append(copy_of(call[4].at[unit[4]], lbuf.at[index], ssem.at[4, index]))
+        w_copies = groups[0] + groups[1] + groups[2]
+        late = [copy_of(source, sums[index], lsem.at[index]) for index, source in enumerate(acc_in)]
+        if last:
+            late += [copy_of(late_in[0], hat, lsem.at[2]), copy_of(late_in[1], inv, lsem.at[3])]
+        for copy in s_copies + w_copies + late:
             copy.start()
-        if last:
-            late = [copy_of(late_in[0], hat, lsem.at[0]), copy_of(late_in[1], inv, lsem.at[1])]
-            for copy in late:
-                copy.start()
         if causal:
             fill_diagonal(diagonal)
         transpose_shards(h_ref, h_t, dp)
         for ref, target in zip(in_refs, in_t):
             transpose_shards(ref, target, dp)
-        for copy in o_copies:
+        for copy in groups[3]:
             copy.wait()
-        grad_att = dot_nt(h_ref[...], obuf[...]).astype(BF16)
+        grad_att = dot(h_ref[...], wbuf[:, 3 * wide :]).astype(BF16)
         for index in range(number):
             grad_all[index] = grad_att[:, index * UNIT : (index + 1) * UNIT]
         for copy in s_copies:
@@ -439,86 +403,74 @@
         def keep(weight, column):
             for index in range(number):
                 part = weight[:, index * UNIT : (index + 1) * UNIT].astype(BF16)
-                stage[index, :, :, column * UNIT : (column + 1) * UNIT] = part.reshape(8, UNIT, UNIT)
+                low = ((index % 2) * 4 + column) * UNIT
+                stage[index // 2, :, :, low : low + UNIT] = part.reshape(8, UNIT, UNIT)
 
         for c in range(3):
             rows_t = in_t[0] if causal or c == 0 else in_t[1]
             keep(dot(rows_t[...], dall[:, c * wide : (c + 1) * wide]), c)
         keep(dot(h_t[...], att_all[...]), 3)
+        share = number // 2 // results
         g_copies = [
-            copy_of(stage.at[index], g_ref.at[natural_index(index, 2, 2, swap)], gsem.at[index]) for index in range(number)
+            copy_of(stage.at[index * share : (index + 1) * share], ref, gsem.at[index]) for index, ref in enumerate(g_refs)
         ]
         for copy in g_copies:
             copy.start()
-        for copy in w_copies:
+        for copy in w_copies + late[: len(acc_in)]:
             copy.wait()
         if causal:
-            sums[0][...] = acc_in[0][...] + dot_nt(dall[...], wbuf[...])
+            sums[0][...] += dot_nt(dall[...], wbuf[:, : 3 * wide])
         else:
-            sums[0][...] = acc_in[0][...] + dot_nt(dall[:, :wide], wbuf[:, :wide])
-            memory_sum = dot_nt(dall[:, wide:], wbuf[:, wide:])
-            sums[1][...] = memory_sum + acc_in[1][...] if n_in == len(acc_in) else memory_sum
-        if last:
-            for copy in late:
+            sums[0][...] += dot_nt(dall[:, :wide], wbuf[:, :wide])
+            memory_sum = dot_nt(dall[:, wide:], wbuf[:, wide : 3 * wide])
+            sums[1][...] = memory_sum + sums[1][...] if len(acc_in) == n_in else memory_sum
+        if last:
+            for copy in late[len(acc_in) :]:
                 copy.wait()
             norm_back_rows(acc, hat, inv, gain_ref, low_ref, scaled_ref, gsum_ref, bsum_ref, rows)
         for copy in g_copies:
             copy.wait()
 
     big = sds((rows, depth), F32)
-    sum_shapes = [big] * (n_in - 1 if last else n_in)
-    shapes = list(sum_shapes)
+    shapes = [big] * (n_in - 1 if last else n_in)
     if last:
         shapes += [sds((rows, depth), BF16), big, sds((8, depth), F32), sds((8, depth), F32)]
-    specs_out = [VMEM] * len(shapes) + [ANY]
-    shapes.append(sds((number, 8, UNIT, 4 * UNIT), BF16))
-    args = [scalars, grad_low, *others, *carried]
-    if last:
-        args.append(norm[2])
-    specs = [SMEM] + [VMEM] * (len(args) - 1)
-    tail = []
-    if last:
-        tail += [norm[0], norm[1]]
-    for group in weights:
-        tail += group
-    tail += outs
+    specs_out = [VMEM] * len(shapes) + [ANY] * results
+    shapes += [sds((number // 2 // results, 8, UNIT, 8 * UNIT), BF16)] * results
+    args = [scalars, grad_low, *others] + ([norm[2]] if last else [])
+    tail = ([norm[0], norm[1]] if last else []) + list(carried) + list(packs)
     for call in saved:
         tail += call
     scratch = [
-        pltpu.VMEM((depth, 3 * number * UNIT), BF16),
-        pltpu.VMEM((number * UNIT, depth), BF16),
+        pltpu.VMEM((depth, 4 * wide), BF16),
         pltpu.VMEM((number, 3, rows, UNIT), BF16),
         pltpu.VMEM((number, 2, rows), F32),
-        pltpu.VMEM((rows, number * UNIT), BF16),
+        pltpu.VMEM((rows, wide), BF16),
         pltpu.VMEM((number, rows, UNIT), BF16),
         pltpu.VMEM((depth, rows), BF16),
     ]
     scratch += [pltpu.VMEM((depth, rows), BF16)] * n_in
     scratch += [
-        pltpu.VMEM((rows, 3 * number * UNIT), BF16),
-        pltpu.VMEM((number, 8, UNIT, 4 * UNIT), BF16),
+        pltpu.VMEM((rows, 3 * wide), BF16),
+        pltpu.VMEM((number // 2, 8, UNIT, 8 * UNIT), BF16),
         pltpu.VMEM((QUERY_BLOCK, QUERY_BLOCK), F32),
     ]
     if last:
-        scratch += [
-            pltpu.VMEM((rows, depth), F32),
-            pltpu.VMEM((rows, depth), F32),
-            pltpu.VMEM((rows, 128), F32),
-            pltpu.SemaphoreType.DMA((2,)),
-        ]
+        scratch += [pltpu.VMEM((rows, depth), F32), pltpu.VMEM((rows, depth), F32), pltpu.VMEM((rows, 128), F32)]
     scratch += [
         pltpu.SemaphoreType.DMA((4, number)),
         pltpu.SemaphoreType.DMA((5, number)),
-        pltpu.SemaphoreType.DMA((number,)),
+        pltpu.SemaphoreType.DMA((results,)),
+        pltpu.SemaphoreType.DMA((4,)),
     ]
     return pl.pallas_call(
         kernel,
         out_shape=shapes,
-        in_specs=specs + [ANY] * len(tail),
+        in_specs=[SMEM] + [VMEM] * (len(args) - 1) + [ANY] * len(tail),
         out_specs=specs_out,
         scratch_shapes=scratch,
         compiler_params=params(),
-        cost_estimate=cost_of(number * 3.5),
+        cost_estimate=cost_of(4.5 * number),
         name="self_bwd" if causal else "cross_bwd",
     )(*args, *tail)
 
@@ -551,7 +503,10 @@
     return pre * half, slope
 
 
-def ffn_fwd_call(scalars, inputs, ups, downs, plan, halved, partial, final):
+FFN_PART = FFN_UNIT // 2
+
+
+def ffn_fwd_call(scalars, inputs, arrays, plan, partial, final):
     rows, depth = inputs.shape
     number = len(plan)
     last, has_partial = final is not None, partial is not None
@@ -563,8 +518,7 @@
             gain_old, bias_old, gain_ref, bias_ref = (next(it) for _ in range(4))
             late_in = [next(it), next(it)]
         part_in = next(it) if has_partial else None
-        up_refs = [next(it) for _ in ups]
-        down_refs = [next(it) for _ in downs]
+        w_refs = [next(it) for _ in arrays]
         if last:
             out_ref, low_ref, scaled_ref, gsum_ref, bsum_ref = (next(it) for _ in range(5))
         else:
@@ -574,17 +528,17 @@
         if last:
             acc, hat, cot, lsem = (next(it) for _ in range(4))
         wsem, gsem = next(it), next(it)
-        swap = sc[1]
         target = acc if last else sum_ref
 
         up_copies, down_copies = [], []
         for index, unit in enumerate(plan):
-            low = pl.multiple_of((unit[1] ^ swap) * FFN_UNIT, FFN_UNIT) if halved[unit[0]] else 0
-            at = pl.ds(low, FFN_UNIT)
-            up_copies.append(copy_of(up_refs[unit[0]].at[:, at], ubuf.at[index], wsem.at[0, index]))
-            down_copies.append(
-                copy_of(down_refs[unit[0]].at[at, :], dbuf.at[index * FFN_UNIT : (index + 1) * FFN_UNIT, :], wsem.at[1, index])
-            )
+            for inner, (up, down) in enumerate(unit):
+                at = slice(inner * FFN_PART, (inner + 1) * FFN_PART)
+                low = index * FFN_UNIT + inner * FFN_PART
+                up_copies.append(copy_of(w_refs[up[0]].at[up[1]], ubuf.at[index, :, at], wsem.at[0, 2 * index + inner]))
+                down_copies.append(
+                    copy_of(w_refs[down[0]].at[down[1]], dbuf.at[:, low : low + FFN_PART], wsem.at[1, 2 * index + inner])
+                )
         for copy in up_copies + down_copies:
             copy.start()
         if has_partial:
@@ -602,7 +556,8 @@
             sbuf[:, index * FFN_UNIT : (index + 1) * FFN_UNIT] = slope.astype(BF16)
 
         for index in range(number):
-            up_copies[index].wait()
+            up_copies[2 * index].wait()
+            up_copies[2 * index + 1].wait()
             if index:
                 gate(pbuf[(index - 1) % 2], index - 1)
             pbuf[index % 2] = dot(x_ref[...], ubuf[index])
@@ -619,9 +574,9 @@
             copy.wait()
         if has_partial:
             part_copy.wait()
-            target[...] += dot(abuf[...], dbuf[...])
+            target[...] += dot_nt(abuf[...], dbuf[...])
         else:
-            target[...] = dot(abuf[...], dbuf[...])
+            target[...] = dot_nt(abuf[...], dbuf[...])
         if last:
             for copy in late:
                 copy.wait()
@@ -654,10 +609,10 @@
     if last:
         args += [final[1], final[2], final[4], final[5]]
     specs = [SMEM] + [VMEM] * (len(args) - 1)
-    tail = ([final[0], final[3]] if last else []) + ([partial] if has_partial else []) + list(ups) + list(downs)
+    tail = ([final[0], final[3]] if last else []) + ([partial] if has_partial else []) + list(arrays)
     scratch = [
         pltpu.VMEM((number, depth, FFN_UNIT), BF16),
-        pltpu.VMEM((number * FFN_UNIT, depth), BF16),
+        pltpu.VMEM((depth, number * FFN_UNIT), BF16),
         pltpu.VMEM((rows, number * FFN_UNIT), BF16),
         pltpu.VMEM((rows, number * FFN_UNIT), BF16),
         pltpu.VMEM((2, rows, FFN_UNIT), F32),
@@ -670,7 +625,7 @@
             pltpu.VMEM((rows, depth), BF16),
             pltpu.SemaphoreType.DMA((2,)),
         ]
-    scratch += [pltpu.SemaphoreType.DMA((2, number)), pltpu.SemaphoreType.DMA((2, number))]
+    scratch += [pltpu.SemaphoreType.DMA((2, 2 * number)), pltpu.SemaphoreType.DMA((2, number))]
     return pl.pallas_call(
         kernel,
         out_shape=shapes,
@@ -678,12 +633,12 @@
         out_specs=specs_out,
         scratch_shapes=scratch,
         compiler_params=params(),
-        cost_estimate=cost_of(number * 2.2),
+        cost_estimate=cost_of(12),
         name="ffn_fwd",
     )(*args, *tail)
 
 
-def ffn_bwd_call(scalars, grad_low, inputs, ups, downs, saved, plan, halved, carried, norm):
+def ffn_bwd_call(scalars, grad_low, inputs, arrays, saved, plan, carried, norm):
     rows, depth = inputs.shape
     number = len(plan)
     last = norm is not None
@@ -694,8 +649,7 @@
         gain_ref = next(it) if last else None
         late_in = [next(it), next(it)] if last else []
         acc_in = next(it)
-        up_refs = [next(it) for _ in ups]
-        down_refs = [next(it) for _ in downs]
+        w_refs = [next(it) for _ in arrays]
         s_refs = [[next(it) for _ in call] for call in saved]
         if last:
             low_ref, scaled_ref, gsum_ref, bsum_ref = (next(it) for _ in range(4))
@@ -706,18 +660,18 @@
         if last:
             acc, hat, inv, lsem = (next(it) for _ in range(4))
         wsem, gsem = next(it), next(it)
-        swap, dp = sc[1], sc[2]
+        order, dp = sc[1], sc[2]
         target = acc if last else sum_ref
 
         copies = [[], [], [], []]
-        for index, unit in enumerate(plan):
-            low = pl.multiple_of((unit[1] ^ swap) * FFN_UNIT, FFN_UNIT) if halved[unit[0]] else 0
-            at, lanes = pl.ds(low, FFN_UNIT), slice(index * FFN_UNIT, (index + 1) * FFN_UNIT)
-            call = s_refs[unit[2]]
-            copies[0].append(copy_of(down_refs[unit[0]].at[at, :], dbuf.at[lanes, :], wsem.at[0, index]))
-            copies[1].append(copy_of(call[1].at[unit[3]], sbuf.at[index], wsem.at[1, index]))
-            copies[2].append(copy_of(call[0].at[unit[3]], abuf.at[:, lanes], wsem.at[2, index]))
-            copies[3].append(copy_of(up_refs[unit[0]].at[:, at], ubuf.at[:, lanes], wsem.at[3, index]))
+        for index, (quarters, _, _, call, at) in enumerate(plan):
+            for inner, (up, down) in enumerate(quarters):
+                low, number_of = index * FFN_UNIT + inner * FFN_PART, 2 * index + inner
+                copies[0].append(copy_of(w_refs[down[0]].at[down[1]], dbuf.at[:, low : low + FFN_PART], wsem.at[0, number_of]))
+                copies[3].append(copy_of(w_refs[up[0]].at[up[1]], ubuf.at[:, low : low + FFN_PART], wsem.at[3, number_of]))
+            lanes = slice(index * FFN_UNIT, (index + 1) * FFN_UNIT)
+            copies[1].append(copy_of(s_refs[call][1].at[at], sbuf.at[index], wsem.at[1, index]))
+            copies[2].append(copy_of(s_refs[call][0].at[at], abuf.at[:, lanes], wsem.at[2, index]))
         for group in copies:
             for copy in group:
                 copy.start()
@@ -730,9 +684,10 @@
         transpose_shards(g_in, g_t, dp)
         transpose_shards(x_ref, x_t, dp)
         for index in range(number):
-            copies[0][index].wait()
+            copies[0][2 * index].wait()
+            copies[0][2 * index + 1].wait()
             copies[1][index].wait()
-            grad_act = dot_nt(g_in[...], dbuf[index * FFN_UNIT : (index + 1) * FFN_UNIT, :]) * sbuf[index].astype(F32)
+            grad_act = dot(g_in[...], dbuf[:, index * FFN_UNIT : (index + 1) * FFN_UNIT]) * sbuf[index].astype(F32)
             gbuf[:, index * FFN_UNIT : (index + 1) * FFN_UNIT] = grad_act.astype(BF16)
         for copy in copies[2]:
             copy.wait()
@@ -741,15 +696,20 @@
             for half in range(number // 2):
                 wide = 2 * FFN_UNIT
                 weight = dot(rows_t[...], source[:, half * wide : (half + 1) * wide]).astype(BF16)
-                for inner in (0, 1):
-                    part = weight[:, inner * FFN_UNIT : (inner + 1) * FFN_UNIT]
-                    stage[2 * half + inner, :, :, column * FFN_UNIT : (column + 1) * FFN_UNIT] = part.reshape(8, UNIT, FFN_UNIT)
+                for inner in range(4):
+                    part = weight[:, inner * FFN_PART : (inner + 1) * FFN_PART]
+                    stage[4 * half + inner, :, :, column * FFN_PART : (column + 1) * FFN_PART] = part.reshape(8, UNIT, FFN_PART)
 
         keep(x_t, gbuf, 0)
         keep(g_t, abuf, 1)
-        g_copies = [
-            copy_of(stage.at[index], g_ref.at[natural_index(index, 2, 2, swap)], gsem.at[index]) for index in range(number)
-        ]
+        g_copies = []
+        for index, (_, places, relative, _, _) in enumerate(plan):
+            for inner, place in enumerate(places):
+                place = place ^ order if relative else place
+                at = pl.ds(pl.multiple_of(place * FFN_UNIT, FFN_UNIT), FFN_UNIT)
+                g_copies.append(
+                    copy_of(stage.at[2 * index + inner], g_ref.at[index // 2, :, :, at], gsem.at[2 * index + inner])
+                )
         for copy in g_copies:
             copy.start()
         for copy in copies[3]:
@@ -766,21 +726,21 @@
     big, low = sds((rows, depth), F32), sds((rows, depth), BF16)
     shapes = [low, big, sds((8, depth), F32), sds((8, depth), F32)] if last else [big]
     specs_out = [VMEM] * len(shapes) + [ANY]
-    shapes.append(sds((number, 8, UNIT, 2 * FFN_UNIT), BF16))
+    shapes.append(sds((number // 2, 8, UNIT, 4 * FFN_UNIT), BF16))
     args = [scalars, grad_low, inputs] + ([norm[2]] if last else [])
     specs = [SMEM] + [VMEM] * (len(args) - 1)
-    tail = ([norm[0], norm[1]] if last else []) + [carried] + list(ups) + list(downs)
+    tail = ([norm[0], norm[1]] if last else []) + [carried] + list(arrays)
     for call in saved:
         tail += call
     scratch = [
         pltpu.VMEM((depth, number * FFN_UNIT), BF16),
-        pltpu.VMEM((number * FFN_UNIT, depth), BF16),
+        pltpu.VMEM((depth, number * FFN_UNIT), BF16),
         pltpu.VMEM((rows, number * FFN_UNIT), BF16),
         pltpu.VMEM((number, rows, FFN_UNIT), BF16),
         pltpu.VMEM((rows, number * FFN_UNIT), BF16),
         pltpu.VMEM((depth, rows), BF16),
         pltpu.VMEM((depth, rows), BF16),
-        pltpu.VMEM((number, 8, UNIT, 2 * FFN_UNIT), BF16),
+        pltpu.VMEM((2 * number, 8, UNIT, 2 * FFN_PART), BF16),
         pltpu.SemaphoreType.DMA,
     ]
     if last:
@@ -790,7 +750,7 @@
             pltpu.VMEM((rows, 128), F32),
             pltpu.SemaphoreType.DMA((2,)),
         ]
-    scratch += [pltpu.SemaphoreType.DMA((4, number)), pltpu.SemaphoreType.DMA((number,))]
+    scratch += [pltpu.SemaphoreType.DMA((4, 2 * number)), pltpu.SemaphoreType.DMA((2 * number,))]
     return pl.pallas_call(
         kernel,
         out_shape=shapes,
@@ -798,7 +758,7 @@
         out_specs=specs_out,
         scratch_shapes=scratch,
         compiler_params=params(),
-        cost_estimate=cost_of(number * 3.6),
+        cost_estimate=cost_of(17),
         name="ffn_bwd",
     )(*args, *tail)
 
@@ -842,49 +802,44 @@
     return total.astype(BF16)
 
 
+MOVES = {"y": over_y, "x": over_x, "z": over_z_near}
+
+
 class Reduction:
-    def __init__(self, sent):
-        self.sent = sent
-
-    def first(self, kept):
-        other = to_sibling(self.sent)
-        units = kept.shape[0] // 2
-        half = units // 2
-        pair_kept = kept.reshape(2, units, *kept.shape[1:])[:, half:]
-        pair_other = other.reshape(2, units, *other.shape[1:])[:, half:]
-        self.left = (kept[:half], other[:half])
-        self.right = (pair_kept[:, :, :4], pair_other[:, :, :4])
-        self.sends = (
-            add(kept[units : units + half], other[units : units + half]),
-            add(pair_kept[:, :, 4:], pair_other[:, :, 4:]),
-        )
+    def __init__(self, sent, portions):
+        self.other = to_sibling(sent)
+        self.portions = portions
+
+    def start(self, kept, *earlier):
+        other = after(self.other, *earlier) if earlier else self.other
+        split = (2, 2, 2, 2, *kept.shape[2:])
+        kept, other = kept.reshape(split), other.reshape(split)
+        self.states = []
+        for low, high, orders in self.portions:
+            self.states.append(([kept[..., low:high], other[..., low:high]], ["y", "x", "z", "w"], list(orders)))
+        return self.send()
+
+    def send(self):
+        self.sends = []
+        for terms, axes, orders in self.states:
+            axis = axes.index(orders[0])
+            self.sends.append(add(*[lax.index_in_dim(t, 1, axis, False) for t in terms]))
+            terms[:] = [lax.index_in_dim(t, 0, axis, False) for t in terms]
+            axes.remove(orders[0])
         return self.sends
 
-    def second(self):
-        over = over_y(self.sends[0])
-        cross = over_x(self.sends[1])
-        left, right = self.left, self.right
-        self.sends = (
-            add(left[0][:, 4:], left[1][:, 4:], over[:, 4:]),
-            add(right[0][1], right[1][1], cross[1]),
-        )
-        self.left = (left[0][:, :4], left[1][:, :4], over[:, :4])
-        self.right = (right[0][0], right[1][0], cross[0])
+    def step(self, *earlier):
+        for send, (terms, _, orders) in zip(self.sends, self.states):
+            moved = MOVES[orders.pop(0)](send)
+            terms.append(after(moved, *earlier) if earlier else moved)
+        if self.states[0][2]:
+            return self.send()
+        whole = [jnp.concatenate([add(*[t[i] for t in terms]) for terms, _, _ in self.states], axis=-1) for i in (0, 1)]
+        self.states, self.sends = whole[0], [whole[1]]
         return self.sends
 
-    def third(self):
-        left, right = over_x(self.sends[0]), over_y(self.sends[1])
-        self.low = jnp.concatenate([add(*self.left, left), add(*self.right, right)], axis=0)
-        self.sends = self.low[:, 2:]
-        return self.sends
-
-    def fourth(self):
-        low = add(self.low[:, :2], over_z_near(self.sends))
-        self.low, self.sends = low[:, 0], low[:, 1]
-        return self.sends
-
     def last(self):
-        return add(self.low, over_z_far(self.sends)).astype(F32)
+        return add(self.states, over_z_far(self.sends[0])).astype(F32)
 
 
 def sentence_body(
@@ -905,170 +860,159 @@
 ):
     dp = lax.axis_index("dp")
     mine = lax.axis_index("tensor")
-    swap = dp & 1
-    self_scalars = jnp.stack([dec_lengths[0, mine], swap, dp, mine]).astype(jnp.int32)
-    cross_scalars = jnp.stack([mem_lengths[0, mine], swap, dp, mine]).astype(jnp.int32)
+    order = dp & 3
+    self_scalars = jnp.stack([dec_lengths[0, mine], order, dp, mine]).astype(jnp.int32)
+    cross_scalars = jnp.stack([mem_lengths[0, mine], order, dp, mine]).astype(jnp.int32)
     gains = [norm_gains[i : i + 1] for i in range(3)]
     biases = [norm_biases[i : i + 1] for i in range(3)]
 
-    def own_half(values, axis):
-        half = values.shape[axis] // 2
-        return lax.dynamic_slice_in_dim(values, swap * half, half, axis)
-
-    def fetch(values, axis, *earlier):
-        send = own_half(values, axis)
-        if earlier:
-            send = after(send, *earlier)
-        near = over_y(send)
-        far = over_dp(near, 1)
-        return [values, to_sibling(values), near, far, to_sibling(near), to_sibling(far)]
-
-    halves = [True, True]
-    early = [(0, 0), (0, 1), (1, 0), (1, 1)]
-    pair = [(0, 0), (1, 0)]
-
-    qkv_sib, out_sib = to_sibling(self_qkv), to_sibling(self_out)
-    qkv_near = over_y(own_half(self_qkv, 2))
-    out_near = over_y(own_half(self_out, 0))
+    def quarters(matrices):
+        halves = matrices.reshape(2, 2, matrices.shape[1], 2, UNIT).transpose(0, 3, 1, 2, 4)
+        return halves.reshape(4, 2, matrices.shape[1], UNIT)
+
+    def own_quarter(pack):
+        return lax.dynamic_index_in_dim(pack, order, 0, False)
+
+    def joined(near, side, up, corner):
+        return jnp.stack([near, side, up, corner])
+
+    self_pack = quarters(jnp.concatenate([self_qkv, self_out.T[None]], axis=0))
+    self_near = over_y(own_quarter(self_pack))
+    self_sib = to_sibling(self_pack)
+    cross_pack = quarters(jnp.concatenate([cross_q[None], cross_kv, cross_out.T[None]], axis=0))
+    ffn_pack = jnp.stack([ffn_in, ffn_out.T]).reshape(2, ffn_in.shape[0], 4, FFN_PART).transpose(2, 0, 1, 3)
+    cross_quarter, ffn_quarter = own_quarter(cross_pack), own_quarter(ffn_pack)
+
+    cross_near = over_y(after(cross_quarter, self_near))
+    self_side, self_up = over_x(self_near), over_z_near(self_near)
+    early = [(0, 0, False), (0, 1, False), (1, 0, False), (1, 1, False)]
+    late = [(0, 0, True), (0, 1, True), (1, 0, True), (1, 1, True)]
     self_a = attention_fwd_call(
-        self_scalars, [], [tokens], [[self_qkv, qkv_sib]], [self_out, out_sib], early, halves, None, None, None
-    )
-    cq_near = over_y(after(own_half(cross_q, 1), out_near))
-    ckv_near = over_y(after(own_half(cross_kv, 2), out_near))
-    cout_near = over_y(after(own_half(cross_out, 0), out_near))
-    qkv_gone, out_gone = after(qkv_near, self_a[5]), after(out_near, self_a[5])
-    qkv_far, qkv_near3 = over_x(qkv_gone), to_sibling(qkv_gone)
-    out_far, out_near3 = over_x(out_gone), to_sibling(out_gone)
+        after(self_scalars, self_near, cross_quarter, ffn_quarter), [], [tokens], [self_pack, self_sib], early, None, None
+    )
+    self_side, self_up, cross_near = after(self_side, self_a[4]), after(self_up, self_a[4]), after(cross_near, self_a[4])
+    self_corner = over_x(self_up)
+    ffn_near = over_y(after(ffn_quarter, cross_near))
+    cross_side, cross_up = over_x(cross_near), over_z_near(cross_near)
+    self_rest = joined(self_near, self_side, self_up, self_corner)
+    self_far = to_sibling(self_rest)
+    cross_sib = to_sibling(after(cross_pack, self_near))
+    ffn_sib = to_sibling(after(ffn_pack, self_side))
+    self_packs = [self_pack, self_sib, self_rest, self_far]
+    cross_corner = over_x(cross_up)
     self_b = attention_fwd_call(
-        self_scalars, [], [tokens], [[qkv_near, qkv_near3]], [out_near, out_near3], pair, [False] * 2,
-        self_a[5], None, None,
-    )
-    qkv_far3, out_far3 = to_sibling(qkv_far), to_sibling(out_far)
-    self_c = attention_fwd_call(
-        self_scalars, [tokens], [tokens], [[qkv_far, qkv_far3]], [out_far, out_far3], pair, [False] * 2,
-        self_b[5], gains[0], biases[0],
-    )
-    first_low, first_hat, first_inv = self_c[5:]
-    w_qkv = [self_qkv, qkv_sib, qkv_near, qkv_far, qkv_near3, qkv_far3]
-    w_self = [self_out, out_sib, out_near, out_far, out_near3, out_far3]
-
-    cq_sib, ckv_sib, cout_sib = (
-        to_sibling(after(w, out_near)) for w in (cross_q, cross_kv, cross_out)
-    )
-    cq_far, ckv_far, cout_far = (over_x(w) for w in (cq_near, ckv_near, cout_near))
-    cq_near3, ckv_near3, cout_near3 = (to_sibling(w) for w in (cq_near, ckv_near, cout_near))
+        after(self_scalars, cross_up), [tokens], [tokens], self_packs[2:], late, self_a[5], (gains[0], biases[0])
+    )
+    first_low, first_hat, first_inv = self_b[5:]
     cross_in = [first_low, memory]
-    cross_a = attention_fwd_call(
-        cross_scalars, [], cross_in, [[cross_q, cq_sib], [cross_kv, ckv_sib]], [cross_out, cout_sib], early,
-        halves, None, None, None,
-    )
-    in_near = over_y(after(own_half(ffn_in, 1), cout_near))
-    down_near = over_y(after(own_half(ffn_out, 0), cout_near))
+    cross_rest = joined(cross_near, cross_side, cross_up, after(cross_corner, self_b[4]))
+    ffn_near = after(ffn_near, self_b[4])
+    ffn_side, ffn_up = over_x(ffn_near), over_z_near(ffn_near)
+    cross_far = to_sibling(cross_rest)
+    ffn_near_far = to_sibling(ffn_near)
+    cross_packs = [cross_pack, cross_sib, cross_rest, cross_far]
     cross_b = attention_fwd_call(
-        cross_scalars, [], cross_in, [[cq_near, cq_near3], [ckv_near, ckv_near3]], [cout_near, cout_near3],
-        pair, [False] * 2, cross_a[5], None, None,
-    )
-    cq_far3, ckv_far3, cout_far3 = (to_sibling(w) for w in (cq_far, ckv_far, cout_far))
-    cross_c = attention_fwd_call(
-        cross_scalars, [first_hat, gains[0], biases[0]], cross_in, [[cq_far, cq_far3], [ckv_far, ckv_far3]],
-        [cout_far, cout_far3], pair, [False] * 2, cross_b[5], gains[1], biases[1],
-    )
-    second_low, second_hat, second_inv = cross_c[5:]
-    w_cq = [cross_q, cq_sib, cq_near, cq_far, cq_near3, cq_far3]
-    w_ckv = [cross_kv, ckv_sib, ckv_near, ckv_far, ckv_near3, ckv_far3]
-    w_cross = [cross_out, cout_sib, cout_near, cout_far, cout_near3, cout_far3]
-
-    in_sib, down_sib = to_sibling(after(ffn_in, cout_near)), to_sibling(after(ffn_out, cout_near))
-    in_far, down_far = over_x(in_near), over_x(down_near)
-    in_near3, down_near3 = to_sibling(in_near), to_sibling(down_near)
-    in_far3, down_far3 = to_sibling(in_far), to_sibling(down_far)
-    w_in = [ffn_in, in_sib, in_near, in_far, in_near3, in_far3]
-    w_down = [ffn_out, down_sib, down_near, down_far, down_near3, down_far3]
+        cross_scalars, [first_hat, gains[0], biases[0]], cross_in, cross_packs,
+        early + [(a + 2, h, r) for a, h, r in late], None, (gains[1], biases[1]),
+    )
+    second_low, second_hat, second_inv = cross_b[5:]
+    ffn_side, ffn_up = after(ffn_side, cross_b[4]), after(ffn_up, cross_b[4])
+    up_corner, down_corner = over_x(ffn_up[:1]), over_z_near(ffn_side[1:])
+    ffn_side_far, ffn_up_far = to_sibling(ffn_side), to_sibling(ffn_up)
     ffn_a = ffn_fwd_call(
-        cross_scalars, second_low, w_in[:2], w_down[:2], early, halves, None, None
-    )
+        cross_scalars, second_low, [ffn_pack, ffn_sib],
+        [[((p, (q, 0)), (p, (q, 1))) for q in (2 * h, 2 * h + 1)] for p in (0, 1) for h in (0, 1)], None, None,
+    )
+    up_corner, down_corner = after(up_corner, ffn_a[0]), after(down_corner, ffn_a[0])
+    up_corner_far, down_corner_far = to_sibling(up_corner), to_sibling(down_corner)
+    ffn_arrays = [ffn_pack, ffn_sib, ffn_near, ffn_side, ffn_up, up_corner, down_corner]
+    ffn_arrays += [ffn_near_far, ffn_side_far, ffn_up_far, up_corner_far, down_corner_far]
+
+    def parts(piece, base):
+        if piece < 2:
+            return [((piece, (q, 0)), (piece, (q, 1))) for q in range(4)]
+        low = base + 5 * (piece - 2)
+        return [((low + q, (0,)), (low + q, (1,))) for q in range(3)] + [((low + 3, (0,)), (low + 4, (0,)))]
+
+    def units_of(piece, base):
+        quarter = parts(piece, base)
+        return [quarter[:2], quarter[2:]]
+
     ffn_b = ffn_fwd_call(
-        cross_scalars, second_low, w_in[2::2], w_down[2::2], pair, [False] * 2, ffn_a[0], None
-    )
-    ffn_c = ffn_fwd_call(
-        cross_scalars, second_low, w_in[3::2], w_down[3::2], pair, [False] * 2, ffn_b[0],
+        cross_scalars, second_low, ffn_arrays[2:], units_of(2, 0) + units_of(3, 0), ffn_a[0],
         (second_hat, gains[1], biases[1], cotangent, gains[2], biases[2]),
     )
-    out_rows, third_low, third_scaled, third_gain, third_bias = ffn_c[:5]
+    out_rows, third_low, third_scaled, third_gain, third_bias = ffn_b[:5]
+
+    def ffn_plan(pieces):
+        return [
+            (unit, (2 * u, 2 * u + 1), piece > 1, piece // 2, 2 * (piece % 2) + u)
+            for piece in pieces
+            for u, unit in enumerate(units_of(piece, 2))
+        ]
 
     def plan_of(pieces):
-        units = []
-        for piece in pieces:
-            for half in (0, 1):
-                if piece < 2:
-                    units.append((piece, half, 0, 2 * piece + half))
-                else:
-                    units.append((2 * piece - 2 + half, 0, 1 + half, piece - 2))
-        return units
-
-    halved = [True, True, False, False, False, False]
-    ffn_saved = [ffn_a[1:3], ffn_b[1:3], ffn_c[5:7]]
+        return [
+            (piece, half, piece > 1, piece // 2, 2 * (piece % 2) + half) for piece in pieces for half in (0, 1)
+        ]
+
+    ffn_saved = [ffn_a[1:3], ffn_b[5:7]]
     ffn_d = ffn_bwd_call(
-        cross_scalars, third_low, second_low, w_in, w_down, ffn_saved, plan_of((1, 3)), halved,
-        third_scaled, None,
-    )
-    ffn_sum = Reduction(ffn_d[1])
+        cross_scalars, third_low, second_low, ffn_arrays, ffn_saved, ffn_plan((1, 3)), third_scaled, None
+    )
+    ffn_sum = Reduction(ffn_d[1], [(0, 768, "yxz"), (768, 1408, "xzy"), (1408, 2048, "zyx")])
     ffn_e = ffn_bwd_call(
-        cross_scalars, third_low, second_low, w_in, w_down, ffn_saved, plan_of((0, 2)), halved,
-        ffn_d[0], (second_hat, second_inv, gains[1]),
+        cross_scalars, third_low, second_low, ffn_arrays, ffn_saved, ffn_plan((0, 2)), ffn_d[0],
+        (second_hat, second_inv, gains[1]),
     )
     second_back, second_scaled, second_gain, second_bias = ffn_e[:4]
-    second_back = after(second_back, *ffn_sum.first(ffn_e[4]))
-
-    cross_saved = [cross_a[:5], cross_b[:5], cross_c[:5]]
-    cross_d = attention_bwd_call(
-        cross_scalars, second_back, cross_in, [w_cq, w_ckv], w_cross, cross_saved, plan_of((1, 3)), halved,
-        [second_scaled], None,
-    )
-    cross_sum = Reduction(cross_d[2])
+    second_back = after(second_back, *ffn_sum.start(ffn_e[4], second_gain))
+
     cross_e = attention_bwd_call(
-        cross_scalars, second_back, cross_in, [w_cq, w_ckv], w_cross, cross_saved, plan_of((0, 2)), halved,
-        cross_d[:2], (first_hat, first_inv, gains[0]),
+        cross_scalars, second_back, cross_in, cross_packs, [cross_b[:5]],
+        [(p, h, p > 1, 0, 2 * p + h) for p in (1, 3, 0, 2) for h in (0, 1)], [second_scaled],
+        (first_hat, first_inv, gains[0]), 2,
     )
     grad_memory, first_back, first_scaled, first_gain, first_bias = cross_e[:5]
     norm_sums = jnp.stack([first_gain, second_gain, third_gain, first_bias, second_bias, third_bias])
     norm_total = jnp.sum(norm_sums, axis=1)
-    first_back = after(first_back, *ffn_sum.second(), *cross_sum.first(cross_e[5]), norm_total)
-
-    self_saved = [self_a[:5], self_b[:5], self_c[:5]]
+    sends = ffn_sum.step(first_gain)
+    cross_sum = Reduction(after(cross_e[5], *sends), [(0, 512, "xzy"), (512, 1024, "yxz")])
+    first_back = after(first_back, *sends, norm_total)
+
+    self_saved = [self_a[:5], self_b[:5]]
     self_d = attention_bwd_call(
-        self_scalars, first_back, [tokens], [w_qkv], w_self, self_saved, plan_of((1, 3)), halved,
-        [first_scaled], None,
-    )
-    self_sum = Reduction(self_d[1])
-    norm_total = norm_total + to_sibling(norm_total)
-    gate = after(self_d[0], ffn_sum.third(), norm_total)
+        self_scalars, first_back, [tokens], self_packs, self_saved, plan_of((1, 3)), [first_scaled], None
+    )
+    sends = ffn_sum.step(self_d[0]) + cross_sum.start(cross_e[6], self_d[0])
+    self_sum = Reduction(after(self_d[1], *sends), [(0, 512, "xzy"), (512, 1024, "yxz")])
+    gate = after(self_d[0], *sends)
     self_e = attention_bwd_call(
-        self_scalars, first_back, [tokens], [w_qkv], w_self, self_saved, plan_of((0, 2)), halved,
-        [gate], None,
+        self_scalars, first_back, [tokens], self_packs, self_saved, plan_of((0, 2)), [gate], None
     )
     grad_tokens = self_e[0]
-    own_sends = self_sum.first(self_e[1])
-    cross_sum.second()
-    ffn_sum.fourth()
+    sends = self_sum.start(self_e[1], grad_tokens)
+    sends = cross_sum.step(*sends)
+    sends = ffn_sum.step(*sends)
+    norm_total = norm_total + after(to_sibling(norm_total), *sends)
     norm_total = norm_total + over_y(norm_total)
-    self_sum.second()
-    cross_sum.third()
+    sends = self_sum.step(*sends, norm_total)
+    sends = cross_sum.step(*sends)
+    norm_total = norm_total + after(over_x(norm_total), *sends)
+    sends = self_sum.step(*sends, norm_total)
+    cross_sum.step(*sends)
+    norm_total = norm_total + after(over_z_near(norm_total), *sends)
+    sends = self_sum.step(*sends, norm_total)
+    norm_total = norm_total + after(over_z_far(norm_total), *sends)
     ffn_sum = ffn_sum.last()
-    norm_total = norm_total + over_x(norm_total)
-    self_sum.third()
-    cross_sum.fourth()
-    norm_total = norm_total + over_z_near(norm_total)
-    self_sum.fourth()
     cross_sum = cross_sum.last()
-    norm_total = norm_total + over_z_far(norm_total)
     self_sum = self_sum.last()
 
     def matrices(total):
-        return total.reshape(2, UNIT, 4, UNIT).transpose(2, 1, 0, 3).reshape(4, UNIT, 2 * UNIT)
+        return total.reshape(UNIT, 2, 4, UNIT).transpose(2, 0, 1, 3).reshape(4, UNIT, 2 * UNIT)
 
     self_grads, cross_grads = matrices(self_sum), matrices(cross_sum)
-    ffn_grads = ffn_sum.transpose(1, 0, 2)
+    ffn_grads = ffn_sum.reshape(UNIT, 4, 2, FFN_PART).transpose(2, 0, 1, 3).reshape(2, UNIT, -1)
     return (
         out_rows,
         grad_tokens,
@@ -1078,8 +1022,8 @@
         cross_grads[0],
         cross_grads[1:3],
         cross_grads[3].T,
-        ffn_grads[:, :, :FFN_UNIT].reshape(UNIT, -1),
-        ffn_grads[:, :, FFN_UNIT:].reshape(UNIT, -1).T,
+        ffn_grads[0],
+        ffn_grads[1].T,
         norm_total[:3],
         norm_total[3:],
     )

time: 512 us -> 471 us (0.920)
  waiting for transfers between devices: 179 us -> 111 us
  local copies, waits for them, and re-layouts: 19.2 us -> 53 us
  other arithmetic: 47.7 us -> 67.3 us
  Pallas kernels: 204 us -> 186 us
  starting transfers between devices: 57.3 us -> 49.7 us
    ppermute x14 -> x11, waiting for transfers between devices: 94.7 us -> 51 us  [over_y(): return lax.ppermute(values, 'tensor', swap_pairs(4, 2))]
    ppermute x22 -> x30, waiting for transfers between devices: 79.7 us -> 57.4 us  [over_dp(): return lax.ppermute(values, 'dp', swap_pairs(8, mask))]
    pallas_call x10 -> x6, Pallas kernels: 137 us -> 122 us  [the longest x3 64.7 us: attention_bwd_call(): pl.pallas_call(kernel, out_shape=shapes, in_specs=[SMEM] + [VMEM] * (len(...]
    convert_element_type x21 -> x28, other arithmetic: 41.9 us -> 56.5 us  [add(): return total.astype(BF16)]
    squeeze x3 -> x10, local copies, waits for them, and re-layouts: 0.07 us -> 13.6 us  [the longest x6 7.84 us: send(): terms[:] = [lax.index_in_dim(t, 0, axis, False) for t in terms]]
    reshape x0 -> x4, local copies, waits for them, and re-layouts: none -> 10.5 us  [quarters(): matrices.reshape(2, 2, matrices.shape[1], 2, UNIT).transpose(0, 3, 1, 2, 4)]
    ppermute x14 -> x11, starting transfers between devices: 22.2 us -> 13.3 us  [over_y(): return lax.ppermute(values, 'tensor', swap_pairs(4, 2))]
    another operation x0 -> x2, local copies, waits for them, and re-layouts: none -> 6.8 us  [sentence_body(): jnp.stack([ffn_in, ffn_out.T]).reshape(2, ffn_in.shape[0], 4, FFN_PART)]
  transfers between devices with their start and end apart: 61 -> 55, of which waited for: 23 -> 18; matrix products, arithmetic and copies ran while one was open for 10% -> 18% of each run, Pallas kernels for 28% -> 33%
where the time goes in v1:
time: 471 us; the launch traced here: 468 us
  Pallas kernels  186 us (39%)
  waiting for transfers between devices  111 us (24%)
  other arithmetic  67.3 us (14%)
  local copies, waits for them, and re-layouts  53 us (11%)
  starting transfers between devices  49.7 us (11%)
    pallas_call x3, Pallas kernels, attention_bwd_call(): pl.pallas_call(kernel, out_shape=shapes, in_specs=[SMEM] + [VMEM] * (len(...  64.7 us
    pallas_call x3, Pallas kernels, attention_fwd_call(): pl.pallas_call(kernel, out_shape=shapes, in_specs=[SMEM] + [VMEM] * (len(...  57.5 us
    ppermute x30, waiting for transfers between devices, over_dp(): return lax.ppermute(values, 'dp', swap_pairs(8, mask))  57.4 us
    convert_element_type x28, other arithmetic, add(): return total.astype(BF16)  56.5 us
    ppermute x11, waiting for transfers between devices, over_y(): return lax.ppermute(values, 'tensor', swap_pairs(4, 2))  51 us
    pallas_call x2, Pallas kernels, ffn_bwd_call(): pl.pallas_call(kernel, out_shape=shapes, in_specs=specs + [ANY] * len(tai...  34.8 us
    ppermute x30, starting transfers between devices, over_dp(): return lax.ppermute(values, 'dp', swap_pairs(8, mask))  33.9 us
    pallas_call x2, Pallas kernels, ffn_fwd_call(): pl.pallas_call(kernel, out_shape=shapes, in_specs=specs + [ANY] * len(tai...  29.2 us
  transfers between devices with their start and end apart: 55, of which 18 were waited for; matrix products, arithmetic and copies ran while one was open for 18% of the time, Pallas kernels for 33%

profile of v1, /device:TPU:0, one launch (start us, length us, event | category | flops | bytes accessed | tf_op | source)
XLA Modules:
  0.0 468.4 jit_solution(3778798523063633933)
XLA Ops:
  5.5 3.2 copy.49
  17.4 3.2 copy.47
  23.4 3.9 copy.50
  27.3 4.0 copy.51
  38.5 10.5 %self_fwd.2 = (bf16[4,512,128]{2,1,0:T(8,128)(2,1)}, bf16[4,512,128]{2,1,0:T(8,128)(2,1)}, bf16[4,512,128]{2,1,0:T(8,128)(2,1)}, bf16[4,512,128]{2,1,0:T(8,128)(...) custom-call(s32[4]{0:T(128)} %add_add_fusion.1.refs_0_, bf16[512,1024]{1,0:T(8,128)(2,1)} %refs_2_.5, ...), custom_call_target="tpu_custom_call" | custom-call | flops 11879999488 | bytes 4194304 | tf_op jit(solution)/shard_map/self_fwd/pallas_call | solution.py:321
  51.1 11.7 %collective-permute-done.6 = bf16[2,1024,128]{2,1,0:T(8,128)(2,1)S(1)} collective-permute-done((bf16[2,1024,128]{2,1,0:T(8,128)(2,1)S(1)}, bf16[2,1024,128]{2,1,0:T(8,128)(2,1)S(1)}, u32[]{:S(2)}, u32[]{:S(2)}) %collective-permute-start.6) | collective-permute-done | bytes 524320 | tf_op jit(solution)/shard_map/ppermute | solution.py:779
  64.9 13.6 %collective-permute-done.1 = bf16[2,1024,128]{2,1,0:T(8,128)(2,1)S(1)} collective-permute-done((bf16[2,1024,128]{2,1,0:T(8,128)(2,1)S(1)}, bf16[2,1024,128]{2,1,0:T(8,128)(2,1)S(1)}, u32[]{:S(2)}, u32[]{:S(2)}) %collective-permute-start.1) | collective-permute-done | bytes 524320 | tf_op jit(solution)/shard_map/ppermute | solution.py:775
  82.3 9.7 %collective-permute-done.3 = bf16[2,1024,128]{2,1,0:T(8,128)(2,1)S(1)} collective-permute-done((bf16[2,1024,128]{2,1,0:T(8,128)(2,1)S(1)}, bf16[2,1024,128]{2,1,0:T(8,128)(2,1)S(1)}, u32[]{:S(2)}, u32[]{:S(2)}) %collective-permute-start.3) | collective-permute-done | bytes 524320 | tf_op jit(solution)/shard_map/ppermute | solution.py:779
  94.9 25.2 %self_fwd.3 = (bf16[4,512,128]{2,1,0:T(8,128)(2,1)}, bf16[4,512,128]{2,1,0:T(8,128)(2,1)}, bf16[4,512,128]{2,1,0:T(8,128)(2,1)}, bf16[4,512,128]{2,1,0:T(8,128)(...) custom-call(s32[4]{0:T(128)} %add_add_fusion.1.refs_0_, ...), custom_call_target="tpu_custom_call" | custom-call | flops 11879999488 | bytes 4194304 | tf_op jit(solution)/shard_map/self_fwd/pallas_call | solution.py:321
  124.9 23.8 %collective-permute-done.13.refs_9_.refs_6_ = bf16[2,1024,256]{2,1,0:T(8,128)(2,1)} collective-permute-done((bf16[2,1024,256]{2,1,0:T(8,128)(2,1)S(1)}, bf16[2,1024,256]{2,1,0:T(8,128)(2,1)}, u32[]{:S(2)}, u32[]{:S(2)}) %collective-permute-start.13) | collective-permute-done | bytes 1048608 | tf_op jit(solution)/shard_map/ppermute | solution.py:775
  152.0 21.9 %cross_fwd.1 = (bf16[8,512,128]{2,1,0:T(8,128)(2,1)}, bf16[8,512,128]{2,1,0:T(8,128)(2,1)}, bf16[8,512,128]{2,1,0:T(8,128)(2,1)}, bf16[8,512,128]{2,1,0:T(8,128)...) custom-call(s32[4]{0:T(128)} %add_add_fusion.refs_0_, ...), custom_call_target="tpu_custom_call" | custom-call | flops 23759998976 | bytes 4194304 | tf_op jit(solution)/shard_map/cross_fwd/pallas_call | solution.py:321
  177.4 12.7 %ffn_fwd.2 = (f32[512,1024]{1,0:T(8,128)}, bf16[4,512,512]{2,1,0:T(8,128)(2,1)}, bf16[4,512,512]{2,1,0:T(8,128)(2,1)}) custom-call(s32[4]{0:T(128)} %add_add_fusion.refs_0_, bf16[512,1024]{1,0:T(8,128)(2,1)} %get-tuple-element.123.refs_1_.refs_2_, bf16[4,2,1024,256]{3,2,1,0:T(8,128)(2,1)} %copy-done.3, ...), custom_call_target="tpu_custom_call" | custom-call | flops 13200000000 | bytes 4194304 | tf_op jit(solution)/shard_map/ffn_fwd/pallas_call | solution.py:629
  194.1 16.5 %ffn_fwd.3 = (bf16[512,1024]{1,0:T(8,128)(2,1)}, bf16[512,1024]{1,0:T(8,128)(2,1)}, f32[512,1024]{1,0:T(8,128)}, f32[8,1024]{1,0:T(8,128)}, f32[8,1024]{1,0:T(8,...) custom-call(s32[4]{0:T(128)} %add_add_fusion.refs_0_, ...), custom_call_target="tpu_custom_call" | custom-call | flops 13200000000 | bytes 4194304 | tf_op jit(solution)/shard_map/ffn_fwd/pallas_call | solution.py:629
  210.7 16.9 %ffn_bwd.2 = (f32[512,1024]{1,0:T(8,128)}, bf16[2,8,128,2048]{3,2,1,0:T(8,128)(2,1)}) custom-call(s32[4]{0:T(128)} %add_add_fusion.refs_0_, bf16[512,1024]{1,0:T(8,128)(2,1)} %get-tuple-element.135.refs_1_, bf16[512,1024]{1,0:T(8,128)(2,1)} %get-tuple-element.123.refs_1_.refs_2_, f32[512,1024]{1,0:T(8,128)} %get-tuple-element.137.refs_3_, ...), custom_call_target="tpu_custom_call" | custom-call | flops 18699999232 | bytes 4194304 | tf_op jit(solution)/shard_map/ffn_bwd/pallas_call | solution.py:754
  227.8 17.9 %ffn_bwd.3 = (bf16[512,1024]{1,0:T(8,128)(2,1)}, f32[512,1024]{1,0:T(8,128)}, f32[8,1024]{1,0:T(8,128)}, f32[8,1024]{1,0:T(8,128)}, bf16[2,8,128,2048]{3,2,1,0:T(8,128)(2,1)}) custom-call(s32[4]{0:T(128)} %add_add_fusion.refs_0_, bf16[512,1024]{1,0:T(8,128)(2,1)} %get-tuple-element.135.refs_1_, bf16[512,1024]{1,0:T(8,128)(2,1)} %get-tuple-element.123.refs_1_.refs_2_, ...), custom_call_target="tpu_custom_call" | custom-call | flops 18699999232 | bytes 4194304 | tf_op jit(solution)/shard_map/ffn_bwd/pallas_call | solution.py:754
  258.9 32.3 %cross_bwd.1 = (f32[512,1024]{1,0:T(8,128)}, bf16[512,1024]{1,0:T(8,128)(2,1)}, f32[512,1024]{1,0:T(8,128)}, f32[8,1024]{1,0:T(8,128)}, f32[8,1024]{1,0:T(8,128)...) custom-call(s32[4]{0:T(128)} %add_add_fusion.refs_0_, ...), custom_call_target="tpu_custom_call" | custom-call | flops 39600001024 | bytes 4194304 | tf_op jit(solution)/shard_map/cross_bwd/pallas_call | solution.py:466
  303.8 16.4 %self_bwd.2 = (f32[512,1024]{1,0:T(8,128)}, bf16[2,8,128,1024]{3,2,1,0:T(8,128)(2,1)}) custom-call(s32[4]{0:T(128)} %add_add_fusion.1.refs_0_, bf16[512,1024]{1,0:T(8,128)(2,1)} %get-tuple-element.164.refs_1_, bf16[512,1024]{1,0:T(8,128)(2,1)} %refs_2_.5, f32[512,1024]{1,0:T(8,128)} %get-tuple-element.165.refs_3_, ...), custom_call_target="tpu_custom_call" | custom-call | flops 19800000512 | bytes 4194304 | tf_op jit(solution)/shard_map/self_bwd/pallas_call | solution.py:466
  336.9 16.1 %self_bwd.3 = (f32[512,1024]{1,0:T(8,128)}, bf16[2,8,128,1024]{3,2,1,0:T(8,128)(2,1)}) custom-call(s32[4]{0:T(128)} %add_add_fusion.1.refs_0_, bf16[512,1024]{1,0:T(8,128)(2,1)} %get-tuple-element.164.refs_1_, bf16[512,1024]{1,0:T(8,128)(2,1)} %refs_2_.5, f32[512,1024]{1,0:T(8,128)} %get-tuple-element.182.refs_3_, ...), custom_call_target="tpu_custom_call" | custom-call | flops 19800000512 | bytes 4194304 | tf_op jit(solution)/shard_map/self_bwd/pallas_call | solution.py:466
  382.7 12.5 %collective-permute-done.39 = f32[6,1024]{1,0:T(8,128)S(1)} collective-permute-done((f32[6,1024]{1,0:T(8,128)S(1)}, f32[6,1024]{1,0:T(8,128)S(1)}, u32[]{:S(2)}, u32[]{:S(2)}) %collective-permute-start.39) | collective-permute-done | bytes 24608 | tf_op jit(solution)/shard_map/ppermute | solution.py:775
  396.3 3.9 collective-permute-done.53
  407.3 4.2 collective-permute-done.41
  417.7 4.9 %collective-permute-done.40 = bf16[2,2,128,512]{3,2,1,0:T(8,128)(2,1)S(1)} collective-permute-done((bf16[2,2,128,512]{3,2,1,0:T(8,128)(2,1)S(1)}, bf16[2,2,128,512]{3,2,1,0:T(8,128)(2,1)S(1)}, u32[]{:S(2)}, u32[]{:S(2)}) %collective-permute-start.40) | collective-permute-done | bytes 524320 | tf_op jit(solution)/shard_map/ppermute | solution.py:779
  439.2 8.6 %collective-permute-done.52 = bf16[128,1024]{1,0:T(8,128)(2,1)} collective-permute-done((bf16[128,1024]{1,0:T(8,128)(2,1)}, bf16[128,1024]{1,0:T(8,128)(2,1)}, u32[]{:S(2)}, u32[]{:S(2)}) %collective-permute-start.52) | collective-permute-done | bytes 262176 | tf_op jit(solution)/shard_map/ppermute | solution.py:779
  455.6 10.5 %collective-permute-done.49 = bf16[128,1024]{1,0:T(8,128)(2,1)S(1)} collective-permute-done((bf16[128,1024]{1,0:T(8,128)(2,1)S(1)}, bf16[128,1024]{1,0:T(8,128)(2,1)S(1)}, u32[]{:S(2)}, u32[]{:S(2)}) %collective-permute-start.49) | collective-permute-done | bytes 262176 | tf_op jit(solution)/shard_map/ppermute | solution.py:779
  (263 shorter events, 162.8 us)
Async XLA Ops:
  8.7 29.7 %collective-permute-start.2 = (bf16[4,2,1024,128]{3,2,1,0:T(8,128)(2,1)}, bf16[4,2,1024,128]{3,2,1,0:T(8,128)(2,1)}, u32[]{:S(2)}, u32[]{:S(2)}) collective-permute-start(bf16[4,2,1024,128]{3,2,1,0:T(8,128)(2,1)} %bitcast.14.refs_2_.refs_4_), channel_id=1, source_target_pairs={{0,1},{1,0},{2,3},{3,2},{4,5},{5,4},{6,7},{7,6},{8,9},{9,8},{10,11... | collective-permute-start | bytes 6291464 | tf_op jit(solution)/shard_map/ppermute | solution.py:771
  11.1 24.3 %collective-permute-start = (bf16[2,1024,128]{2,1,0:T(8,128)(2,1)}, bf16[2,1024,128]{2,1,0:T(8,128)(2,1)}, u32[]{:S(2)}, u32[]{:S(2)}) collective-permute-start(bf16[2,1024,128]{2,1,0:T(8,128)(2,1)} %dynamic-slice_bitcast_fusion), channel_id=1, source_target_pairs={{0,2},{1,3},{2,0},{3,1},{4,6},{5,7},{6,4},{7,5},{8,10},{9,11},{10,... | collective-permute-start | bytes 1572872 | tf_op jit(solution)/shard_map/ppermute | solution.py:775
  64.1 29.4 %collective-permute-start.7 = (bf16[4,2,1024,128]{3,2,1,0:T(8,128)(2,1)S(1)}, bf16[4,2,1024,128]{3,2,1,0:T(8,128)(2,1)S(1)}, u32[]{:S(2)}, u32[]{:S(2)}) collective-permute-start(bf16[4,2,1024,128]{3,2,1,0:T(8,128)(2,1)S(1)} %pad_maximum_fusion.3.refs_6_), channel_id=1, source_target_pairs={{0,1},{1,0},{2,3},{3,2},{4,5},{5,4},{6,7},{7,6},{8,9},{9,8},{10,11... | collective-permute-start | bytes 6291464 | tf_op jit(solution)/shard_map/ppermute | solution.py:771
  80.7 69.5 %collective-permute-start.8 = (bf16[4,2,1024,128]{3,2,1,0:T(8,128)(2,1)}, bf16[4,2,1024,128]{3,2,1,0:T(8,128)(2,1)}, u32[]{:S(2)}, u32[]{:S(2)}) collective-permute-start(bf16[4,2,1024,128]{3,2,1,0:T(8,128)(2,1)} %bitcast.9.refs_8_), channel_id=1, source_target_pairs={{0,1},{1,0},{2,3},{3,2},{4,5},{5,4},{6,7},{7,6},{8,9},{9,8},{10,11... | collective-permute-start | bytes 6291464 | tf_op jit(solution)/shard_map/ppermute | solution.py:771
  80.7 39.4 %collective-permute-start.9 = (bf16[2,1024,128]{2,1,0:T(8,128)(2,1)S(1)}, bf16[2,1024,128]{2,1,0:T(8,128)(2,1)S(1)}, u32[]{:S(2)}, u32[]{:S(2)}) collective-permute-start(bf16[2,1024,128]{2,1,0:T(8,128)(2,1)S(1)} %collective-permute-done.1), channel_id=1, source_target_pairs={{0,4},{4,0},{8,12},{12,8},{16,20},{20,16},{24,28},{28,24},{1,5},{5... | collective-permute-start | bytes 1572872 | tf_op jit(solution)/shard_map/ppermute | solution.py:779
  92.0 28.1 %collective-permute-start.10 = (bf16[2,1024,128]{2,1,0:T(8,128)(2,1)S(1)}, bf16[2,1024,128]{2,1,0:T(8,128)(2,1)S(1)}, u32[]{:S(2)}, u32[]{:S(2)}) collective-permute-start(bf16[2,1024,128]{2,1,0:T(8,128)(2,1)S(1)} %collective-permute-done.3), channel_id=1, source_target_pairs={{0,4},{4,0},{8,12},{12,8},{16,20},{20,16},{24,28},{28,24},{1,5},{5... | collective-permute-start | bytes 1572872 | tf_op jit(solution)/shard_map/ppermute | solution.py:779
  120.4 30.3 %collective-permute-start.11 = (bf16[4,2,1024,128]{3,2,1,0:T(8,128)(2,1)S(1)}, bf16[4,2,1024,128]{3,2,1,0:T(8,128)(2,1)S(1)}, u32[]{:S(2)}, u32[]{:S(2)}) collective-permute-start(bf16[4,2,1024,128]{3,2,1,0:T(8,128)(2,1)S(1)} %pad_maximum_fusion.4.refs_10_), channel_id=1, source_target_pairs={{0,1},{1,0},{2,3},{3,2},{4,5},{5,4},{6,7},{7,6},{8,9},{9,8},{10,11... | collective-permute-start | bytes 6291464 | tf_op jit(solution)/shard_map/ppermute | solution.py:771
  122.9 54.1 %collective-permute-start.12 = (bf16[4,2,1024,256]{3,2,1,0:T(8,128)(2,1)S(1)}, bf16[4,2,1024,256]{3,2,1,0:T(8,128)(2,1)}, u32[]{:S(2)}, u32[]{:S(2)}) collective-permute-start(bf16[4,2,1024,256]{3,2,1,0:T(8,128)(2,1)S(1)} %fusion.refs_2_.refs_4_.refs_7_), channel_id=1, source_target_pairs={{0,1},{1,0},{2,3},{3,2},{4,5},{5,4},{6,7},{7,6},{8,9},{9,8},{10,11... | collective-permute-start | bytes 12582920 | tf_op jit(solution)/shard_map/ppermute | solution.py:771
  123.0 25.7 %collective-permute-start.13 = (bf16[2,1024,256]{2,1,0:T(8,128)(2,1)S(1)}, bf16[2,1024,256]{2,1,0:T(8,128)(2,1)}, u32[]{:S(2)}, u32[]{:S(2)}) collective-permute-start(bf16[2,1024,256]{2,1,0:T(8,128)(2,1)S(1)} %fusion.11), channel_id=1, source_target_pairs={{0,2},{1,3},{2,0},{3,1},{4,6},{5,7},{6,4},{7,5},{8,10},{9,11},{10,... | collective-permute-start | bytes 3145736 | tf_op jit(solution)/shard_map/ppermute | solution.py:775
  148.6 42.6 %collective-permute-start.18 = (bf16[2,1024,256]{2,1,0:T(8,128)(2,1)}, bf16[2,1024,256]{2,1,0:T(8,128)(2,1)}, u32[]{:S(2)}, u32[]{:S(2)}) collective-permute-start(bf16[2,1024,256]{2,1,0:T(8,128)(2,1)} %collective-permute-done.13.refs_9_.refs_6_), channel_id=1, source_target_pairs={{0,1},{1,0},{2,3},{3,2},{4,5},{5,4},{6,7},{7,6},{8,9},{9,8},{10,11... | collective-permute-start | bytes 3145736 | tf_op jit(solution)/shard_map/ppermute | solution.py:771
  148.6 27.2 %collective-permute-start.15 = (bf16[2,1024,256]{2,1,0:T(8,128)(2,1)}, bf16[2,1024,256]{2,1,0:T(8,128)(2,1)S(1)}, u32[]{:S(2)}, u32[]{:S(2)}) collective-permute-start(bf16[2,1024,256]{2,1,0:T(8,128)(2,1)} %collective-permute-done.13.refs_9_.refs_6_), channel_id=1, source_target_pairs={{0,8},{4,12},{8,0},{12,4},{16,24},{20,28},{24,16},{28,20},{1,9},{5... | collective-permute-start | bytes 3145736 | tf_op jit(solution)/shard_map/ppermute | solution.py:779
  150.2 25.5 %collective-permute-start.14 = (bf16[2,1024,256]{2,1,0:T(8,128)(2,1)}, bf16[2,1024,256]{2,1,0:T(8,128)(2,1)S(1)}, u32[]{:S(2)}, u32[]{:S(2)}) collective-permute-start(bf16[2,1024,256]{2,1,0:T(8,128)(2,1)} %collective-permute-done.13.refs_9_.refs_6_), channel_id=1, source_target_pairs={{0,4},{4,0},{8,12},{12,8},{16,20},{20,16},{24,28},{28,24},{1,5},{5... | collective-permute-start | bytes 3145736 | tf_op jit(solution)/shard_map/ppermute | solution.py:779
  255.7 36.9 %collective-permute-start.26 = (bf16[2,2,2,128,640]{4,3,2,1,0:T(8,128)(2,1)}, bf16[2,2,2,128,640]{4,3,2,1,0:T(8,128)(2,1)}, u32[]{:S(2)}, u32[]{:S(2)}) collective-permute-start(bf16[2,2,2,128,640]{4,3,2,1,0:T(8,128)(2,1)} %fusion.4), channel_id=1, source_target_pairs={{0,8},{4,12},{8,0},{12,4},{16,24},{20,28},{24,16},{28,20},{1,9},{5... | collective-permute-start | bytes 3932168 | tf_op jit(solution)/shard_map/ppermute | solution.py:779
  256.9 35.8 %collective-permute-start.25 = (bf16[2,2,2,128,640]{4,3,2,1,0:T(8,128)(2,1)}, bf16[2,2,2,128,640]{4,3,2,1,0:T(8,128)(2,1)S(1)}, u32[]{:S(2)}, u32[]{:S(2)}) collective-permute-start(bf16[2,2,2,128,640]{4,3,2,1,0:T(8,128)(2,1)} %fusion.3), channel_id=1, source_target_pairs={{0,4},{4,0},{8,12},{12,8},{16,20},{20,16},{24,28},{28,24},{1,5},{5... | collective-permute-start | bytes 3932168 | tf_op jit(solution)/shard_map/ppermute | solution.py:779
  258.4 38.5 %collective-permute-start.24 = (bf16[2,2,2,128,768]{4,3,2,1,0:T(8,128)(2,1)S(1)}, bf16[2,2,2,128,768]{4,3,2,1,0:T(8,128)(2,1)S(1)}, u32[]{:S(2)}, u32[]{:S(2)}) collective-permute-start(bf16[2,2,2,128,768]{4,3,2,1,0:T(8,128)(2,1)S(1)} %fusion.1), channel_id=1, source_target_pairs={{0,2},{1,3},{2,0},{3,1},{4,6},{5,7},{6,4},{7,5},{8,10},{9,11},{10,... | collective-permute-start | bytes 4718600 | tf_op jit(solution)/shard_map/ppermute | solution.py:775
  300.6 26.9 %collective-permute-start.30 = (bf16[2,8,128,1024]{3,2,1,0:T(8,128)(2,1)}, bf16[2,8,128,1024]{3,2,1,0:T(8,128)(2,1)}, u32[]{:S(2)}, u32[]{:S(2)}) collective-permute-start(bf16[2,8,128,1024]{3,2,1,0:T(8,128)(2,1)} %get-tuple-element.180), channel_id=1, source_target_pairs={{0,1},{1,0},{2,3},{3,2},{4,5},{5,4},{6,7},{7,6},{8,9},{9,8},{10,11... | collective-permute-start | bytes 12582920 | tf_op jit(solution)/shard_map/ppermute | solution.py:771
  332.7 46.1 %collective-permute-start.38 = (f32[6,1024]{1,0:T(8,128)S(1)}, f32[6,1024]{1,0:T(8,128)S(1)}, u32[]{:S(2)}, u32[]{:S(2)}) collective-permute-start(f32[6,1024]{1,0:T(8,128)S(1)} %reduce_sum.9), channel_id=1, source_target_pairs={{0,1},{1,0},{2,3},{3,2},{4,5},{5,4},{6,7},{7,6},{8,9},{9,8},{10,11... | collective-permute-start | bytes 73736 | tf_op jit(solution)/shard_map/ppermute | solution.py:771
  334.3 36.0 %collective-permute-start.37 = (bf16[2,128,640]{2,1,0:T(8,128)(2,1)}, bf16[2,128,640]{2,1,0:T(8,128)(2,1)}, u32[]{:S(2)}, u32[]{:S(2)}) collective-permute-start(bf16[2,128,640]{2,1,0:T(8,128)(2,1)} %fusion.16), channel_id=1, source_target_pairs={{0,4},{4,0},{8,12},{12,8},{16,20},{20,16},{24,28},{28,24},{1,5},{5... | collective-permute-start | bytes 983048 | tf_op jit(solution)/shard_map/ppermute | solution.py:779
  335.8 30.9 %collective-permute-start.34 = (bf16[2,2,2,128,512]{4,3,2,1,0:T(8,128)(2,1)}, bf16[2,2,2,128,512]{4,3,2,1,0:T(8,128)(2,1)}, u32[]{:S(2)}, u32[]{:S(2)}) collective-permute-start(bf16[2,2,2,128,512]{4,3,2,1,0:T(8,128)(2,1)} %fusion.6), channel_id=1, source_target_pairs={{0,4},{4,0},{8,12},{12,8},{16,20},{20,16},{24,28},{28,24},{1,5},{5... | collective-permute-start | bytes 3145736 | tf_op jit(solution)/shard_map/ppermute | solution.py:779
  336.4 26.4 %collective-permute-start.35 = (bf16[2,2,2,128,512]{4,3,2,1,0:T(8,128)(2,1)}, bf16[2,2,2,128,512]{4,3,2,1,0:T(8,128)(2,1)}, u32[]{:S(2)}, u32[]{:S(2)}) collective-permute-start(bf16[2,2,2,128,512]{4,3,2,1,0:T(8,128)(2,1)} %fusion.7), channel_id=1, source_target_pairs={{0,2},{1,3},{2,0},{3,1},{4,6},{5,7},{6,4},{7,5},{8,10},{9,11},{10,... | collective-permute-start | bytes 3145736 | tf_op jit(solution)/shard_map/ppermute | solution.py:775
  366.7 35.5 %collective-permute-start.32 = (bf16[2,2,2,128,512]{4,3,2,1,0:T(8,128)(2,1)}, bf16[2,2,2,128,512]{4,3,2,1,0:T(8,128)(2,1)}, u32[]{:S(2)}, u32[]{:S(2)}) collective-permute-start(bf16[2,2,2,128,512]{4,3,2,1,0:T(8,128)(2,1)} %fusion.8), channel_id=1, source_target_pairs={{0,4},{4,0},{8,12},{12,8},{16,20},{20,16},{24,28},{28,24},{1,5},{5... | collective-permute-start | bytes 3145736 | tf_op jit(solution)/shard_map/ppermute | solution.py:779
  370.3 33.9 %collective-permute-start.42 = (bf16[2,2,2,128,512]{4,3,2,1,0:T(8,128)(2,1)}, bf16[2,2,2,128,512]{4,3,2,1,0:T(8,128)(2,1)}, u32[]{:S(2)}, u32[]{:S(2)}) collective-permute-start(bf16[2,2,2,128,512]{4,3,2,1,0:T(8,128)(2,1)} %fusion.9), channel_id=1, source_target_pairs={{0,2},{1,3},{2,0},{3,1},{4,6},{5,7},{6,4},{7,5},{8,10},{9,11},{10,... | collective-permute-start | bytes 3145736 | tf_op jit(solution)/shard_map/ppermute | solution.py:775
  375.4 24.7 %collective-permute-start.53 = (bf16[128,2048]{1,0:T(8,128)(2,1)S(1)}, bf16[128,2048]{1,0:T(8,128)(2,1)S(1)}, u32[]{:S(2)}, u32[]{:S(2)}) collective-permute-start(bf16[128,2048]{1,0:T(8,128)(2,1)S(1)} %pad_maximum_fusion.5), channel_id=1, source_target_pairs={{0,16},{4,20},{8,24},{12,28},{16,0},{20,4},{24,8},{28,12},{1,17},{... | collective-permute-start | bytes 1572872 | tf_op jit(solution)/shard_map/ppermute | solution.py:779
  378.2 34.4 %collective-permute-start.43 = (bf16[2,2,128,512]{3,2,1,0:T(8,128)(2,1)}, bf16[2,2,128,512]{3,2,1,0:T(8,128)(2,1)}, u32[]{:S(2)}, u32[]{:S(2)}) collective-permute-start(bf16[2,2,128,512]{3,2,1,0:T(8,128)(2,1)} %fusion.13), channel_id=1, source_target_pairs={{0,4},{4,0},{8,12},{12,8},{16,20},{20,16},{24,28},{28,24},{1,5},{5... | collective-permute-start | bytes 1572872 | tf_op jit(solution)/shard_map/ppermute | solution.py:779
  (69 other events, 791.9 us)

commit v2 on v1

--- a/solution.py
+++ b/solution.py
@@ -210,26 +210,49 @@
     return jax.ShapeDtypeStruct(shape, dtype)
 
 
-def pack_copies(packs, plan, number, order, buffer, sems):
-    groups = []
-    for matrix in range(4):
-        copies = []
-        for index, (array, half, relative) in enumerate(plan):
-            quarter = half + 2 * (matrix // 2)
-            if relative:
-                quarter = quarter ^ order
-            low = (matrix * number + index) * UNIT
-            copies.append(
-                copy_of(packs[array].at[quarter, matrix % 2], buffer.at[:, low : low + UNIT], sems.at[matrix, index])
-            )
-        groups.append(copies)
-    return groups
-
-
-def attention_fwd_call(scalars, residual, others, packs, plan, partial, norm):
+def weight_copies(pieces, order, wbuf, obuf, wsem, osem):
+    groups, outs = [[], [], []], []
+    wide = 2 * UNIT
+    for index, refs in enumerate(pieces):
+        at = slice(index * wide, (index + 1) * wide)
+        if len(refs) > 1:
+            column = 0
+            for ref in refs[:-1]:
+                for source in [ref] if len(ref.shape) == 2 else [ref.at[c] for c in range(ref.shape[0])]:
+                    low = (column * len(pieces) + index) * wide
+                    groups[column].append(copy_of(source, wbuf.at[:, low : low + wide], wsem.at[column, index, 0]))
+                    column += 1
+            outs.append(copy_of(refs[-1], obuf.at[at, :], osem.at[index, 0]))
+            continue
+        rest, = refs
+        rows = rest.shape[2]
+        part = wide // 4
+        for quarter in range(4):
+            place = quarter ^ order
+            for column in range(3):
+                low = (column * len(pieces) + index) * wide
+                groups[column].append(
+                    copy_of(
+                        rest.at[quarter, column],
+                        wbuf.at[pl.ds(pl.multiple_of(place * rows, rows), rows), low : low + wide],
+                        wsem.at[column, index, quarter],
+                    )
+                )
+            for block in range(4):
+                outs.append(
+                    copy_of(
+                        rest.at[quarter, 3, block * part : (block + 1) * part, :],
+                        obuf.at[pl.ds(pl.multiple_of(index * wide + place * part, part), part), block * wide : (block + 1) * wide],
+                        osem.at[index, 4 * quarter + block],
+                    )
+                )
+    return groups, outs
+
+
+def attention_fwd_call(scalars, residual, others, pieces, partial, norm):
     rows, depth = others[0].shape
     causal = len(others) == 1
-    number, wide = len(plan), len(plan) * UNIT
+    number, wide = 2 * len(pieces), 2 * len(pieces) * UNIT
     last, has_partial = norm is not None, partial is not None
 
     def kernel(*refs):
@@ -240,18 +263,18 @@
         old_rows = [next(it) for _ in residual[1:]] if last else []
         res_in = next(it) if last else None
         part_in = next(it) if has_partial else None
-        w_refs = [next(it) for _ in packs]
+        w_refs = [[next(it) for _ in piece] for piece in pieces]
         q_ref, k_ref, v_ref, att_ref, lse_ref = (next(it) for _ in range(5))
         if last:
             low_ref, hat_ref, inv_ref = next(it), next(it), next(it)
         else:
             sum_ref = next(it)
-        wbuf, att_all, diagonal, wsem, lsem = (next(it) for _ in range(5))
+        wbuf, obuf, att_all, diagonal, wsem, osem, lsem = (next(it) for _ in range(7))
         if last:
             acc, old = next(it), next(it)
         length, order = sc[0], sc[1]
-        groups = pack_copies(w_refs, plan, number, order, wbuf, wsem)
-        for copies in groups:
+        groups, outs = weight_copies(w_refs, order, wbuf, obuf, wsem, osem)
+        for copies in groups + [outs]:
             for copy in copies:
                 copy.start()
         target = acc if last else sum_ref
@@ -281,12 +304,12 @@
             return carry
 
         lax.fori_loop(0, number, step, 0)
-        for copy in groups[3] + late:
+        for copy in outs + late:
             copy.wait()
         if has_partial:
-            target[...] += dot_nt(att_all[...], wbuf[:, 3 * wide :])
+            target[...] += dot(att_all[...], obuf[...])
         else:
-            target[...] = dot_nt(att_all[...], wbuf[:, 3 * wide :])
+            target[...] = dot(att_all[...], obuf[...])
         if last:
             def chunk(at):
                 before = old[at, :].astype(F32)
@@ -308,12 +331,15 @@
     args = [scalars, *others]
     if last:
         args += [*norm, *residual[1:]]
-    tail = ([residual[0]] if last else []) + ([partial] if has_partial else []) + list(packs)
+    tail = ([residual[0]] if last else []) + ([partial] if has_partial else [])
+    tail += [array for piece in pieces for array in piece]
     scratch = [
-        pltpu.VMEM((depth, 4 * wide), BF16),
+        pltpu.VMEM((depth, 3 * wide), BF16),
+        pltpu.VMEM((wide, depth), BF16),
         pltpu.VMEM((rows, wide), BF16),
         pltpu.VMEM((QUERY_BLOCK, QUERY_BLOCK), F32),
-        pltpu.SemaphoreType.DMA((4, number)),
+        pltpu.SemaphoreType.DMA((3, len(pieces), 4)),
+        pltpu.SemaphoreType.DMA((len(pieces), 16)),
         pltpu.SemaphoreType.DMA((2,)),
     ]
     if last:
@@ -330,7 +356,7 @@
     )(*args, *tail)
 
 
-def attention_bwd_call(scalars, grad_low, others, packs, saved, plan, carried, norm, results=1):
+def attention_bwd_call(scalars, grad_low, others, pieces, saved, plan, carried, norm, results=1):
     rows, depth = grad_low.shape
     causal = len(others) == 1
     number, n_in, wide = len(plan), len(others), len(plan) * UNIT
@@ -344,32 +370,32 @@
         gain_ref = next(it) if last else None
         late_in = [next(it), next(it)] if last else []
         acc_in = [next(it) for _ in carried]
-        w_refs = [next(it) for _ in packs]
+        w_refs = [[next(it) for _ in piece] for piece in pieces]
         s_refs = [[next(it) for _ in call] for call in saved]
         sums = [None if last and not index else next(it) for index in range(n_in)]
         if last:
             low_ref, scaled_ref, gsum_ref, bsum_ref = (next(it) for _ in range(4))
         g_refs = [next(it) for _ in range(results)]
-        wbuf, sbuf, lbuf, att_all, grad_all, h_t = (next(it) for _ in range(6))
+        wbuf, obuf, sbuf, lbuf, att_all, grad_all, h_t = (next(it) for _ in range(7))
         in_t = [next(it) for _ in range(n_in)]
         dall, stage, diagonal = next(it), next(it), next(it)
         if last:
             acc, hat, inv = next(it), next(it), next(it)
             sums[0] = acc
-        wsem, ssem, gsem, lsem = (next(it) for _ in range(4))
+        wsem, osem, ssem, gsem, lsem = (next(it) for _ in range(5))
         length, order, dp = sc[0], sc[1], sc[2]
 
-        groups = pack_copies(w_refs, [unit[:3] for unit in plan], number, order, wbuf, wsem)
-        for copy in groups[3]:
+        groups, o_copies = weight_copies(w_refs, order, wbuf, obuf, wsem, osem)
+        for copy in o_copies:
             copy.start()
         s_copies = []
         for index, unit in enumerate(plan):
             lanes = slice(index * UNIT, (index + 1) * UNIT)
-            call = s_refs[unit[3]]
+            call = s_refs[unit[0]]
             for c in range(3):
-                s_copies.append(copy_of(call[c].at[unit[4]], sbuf.at[index, c], ssem.at[c, index]))
-            s_copies.append(copy_of(call[3].at[unit[4]], att_all.at[:, lanes], ssem.at[3, index]))
-            s_copies.append(copy_of(call[4].at[unit[4]], lbuf.at[index], ssem.at[4, index]))
+                s_copies.append(copy_of(call[c].at[unit[1]], sbuf.at[index, c], ssem.at[c, index]))
+            s_copies.append(copy_of(call[3].at[unit[1]], att_all.at[:, lanes], ssem.at[3, index]))
+            s_copies.append(copy_of(call[4].at[unit[1]], lbuf.at[index], ssem.at[4, index]))
         w_copies = groups[0] + groups[1] + groups[2]
         late = [copy_of(source, sums[index], lsem.at[index]) for index, source in enumerate(acc_in)]
         if last:
@@ -381,9 +407,9 @@
         transpose_shards(h_ref, h_t, dp)
         for ref, target in zip(in_refs, in_t):
             transpose_shards(ref, target, dp)
-        for copy in groups[3]:
+        for copy in o_copies:
             copy.wait()
-        grad_att = dot(h_ref[...], wbuf[:, 3 * wide :]).astype(BF16)
+        grad_att = dot_nt(h_ref[...], obuf[...]).astype(BF16)
         for index in range(number):
             grad_all[index] = grad_att[:, index * UNIT : (index + 1) * UNIT]
         for copy in s_copies:
@@ -400,29 +426,28 @@
 
         lax.fori_loop(0, number, step, 0)
 
+        share = number // 2 // results
+
         def keep(weight, column):
             for index in range(number):
                 part = weight[:, index * UNIT : (index + 1) * UNIT].astype(BF16)
-                low = ((index % 2) * 4 + column) * UNIT
-                stage[index // 2, :, :, low : low + UNIT] = part.reshape(8, UNIT, UNIT)
+                piece = index // 2
+                stage[piece // share, (index % 2) * 4 + column, piece % share] = part.reshape(8, UNIT, UNIT)
 
         for c in range(3):
             rows_t = in_t[0] if causal or c == 0 else in_t[1]
             keep(dot(rows_t[...], dall[:, c * wide : (c + 1) * wide]), c)
         keep(dot(h_t[...], att_all[...]), 3)
-        share = number // 2 // results
-        g_copies = [
-            copy_of(stage.at[index * share : (index + 1) * share], ref, gsem.at[index]) for index, ref in enumerate(g_refs)
-        ]
+        g_copies = [copy_of(stage.at[index], ref, gsem.at[index]) for index, ref in enumerate(g_refs)]
         for copy in g_copies:
             copy.start()
         for copy in w_copies + late[: len(acc_in)]:
             copy.wait()
         if causal:
-            sums[0][...] += dot_nt(dall[...], wbuf[:, : 3 * wide])
+            sums[0][...] += dot_nt(dall[...], wbuf[...])
         else:
             sums[0][...] += dot_nt(dall[:, :wide], wbuf[:, :wide])
-            memory_sum = dot_nt(dall[:, wide:], wbuf[:, wide : 3 * wide])
+            memory_sum = dot_nt(dall[:, wide:], wbuf[:, wide:])
             sums[1][...] = memory_sum + sums[1][...] if len(acc_in) == n_in else memory_sum
         if last:
             for copy in late[len(acc_in) :]:
@@ -436,13 +461,15 @@
     if last:
         shapes += [sds((rows, depth), BF16), big, sds((8, depth), F32), sds((8, depth), F32)]
     specs_out = [VMEM] * len(shapes) + [ANY] * results
-    shapes += [sds((number // 2 // results, 8, UNIT, 8 * UNIT), BF16)] * results
+    shapes += [sds((8, number // 2 // results, 8, UNIT, UNIT), BF16)] * results
     args = [scalars, grad_low, *others] + ([norm[2]] if last else [])
-    tail = ([norm[0], norm[1]] if last else []) + list(carried) + list(packs)
+    tail = ([norm[0], norm[1]] if last else []) + list(carried)
+    tail += [array for piece in pieces for array in piece]
     for call in saved:
         tail += call
     scratch = [
-        pltpu.VMEM((depth, 4 * wide), BF16),
+        pltpu.VMEM((depth, 3 * wide), BF16),
+        pltpu.VMEM((wide, depth), BF16),
         pltpu.VMEM((number, 3, rows, UNIT), BF16),
         pltpu.VMEM((number, 2, rows), F32),
         pltpu.VMEM((rows, wide), BF16),
@@ -452,13 +479,14 @@
     scratch += [pltpu.VMEM((depth, rows), BF16)] * n_in
     scratch += [
         pltpu.VMEM((rows, 3 * wide), BF16),
-        pltpu.VMEM((number // 2, 8, UNIT, 8 * UNIT), BF16),
+        pltpu.VMEM((results, 8, number // 2 // results, 8, UNIT, UNIT), BF16),
         pltpu.VMEM((QUERY_BLOCK, QUERY_BLOCK), F32),
     ]
     if last:
         scratch += [pltpu.VMEM((rows, depth), F32), pltpu.VMEM((rows, depth), F32), pltpu.VMEM((rows, 128), F32)]
     scratch += [
-        pltpu.SemaphoreType.DMA((4, number)),
+        pltpu.SemaphoreType.DMA((3, len(pieces), 4)),
+        pltpu.SemaphoreType.DMA((len(pieces), 16)),
         pltpu.SemaphoreType.DMA((5, number)),
         pltpu.SemaphoreType.DMA((results,)),
         pltpu.SemaphoreType.DMA((4,)),
@@ -506,9 +534,32 @@
 FFN_PART = FFN_UNIT // 2
 
 
-def ffn_fwd_call(scalars, inputs, arrays, plan, partial, final):
+def ffn_copies(pieces, order, ubuf, dbuf, usem, dsem):
+    ups, downs = [], []
+    for index, refs in enumerate(pieces):
+        wide = 2 * FFN_UNIT
+        at = slice(index * wide, (index + 1) * wide)
+        if len(refs) == 2:
+            ups.append([copy_of(refs[0], ubuf.at[:, at], usem.at[index, 0])])
+            downs.append([copy_of(refs[1], dbuf.at[at, :], dsem.at[index, 0])])
+            continue
+        ups.append([])
+        downs.append([])
+        rows = refs[0].shape[1]
+        for quarter in range(4):
+            up = refs[quarter].at[0]
+            down = refs[quarter].at[1] if quarter < 3 else refs[4].at[0]
+            place = (quarter ^ order) * rows
+            ups[-1].append(copy_of(up, ubuf.at[pl.ds(pl.multiple_of(place, rows), rows), at], usem.at[index, quarter]))
+            downs[-1].append(
+                copy_of(down, dbuf.at[pl.ds(pl.multiple_of(index * wide + place, rows), rows), :], dsem.at[index, quarter])
+            )
+    return ups, downs
+
+
+def ffn_fwd_call(scalars, inputs, pieces, partial, final):
     rows, depth = inputs.shape
-    number = len(plan)
+    number = 2 * len(pieces)
     last, has_partial = final is not None, partial is not None
 
     def kernel(*refs):
@@ -518,7 +569,7 @@
             gain_old, bias_old, gain_ref, bias_ref = (next(it) for _ in range(4))
             late_in = [next(it), next(it)]
         part_in = next(it) if has_partial else None
-        w_refs = [next(it) for _ in arrays]
+        w_refs = [[next(it) for _ in piece] for piece in pieces]
         if last:
             out_ref, low_ref, scaled_ref, gsum_ref, bsum_ref = (next(it) for _ in range(5))
         else:
@@ -530,17 +581,10 @@
         wsem, gsem = next(it), next(it)
         target = acc if last else sum_ref
 
-        up_copies, down_copies = [], []
-        for index, unit in enumerate(plan):
-            for inner, (up, down) in enumerate(unit):
-                at = slice(inner * FFN_PART, (inner + 1) * FFN_PART)
-                low = index * FFN_UNIT + inner * FFN_PART
-                up_copies.append(copy_of(w_refs[up[0]].at[up[1]], ubuf.at[index, :, at], wsem.at[0, 2 * index + inner]))
-                down_copies.append(
-                    copy_of(w_refs[down[0]].at[down[1]], dbuf.at[:, low : low + FFN_PART], wsem.at[1, 2 * index + inner])
-                )
-        for copy in up_copies + down_copies:
-            copy.start()
+        up_copies, down_copies = ffn_copies(w_refs, sc[1], ubuf, dbuf, wsem.at[0], wsem.at[1])
+        for copies in up_copies + down_copies:
+            for copy in copies:
+                copy.start()
         if has_partial:
             part_copy = copy_of(part_in, target, psem)
             part_copy.start()
@@ -556,11 +600,12 @@
             sbuf[:, index * FFN_UNIT : (index + 1) * FFN_UNIT] = slope.astype(BF16)
 
         for index in range(number):
-            up_copies[2 * index].wait()
-            up_copies[2 * index + 1].wait()
+            if index % 2 == 0:
+                for copy in up_copies[index // 2]:
+                    copy.wait()
             if index:
                 gate(pbuf[(index - 1) % 2], index - 1)
-            pbuf[index % 2] = dot(x_ref[...], ubuf[index])
+            pbuf[index % 2] = dot(x_ref[...], ubuf[:, index * FFN_UNIT : (index + 1) * FFN_UNIT])
         gate(pbuf[(number - 1) % 2], number - 1)
         for index in range(number):
             at = slice(index * FFN_UNIT, (index + 1) * FFN_UNIT)
@@ -570,13 +615,14 @@
             ]
         for copy in saves:
             copy.start()
-        for copy in down_copies:
-            copy.wait()
+        for copies in down_copies:
+            for copy in copies:
+                copy.wait()
         if has_partial:
             part_copy.wait()
-            target[...] += dot_nt(abuf[...], dbuf[...])
+            target[...] += dot(abuf[...], dbuf[...])
         else:
-            target[...] = dot_nt(abuf[...], dbuf[...])
+            target[...] = dot(abuf[...], dbuf[...])
         if last:
             for copy in late:
                 copy.wait()
@@ -609,10 +655,10 @@
     if last:
         args += [final[1], final[2], final[4], final[5]]
     specs = [SMEM] + [VMEM] * (len(args) - 1)
-    tail = ([final[0], final[3]] if last else []) + ([partial] if has_partial else []) + list(arrays)
+    tail = ([final[0], final[3]] if last else []) + ([partial] if has_partial else []) + [array for piece in pieces for array in piece]
     scratch = [
-        pltpu.VMEM((number, depth, FFN_UNIT), BF16),
         pltpu.VMEM((depth, number * FFN_UNIT), BF16),
+        pltpu.VMEM((number * FFN_UNIT, depth), BF16),
         pltpu.VMEM((rows, number * FFN_UNIT), BF16),
         pltpu.VMEM((rows, number * FFN_UNIT), BF16),
         pltpu.VMEM((2, rows, FFN_UNIT), F32),
@@ -625,7 +671,7 @@
             pltpu.VMEM((rows, depth), BF16),
             pltpu.SemaphoreType.DMA((2,)),
         ]
-    scratch += [pltpu.SemaphoreType.DMA((2, 2 * number)), pltpu.SemaphoreType.DMA((2, number))]
+    scratch += [pltpu.SemaphoreType.DMA((2, len(pieces), 4)), pltpu.SemaphoreType.DMA((2, number))]
     return pl.pallas_call(
         kernel,
         out_shape=shapes,
@@ -638,7 +684,7 @@
     )(*args, *tail)
 
 
-def ffn_bwd_call(scalars, grad_low, inputs, arrays, saved, plan, carried, norm):
+def ffn_bwd_call(scalars, grad_low, inputs, pieces, saved, plan, carried, norm):
     rows, depth = inputs.shape
     number = len(plan)
     last = norm is not None
@@ -649,7 +695,7 @@
         gain_ref = next(it) if last else None
         late_in = [next(it), next(it)] if last else []
         acc_in = next(it)
-        w_refs = [next(it) for _ in arrays]
+        w_refs = [[next(it) for _ in piece] for piece in pieces]
         s_refs = [[next(it) for _ in call] for call in saved]
         if last:
             low_ref, scaled_ref, gsum_ref, bsum_ref = (next(it) for _ in range(4))
@@ -659,21 +705,18 @@
         ubuf, dbuf, abuf, sbuf, gbuf, x_t, g_t, stage, psem = (next(it) for _ in range(9))
         if last:
             acc, hat, inv, lsem = (next(it) for _ in range(4))
-        wsem, gsem = next(it), next(it)
+        wsem, ssem, gsem = next(it), next(it), next(it)
         order, dp = sc[1], sc[2]
         target = acc if last else sum_ref
 
-        copies = [[], [], [], []]
-        for index, (quarters, _, _, call, at) in enumerate(plan):
-            for inner, (up, down) in enumerate(quarters):
-                low, number_of = index * FFN_UNIT + inner * FFN_PART, 2 * index + inner
-                copies[0].append(copy_of(w_refs[down[0]].at[down[1]], dbuf.at[:, low : low + FFN_PART], wsem.at[0, number_of]))
-                copies[3].append(copy_of(w_refs[up[0]].at[up[1]], ubuf.at[:, low : low + FFN_PART], wsem.at[3, number_of]))
+        ups, downs = ffn_copies(w_refs, order, ubuf, dbuf, wsem.at[0], wsem.at[1])
+        slopes, acts = [], []
+        for index, (call, at) in enumerate(plan):
             lanes = slice(index * FFN_UNIT, (index + 1) * FFN_UNIT)
-            copies[1].append(copy_of(s_refs[call][1].at[at], sbuf.at[index], wsem.at[1, index]))
-            copies[2].append(copy_of(s_refs[call][0].at[at], abuf.at[:, lanes], wsem.at[2, index]))
-        for group in copies:
-            for copy in group:
+            slopes.append(copy_of(s_refs[call][1].at[at], sbuf.at[index], ssem.at[0, index]))
+            acts.append(copy_of(s_refs[call][0].at[at], abuf.at[:, lanes], ssem.at[1, index]))
+        for copies in downs + [slopes, acts] + ups:
+            for copy in copies:
                 copy.start()
         part_copy = copy_of(acc_in, target, psem)
         part_copy.start()
@@ -684,12 +727,13 @@
         transpose_shards(g_in, g_t, dp)
         transpose_shards(x_ref, x_t, dp)
         for index in range(number):
-            copies[0][2 * index].wait()
-            copies[0][2 * index + 1].wait()
-            copies[1][index].wait()
-            grad_act = dot(g_in[...], dbuf[:, index * FFN_UNIT : (index + 1) * FFN_UNIT]) * sbuf[index].astype(F32)
+            if index % 2 == 0:
+                for copy in downs[index // 2]:
+                    copy.wait()
+            slopes[index].wait()
+            grad_act = dot_nt(g_in[...], dbuf[index * FFN_UNIT : (index + 1) * FFN_UNIT, :]) * sbuf[index].astype(F32)
             gbuf[:, index * FFN_UNIT : (index + 1) * FFN_UNIT] = grad_act.astype(BF16)
-        for copy in copies[2]:
+        for copy in acts:
             copy.wait()
 
         def keep(rows_t, source, column):
@@ -698,22 +742,16 @@
                 weight = dot(rows_t[...], source[:, half * wide : (half + 1) * wide]).astype(BF16)
                 for inner in range(4):
                     part = weight[:, inner * FFN_PART : (inner + 1) * FFN_PART]
-                    stage[4 * half + inner, :, :, column * FFN_PART : (column + 1) * FFN_PART] = part.reshape(8, UNIT, FFN_PART)
+                    stage[2 * inner + column, half] = part.reshape(8, UNIT, FFN_PART)
 
         keep(x_t, gbuf, 0)
         keep(g_t, abuf, 1)
-        g_copies = []
-        for index, (_, places, relative, _, _) in enumerate(plan):
-            for inner, place in enumerate(places):
-                place = place ^ order if relative else place
-                at = pl.ds(pl.multiple_of(place * FFN_UNIT, FFN_UNIT), FFN_UNIT)
-                g_copies.append(
-                    copy_of(stage.at[2 * index + inner], g_ref.at[index // 2, :, :, at], gsem.at[2 * index + inner])
-                )
+        g_copies = [copy_of(stage, g_ref, gsem)]
         for copy in g_copies:
             copy.start()
-        for copy in copies[3]:
-            copy.wait()
+        for copies in ups:
+            for copy in copies:
+                copy.wait()
         part_copy.wait()
         target[...] += dot_nt(gbuf[...], ubuf[...])
         if last:
@@ -726,21 +764,21 @@
     big, low = sds((rows, depth), F32), sds((rows, depth), BF16)
     shapes = [low, big, sds((8, depth), F32), sds((8, depth), F32)] if last else [big]
     specs_out = [VMEM] * len(shapes) + [ANY]
-    shapes.append(sds((number // 2, 8, UNIT, 4 * FFN_UNIT), BF16))
+    shapes.append(sds((8, number // 2, 8, UNIT, FFN_PART), BF16))
     args = [scalars, grad_low, inputs] + ([norm[2]] if last else [])
     specs = [SMEM] + [VMEM] * (len(args) - 1)
-    tail = ([norm[0], norm[1]] if last else []) + [carried] + list(arrays)
+    tail = ([norm[0], norm[1]] if last else []) + [carried] + [array for piece in pieces for array in piece]
     for call in saved:
         tail += call
     scratch = [
         pltpu.VMEM((depth, number * FFN_UNIT), BF16),
-        pltpu.VMEM((depth, number * FFN_UNIT), BF16),
+        pltpu.VMEM((number * FFN_UNIT, depth), BF16),
         pltpu.VMEM((rows, number * FFN_UNIT), BF16),
         pltpu.VMEM((number, rows, FFN_UNIT), BF16),
         pltpu.VMEM((rows, number * FFN_UNIT), BF16),
         pltpu.VMEM((depth, rows), BF16),
         pltpu.VMEM((depth, rows), BF16),
-        pltpu.VMEM((2 * number, 8, UNIT, 2 * FFN_PART), BF16),
+        pltpu.VMEM((8, number // 2, 8, UNIT, FFN_PART), BF16),
         pltpu.SemaphoreType.DMA,
     ]
     if last:
@@ -750,7 +788,7 @@
             pltpu.VMEM((rows, 128), F32),
             pltpu.SemaphoreType.DMA((2,)),
         ]
-    scratch += [pltpu.SemaphoreType.DMA((4, 2 * number)), pltpu.SemaphoreType.DMA((2 * number,))]
+    scratch += [pltpu.SemaphoreType.DMA((2, len(pieces), 4)), pltpu.SemaphoreType.DMA((2, number)), pltpu.SemaphoreType.DMA]
     return pl.pallas_call(
         kernel,
         out_shape=shapes,
@@ -763,6 +801,81 @@
     )(*args, *tail)
 
 
+def combine(jobs, shapes):
+    arrays = []
+    for terms, _, _ in jobs:
+        for array, _ in terms:
+            if not any(array is known for known in arrays):
+                arrays.append(array)
+    position = {id(array): index for index, array in enumerate(arrays)}
+
+    def part_shape(array, index):
+        kept = []
+        for extent, at in zip(array.shape, index + (slice(None),) * (array.ndim - len(index))):
+            if isinstance(at, slice):
+                kept.append(len(range(*at.indices(extent))))
+        return tuple(kept)
+
+    part_shapes = [part_shape(*terms[0]) for terms, _, _ in jobs]
+    count = sum(len(terms) for terms, _, _ in jobs)
+
+    def kernel(*refs):
+        ins, outs = refs[: len(arrays)], refs[len(arrays) : len(arrays) + len(shapes)]
+        rest = refs[len(arrays) + len(shapes) :]
+        term_bufs, sum_bufs, isem, osem = rest[:count], rest[count : count + len(jobs)], rest[-2], rest[-1]
+        loads, number = [], 0
+        for terms, _, _ in jobs:
+            loads.append([])
+            for array, index in terms:
+                loads[-1].append(copy_of(ins[position[id(array)]].at[index], term_bufs[number], isem.at[number]))
+                number += 1
+        for group in loads:
+            for copy in group:
+                copy.start()
+        stores, number = [], 0
+        for job, (terms, out, place) in enumerate(jobs):
+            for copy in loads[job]:
+                copy.wait()
+            bufs = term_bufs[number : number + len(terms)]
+            number += len(terms)
+            lead = part_shapes[job][:-2]
+            size = 1
+            for extent in lead:
+                size *= extent
+
+            def one(flat, carry, bufs=bufs, lead=lead, target=sum_bufs[job]):
+                index, left = [], flat
+                for extent in reversed(lead):
+                    index.append(lax.rem(left, extent))
+                    left = lax.div(left, extent)
+                index = tuple(reversed(index))
+                total = bufs[0][index].astype(F32)
+                for buf in bufs[1:]:
+                    total = total + buf[index].astype(F32)
+                target[index] = total.astype(target.dtype)
+                return carry
+
+            lax.fori_loop(0, size, one, 0)
+            stores.append(copy_of(sum_bufs[job], outs[out].at[place], osem.at[job]))
+            stores[-1].start()
+        for copy in stores:
+            copy.wait()
+
+    scratch = [pltpu.VMEM(part_shapes[job], array.dtype) for job, (terms, _, _) in enumerate(jobs) for array, _ in terms]
+    scratch += [pltpu.VMEM(part_shapes[job], shapes[out].dtype) for job, (_, out, _) in enumerate(jobs)]
+    scratch += [pltpu.SemaphoreType.DMA((count,)), pltpu.SemaphoreType.DMA((len(jobs),))]
+    return pl.pallas_call(
+        kernel,
+        out_shape=list(shapes),
+        in_specs=[ANY] * len(arrays),
+        out_specs=[ANY] * len(shapes),
+        scratch_shapes=scratch,
+        compiler_params=params(),
+        cost_estimate=cost_of(3),
+        name="combine",
+    )(*arrays)
+
+
 def swap_pairs(count, mask):
     return [(i, i ^ mask) for i in range(count)]
 
@@ -793,13 +906,6 @@
 
 def after(values, *earlier):
     return lax.optimization_barrier((values, *earlier))[0]
-
-
-def add(*terms):
-    total = terms[0].astype(F32)
-    for term in terms[1:]:
-        total = total + term.astype(F32)
-    return total.astype(BF16)
 
 
 MOVES = {"y": over_y, "x": over_x, "z": over_z_near}
@@ -808,38 +914,61 @@
 class Reduction:
     def __init__(self, sent, portions):
         self.other = to_sibling(sent)
-        self.portions = portions
-
-    def start(self, kept, *earlier):
-        other = after(self.other, *earlier) if earlier else self.other
-        split = (2, 2, 2, 2, *kept.shape[2:])
-        kept, other = kept.reshape(split), other.reshape(split)
-        self.states = []
-        for low, high, orders in self.portions:
-            self.states.append(([kept[..., low:high], other[..., low:high]], ["y", "x", "z", "w"], list(orders)))
-        return self.send()
-
-    def send(self):
-        self.sends = []
-        for terms, axes, orders in self.states:
-            axis = axes.index(orders[0])
-            self.sends.append(add(*[lax.index_in_dim(t, 1, axis, False) for t in terms]))
-            terms[:] = [lax.index_in_dim(t, 0, axis, False) for t in terms]
-            axes.remove(orders[0])
-        return self.sends
-
-    def step(self, *earlier):
-        for send, (terms, _, orders) in zip(self.sends, self.states):
-            moved = MOVES[orders.pop(0)](send)
-            terms.append(after(moved, *earlier) if earlier else moved)
-        if self.states[0][2]:
-            return self.send()
-        whole = [jnp.concatenate([add(*[t[i] for t in terms]) for terms, _, _ in self.states], axis=-1) for i in (0, 1)]
-        self.states, self.sends = whole[0], [whole[1]]
-        return self.sends
-
-    def last(self):
-        return add(self.states, over_z_far(self.sends[0])).astype(F32)
+        self.portions, self.stage, self.sends, self.total = portions, 0, None, None
+
+    def begin(self, kept, *earlier):
+        other = after(self.other, *earlier)
+        split = (kept.shape[0], 2, 2, 2, 2, *kept.shape[3:])
+        arrays = (kept.reshape(split), other.reshape(split))
+        self.blocks, self.tail = kept.shape[0], kept.shape[3:]
+        self.terms = [[(array, ("b", "y", "x", "z", "w"), low, {}) for array in arrays] for low, _, _ in self.portions]
+
+    def receive(self, *earlier):
+        if self.stage == 4:
+            moved = after(over_z_far(self.sends[0]), *earlier)
+            for (low, _, _), terms in zip(self.portions, self.terms):
+                terms.append((moved, ("b",), low, {}))
+        elif self.stage:
+            for send, (_, _, orders), terms in zip(self.sends, self.portions, self.terms):
+                left = tuple(a for a in ("b", "y", "x", "z", "w") if a not in orders[: self.stage])
+                terms.append((after(MOVES[orders[self.stage - 1]](send), *earlier), left, 0, {}))
+
+    def jobs(self, first_out):
+        jobs, shapes = [], []
+        stage = self.stage
+        for number, ((low, high, orders), terms) in enumerate(zip(self.portions, self.terms)):
+            axis = (*orders, "w", None)[stage]
+            picked = []
+            for array, axes, start, fixed in terms:
+                index = [slice(start, start + high - low)]
+                for name in axes[1:]:
+                    index.append(1 if name == axis else fixed.get(name, 0 if name in orders[:stage] or (stage > 3 and name == "w") else slice(None)))
+                picked.append((array, tuple(index)))
+            if stage < 3:
+                left = 3 - stage + 1 - 1
+                shapes.append(sds((high - low, *(2,) * left, *self.tail), BF16))
+                jobs.append((picked, first_out + number, slice(0, high - low)))
+            else:
+                if not number:
+                    shapes.append(sds((self.blocks, *self.tail), BF16 if stage == 3 else F32))
+                jobs.append((picked, first_out, slice(low, high)))
+        self.stage += 1
+        return jobs, shapes
+
+
+def advance(reductions, *earlier):
+    jobs, shapes, bounds = [], [], []
+    for reduction in reductions:
+        reduction.receive(*earlier)
+        more, made = reduction.jobs(len(shapes))
+        bounds.append((len(shapes), len(shapes) + len(made)))
+        jobs, shapes = jobs + more, shapes + made
+    results = combine(jobs, shapes)
+    for reduction, (low, high) in zip(reductions, bounds):
+        reduction.sends = list(results[low:high])
+        if reduction.stage == 5:
+            reduction.total = results[low]
+    return list(results)
 
 
 def sentence_body(
@@ -866,153 +995,118 @@
     gains = [norm_gains[i : i + 1] for i in range(3)]
     biases = [norm_biases[i : i + 1] for i in range(3)]
 
-    def quarters(matrices):
-        halves = matrices.reshape(2, 2, matrices.shape[1], 2, UNIT).transpose(0, 3, 1, 2, 4)
-        return halves.reshape(4, 2, matrices.shape[1], UNIT)
-
-    def own_quarter(pack):
-        return lax.dynamic_index_in_dim(pack, order, 0, False)
-
-    def joined(near, side, up, corner):
-        return jnp.stack([near, side, up, corner])
-
-    self_pack = quarters(jnp.concatenate([self_qkv, self_out.T[None]], axis=0))
-    self_near = over_y(own_quarter(self_pack))
-    self_sib = to_sibling(self_pack)
-    cross_pack = quarters(jnp.concatenate([cross_q[None], cross_kv, cross_out.T[None]], axis=0))
-    ffn_pack = jnp.stack([ffn_in, ffn_out.T]).reshape(2, ffn_in.shape[0], 4, FFN_PART).transpose(2, 0, 1, 3)
-    cross_quarter, ffn_quarter = own_quarter(cross_pack), own_quarter(ffn_pack)
-
-    cross_near = over_y(after(cross_quarter, self_near))
+    def quarter_rows(values):
+        rows = values.shape[-2] // 4
+        return lax.dynamic_slice_in_dim(values, order * rows, rows, values.ndim - 2)
+
+    def folded(values):
+        blocks = values.reshape(values.shape[0], 4, 2 * UNIT)
+        return blocks.transpose(1, 0, 2).reshape(1, 4 * values.shape[0], 2 * UNIT)
+
+    self_near = over_y(jnp.concatenate([quarter_rows(self_qkv), folded(quarter_rows(self_out))]))
+    cross_near = over_y(
+        jnp.concatenate([quarter_rows(cross_q)[None], quarter_rows(cross_kv), folded(quarter_rows(cross_out))])
+    )
+    ffn_near = over_y(jnp.stack([quarter_rows(ffn_in), quarter_rows(ffn_out)]))
+    self_own = (self_qkv, self_out)
+    self_sib = tuple(to_sibling(w) for w in self_own)
     self_side, self_up = over_x(self_near), over_z_near(self_near)
-    early = [(0, 0, False), (0, 1, False), (1, 0, False), (1, 1, False)]
-    late = [(0, 0, True), (0, 1, True), (1, 0, True), (1, 1, True)]
-    self_a = attention_fwd_call(
-        after(self_scalars, self_near, cross_quarter, ffn_quarter), [], [tokens], [self_pack, self_sib], early, None, None
-    )
-    self_side, self_up, cross_near = after(self_side, self_a[4]), after(self_up, self_a[4]), after(cross_near, self_a[4])
+    self_a = attention_fwd_call(after(self_scalars, self_near), [], [tokens], [self_own, self_sib], None, None)
+    self_side, self_up, cross_near = (after(w, self_a[4]) for w in (self_side, self_up, cross_near))
     self_corner = over_x(self_up)
-    ffn_near = over_y(after(ffn_quarter, cross_near))
     cross_side, cross_up = over_x(cross_near), over_z_near(cross_near)
-    self_rest = joined(self_near, self_side, self_up, self_corner)
+    self_rest = jnp.stack([self_near, self_side, self_up, self_corner])
     self_far = to_sibling(self_rest)
-    cross_sib = to_sibling(after(cross_pack, self_near))
-    ffn_sib = to_sibling(after(ffn_pack, self_side))
-    self_packs = [self_pack, self_sib, self_rest, self_far]
+    self_pieces = [self_own, self_sib, (self_rest,), (self_far,)]
+    self_b = attention_fwd_call(
+        after(self_scalars, cross_near, ffn_near), [tokens], [tokens], self_pieces[2:], self_a[5], (gains[0], biases[0])
+    )
+    first_low, first_hat, first_inv = self_b[5:]
+    cross_own = (cross_q, cross_kv, cross_out)
+    cross_sib = tuple(to_sibling(after(w, self_near)) for w in cross_own)
+    ffn_own = (ffn_in, ffn_out)
+    ffn_sib = tuple(to_sibling(after(w, self_near)) for w in ffn_own)
+    cross_in = [first_low, memory]
     cross_corner = over_x(cross_up)
-    self_b = attention_fwd_call(
-        after(self_scalars, cross_up), [tokens], [tokens], self_packs[2:], late, self_a[5], (gains[0], biases[0])
-    )
-    first_low, first_hat, first_inv = self_b[5:]
-    cross_in = [first_low, memory]
-    cross_rest = joined(cross_near, cross_side, cross_up, after(cross_corner, self_b[4]))
-    ffn_near = after(ffn_near, self_b[4])
+    cross_rest = jnp.stack([cross_near, cross_side, cross_up, cross_corner])
+    cross_far = to_sibling(cross_rest)
     ffn_side, ffn_up = over_x(ffn_near), over_z_near(ffn_near)
-    cross_far = to_sibling(cross_rest)
-    ffn_near_far = to_sibling(ffn_near)
-    cross_packs = [cross_pack, cross_sib, cross_rest, cross_far]
+    cross_pieces = [cross_own, cross_sib, (cross_rest,), (cross_far,)]
     cross_b = attention_fwd_call(
-        cross_scalars, [first_hat, gains[0], biases[0]], cross_in, cross_packs,
-        early + [(a + 2, h, r) for a, h, r in late], None, (gains[1], biases[1]),
+        cross_scalars, [first_hat, gains[0], biases[0]], cross_in, cross_pieces, None, (gains[1], biases[1])
     )
     second_low, second_hat, second_inv = cross_b[5:]
     ffn_side, ffn_up = after(ffn_side, cross_b[4]), after(ffn_up, cross_b[4])
     up_corner, down_corner = over_x(ffn_up[:1]), over_z_near(ffn_side[1:])
-    ffn_side_far, ffn_up_far = to_sibling(ffn_side), to_sibling(ffn_up)
-    ffn_a = ffn_fwd_call(
-        cross_scalars, second_low, [ffn_pack, ffn_sib],
-        [[((p, (q, 0)), (p, (q, 1))) for q in (2 * h, 2 * h + 1)] for p in (0, 1) for h in (0, 1)], None, None,
-    )
+    ffn_pieces = [ffn_own, ffn_sib]
+    ffn_a = ffn_fwd_call(cross_scalars, second_low, ffn_pieces, None, None)
     up_corner, down_corner = after(up_corner, ffn_a[0]), after(down_corner, ffn_a[0])
-    up_corner_far, down_corner_far = to_sibling(up_corner), to_sibling(down_corner)
-    ffn_arrays = [ffn_pack, ffn_sib, ffn_near, ffn_side, ffn_up, up_corner, down_corner]
-    ffn_arrays += [ffn_near_far, ffn_side_far, ffn_up_far, up_corner_far, down_corner_far]
-
-    def parts(piece, base):
-        if piece < 2:
-            return [((piece, (q, 0)), (piece, (q, 1))) for q in range(4)]
-        low = base + 5 * (piece - 2)
-        return [((low + q, (0,)), (low + q, (1,))) for q in range(3)] + [((low + 3, (0,)), (low + 4, (0,)))]
-
-    def units_of(piece, base):
-        quarter = parts(piece, base)
-        return [quarter[:2], quarter[2:]]
-
+    ffn_rest = (ffn_near, ffn_side, ffn_up, up_corner, down_corner)
+    ffn_pieces += [ffn_rest, tuple(to_sibling(w) for w in ffn_rest)]
     ffn_b = ffn_fwd_call(
-        cross_scalars, second_low, ffn_arrays[2:], units_of(2, 0) + units_of(3, 0), ffn_a[0],
+        cross_scalars, second_low, ffn_pieces[2:], ffn_a[0],
         (second_hat, gains[1], biases[1], cotangent, gains[2], biases[2]),
     )
     out_rows, third_low, third_scaled, third_gain, third_bias = ffn_b[:5]
 
-    def ffn_plan(pieces):
-        return [
-            (unit, (2 * u, 2 * u + 1), piece > 1, piece // 2, 2 * (piece % 2) + u)
-            for piece in pieces
-            for u, unit in enumerate(units_of(piece, 2))
-        ]
-
     def plan_of(pieces):
-        return [
-            (piece, half, piece > 1, piece // 2, 2 * (piece % 2) + half) for piece in pieces for half in (0, 1)
-        ]
+        return [(piece // 2, 2 * (piece % 2) + half) for piece in pieces for half in (0, 1)]
 
     ffn_saved = [ffn_a[1:3], ffn_b[5:7]]
     ffn_d = ffn_bwd_call(
-        cross_scalars, third_low, second_low, ffn_arrays, ffn_saved, ffn_plan((1, 3)), third_scaled, None
-    )
-    ffn_sum = Reduction(ffn_d[1], [(0, 768, "yxz"), (768, 1408, "xzy"), (1408, 2048, "zyx")])
+        cross_scalars, third_low, second_low, ffn_pieces[1::2], ffn_saved, plan_of((1, 3)), third_scaled, None
+    )
+    ffn_sum = Reduction(ffn_d[1], [(0, 3, "yxz"), (3, 6, "xzy"), (6, 8, "zyx")])
     ffn_e = ffn_bwd_call(
-        cross_scalars, third_low, second_low, ffn_arrays, ffn_saved, ffn_plan((0, 2)), ffn_d[0],
+        cross_scalars, third_low, second_low, ffn_pieces[::2], ffn_saved, plan_of((0, 2)), ffn_d[0],
         (second_hat, second_inv, gains[1]),
     )
     second_back, second_scaled, second_gain, second_bias = ffn_e[:4]
-    second_back = after(second_back, *ffn_sum.start(ffn_e[4], second_gain))
+    ffn_sum.begin(ffn_e[4], second_gain)
+    second_back = after(second_back, *advance([ffn_sum]))
 
     cross_e = attention_bwd_call(
-        cross_scalars, second_back, cross_in, cross_packs, [cross_b[:5]],
-        [(p, h, p > 1, 0, 2 * p + h) for p in (1, 3, 0, 2) for h in (0, 1)], [second_scaled],
+        cross_scalars, second_back, cross_in, cross_pieces[1::2] + cross_pieces[::2], [cross_b[:5]],
+        [(0, 2 * p + h) for p in (1, 3, 0, 2) for h in (0, 1)], [second_scaled],
         (first_hat, first_inv, gains[0]), 2,
     )
     grad_memory, first_back, first_scaled, first_gain, first_bias = cross_e[:5]
     norm_sums = jnp.stack([first_gain, second_gain, third_gain, first_bias, second_bias, third_bias])
-    norm_total = jnp.sum(norm_sums, axis=1)
-    sends = ffn_sum.step(first_gain)
-    cross_sum = Reduction(after(cross_e[5], *sends), [(0, 512, "xzy"), (512, 1024, "yxz")])
-    first_back = after(first_back, *sends, norm_total)
+    norm_sums = jnp.concatenate([jnp.sum(norm_sums, axis=1), jnp.zeros((2, norm_sums.shape[2]), F32)])
+    norm_total = jnp.sum(lax.all_gather(norm_sums, ("dp", "tensor"), axis=0), axis=0)
+    sends = advance([ffn_sum], first_gain)
+    cross_sum = Reduction(after(cross_e[5], *sends), [(0, 4, "xzy"), (4, 8, "yxz")])
+    first_back = after(first_back, *sends, norm_sums)
 
     self_saved = [self_a[:5], self_b[:5]]
     self_d = attention_bwd_call(
-        self_scalars, first_back, [tokens], self_packs, self_saved, plan_of((1, 3)), [first_scaled], None
-    )
-    sends = ffn_sum.step(self_d[0]) + cross_sum.start(cross_e[6], self_d[0])
-    self_sum = Reduction(after(self_d[1], *sends), [(0, 512, "xzy"), (512, 1024, "yxz")])
+        self_scalars, first_back, [tokens], self_pieces[1::2], self_saved, plan_of((1, 3)), [first_scaled], None
+    )
+    cross_sum.begin(cross_e[6], self_d[0])
+    sends = advance([cross_sum, ffn_sum], self_d[0])
+    self_sum = Reduction(after(self_d[1], *sends), [(0, 4, "xzy"), (4, 8, "yxz")])
     gate = after(self_d[0], *sends)
     self_e = attention_bwd_call(
-        self_scalars, first_back, [tokens], self_packs, self_saved, plan_of((0, 2)), [gate], None
+        self_scalars, first_back, [tokens], self_pieces[::2], self_saved, plan_of((0, 2)), [gate], None
     )
     grad_tokens = self_e[0]
-    sends = self_sum.start(self_e[1], grad_tokens)
-    sends = cross_sum.step(*sends)
-    sends = ffn_sum.step(*sends)
-    norm_total = norm_total + after(to_sibling(norm_total), *sends)
-    norm_total = norm_total + over_y(norm_total)
-    sends = self_sum.step(*sends, norm_total)
-    sends = cross_sum.step(*sends)
-    norm_total = norm_total + after(over_x(norm_total), *sends)
-    sends = self_sum.step(*sends, norm_total)
-    cross_sum.step(*sends)
-    norm_total = norm_total + after(over_z_near(norm_total), *sends)
-    sends = self_sum.step(*sends, norm_total)
-    norm_total = norm_total + after(over_z_far(norm_total), *sends)
-    ffn_sum = ffn_sum.last()
-    cross_sum = cross_sum.last()
-    self_sum = self_sum.last()
+    self_sum.begin(self_e[1], grad_tokens)
+    sends = advance([self_sum])
+    sends = advance([cross_sum, ffn_sum], *sends)
+    sends = advance([self_sum], *sends)
+    sends = advance([cross_sum, ffn_sum], *sends)
+    sends = advance([self_sum], *sends)
+    sends = advance([cross_sum], *sends)
+    sends = advance([self_sum], *sends)
+    sends = advance([cross_sum], *sends)
+    advance([self_sum], *sends)
+    self_sum, cross_sum, ffn_sum = self_sum.total, cross_sum.total, ffn_sum.total
 
     def matrices(total):
-        return total.reshape(UNIT, 2, 4, UNIT).transpose(2, 0, 1, 3).reshape(4, UNIT, 2 * UNIT)
+        return total.reshape(2, 4, UNIT, UNIT).transpose(1, 2, 0, 3).reshape(4, UNIT, 2 * UNIT)
 
     self_grads, cross_grads = matrices(self_sum), matrices(cross_sum)
-    ffn_grads = ffn_sum.reshape(UNIT, 4, 2, FFN_PART).transpose(2, 0, 1, 3).reshape(2, UNIT, -1)
+    ffn_grads = ffn_sum.reshape(4, 2, UNIT, FFN_PART).transpose(1, 2, 0, 3).reshape(2, UNIT, -1)
     return (
         out_rows,
         grad_tokens,
@@ -1025,7 +1119,7 @@
         ffn_grads[0],
         ffn_grads[1].T,
         norm_total[:3],
-        norm_total[3:],
+        norm_total[3:6],
     )
 
 

time: 471 us -> 427 us (0.907)
  other arithmetic: 67.3 us -> 4.57 us
  Pallas kernels: 186 us -> 218 us
  local copies, waits for them, and re-layouts: 53 us -> 35.9 us
  between operations: 1.66 us -> 15.1 us
  waiting for transfers between devices: 111 us -> 105 us
    convert_element_type x28 -> x0, other arithmetic: 56.5 us -> none  [add(): return total.astype(BF16)]
    ppermute x11 -> x10, waiting for transfers between devices: 51 us -> 7.92 us  [over_y(): return lax.ppermute(values, 'tensor', swap_pairs(4, 2))]
    pallas_call x0 -> x12, Pallas kernels: none -> 40.1 us  [combine(): pl.pallas_call(kernel, out_shape=list(shapes), in_specs=[ANY] * len(array...]
    all_gather x0 -> x1, waiting for transfers between devices: none -> 27.6 us  [sentence_body(): lax.all_gather(norm_sums, ('dp', 'tensor'), axis=0)]
    squeeze x10 -> x0, local copies, waits for them, and re-layouts: 13.6 us -> none  [the longest x6 7.84 us: send(): terms[:] = [lax.index_in_dim(t, 0, axis, False) for t in terms]]
    reshape x4 -> x2, local copies, waits for them, and re-layouts: 10.5 us -> 0.15 us  [folded(): blocks = values.reshape(values.shape[0], 4, 2 * UNIT)]
    ppermute x30 -> x27, waiting for transfers between devices: 57.4 us -> 66.9 us  [over_dp(): return lax.ppermute(values, 'dp', swap_pairs(8, mask))]
    pallas_call x3, Pallas kernels: 57.5 us -> 48.4 us  [attention_fwd_call(): pl.pallas_call(kernel, out_shape=shapes, in_specs=[SMEM] + [VMEM] * (len(...]
  transfers between devices with their start and end apart: 55 -> 55, of which waited for: 18 -> 16; matrix products, arithmetic and copies ran while one was open for 18% -> 5% of each run, Pallas kernels for 33% -> 40%
where the time goes in v2:
time: 427 us; the launch traced here: 423 us
  Pallas kernels  218 us (51%)
  waiting for transfers between devices  105 us (25%)
  starting transfers between devices  45.2 us (11%)
  local copies, waits for them, and re-layouts  35.9 us (8%)
  between operations  15.1 us (4%)
  other arithmetic  4.57 us (1%)
    pallas_call x3, Pallas kernels, attention_bwd_call(): pl.pallas_call(kernel, out_shape=shapes, in_specs=[SMEM] + [VMEM] * (len(...  68.7 us
    ppermute x27, waiting for transfers between devices, over_dp(): return lax.ppermute(values, 'dp', swap_pairs(8, mask))  66.9 us
    pallas_call x3, Pallas kernels, attention_fwd_call(): pl.pallas_call(kernel, out_shape=shapes, in_specs=[SMEM] + [VMEM] * (len(...  48.4 us
    pallas_call x12, Pallas kernels, combine(): pl.pallas_call(kernel, out_shape=list(shapes), in_specs=[ANY] * len(array...  40.1 us
    pallas_call x2, Pallas kernels, ffn_bwd_call(): pl.pallas_call(kernel, out_shape=shapes, in_specs=specs + [ANY] * len(tai...  34 us
    ppermute x27, starting transfers between devices, over_dp(): return lax.ppermute(values, 'dp', swap_pairs(8, mask))  28.7 us
    all_gather x1, waiting for transfers between devices, sentence_body(): lax.all_gather(norm_sums, ('dp', 'tensor'), axis=0)  27.6 us
    pallas_call x2, Pallas kernels, ffn_fwd_call(): pl.pallas_call(kernel, out_shape=shapes, in_specs=specs + [ANY] * len(tai...  26.8 us
  transfers between devices with their start and end apart: 55, of which 16 were waited for; matrix products, arithmetic and copies ran while one was open for 5% of the time, Pallas kernels for 40%

profile of v2, /device:TPU:0, one launch (start us, length us, event | category | flops | bytes accessed | tf_op | source)
XLA Modules:
  0.0 423.4 jit_solution(4115621217297373676)
XLA Ops:
  17.9 7.8 %collective-permute-done.1 = bf16[4,256,256]{2,1,0:T(8,128)(2,1)S(1)} collective-permute-done((bf16[4,256,256]{2,1,0:T(8,128)(2,1)S(1)}, bf16[4,256,256]{2,1,0:T(8,128)(2,1)S(1)}, u32[]{:S(2)}, u32[]{:S(2)}) %collective-permute-start.1) | collective-permute-done | bytes 524320 | tf_op jit(solution)/shard_map/ppermute | solution.py:888
  30.1 11.3 %self_fwd.2 = (bf16[4,512,128]{2,1,0:T(8,128)(2,1)}, bf16[4,512,128]{2,1,0:T(8,128)(2,1)}, bf16[4,512,128]{2,1,0:T(8,128)(2,1)}, bf16[4,512,128]{2,1,0:T(8,128)(...) custom-call(s32[4]{0:T(128)} %add_add_fusion.1.refs_0_, bf16[512,1024]{1,0:T(8,128)(2,1)} %refs_2_.9, ...), custom_call_target="tpu_custom_call" | custom-call | flops 11879999488 | bytes 4194304 | tf_op jit(solution)/shard_map/self_fwd/pallas_call | solution.py:347
  42.1 11.1 %collective-permute-done.7 = bf16[4,256,256]{2,1,0:T(8,128)(2,1)S(1)} collective-permute-done((bf16[4,256,256]{2,1,0:T(8,128)(2,1)S(1)}, bf16[4,256,256]{2,1,0:T(8,128)(2,1)S(1)}, u32[]{:S(2)}, u32[]{:S(2)}) %collective-permute-start.7) | collective-permute-done | bytes 524320 | tf_op jit(solution)/shard_map/ppermute | solution.py:892
  58.4 9.9 %collective-permute-done.12 = bf16[4,256,256]{2,1,0:T(8,128)(2,1)S(1)} collective-permute-done((bf16[4,256,256]{2,1,0:T(8,128)(2,1)S(1)}, bf16[4,256,256]{2,1,0:T(8,128)(2,1)S(1)}, u32[]{:S(2)}, u32[]{:S(2)}) %collective-permute-start.12) | collective-permute-done | bytes 524320 | tf_op jit(solution)/shard_map/ppermute | solution.py:892
  68.3 10.8 %collective-permute-done.14 = bf16[4,256,256]{2,1,0:T(8,128)(2,1)S(1)} collective-permute-done((bf16[4,256,256]{2,1,0:T(8,128)(2,1)S(1)}, bf16[4,256,256]{2,1,0:T(8,128)(2,1)S(1)}, u32[]{:S(2)}, u32[]{:S(2)}) %collective-permute-start.14) | collective-permute-done | bytes 524320 | tf_op jit(solution)/shard_map/ppermute | solution.py:892
  83.6 14.0 %self_fwd.3 = (bf16[4,512,128]{2,1,0:T(8,128)(2,1)}, bf16[4,512,128]{2,1,0:T(8,128)(2,1)}, bf16[4,512,128]{2,1,0:T(8,128)(2,1)}, bf16[4,512,128]{2,1,0:T(8,128)(...) custom-call(s32[4]{0:T(128)} %add_add_fusion.1.refs_0_, ...), custom_call_target="tpu_custom_call" | custom-call | flops 11879999488 | bytes 4194304 | tf_op jit(solution)/shard_map/self_fwd/pallas_call | solution.py:347
  99.6 23.0 %cross_fwd.1 = (bf16[8,512,128]{2,1,0:T(8,128)(2,1)}, bf16[8,512,128]{2,1,0:T(8,128)(2,1)}, bf16[8,512,128]{2,1,0:T(8,128)(2,1)}, bf16[8,512,128]{2,1,0:T(8,128)...) custom-call(s32[4]{0:T(128)} %add_add_fusion.refs_0_, ...), custom_call_target="tpu_custom_call" | custom-call | flops 23759998976 | bytes 4194304 | tf_op jit(solution)/shard_map/cross_fwd/pallas_call | solution.py:347
  126.9 11.6 %ffn_fwd.2 = (f32[512,1024]{1,0:T(8,128)}, bf16[4,512,512]{2,1,0:T(8,128)(2,1)}, bf16[4,512,512]{2,1,0:T(8,128)(2,1)}) custom-call(s32[4]{0:T(128)} %add_add_fusion.refs_0_, bf16[512,1024]{1,0:T(8,128)(2,1)} %get-tuple-element.143.refs_1_.refs_2_, bf16[1024,1024]{1,0:T(8,128)(2,1)} %refs_7_.3, bf16[1024,1024]{1,0:T(8,128)(2,1)} %refs_8_.3, ...), custom_call_target="tpu_custom_call" | custom-call | flops 13200000000 | bytes 4194304 | tf_op jit(solution)/shard_map/ffn_fwd/pallas_call | solution.py:675
  142.6 15.2 %ffn_fwd.3 = (bf16[512,1024]{1,0:T(8,128)(2,1)}, bf16[512,1024]{1,0:T(8,128)(2,1)}, f32[512,1024]{1,0:T(8,128)}, f32[8,1024]{1,0:T(8,128)}, f32[8,1024]{1,0:T(8,...) custom-call(s32[4]{0:T(128)} %add_add_fusion.refs_0_, ...), custom_call_target="tpu_custom_call" | custom-call | flops 13200000000 | bytes 4194304 | tf_op jit(solution)/shard_map/ffn_fwd/pallas_call | solution.py:675
  157.8 16.2 %ffn_bwd.2 = (f32[512,1024]{1,0:T(8,128)}, bf16[8,2,8,128,256]{4,3,2,1,0:T(8,128)(2,1)}) custom-call(s32[4]{0:T(128)} %add_add_fusion.refs_0_, bf16[512,1024]{1,0:T(8,128)(2,1)} %get-tuple-element.154.refs_1_, bf16[512,1024]{1,0:T(8,128)(2,1)} %get-tuple-element.143.refs_1_.refs_2_, f32[512,1024]{1,0:T(8,128)} %get-tuple-element.156.refs_3_, ...), custom_call_target="tpu_custom_call" | custom-call | flops 18699999232 | bytes 4194304 | tf_op jit(solution)/shard_map/ffn_bwd/pallas_call | solution.py:792
  174.3 17.8 %ffn_bwd.3 = (bf16[512,1024]{1,0:T(8,128)(2,1)}, f32[512,1024]{1,0:T(8,128)}, f32[8,1024]{1,0:T(8,128)}, f32[8,1024]{1,0:T(8,128)}, bf16[8,2,8,128,256]{4,3,2,1,0:T(8,128)(2,1)}) custom-call(s32[4]{0:T(128)} %add_add_fusion.refs_0_, bf16[512,1024]{1,0:T(8,128)(2,1)} %get-tuple-element.154.refs_1_, bf16[512,1024]{1,0:T(8,128)(2,1)} %get-tuple-element.143.refs_1_.refs_2_, ...), custom_call_target="tpu_custom_call" | custom-call | flops 18699999232 | bytes 4194304 | tf_op jit(solution)/shard_map/ffn_bwd/pallas_call | solution.py:792
  192.1 5.2 %combine.12 = (bf16[3,2,2,2,128,256]{5,4,3,2,1,0:T(8,128)(2,1)}, bf16[3,2,2,2,128,256]{5,4,3,2,1,0:T(8,128)(2,1)}, bf16[2,2,2,2,128,256]{5,4,3,2,1,0:T(8,128)(2,1)}) custom-call(bf16[8,2,2,2,2,128,256]{6,5,4,3,2,1,0:T(8,128)(2,1)} %bitcast.79, bf16[8,2,2,2,2,128,256]{6,5,4,3,2,1,0:T(8,128)(2,1)} %bitcast.21.refs_1_.refs_3_.refs_5_.refs_7_), custom_call_target="tpu_custom_call" | custom-call | flops 3300000000 | bytes 4194304 | tf_op jit(solution)/shard_map/combine/pallas_call | solution.py:867
  201.9 34.4 %cross_bwd.1 = (f32[512,1024]{1,0:T(8,128)}, bf16[512,1024]{1,0:T(8,128)(2,1)}, f32[512,1024]{1,0:T(8,128)}, f32[8,1024]{1,0:T(8,128)}, f32[8,1024]{1,0:T(8,128)...) custom-call(s32[4]{0:T(128)} %add_add_fusion.refs_0_, ...), custom_call_target="tpu_custom_call" | custom-call | flops 39600001024 | bytes 4194304 | tf_op jit(solution)/shard_map/cross_bwd/pallas_call | solution.py:494
  239.1 4.0 combine.13
  246.1 17.2 %self_bwd.2 = (f32[512,1024]{1,0:T(8,128)}, bf16[8,2,8,128,128]{4,3,2,1,0:T(8,128)(2,1)}) custom-call(s32[4]{0:T(128)} %add_add_fusion.1.refs_0_, bf16[512,1024]{1,0:T(8,128)(2,1)} %get-tuple-element.189.refs_1_, bf16[512,1024]{1,0:T(8,128)(2,1)} %refs_2_.9, f32[512,1024]{1,0:T(8,128)} %get-tuple-element.190.refs_3_, ...), custom_call_target="tpu_custom_call" | custom-call | flops 19800000512 | bytes 4194304 | tf_op jit(solution)/shard_map/self_bwd/pallas_call | solution.py:494
  266.1 4.8 %combine.14 = (bf16[4,2,2,2,128,128]{5,4,3,2,1,0:T(8,128)(2,1)}, bf16[4,2,2,2,128,128]{5,4,3,2,1,0:T(8,128)(2,1)}, bf16[3,2,128,256]{3,2,1,0:T(8,128)(2,1)}, bf1...) custom-call(bf16[8,2,2,2,2,128,128]{6,5,4,3,2,1,0:T(8,128)(2,1)} %bitcast.84, ...), custom_call_target="tpu_custom_call" | custom-call | flops 3300000000 | bytes 4194304 | tf_op jit(solution)/shard_map/combine/pallas_call | solution.py:867
  275.1 17.1 %self_bwd.3 = (f32[512,1024]{1,0:T(8,128)}, bf16[8,2,8,128,128]{4,3,2,1,0:T(8,128)(2,1)}) custom-call(s32[4]{0:T(128)} %add_add_fusion.1.refs_0_, bf16[512,1024]{1,0:T(8,128)(2,1)} %get-tuple-element.189.refs_1_, bf16[512,1024]{1,0:T(8,128)(2,1)} %refs_2_.9, f32[512,1024]{1,0:T(8,128)} %get-tuple-element.213.refs_3_, bf16[3,1024,256]{2,1,0:T(8,128)(2,1)} %refs_4_.3, ...), custom_call_target="tpu_custom_call" | custom-call | flops 19800000512 | bytes 4194304 | tf_op jit(solution)/shard_map/self_bwd/pallas_call | solution.py:494
  292.2 4.1 combine.15
  299.2 27.6 %all-gather.3.cloned.1.call-done = f32[256,1024]{1,0:T(8,128)} async-done(((f32[8,1024]{1,0:T(8,128)}), f32[256,1024]{1,0:T(8,128)}) %all-gather.3.cloned.1.call-update) | async-done | bytes 1048592 | tf_op jit(solution)/shard_map/all_gather | solution.py:1076
  330.1 3.6 combine.16
  339.3 3.1 combine.17
  343.6 17.9 %collective-permute-done.46.refs_11_ = bf16[8,128,256]{2,1,0:T(8,128)(2,1)S(1)} collective-permute-done((bf16[8,128,256]{2,1,0:T(8,128)(2,1)}, bf16[8,128,256]{2,1,0:T(8,128)(2,1)S(1)}, u32[]{:S(2)}, u32[]{:S(2)}) %collective-permute-start.46) | collective-permute-done | bytes 524320 | tf_op jit(solution)/shard_map/ppermute | solution.py:892
  363.3 3.6 combine.18
  390.5 12.0 %collective-permute-done.53.refs_5_ = bf16[8,128,128]{2,1,0:T(8,128)(2,1)S(1)} collective-permute-done((bf16[8,128,128]{2,1,0:T(8,128)(2,1)}, bf16[8,128,128]{2,1,0:T(8,128)(2,1)S(1)}, u32[]{:S(2)}, u32[]{:S(2)}) %collective-permute-start.53) | collective-permute-done | bytes 262176 | tf_op jit(solution)/shard_map/ppermute | solution.py:892
  (245 shorter events, 105.1 us)
Async XLA Ops:
  7.2 319.7 %all-gather.3.cloned.1.call-start = ((), (), s32[]{:S(2)}) async-start(), calls=%async_computation | async-start | bytes 1081344 | tf_op jit(solution)/shard_map/all_gather | solution.py:1076
  16.0 26.1 %collective-permute-start = (bf16[4,256,256]{2,1,0:T(8,128)(2,1)S(1)}, bf16[4,256,256]{2,1,0:T(8,128)(2,1)S(1)}, u32[]{:S(2)}, u32[]{:S(2)}) collective-permute-start(bf16[4,256,256]{2,1,0:T(8,128)(2,1)S(1)} %pad_maximum_fusion.3), channel_id=1, source_target_pairs={{0,2},{1,3},{2,0},{3,1},{4,6},{5,7},{6,4},{7,5},{8,10},{9,11},{10,... | collective-permute-start | bytes 1572872 | tf_op jit(solution)/shard_map/ppermute | solution.py:888
  53.4 28.9 %collective-permute-start.8 = (bf16[4,4,256,256]{3,2,1,0:T(8,128)(2,1)S(1)}, bf16[4,4,256,256]{3,2,1,0:T(8,128)(2,1)S(1)}, u32[]{:S(2)}, u32[]{:S(2)}) collective-permute-start(bf16[4,4,256,256]{3,2,1,0:T(8,128)(2,1)S(1)} %pad_maximum_fusion.refs_6_), channel_id=1, source_target_pairs={{0,1},{1,0},{2,3},{3,2},{4,5},{5,4},{6,7},{7,6},{8,9},{9,8},{10,11... | collective-permute-start | bytes 6291464 | tf_op jit(solution)/shard_map/ppermute | solution.py:884
  56.8 25.1 %collective-permute-start.4 = (bf16[2,256,1024]{2,1,0:T(8,128)(2,1)S(1)}, bf16[2,256,1024]{2,1,0:T(8,128)(2,1)}, u32[]{:S(2)}, u32[]{:S(2)}) collective-permute-start(bf16[2,256,1024]{2,1,0:T(8,128)(2,1)S(1)} %pad_maximum_fusion.2), channel_id=1, source_target_pairs={{0,2},{1,3},{2,0},{3,1},{4,6},{5,7},{6,4},{7,5},{8,10},{9,11},{10,... | collective-permute-start | bytes 3145736 | tf_op jit(solution)/shard_map/ppermute | solution.py:888
  82.3 42.5 %collective-permute-start.16 = (bf16[1024,1024]{1,0:T(8,128)(2,1)S(1)}, bf16[1024,1024]{1,0:T(8,128)(2,1)}, u32[]{:S(2)}, u32[]{:S(2)}) collective-permute-start(bf16[1024,1024]{1,0:T(8,128)(2,1)S(1)} %copy-done.26), channel_id=1, source_target_pairs={{0,1},{1,0},{2,3},{3,2},{4,5},{5,4},{6,7},{7,6},{8,9},{9,8},{10,11... | collective-permute-start | bytes 6291464 | tf_op jit(solution)/shard_map/ppermute | solution.py:884
  97.7 27.8 %collective-permute-start.17 = (bf16[1024,1024]{1,0:T(8,128)(2,1)S(1)}, bf16[1024,1024]{1,0:T(8,128)(2,1)}, u32[]{:S(2)}, u32[]{:S(2)}) collective-permute-start(bf16[1024,1024]{1,0:T(8,128)(2,1)S(1)} %copy-done.27), channel_id=1, source_target_pairs={{0,1},{1,0},{2,3},{3,2},{4,5},{5,4},{6,7},{7,6},{8,9},{9,8},{10,11... | collective-permute-start | bytes 6291464 | tf_op jit(solution)/shard_map/ppermute | solution.py:884
  97.9 41.8 %collective-permute-start.22 = (bf16[2,256,1024]{2,1,0:T(8,128)(2,1)}, bf16[2,256,1024]{2,1,0:T(8,128)(2,1)}, u32[]{:S(2)}, u32[]{:S(2)}) collective-permute-start(bf16[2,256,1024]{2,1,0:T(8,128)(2,1)} %collective-permute-done.4.refs_9_), channel_id=1, source_target_pairs={{0,1},{1,0},{2,3},{3,2},{4,5},{5,4},{6,7},{7,6},{8,9},{9,8},{10,11... | collective-permute-start | bytes 3145736 | tf_op jit(solution)/shard_map/ppermute | solution.py:884
  98.5 25.7 %collective-permute-start.19 = (bf16[2,256,1024]{2,1,0:T(8,128)(2,1)}, bf16[2,256,1024]{2,1,0:T(8,128)(2,1)S(1)}, u32[]{:S(2)}, u32[]{:S(2)}) collective-permute-start(bf16[2,256,1024]{2,1,0:T(8,128)(2,1)} %collective-permute-done.4.refs_9_), channel_id=1, source_target_pairs={{0,8},{4,12},{8,0},{12,4},{16,24},{20,28},{24,16},{28,20},{1,9},{5... | collective-permute-start | bytes 3145736 | tf_op jit(solution)/shard_map/ppermute | solution.py:892
  98.9 25.2 %collective-permute-start.18 = (bf16[2,256,1024]{2,1,0:T(8,128)(2,1)}, bf16[2,256,1024]{2,1,0:T(8,128)(2,1)S(1)}, u32[]{:S(2)}, u32[]{:S(2)}) collective-permute-start(bf16[2,256,1024]{2,1,0:T(8,128)(2,1)} %collective-permute-done.4.refs_9_), channel_id=1, source_target_pairs={{0,4},{4,0},{8,12},{12,8},{16,20},{20,16},{24,28},{28,24},{1,5},{5... | collective-permute-start | bytes 3145736 | tf_op jit(solution)/shard_map/ppermute | solution.py:892
  197.3 39.0 %collective-permute-start.30 = (bf16[2,2,2,2,128,256]{5,4,3,2,1,0:T(8,128)(2,1)}, bf16[2,2,2,2,128,256]{5,4,3,2,1,0:T(8,128)(2,1)S(1)}, u32[]{:S(2)}, u32[]{:S(2)}) collective-permute-start(bf16[2,2,2,2,128,256]{5,4,3,2,1,0:T(8,128)(2,1)} %get-tuple-element.169), channel_id=1, source_target_pairs={{0,8},{4,12},{8,0},{12,4},{16,24},{20,28},{24,16},{28,20},{1,9},{5... | collective-permute-start | bytes 3145736 | tf_op jit(solution)/shard_map/ppermute | solution.py:892
  198.9 37.5 %collective-permute-start.28 = (bf16[3,2,2,2,128,256]{5,4,3,2,1,0:T(8,128)(2,1)}, bf16[3,2,2,2,128,256]{5,4,3,2,1,0:T(8,128)(2,1)S(1)}, u32[]{:S(2)}, u32[]{:S(2)}) collective-permute-start(bf16[3,2,2,2,128,256]{5,4,3,2,1,0:T(8,128)(2,1)} %get-tuple-element.167), channel_id=1, source_target_pairs={{0,2},{1,3},{2,0},{3,1},{4,6},{5,7},{6,4},{7,5},{8,10},{9,11},{10,... | collective-permute-start | bytes 4718600 | tf_op jit(solution)/shard_map/ppermute | solution.py:888
  200.4 36.3 %collective-permute-start.29 = (bf16[3,2,2,2,128,256]{5,4,3,2,1,0:T(8,128)(2,1)}, bf16[3,2,2,2,128,256]{5,4,3,2,1,0:T(8,128)(2,1)S(1)}, u32[]{:S(2)}, u32[]{:S(2)}) collective-permute-start(bf16[3,2,2,2,128,256]{5,4,3,2,1,0:T(8,128)(2,1)} %get-tuple-element.168), channel_id=1, source_target_pairs={{0,4},{4,0},{8,12},{12,8},{16,20},{20,16},{24,28},{28,24},{1,5},{5... | collective-permute-start | bytes 4718600 | tf_op jit(solution)/shard_map/ppermute | solution.py:892
  271.0 26.2 %collective-permute-start.41 = (bf16[2,2,128,256]{3,2,1,0:T(8,128)(2,1)}, bf16[2,2,128,256]{3,2,1,0:T(8,128)(2,1)S(1)}, u32[]{:S(2)}, u32[]{:S(2)}) collective-permute-start(bf16[2,2,128,256]{3,2,1,0:T(8,128)(2,1)} %get-tuple-element.212), channel_id=1, source_target_pairs={{0,4},{4,0},{8,12},{12,8},{16,20},{20,16},{24,28},{28,24},{1,5},{5... | collective-permute-start | bytes 786440 | tf_op jit(solution)/shard_map/ppermute | solution.py:892
  271.9 26.8 %collective-permute-start.40 = (bf16[3,2,128,256]{3,2,1,0:T(8,128)(2,1)}, bf16[3,2,128,256]{3,2,1,0:T(8,128)(2,1)S(1)}, u32[]{:S(2)}, u32[]{:S(2)}) collective-permute-start(bf16[3,2,128,256]{3,2,1,0:T(8,128)(2,1)} %get-tuple-element.211), channel_id=1, source_target_pairs={{0,2},{1,3},{2,0},{3,1},{4,6},{5,7},{6,4},{7,5},{8,10},{9,11},{10,... | collective-permute-start | bytes 1179656 | tf_op jit(solution)/shard_map/ppermute | solution.py:888
  273.4 54.7 %collective-permute-start.37 = (bf16[4,2,2,2,128,128]{5,4,3,2,1,0:T(8,128)(2,1)}, bf16[4,2,2,2,128,128]{5,4,3,2,1,0:T(8,128)(2,1)S(1)}, u32[]{:S(2)}, u32[]{:S(2)}) collective-permute-start(bf16[4,2,2,2,128,128]{5,4,3,2,1,0:T(8,128)(2,1)} %get-tuple-element.208), channel_id=1, source_target_pairs={{0,4},{4,0},{8,12},{12,8},{16,20},{20,16},{24,28},{28,24},{1,5},{5... | collective-permute-start | bytes 3145736 | tf_op jit(solution)/shard_map/ppermute | solution.py:892
  274.0 54.2 %collective-permute-start.38 = (bf16[4,2,2,2,128,128]{5,4,3,2,1,0:T(8,128)(2,1)}, bf16[4,2,2,2,128,128]{5,4,3,2,1,0:T(8,128)(2,1)S(1)}, u32[]{:S(2)}, u32[]{:S(2)}) collective-permute-start(bf16[4,2,2,2,128,128]{5,4,3,2,1,0:T(8,128)(2,1)} %get-tuple-element.209), channel_id=1, source_target_pairs={{0,2},{1,3},{2,0},{3,1},{4,6},{5,7},{6,4},{7,5},{8,10},{9,11},{10,... | collective-permute-start | bytes 3145736 | tf_op jit(solution)/shard_map/ppermute | solution.py:888
  296.3 42.0 %collective-permute-start.42 = (bf16[4,2,2,2,128,128]{5,4,3,2,1,0:T(8,128)(2,1)}, bf16[4,2,2,2,128,128]{5,4,3,2,1,0:T(8,128)(2,1)S(1)}, u32[]{:S(2)}, u32[]{:S(2)}) collective-permute-start(bf16[4,2,2,2,128,128]{5,4,3,2,1,0:T(8,128)(2,1)} %get-tuple-element.221), channel_id=1, source_target_pairs={{0,2},{1,3},{2,0},{3,1},{4,6},{5,7},{6,4},{7,5},{8,10},{9,11},{10,... | collective-permute-start | bytes 3145736 | tf_op jit(solution)/shard_map/ppermute | solution.py:888
  297.2 41.1 %collective-permute-start.36 = (bf16[4,2,2,2,128,128]{5,4,3,2,1,0:T(8,128)(2,1)}, bf16[4,2,2,2,128,128]{5,4,3,2,1,0:T(8,128)(2,1)}, u32[]{:S(2)}, u32[]{:S(2)}) collective-permute-start(bf16[4,2,2,2,128,128]{5,4,3,2,1,0:T(8,128)(2,1)} %get-tuple-element.220), channel_id=1, source_target_pairs={{0,4},{4,0},{8,12},{12,8},{16,20},{20,16},{24,28},{28,24},{1,5},{5... | collective-permute-start | bytes 3145736 | tf_op jit(solution)/shard_map/ppermute | solution.py:892
  298.7 29.4 %collective-permute-start.39 = (bf16[3,2,128,256]{3,2,1,0:T(8,128)(2,1)}, bf16[3,2,128,256]{3,2,1,0:T(8,128)(2,1)}, u32[]{:S(2)}, u32[]{:S(2)}) collective-permute-start(bf16[3,2,128,256]{3,2,1,0:T(8,128)(2,1)} %get-tuple-element.210), channel_id=1, source_target_pairs={{0,8},{4,12},{8,0},{12,4},{16,24},{20,28},{24,16},{28,20},{1,9},{5... | collective-permute-start | bytes 1179656 | tf_op jit(solution)/shard_map/ppermute | solution.py:892
  333.7 27.7 %collective-permute-start.44 = (bf16[4,2,2,128,128]{4,3,2,1,0:T(8,128)(2,1)}, bf16[4,2,2,128,128]{4,3,2,1,0:T(8,128)(2,1)S(1)}, u32[]{:S(2)}, u32[]{:S(2)}) collective-permute-start(bf16[4,2,2,128,128]{4,3,2,1,0:T(8,128)(2,1)} %get-tuple-element.227), channel_id=1, source_target_pairs={{0,8},{4,12},{8,0},{12,4},{16,24},{20,28},{24,16},{28,20},{1,9},{5... | collective-permute-start | bytes 1572872 | tf_op jit(solution)/shard_map/ppermute | solution.py:892
  334.3 27.1 %collective-permute-start.45 = (bf16[4,2,2,128,128]{4,3,2,1,0:T(8,128)(2,1)}, bf16[4,2,2,128,128]{4,3,2,1,0:T(8,128)(2,1)S(1)}, u32[]{:S(2)}, u32[]{:S(2)}) collective-permute-start(bf16[4,2,2,128,128]{4,3,2,1,0:T(8,128)(2,1)} %get-tuple-element.228), channel_id=1, source_target_pairs={{0,4},{4,0},{8,12},{12,8},{16,20},{20,16},{24,28},{28,24},{1,5},{5... | collective-permute-start | bytes 1572872 | tf_op jit(solution)/shard_map/ppermute | solution.py:892
  335.4 26.0 %collective-permute-start.46 = (bf16[8,128,256]{2,1,0:T(8,128)(2,1)}, bf16[8,128,256]{2,1,0:T(8,128)(2,1)S(1)}, u32[]{:S(2)}, u32[]{:S(2)}) collective-permute-start(bf16[8,128,256]{2,1,0:T(8,128)(2,1)} %get-tuple-element.229), channel_id=1, source_target_pairs={{0,16},{4,20},{8,24},{12,28},{16,0},{20,4},{24,8},{28,12},{1,17},{... | collective-permute-start | bytes 1572872 | tf_op jit(solution)/shard_map/ppermute | solution.py:892
  342.5 29.0 %collective-permute-start.43 = (bf16[4,2,2,128,128]{4,3,2,1,0:T(8,128)(2,1)}, bf16[4,2,2,128,128]{4,3,2,1,0:T(8,128)(2,1)S(1)}, u32[]{:S(2)}, u32[]{:S(2)}) collective-permute-start(bf16[4,2,2,128,128]{4,3,2,1,0:T(8,128)(2,1)} %get-tuple-element.232), channel_id=1, source_target_pairs={{0,8},{4,12},{8,0},{12,4},{16,24},{20,28},{24,16},{28,20},{1,9},{5... | collective-permute-start | bytes 1572872 | tf_op jit(solution)/shard_map/ppermute | solution.py:892
  342.6 28.8 %collective-permute-start.47 = (bf16[4,2,2,128,128]{4,3,2,1,0:T(8,128)(2,1)}, bf16[4,2,2,128,128]{4,3,2,1,0:T(8,128)(2,1)S(1)}, u32[]{:S(2)}, u32[]{:S(2)}) collective-permute-start(bf16[4,2,2,128,128]{4,3,2,1,0:T(8,128)(2,1)} %get-tuple-element.233), channel_id=1, source_target_pairs={{0,4},{4,0},{8,12},{12,8},{16,20},{20,16},{24,28},{28,24},{1,5},{5... | collective-permute-start | bytes 1572872 | tf_op jit(solution)/shard_map/ppermute | solution.py:892
  (77 other events, 678.1 us)
Sparse Core Ops, SparseCore 0:
  271.1 55.6 all-gather.2

commit v3 on v2

--- a/solution.py
+++ b/solution.py
@@ -21,6 +21,10 @@
 
 def dot(left, right):
     return lax.dot_general(left, right, (((1,), (0,)), ((), ())), preferred_element_type=F32)
+
+
+def dot_tn(left, right):
+    return lax.dot_general(left, right, (((0,), (0,)), ((), ())), preferred_element_type=F32)
 
 
 def dot_nt(left, right):
@@ -184,13 +188,9 @@
     lax.fori_loop(0, rows // ROW_CHUNK, step, 0)
 
 
-def transpose_shards(source, target, dp):
-    for position in range(8):
-        block = dp ^ shard_of(position)
-        columns = source[:, pl.ds(pl.multiple_of(block * UNIT, UNIT), UNIT)]
-        target[position * UNIT : (position + 1) * UNIT, :] = jnp.transpose(
-            columns.astype(F32)
-        ).astype(BF16)
+def store_shards(target, weight, dp):
+    for block in range(8):
+        target[shard_of(block ^ dp)] = weight[block * UNIT : (block + 1) * UNIT]
 
 
 SMEM = pl.BlockSpec(memory_space=pltpu.SMEM)
@@ -198,7 +198,7 @@
 ANY = pl.BlockSpec(memory_space=pl.ANY)
 
 
-def params(limit=56):
+def params(limit=62):
     return pltpu.CompilerParams(vmem_limit_bytes=limit * 1024 * 1024)
 
 
@@ -210,7 +210,7 @@
     return jax.ShapeDtypeStruct(shape, dtype)
 
 
-def weight_copies(pieces, order, wbuf, obuf, wsem, osem):
+def weight_copies(pieces, order, wbuf, obuf, wsem, osem, columns=(0, 1, 2)):
     groups, outs = [[], [], []], []
     wide = 2 * UNIT
     for index, refs in enumerate(pieces):
@@ -219,18 +219,20 @@
             column = 0
             for ref in refs[:-1]:
                 for source in [ref] if len(ref.shape) == 2 else [ref.at[c] for c in range(ref.shape[0])]:
-                    low = (column * len(pieces) + index) * wide
-                    groups[column].append(copy_of(source, wbuf.at[:, low : low + wide], wsem.at[column, index, 0]))
+                    if column in columns:
+                        low = (columns.index(column) * len(pieces) + index) * wide
+                        groups[column].append(copy_of(source, wbuf.at[:, low : low + wide], wsem.at[column, index, 0]))
                     column += 1
-            outs.append(copy_of(refs[-1], obuf.at[at, :], osem.at[index, 0]))
+            if obuf is not None:
+                outs.append(copy_of(refs[-1], obuf.at[at, :], osem.at[index, 0]))
             continue
         rest, = refs
         rows = rest.shape[2]
         part = wide // 4
         for quarter in range(4):
             place = quarter ^ order
-            for column in range(3):
-                low = (column * len(pieces) + index) * wide
+            for column in columns:
+                low = (columns.index(column) * len(pieces) + index) * wide
                 groups[column].append(
                     copy_of(
                         rest.at[quarter, column],
@@ -238,7 +240,7 @@
                         wsem.at[column, index, quarter],
                     )
                 )
-            for block in range(4):
+            for block in range(4 if obuf is not None else 0):
                 outs.append(
                     copy_of(
                         rest.at[quarter, 3, block * part : (block + 1) * part, :],
@@ -351,7 +353,7 @@
         out_specs=[VMEM] * len(shapes),
         scratch_shapes=scratch,
         compiler_params=params(),
-        cost_estimate=cost_of(2.7 * number),
+        cost_estimate=cost_of(0.6 * number),
         name="self_fwd" if causal else "cross_fwd",
     )(*args, *tail)
 
@@ -361,6 +363,7 @@
     causal = len(others) == 1
     number, n_in, wide = len(plan), len(others), len(plan) * UNIT
     last = norm is not None
+    skip = 1 if last else 0
 
     def kernel(*refs):
         it = iter(refs)
@@ -369,23 +372,21 @@
         in_refs = [next(it) for _ in range(n_in)]
         gain_ref = next(it) if last else None
         late_in = [next(it), next(it)] if last else []
-        acc_in = [next(it) for _ in carried]
+        acc_in = next(it) if last else None
         w_refs = [[next(it) for _ in piece] for piece in pieces]
         s_refs = [[next(it) for _ in call] for call in saved]
-        sums = [None if last and not index else next(it) for index in range(n_in)]
         if last:
             low_ref, scaled_ref, gsum_ref, bsum_ref = (next(it) for _ in range(4))
+        dall_ref = next(it)
         g_refs = [next(it) for _ in range(results)]
-        wbuf, obuf, sbuf, lbuf, att_all, grad_all, h_t = (next(it) for _ in range(7))
-        in_t = [next(it) for _ in range(n_in)]
-        dall, stage, diagonal = next(it), next(it), next(it)
-        if last:
-            acc, hat, inv = next(it), next(it), next(it)
-            sums[0] = acc
+        wbuf, obuf, sbuf, lbuf, att_all, grad_all = (next(it) for _ in range(6))
+        stage, diagonal = next(it), next(it)
+        if last:
+            dquery, acc, hat, inv = (next(it) for _ in range(4))
         wsem, osem, ssem, gsem, lsem = (next(it) for _ in range(5))
         length, order, dp = sc[0], sc[1], sc[2]
 
-        groups, o_copies = weight_copies(w_refs, order, wbuf, obuf, wsem, osem)
+        groups, o_copies = weight_copies(w_refs, order, wbuf, obuf, wsem, osem, (0,) if last else ())
         for copy in o_copies:
             copy.start()
         s_copies = []
@@ -396,17 +397,16 @@
                 s_copies.append(copy_of(call[c].at[unit[1]], sbuf.at[index, c], ssem.at[c, index]))
             s_copies.append(copy_of(call[3].at[unit[1]], att_all.at[:, lanes], ssem.at[3, index]))
             s_copies.append(copy_of(call[4].at[unit[1]], lbuf.at[index], ssem.at[4, index]))
-        w_copies = groups[0] + groups[1] + groups[2]
-        late = [copy_of(source, sums[index], lsem.at[index]) for index, source in enumerate(acc_in)]
-        if last:
-            late += [copy_of(late_in[0], hat, lsem.at[2]), copy_of(late_in[1], inv, lsem.at[3])]
-        for copy in s_copies + w_copies + late:
+        late = []
+        if last:
+            late = groups[0] + [
+                copy_of(source, target, lsem.at[index])
+                for index, (source, target) in enumerate(((acc_in, acc), (late_in[0], hat), (late_in[1], inv)))
+            ]
+        for copy in s_copies + late:
             copy.start()
         if causal:
             fill_diagonal(diagonal)
-        transpose_shards(h_ref, h_t, dp)
-        for ref, target in zip(in_refs, in_t):
-            transpose_shards(ref, target, dp)
         for copy in o_copies:
             copy.wait()
         grad_att = dot_nt(h_ref[...], obuf[...]).astype(BF16)
@@ -420,70 +420,63 @@
             parts = attend_back_unit(
                 sbuf[u, 0], sbuf[u, 1], sbuf[u, 2], att_all[:, at], grad_all[u], length, causal, diagonal, lbuf.at[u]
             )
-            for c in range(3):
-                dall[:, pl.ds(pl.multiple_of(c * wide + u * UNIT, UNIT), UNIT)] = parts[c]
+            if last:
+                dquery[:, at] = parts[0]
+            for c in range(skip, 3):
+                dall_ref[:, pl.ds(pl.multiple_of((c - skip) * wide + u * UNIT, UNIT), UNIT)] = parts[c]
             return carry
 
         lax.fori_loop(0, number, step, 0)
 
         share = number // 2 // results
 
-        def keep(weight, column):
+        def keep(rows_in, source, column):
+            weight = dot_tn(rows_in[...], source).astype(BF16)
             for index in range(number):
-                part = weight[:, index * UNIT : (index + 1) * UNIT].astype(BF16)
                 piece = index // 2
-                stage[piece // share, (index % 2) * 4 + column, piece % share] = part.reshape(8, UNIT, UNIT)
-
-        for c in range(3):
-            rows_t = in_t[0] if causal or c == 0 else in_t[1]
-            keep(dot(rows_t[...], dall[:, c * wide : (c + 1) * wide]), c)
-        keep(dot(h_t[...], att_all[...]), 3)
+                target = stage.at[piece // share, (index % 2) * 4 + column, piece % share]
+                store_shards(target, weight[:, index * UNIT : (index + 1) * UNIT], dp)
+
+        if last:
+            keep(in_refs[0], dquery[...], 0)
+        for c in range(skip, 3):
+            keep(in_refs[-1], dall_ref[:, (c - skip) * wide : (c - skip + 1) * wide], c)
+        keep(h_ref, att_all[...], 3)
         g_copies = [copy_of(stage.at[index], ref, gsem.at[index]) for index, ref in enumerate(g_refs)]
         for copy in g_copies:
             copy.start()
-        for copy in w_copies + late[: len(acc_in)]:
+        for copy in late:
             copy.wait()
-        if causal:
-            sums[0][...] += dot_nt(dall[...], wbuf[...])
-        else:
-            sums[0][...] += dot_nt(dall[:, :wide], wbuf[:, :wide])
-            memory_sum = dot_nt(dall[:, wide:], wbuf[:, wide:])
-            sums[1][...] = memory_sum + sums[1][...] if len(acc_in) == n_in else memory_sum
-        if last:
-            for copy in late[len(acc_in) :]:
-                copy.wait()
+        if last:
+            acc[...] += dot_nt(dquery[...], wbuf[...])
             norm_back_rows(acc, hat, inv, gain_ref, low_ref, scaled_ref, gsum_ref, bsum_ref, rows)
         for copy in g_copies:
             copy.wait()
 
     big = sds((rows, depth), F32)
-    shapes = [big] * (n_in - 1 if last else n_in)
+    shapes = []
     if last:
         shapes += [sds((rows, depth), BF16), big, sds((8, depth), F32), sds((8, depth), F32)]
+    shapes.append(sds((rows, (3 - skip) * wide), BF16))
     specs_out = [VMEM] * len(shapes) + [ANY] * results
     shapes += [sds((8, number // 2 // results, 8, UNIT, UNIT), BF16)] * results
     args = [scalars, grad_low, *others] + ([norm[2]] if last else [])
-    tail = ([norm[0], norm[1]] if last else []) + list(carried)
+    tail = [norm[0], norm[1], carried] if last else []
     tail += [array for piece in pieces for array in piece]
     for call in saved:
         tail += call
     scratch = [
-        pltpu.VMEM((depth, 3 * wide), BF16),
+        pltpu.VMEM((depth, wide) if last else (16, 128), BF16),
         pltpu.VMEM((wide, depth), BF16),
         pltpu.VMEM((number, 3, rows, UNIT), BF16),
         pltpu.VMEM((number, 2, rows), F32),
         pltpu.VMEM((rows, wide), BF16),
         pltpu.VMEM((number, rows, UNIT), BF16),
-        pltpu.VMEM((depth, rows), BF16),
-    ]
-    scratch += [pltpu.VMEM((depth, rows), BF16)] * n_in
-    scratch += [
-        pltpu.VMEM((rows, 3 * wide), BF16),
         pltpu.VMEM((results, 8, number // 2 // results, 8, UNIT, UNIT), BF16),
         pltpu.VMEM((QUERY_BLOCK, QUERY_BLOCK), F32),
     ]
     if last:
-        scratch += [pltpu.VMEM((rows, depth), F32), pltpu.VMEM((rows, depth), F32), pltpu.VMEM((rows, 128), F32)]
+        scratch += [pltpu.VMEM((rows, wide), BF16), pltpu.VMEM((rows, depth), F32), pltpu.VMEM((rows, depth), F32), pltpu.VMEM((rows, 128), F32)]
     scratch += [
         pltpu.SemaphoreType.DMA((3, len(pieces), 4)),
         pltpu.SemaphoreType.DMA((len(pieces), 16)),
@@ -498,8 +491,49 @@
         out_specs=specs_out,
         scratch_shapes=scratch,
         compiler_params=params(),
-        cost_estimate=cost_of(4.5 * number),
+        cost_estimate=cost_of(4.2 * number),
         name="self_bwd" if causal else "cross_bwd",
+    )(*args, *tail)
+
+
+def inputs_back_call(scalars, base, parts, memory_part):
+    rows, depth = base.shape
+    jobs = [(0, grad, pieces, (0, 1, 2)) for grad, pieces in parts] + [(1, *memory_part, (1, 2))]
+
+    def kernel(*refs):
+        it = iter(refs)
+        sc, base_ref = next(it), next(it)
+        grads = [next(it) for _ in jobs]
+        w_refs = [[[next(it) for _ in piece] for piece in pieces] for _, _, pieces, _ in jobs]
+        outs = [next(it), next(it)]
+        bufs, sems = [next(it) for _ in jobs], [next(it) for _ in jobs]
+        copies = []
+        for index, (_, _, _, columns) in enumerate(jobs):
+            groups, _ = weight_copies(w_refs[index], sc[1], bufs[index], None, sems[index], None, columns)
+            copies.append([copy for group in groups for copy in group])
+            for copy in copies[-1]:
+                copy.start()
+        outs[0][...] = base_ref[...]
+        for index, (out, _, _, _) in enumerate(jobs):
+            for copy in copies[index]:
+                copy.wait()
+            if out:
+                outs[1][...] = dot_nt(grads[index][...], bufs[index][...])
+            else:
+                outs[0][...] += dot_nt(grads[index][...], bufs[index][...])
+
+    args = [scalars, base] + [grad for _, grad, _, _ in jobs]
+    tail = [array for _, _, pieces, _ in jobs for piece in pieces for array in piece]
+    return pl.pallas_call(
+        kernel,
+        out_shape=[sds((rows, depth), F32)] * 2,
+        in_specs=[SMEM] + [VMEM] * (len(args) - 1) + [ANY] * len(tail),
+        out_specs=[VMEM] * 2,
+        scratch_shapes=[pltpu.VMEM((depth, grad.shape[1]), BF16) for _, grad, _, _ in jobs]
+        + [pltpu.SemaphoreType.DMA((3, len(pieces), 4)) for _, _, pieces, _ in jobs],
+        compiler_params=params(),
+        cost_estimate=cost_of(12),
+        name="inputs_back",
     )(*args, *tail)
 
 
@@ -702,7 +736,7 @@
         else:
             sum_ref = next(it)
         g_ref = next(it)
-        ubuf, dbuf, abuf, sbuf, gbuf, x_t, g_t, stage, psem = (next(it) for _ in range(9))
+        ubuf, dbuf, abuf, sbuf, gbuf, stage, psem = (next(it) for _ in range(7))
         if last:
             acc, hat, inv, lsem = (next(it) for _ in range(4))
         wsem, ssem, gsem = next(it), next(it), next(it)
@@ -724,8 +758,6 @@
             late = [copy_of(late_in[0], hat, lsem.at[0]), copy_of(late_in[1], inv, lsem.at[1])]
             for copy in late:
                 copy.start()
-        transpose_shards(g_in, g_t, dp)
-        transpose_shards(x_ref, x_t, dp)
         for index in range(number):
             if index % 2 == 0:
                 for copy in downs[index // 2]:
@@ -736,16 +768,16 @@
         for copy in acts:
             copy.wait()
 
-        def keep(rows_t, source, column):
+        def keep(rows_in, source, column):
             for half in range(number // 2):
                 wide = 2 * FFN_UNIT
-                weight = dot(rows_t[...], source[:, half * wide : (half + 1) * wide]).astype(BF16)
+                weight = dot_tn(rows_in[...], source[:, half * wide : (half + 1) * wide]).astype(BF16)
                 for inner in range(4):
                     part = weight[:, inner * FFN_PART : (inner + 1) * FFN_PART]
-                    stage[2 * inner + column, half] = part.reshape(8, UNIT, FFN_PART)
-
-        keep(x_t, gbuf, 0)
-        keep(g_t, abuf, 1)
+                    store_shards(stage.at[2 * inner + column, half], part, dp)
+
+        keep(x_ref, gbuf, 0)
+        keep(g_in, abuf, 1)
         g_copies = [copy_of(stage, g_ref, gsem)]
         for copy in g_copies:
             copy.start()
@@ -776,8 +808,6 @@
         pltpu.VMEM((rows, number * FFN_UNIT), BF16),
         pltpu.VMEM((number, rows, FFN_UNIT), BF16),
         pltpu.VMEM((rows, number * FFN_UNIT), BF16),
-        pltpu.VMEM((depth, rows), BF16),
-        pltpu.VMEM((depth, rows), BF16),
         pltpu.VMEM((8, number // 2, 8, UNIT, FFN_PART), BF16),
         pltpu.SemaphoreType.DMA,
     ]
@@ -1015,11 +1045,11 @@
     self_side, self_up, cross_near = (after(w, self_a[4]) for w in (self_side, self_up, cross_near))
     self_corner = over_x(self_up)
     cross_side, cross_up = over_x(cross_near), over_z_near(cross_near)
-    self_rest = jnp.stack([self_near, self_side, self_up, self_corner])
+    self_rest = jnp.stack([after(self_near, cross_near), self_side, self_up, self_corner])
     self_far = to_sibling(self_rest)
     self_pieces = [self_own, self_sib, (self_rest,), (self_far,)]
     self_b = attention_fwd_call(
-        after(self_scalars, cross_near, ffn_near), [tokens], [tokens], self_pieces[2:], self_a[5], (gains[0], biases[0])
+        after(self_scalars, cross_near), [tokens], [tokens], self_pieces[2:], self_a[5], (gains[0], biases[0])
     )
     first_low, first_hat, first_inv = self_b[5:]
     cross_own = (cross_q, cross_kv, cross_out)
@@ -1028,7 +1058,7 @@
     ffn_sib = tuple(to_sibling(after(w, self_near)) for w in ffn_own)
     cross_in = [first_low, memory]
     cross_corner = over_x(cross_up)
-    cross_rest = jnp.stack([cross_near, cross_side, cross_up, cross_corner])
+    cross_rest = jnp.stack([cross_near, cross_side, cross_up, after(cross_corner, self_b[4], ffn_near)])
     cross_far = to_sibling(cross_rest)
     ffn_side, ffn_up = over_x(ffn_near), over_z_near(ffn_near)
     cross_pieces = [cross_own, cross_sib, (cross_rest,), (cross_far,)]
@@ -1067,39 +1097,41 @@
 
     cross_e = attention_bwd_call(
         cross_scalars, second_back, cross_in, cross_pieces[1::2] + cross_pieces[::2], [cross_b[:5]],
-        [(0, 2 * p + h) for p in (1, 3, 0, 2) for h in (0, 1)], [second_scaled],
+        [(0, 2 * p + h) for p in (1, 3, 0, 2) for h in (0, 1)], second_scaled,
         (first_hat, first_inv, gains[0]), 2,
     )
-    grad_memory, first_back, first_scaled, first_gain, first_bias = cross_e[:5]
+    first_back, first_scaled, first_gain, first_bias, memory_part = cross_e[:5]
     norm_sums = jnp.stack([first_gain, second_gain, third_gain, first_bias, second_bias, third_bias])
     norm_sums = jnp.concatenate([jnp.sum(norm_sums, axis=1), jnp.zeros((2, norm_sums.shape[2]), F32)])
-    norm_total = jnp.sum(lax.all_gather(norm_sums, ("dp", "tensor"), axis=0), axis=0)
+    norm_sums = lax.all_gather(norm_sums, ("dp", "tensor"), axis=0)
     sends = advance([ffn_sum], first_gain)
     cross_sum = Reduction(after(cross_e[5], *sends), [(0, 4, "xzy"), (4, 8, "yxz")])
-    first_back = after(first_back, *sends, norm_sums)
+    first_back = after(first_back, *sends)
 
     self_saved = [self_a[:5], self_b[:5]]
     self_d = attention_bwd_call(
-        self_scalars, first_back, [tokens], self_pieces[1::2], self_saved, plan_of((1, 3)), [first_scaled], None
+        self_scalars, first_back, [tokens], self_pieces[1::2], self_saved, plan_of((1, 3)), None, None
     )
     cross_sum.begin(cross_e[6], self_d[0])
     sends = advance([cross_sum, ffn_sum], self_d[0])
     self_sum = Reduction(after(self_d[1], *sends), [(0, 4, "xzy"), (4, 8, "yxz")])
-    gate = after(self_d[0], *sends)
+    first_back = after(first_back, *sends)
     self_e = attention_bwd_call(
-        self_scalars, first_back, [tokens], self_pieces[::2], self_saved, plan_of((0, 2)), [gate], None
-    )
-    grad_tokens = self_e[0]
-    self_sum.begin(self_e[1], grad_tokens)
+        self_scalars, first_back, [tokens], self_pieces[::2], self_saved, plan_of((0, 2)), None, None
+    )
+    self_sum.begin(self_e[1], self_e[0])
     sends = advance([self_sum])
+    grad_tokens, grad_memory = inputs_back_call(
+        self_scalars, after(first_scaled, *sends),
+        [(self_d[0], self_pieces[1::2]), (self_e[0], self_pieces[::2])],
+        (memory_part, cross_pieces[1::2] + cross_pieces[::2]),
+    )
     sends = advance([cross_sum, ffn_sum], *sends)
+    sends = advance([self_sum, cross_sum], *sends, grad_tokens)
+    sends = advance([self_sum, cross_sum, ffn_sum], *sends)
+    sends = advance([self_sum, cross_sum], *sends)
     sends = advance([self_sum], *sends)
-    sends = advance([cross_sum, ffn_sum], *sends)
-    sends = advance([self_sum], *sends)
-    sends = advance([cross_sum], *sends)
-    sends = advance([self_sum], *sends)
-    sends = advance([cross_sum], *sends)
-    advance([self_sum], *sends)
+    norm_total = jnp.sum(after(norm_sums, *sends), axis=0)
     self_sum, cross_sum, ffn_sum = self_sum.total, cross_sum.total, ffn_sum.total
 
     def matrices(total):

time: 427 us -> 434 us (1.016)
  starting transfers between devices: 45.2 us -> 50.2 us
    all_gather x1, waiting for transfers between devices: 27.6 us -> 0.01 us  [sentence_body(): norm_sums = lax.all_gather(norm_sums, ('dp', 'tensor'), axis=0)]
    ppermute x10, waiting for transfers between devices: 7.92 us -> 24.3 us  [over_y(): return lax.ppermute(values, 'tensor', swap_pairs(4, 2))]
    pallas_call x0 -> x1, Pallas kernels: none -> 15.3 us  [inputs_back_call(): pl.pallas_call(kernel, out_shape=[sds((rows, depth), F32)] * 2, in_specs=...]
    ppermute x17, waiting for transfers between devices: 2.18 us -> 11.3 us  [to_sibling(): return lax.ppermute(values, 'tensor', swap_pairs(4, 1))]
    unnamed x99 -> x87, local copies, waits for them, and re-layouts: 17.7 us -> 12.3 us
    pallas_call x12 -> x9, Pallas kernels: 40.1 us -> 34.9 us  [combine(): pl.pallas_call(kernel, out_shape=list(shapes), in_specs=[ANY] * len(array...]
    pallas_call x3, Pallas kernels: 68.7 us -> 63.5 us  [attention_bwd_call(): pl.pallas_call(kernel, out_shape=shapes, in_specs=[SMEM] + [VMEM] * (len(...]
  transfers between devices with their start and end apart: 55 -> 55, of which waited for: 16 -> 23; matrix products, arithmetic and copies ran while one was open for 5% -> 6% of each run, Pallas kernels for 40% -> 41%
where the time goes in v3:
time: 434 us; the launch traced here: 431 us
  Pallas kernels  222 us (51%)
  waiting for transfers between devices  102 us (24%)
  starting transfers between devices  50.2 us (12%)
  local copies, waits for them, and re-layouts  33.9 us (8%)
  between operations  15 us (3%)
  other arithmetic  7.23 us (2%)
    ppermute x27, waiting for transfers between devices, over_dp(): return lax.ppermute(values, 'dp', swap_pairs(8, mask))  66.3 us
    pallas_call x3, Pallas kernels, attention_bwd_call(): pl.pallas_call(kernel, out_shape=shapes, in_specs=[SMEM] + [VMEM] * (len(...  63.5 us
    pallas_call x3, Pallas kernels, attention_fwd_call(): pl.pallas_call(kernel, out_shape=shapes, in_specs=[SMEM] + [VMEM] * (len(...  47.9 us
    pallas_call x9, Pallas kernels, combine(): pl.pallas_call(kernel, out_shape=list(shapes), in_specs=[ANY] * len(array...  34.9 us
    pallas_call x2, Pallas kernels, ffn_bwd_call(): pl.pallas_call(kernel, out_shape=shapes, in_specs=specs + [ANY] * len(tai...  33.9 us
    ppermute x27, starting transfers between devices, over_dp(): return lax.ppermute(values, 'dp', swap_pairs(8, mask))  33 us
    pallas_call x2, Pallas kernels, ffn_fwd_call(): pl.pallas_call(kernel, out_shape=shapes, in_specs=specs + [ANY] * len(tai...  27 us
    ppermute x10, waiting for transfers between devices, over_y(): return lax.ppermute(values, 'tensor', swap_pairs(4, 2))  24.3 us
  transfers between devices with their start and end apart: 55, of which 23 were waited for; matrix products, arithmetic and copies ran while one was open for 6% of the time, Pallas kernels for 41%

profile of v3, /device:TPU:0, one launch (start us, length us, event | category | flops | bytes accessed | tf_op | source)
XLA Modules:
  0.0 430.7 jit_solution(15094683886479905419)
XLA Ops:
  14.6 10.5 %collective-permute-done.1 = bf16[4,256,256]{2,1,0:T(8,128)(2,1)S(1)} collective-permute-done((bf16[4,256,256]{2,1,0:T(8,128)(2,1)S(1)}, bf16[4,256,256]{2,1,0:T(8,128)(2,1)S(1)}, u32[]{:S(2)}, u32[]{:S(2)}) %collective-permute-start.1) | collective-permute-done | bytes 524320 | tf_op jit(solution)/shard_map/ppermute | solution.py:918
  32.8 11.0 %self_fwd.2 = (bf16[4,512,128]{2,1,0:T(8,128)(2,1)}, bf16[4,512,128]{2,1,0:T(8,128)(2,1)}, bf16[4,512,128]{2,1,0:T(8,128)(2,1)}, bf16[4,512,128]{2,1,0:T(8,128)(...) custom-call(s32[4]{0:T(128)} %add_add_fusion.1.refs_0_, bf16[512,1024]{1,0:T(8,128)(2,1)} %refs_2_.9, ...), custom_call_target="tpu_custom_call" | custom-call | flops 2640000000 | bytes 4194304 | tf_op jit(solution)/shard_map/self_fwd/pallas_call | solution.py:349
  44.4 12.3 %collective-permute-done.6 = bf16[4,256,256]{2,1,0:T(8,128)(2,1)S(1)} collective-permute-done((bf16[4,256,256]{2,1,0:T(8,128)(2,1)}, bf16[4,256,256]{2,1,0:T(8,128)(2,1)S(1)}, u32[]{:S(2)}, u32[]{:S(2)}) %collective-permute-start.6) | collective-permute-done | bytes 524320 | tf_op jit(solution)/shard_map/ppermute | solution.py:922
  62.0 13.3 %collective-permute-done.12 = bf16[4,256,256]{2,1,0:T(8,128)(2,1)} collective-permute-done((bf16[4,256,256]{2,1,0:T(8,128)(2,1)S(1)}, bf16[4,256,256]{2,1,0:T(8,128)(2,1)}, u32[]{:S(2)}, u32[]{:S(2)}) %collective-permute-start.12) | collective-permute-done | bytes 524320 | tf_op jit(solution)/shard_map/ppermute | solution.py:922
  79.3 13.9 %self_fwd.3 = (bf16[4,512,128]{2,1,0:T(8,128)(2,1)}, bf16[4,512,128]{2,1,0:T(8,128)(2,1)}, bf16[4,512,128]{2,1,0:T(8,128)(2,1)}, bf16[4,512,128]{2,1,0:T(8,128)(...) custom-call(s32[4]{0:T(128)} %add_add_fusion.1.refs_0_, ...), custom_call_target="tpu_custom_call" | custom-call | flops 2640000000 | bytes 4194304 | tf_op jit(solution)/shard_map/self_fwd/pallas_call | solution.py:349
  93.2 6.4 %collective-permute-done.11 = bf16[4,256,256]{2,1,0:T(8,128)(2,1)} collective-permute-done((bf16[4,256,256]{2,1,0:T(8,128)(2,1)S(1)}, bf16[4,256,256]{2,1,0:T(8,128)(2,1)}, u32[]{:S(2)}, u32[]{:S(2)}) %collective-permute-start.11) | collective-permute-done | bytes 524320 | tf_op jit(solution)/shard_map/ppermute | solution.py:922
  103.8 4.6 %collective-permute-done.8.refs_11_.refs_8_ = bf16[1024,256]{1,0:T(8,128)(2,1)S(1)} collective-permute-done((bf16[1024,256]{1,0:T(8,128)(2,1)S(1)}, bf16[1024,256]{1,0:T(8,128)(2,1)S(1)}, u32[]{:S(2)}, u32[]{:S(2)}) %collective-permute-start.8) | collective-permute-done | bytes 524320 | tf_op jit(solution)/shard_map/ppermute | solution.py:914
  108.5 4.4 %collective-permute-done.10.refs_13_.refs_10_ = bf16[256,1024]{1,0:T(8,128)(2,1)S(1)} collective-permute-done((bf16[256,1024]{1,0:T(8,128)(2,1)S(1)}, bf16[256,1024]{1,0:T(8,128)(2,1)S(1)}, u32[]{:S(2)}, u32[]{:S(2)}) %collective-permute-start.10) | collective-permute-done | bytes 524320 | tf_op jit(solution)/shard_map/ppermute | solution.py:914
  116.8 23.1 %cross_fwd.1 = (bf16[8,512,128]{2,1,0:T(8,128)(2,1)}, bf16[8,512,128]{2,1,0:T(8,128)(2,1)}, bf16[8,512,128]{2,1,0:T(8,128)(2,1)}, bf16[8,512,128]{2,1,0:T(8,128)...) custom-call(s32[4]{0:T(128)} %add_add_fusion.refs_0_, ...), custom_call_target="tpu_custom_call" | custom-call | flops 5280000000 | bytes 4194304 | tf_op jit(solution)/shard_map/cross_fwd/pallas_call | solution.py:349
  145.6 11.6 %ffn_fwd.2 = (f32[512,1024]{1,0:T(8,128)}, bf16[4,512,512]{2,1,0:T(8,128)(2,1)}, bf16[4,512,512]{2,1,0:T(8,128)(2,1)}) custom-call(s32[4]{0:T(128)} %add_add_fusion.refs_0_, bf16[512,1024]{1,0:T(8,128)(2,1)} %get-tuple-element.155.refs_1_.refs_2_, bf16[1024,1024]{1,0:T(8,128)(2,1)} %refs_7_.3, bf16[1024,1024]{1,0:T(8,128)(2,1)} %refs_8_.4, ...), custom_call_target="tpu_custom_call" | custom-call | flops 13200000000 | bytes 4194304 | tf_op jit(solution)/shard_map/ffn_fwd/pallas_call | solution.py:709
  161.7 15.4 %ffn_fwd.3 = (bf16[512,1024]{1,0:T(8,128)(2,1)}, bf16[512,1024]{1,0:T(8,128)(2,1)}, f32[512,1024]{1,0:T(8,128)}, f32[8,1024]{1,0:T(8,128)}, f32[8,1024]{1,0:T(8,...) custom-call(s32[4]{0:T(128)} %add_add_fusion.refs_0_, ...), custom_call_target="tpu_custom_call" | custom-call | flops 13200000000 | bytes 4194304 | tf_op jit(solution)/shard_map/ffn_fwd/pallas_call | solution.py:709
  177.2 16.4 %ffn_bwd.2 = (f32[512,1024]{1,0:T(8,128)}, bf16[8,2,8,128,256]{4,3,2,1,0:T(8,128)(2,1)}) custom-call(s32[4]{0:T(128)} %add_add_fusion.refs_0_, bf16[512,1024]{1,0:T(8,128)(2,1)} %get-tuple-element.166.refs_1_, bf16[512,1024]{1,0:T(8,128)(2,1)} %get-tuple-element.155.refs_1_.refs_2_, f32[512,1024]{1,0:T(8,128)} %get-tuple-element.168.refs_3_, ...), custom_call_target="tpu_custom_call" | custom-call | flops 18699999232 | bytes 4194304 | tf_op jit(solution)/shard_map/ffn_bwd/pallas_call | solution.py:822
  193.8 17.5 %ffn_bwd.3 = (bf16[512,1024]{1,0:T(8,128)(2,1)}, f32[512,1024]{1,0:T(8,128)}, f32[8,1024]{1,0:T(8,128)}, f32[8,1024]{1,0:T(8,128)}, bf16[8,2,8,128,256]{4,3,2,1,0:T(8,128)(2,1)}) custom-call(s32[4]{0:T(128)} %add_add_fusion.refs_0_, bf16[512,1024]{1,0:T(8,128)(2,1)} %get-tuple-element.166.refs_1_, bf16[512,1024]{1,0:T(8,128)(2,1)} %get-tuple-element.155.refs_1_.refs_2_, ...), custom_call_target="tpu_custom_call" | custom-call | flops 18699999232 | bytes 4194304 | tf_op jit(solution)/shard_map/ffn_bwd/pallas_call | solution.py:822
  211.3 5.2 %combine.9 = (bf16[3,2,2,2,128,256]{5,4,3,2,1,0:T(8,128)(2,1)}, bf16[3,2,2,2,128,256]{5,4,3,2,1,0:T(8,128)(2,1)}, bf16[2,2,2,2,128,256]{5,4,3,2,1,0:T(8,128)(2,1)}) custom-call(bf16[8,2,2,2,2,128,256]{6,5,4,3,2,1,0:T(8,128)(2,1)} %bitcast.78, bf16[8,2,2,2,2,128,256]{6,5,4,3,2,1,0:T(8,128)(2,1)} %bitcast.21.refs_1_.refs_3_.refs_5_.refs_15_), custom_call_target="tpu_custom_call" | custom-call | flops 3300000000 | bytes 4194304 | tf_op jit(solution)/shard_map/combine/pallas_call | solution.py:897
  220.4 31.5 %cross_bwd.1 = (bf16[512,1024]{1,0:T(8,128)(2,1)}, f32[512,1024]{1,0:T(8,128)}, f32[8,1024]{1,0:T(8,128)}, f32[8,1024]{1,0:T(8,128)}, bf16[512,2048]{1,0:T(8,128...) custom-call(s32[4]{0:T(128)} %add_add_fusion.refs_0_, ...), custom_call_target="tpu_custom_call" | custom-call | flops 36960002048 | bytes 4194304 | tf_op jit(solution)/shard_map/cross_bwd/pallas_call | solution.py:487
  262.6 15.9 %self_bwd.2 = (bf16[512,1536]{1,0:T(8,128)(2,1)}, bf16[8,2,8,128,128]{4,3,2,1,0:T(8,128)(2,1)}) custom-call(s32[4]{0:T(128)} %add_add_fusion.1.refs_0_, bf16[512,1024]{1,0:T(8,128)(2,1)} %get-tuple-element.220.refs_1_, bf16[512,1024]{1,0:T(8,128)(2,1)} %refs_2_.9, bf16[3,1024,256]{2,1,0:T(8,128)(2,1)} %collective-permute-done.2.refs_4_.refs_3_.refs_5_, ...), custom_call_target="tpu_custom_call" | custom-call | flops 18480001024 | bytes 4194304 | tf_op jit(solution)/shard_map/self_bwd/pallas_call | solution.py:487
  280.5 4.8 %combine.11 = (bf16[4,2,2,2,128,128]{5,4,3,2,1,0:T(8,128)(2,1)}, bf16[4,2,2,2,128,128]{5,4,3,2,1,0:T(8,128)(2,1)}, bf16[3,2,128,256]{3,2,1,0:T(8,128)(2,1)}, bf1...) custom-call(bf16[8,2,2,2,2,128,128]{6,5,4,3,2,1,0:T(8,128)(2,1)} %bitcast.83, ...), custom_call_target="tpu_custom_call" | custom-call | flops 3300000000 | bytes 4194304 | tf_op jit(solution)/shard_map/combine/pallas_call | solution.py:897
  290.4 16.2 %self_bwd.3 = (bf16[512,1536]{1,0:T(8,128)(2,1)}, bf16[8,2,8,128,128]{4,3,2,1,0:T(8,128)(2,1)}) custom-call(s32[4]{0:T(128)} %add_add_fusion.1.refs_0_, bf16[512,1024]{1,0:T(8,128)(2,1)} %get-tuple-element.220.refs_1_, bf16[512,1024]{1,0:T(8,128)(2,1)} %refs_2_.9, bf16[3,1024,256]{2,1,0:T(8,128)(2,1)} %refs_8_.5, bf16[256,1024]{1,0:T(8,128)(2,1)} %refs_9_.3, ...), custom_call_target="tpu_custom_call" | custom-call | flops 18480001024 | bytes 4194304 | tf_op jit(solution)/shard_map/self_bwd/pallas_call | solution.py:487
  314.4 7.0 %collective-permute-done.40.refs_11_.refs_22_ = bf16[3,2,128,256]{3,2,1,0:T(8,128)(2,1)S(1)} collective-permute-done((bf16[3,2,128,256]{3,2,1,0:T(8,128)(2,1)}, bf16[3,2,128,256]{3,2,1,0:T(8,128)(2,1)S(1)}, u32[]{:S(2)}, u32[]{:S(2)}) %collective-permute-start.40) | collective-permute-done | bytes 393248 | tf_op jit(solution)/shard_map/ppermute | solution.py:918
  330.7 15.3 %inputs_back.1 = (f32[512,1024]{1,0:T(8,128)}, f32[512,1024]{1,0:T(8,128)}) custom-call(s32[4]{0:T(128)} %add_add_fusion.1.refs_0_, f32[512,1024]{1,0:T(8,128)} %get-tuple-element.228.refs_1_, bf16[512,1536]{1,0:T(8,128)(2,1)} %get-tuple-element.210.refs_2_, bf16[512,1536]{1,0:T(8,128)(2,1)} %get-tuple-element.224.refs_3_, ...), custom_call_target="tpu_custom_call" | custom-call | flops 13200000000 | bytes 4194304 | tf_op jit(solution)/shard_map/inputs_back/pallas_call | solution.py:527
  360.4 5.2 %collective-permute-done.47.refs_10_.refs_12_ = bf16[4,2,128,128]{3,2,1,0:T(8,128)(2,1)S(1)} collective-permute-done((bf16[4,2,128,128]{3,2,1,0:T(8,128)(2,1)}, bf16[4,2,128,128]{3,2,1,0:T(8,128)(2,1)S(1)}, u32[]{:S(2)}, u32[]{:S(2)}) %collective-permute-start.47) | collective-permute-done | bytes 262176 | tf_op jit(solution)/shard_map/ppermute | solution.py:918
  365.6 9.1 %collective-permute-done.48.refs_13_.refs_16_ = bf16[4,2,128,128]{3,2,1,0:T(8,128)(2,1)S(1)} collective-permute-done((bf16[4,2,128,128]{3,2,1,0:T(8,128)(2,1)}, bf16[4,2,128,128]{3,2,1,0:T(8,128)(2,1)S(1)}, u32[]{:S(2)}, u32[]{:S(2)}) %collective-permute-start.48) | collective-permute-done | bytes 262176 | tf_op jit(solution)/shard_map/ppermute | solution.py:922
  389.9 5.7 %collective-permute-done.51.refs_7_.refs_8_ = bf16[4,2,128,128]{3,2,1,0:T(8,128)(2,1)S(1)} collective-permute-done((bf16[4,2,128,128]{3,2,1,0:T(8,128)(2,1)}, bf16[4,2,128,128]{3,2,1,0:T(8,128)(2,1)S(1)}, u32[]{:S(2)}, u32[]{:S(2)}) %collective-permute-start.51) | collective-permute-done | bytes 262176 | tf_op jit(solution)/shard_map/ppermute | solution.py:922
  406.7 8.5 %collective-permute-done.53.refs_5_ = bf16[8,128,128]{2,1,0:T(8,128)(2,1)S(1)} collective-permute-done((bf16[8,128,128]{2,1,0:T(8,128)(2,1)}, bf16[8,128,128]{2,1,0:T(8,128)(2,1)S(1)}, u32[]{:S(2)}, u32[]{:S(2)}) %collective-permute-start.53) | collective-permute-done | bytes 262176 | tf_op jit(solution)/shard_map/ppermute | solution.py:922
  (231 shorter events, 131.2 us)
Async XLA Ops:
  7.2 414.5 %all-gather.3.cloned.1.call-start = ((), (), s32[]{:S(2)}) async-start(), calls=%async_computation | async-start | bytes 1081344 | tf_op jit(solution)/shard_map/all_gather | solution.py:1106
  7.2 25.6 %collective-permute-start.2 = (bf16[3,1024,256]{2,1,0:T(8,128)(2,1)}, bf16[3,1024,256]{2,1,0:T(8,128)(2,1)}, u32[]{:S(2)}, u32[]{:S(2)}) collective-permute-start(bf16[3,1024,256]{2,1,0:T(8,128)(2,1)} %refs_8_.5), channel_id=1, source_target_pairs={{0,1},{1,0},{2,3},{3,2},{4,5},{5,4},{6,7},{7,6},{8,9},{9,8},{10,11... | collective-permute-start | bytes 4718600 | tf_op jit(solution)/shard_map/ppermute | solution.py:914
  12.5 20.3 %collective-permute-start.3 = (bf16[256,1024]{1,0:T(8,128)(2,1)S(1)}, bf16[256,1024]{1,0:T(8,128)(2,1)}, u32[]{:S(2)}, u32[]{:S(2)}) collective-permute-start(bf16[256,1024]{1,0:T(8,128)(2,1)S(1)} %copy-done.19), channel_id=1, source_target_pairs={{0,1},{1,0},{2,3},{3,2},{4,5},{5,4},{6,7},{7,6},{8,9},{9,8},{10,11... | collective-permute-start | bytes 1572872 | tf_op jit(solution)/shard_map/ppermute | solution.py:914
  61.0 32.2 %collective-permute-start.14 = (bf16[2,256,1024]{2,1,0:T(8,128)(2,1)S(1)}, bf16[2,256,1024]{2,1,0:T(8,128)(2,1)}, u32[]{:S(2)}, u32[]{:S(2)}) collective-permute-start(bf16[2,256,1024]{2,1,0:T(8,128)(2,1)S(1)} %pad_maximum_fusion.2), channel_id=1, source_target_pairs={{0,2},{1,3},{2,0},{3,1},{4,6},{5,7},{6,4},{7,5},{8,10},{9,11},{10,... | collective-permute-start | bytes 3145736 | tf_op jit(solution)/shard_map/ppermute | solution.py:918
  75.9 23.8 %collective-permute-start.11 = (bf16[4,256,256]{2,1,0:T(8,128)(2,1)S(1)}, bf16[4,256,256]{2,1,0:T(8,128)(2,1)}, u32[]{:S(2)}, u32[]{:S(2)}) collective-permute-start(bf16[4,256,256]{2,1,0:T(8,128)(2,1)S(1)} %collective-permute-done), channel_id=1, source_target_pairs={{0,4},{4,0},{8,12},{12,8},{16,20},{20,16},{24,28},{28,24},{1,5},{5... | collective-permute-start | bytes 1572872 | tf_op jit(solution)/shard_map/ppermute | solution.py:922
  103.3 39.3 %collective-permute-start.16 = (bf16[1024,1024]{1,0:T(8,128)(2,1)}, bf16[1024,1024]{1,0:T(8,128)(2,1)}, u32[]{:S(2)}, u32[]{:S(2)}) collective-permute-start(bf16[1024,1024]{1,0:T(8,128)(2,1)} %refs_7_.3), channel_id=1, source_target_pairs={{0,1},{1,0},{2,3},{3,2},{4,5},{5,4},{6,7},{7,6},{8,9},{9,8},{10,11... | collective-permute-start | bytes 6291464 | tf_op jit(solution)/shard_map/ppermute | solution.py:914
  103.7 40.2 %collective-permute-start.17 = (bf16[1024,1024]{1,0:T(8,128)(2,1)}, bf16[1024,1024]{1,0:T(8,128)(2,1)}, u32[]{:S(2)}, u32[]{:S(2)}) collective-permute-start(bf16[1024,1024]{1,0:T(8,128)(2,1)} %refs_8_.4), channel_id=1, source_target_pairs={{0,1},{1,0},{2,3},{3,2},{4,5},{5,4},{6,7},{7,6},{8,9},{9,8},{10,11... | collective-permute-start | bytes 6291464 | tf_op jit(solution)/shard_map/ppermute | solution.py:914
  112.9 26.9 %collective-permute-start.18 = (bf16[2,256,1024]{2,1,0:T(8,128)(2,1)}, bf16[2,256,1024]{2,1,0:T(8,128)(2,1)}, u32[]{:S(2)}, u32[]{:S(2)}) collective-permute-start(bf16[2,256,1024]{2,1,0:T(8,128)(2,1)} %collective-permute-done.14.refs_9_), channel_id=1, source_target_pairs={{0,4},{4,0},{8,12},{12,8},{16,20},{20,16},{24,28},{28,24},{1,5},{5... | collective-permute-start | bytes 3145736 | tf_op jit(solution)/shard_map/ppermute | solution.py:922
  113.7 27.8 %collective-permute-start.19 = (bf16[2,256,1024]{2,1,0:T(8,128)(2,1)}, bf16[2,256,1024]{2,1,0:T(8,128)(2,1)}, u32[]{:S(2)}, u32[]{:S(2)}) collective-permute-start(bf16[2,256,1024]{2,1,0:T(8,128)(2,1)} %collective-permute-done.14.refs_9_), channel_id=1, source_target_pairs={{0,8},{4,12},{8,0},{12,4},{16,24},{20,28},{24,16},{28,20},{1,9},{5... | collective-permute-start | bytes 3145736 | tf_op jit(solution)/shard_map/ppermute | solution.py:922
  116.7 41.9 %collective-permute-start.22 = (bf16[2,256,1024]{2,1,0:T(8,128)(2,1)}, bf16[2,256,1024]{2,1,0:T(8,128)(2,1)}, u32[]{:S(2)}, u32[]{:S(2)}) collective-permute-start(bf16[2,256,1024]{2,1,0:T(8,128)(2,1)} %collective-permute-done.14.refs_9_), channel_id=1, source_target_pairs={{0,1},{1,0},{2,3},{3,2},{4,5},{5,4},{6,7},{7,6},{8,9},{9,8},{10,11... | collective-permute-start | bytes 3145736 | tf_op jit(solution)/shard_map/ppermute | solution.py:914
  216.5 36.9 %collective-permute-start.28 = (bf16[3,2,2,2,128,256]{5,4,3,2,1,0:T(8,128)(2,1)}, bf16[3,2,2,2,128,256]{5,4,3,2,1,0:T(8,128)(2,1)S(1)}, u32[]{:S(2)}, u32[]{:S(2)}) collective-permute-start(bf16[3,2,2,2,128,256]{5,4,3,2,1,0:T(8,128)(2,1)} %get-tuple-element.179), channel_id=1, source_target_pairs={{0,2},{1,3},{2,0},{3,1},{4,6},{5,7},{6,4},{7,5},{8,10},{9,11},{10,... | collective-permute-start | bytes 4718600 | tf_op jit(solution)/shard_map/ppermute | solution.py:918
  218.1 36.7 %collective-permute-start.29 = (bf16[3,2,2,2,128,256]{5,4,3,2,1,0:T(8,128)(2,1)}, bf16[3,2,2,2,128,256]{5,4,3,2,1,0:T(8,128)(2,1)}, u32[]{:S(2)}, u32[]{:S(2)}) collective-permute-start(bf16[3,2,2,2,128,256]{5,4,3,2,1,0:T(8,128)(2,1)} %get-tuple-element.180), channel_id=1, source_target_pairs={{0,4},{4,0},{8,12},{12,8},{16,20},{20,16},{24,28},{28,24},{1,5},{5... | collective-permute-start | bytes 4718600 | tf_op jit(solution)/shard_map/ppermute | solution.py:922
  218.9 33.1 %collective-permute-start.30 = (bf16[2,2,2,2,128,256]{5,4,3,2,1,0:T(8,128)(2,1)}, bf16[2,2,2,2,128,256]{5,4,3,2,1,0:T(8,128)(2,1)}, u32[]{:S(2)}, u32[]{:S(2)}) collective-permute-start(bf16[2,2,2,2,128,256]{5,4,3,2,1,0:T(8,128)(2,1)} %get-tuple-element.181), channel_id=1, source_target_pairs={{0,8},{4,12},{8,0},{12,4},{16,24},{20,28},{24,16},{28,20},{1,9},{5... | collective-permute-start | bytes 3145736 | tf_op jit(solution)/shard_map/ppermute | solution.py:922
  258.8 20.7 %collective-permute-start.31 = (bf16[8,2,8,128,128]{4,3,2,1,0:T(8,128)(2,1)}, bf16[8,2,8,128,128]{4,3,2,1,0:T(8,128)(2,1)}, u32[]{:S(2)}, u32[]{:S(2)}) collective-permute-start(bf16[8,2,8,128,128]{4,3,2,1,0:T(8,128)(2,1)} %get-tuple-element.201), channel_id=1, source_target_pairs={{0,1},{1,0},{2,3},{3,2},{4,5},{5,4},{6,7},{7,6},{8,9},{9,8},{10,11... | collective-permute-start | bytes 12582920 | tf_op jit(solution)/shard_map/ppermute | solution.py:914
  285.3 21.3 %collective-permute-start.35 = (bf16[8,2,8,128,128]{4,3,2,1,0:T(8,128)(2,1)}, bf16[8,2,8,128,128]{4,3,2,1,0:T(8,128)(2,1)}, u32[]{:S(2)}, u32[]{:S(2)}) collective-permute-start(bf16[8,2,8,128,128]{4,3,2,1,0:T(8,128)(2,1)} %get-tuple-element.223), channel_id=1, source_target_pairs={{0,1},{1,0},{2,3},{3,2},{4,5},{5,4},{6,7},{7,6},{8,9},{9,8},{10,11... | collective-permute-start | bytes 12582920 | tf_op jit(solution)/shard_map/ppermute | solution.py:914
  285.4 26.2 %collective-permute-start.37 = (bf16[4,2,2,2,128,128]{5,4,3,2,1,0:T(8,128)(2,1)}, bf16[4,2,2,2,128,128]{5,4,3,2,1,0:T(8,128)(2,1)S(1)}, u32[]{:S(2)}, u32[]{:S(2)}) collective-permute-start(bf16[4,2,2,2,128,128]{5,4,3,2,1,0:T(8,128)(2,1)} %get-tuple-element.215), channel_id=1, source_target_pairs={{0,4},{4,0},{8,12},{12,8},{16,20},{20,16},{24,28},{28,24},{1,5},{5... | collective-permute-start | bytes 3145736 | tf_op jit(solution)/shard_map/ppermute | solution.py:922
  286.8 26.3 %collective-permute-start.38 = (bf16[4,2,2,2,128,128]{5,4,3,2,1,0:T(8,128)(2,1)}, bf16[4,2,2,2,128,128]{5,4,3,2,1,0:T(8,128)(2,1)}, u32[]{:S(2)}, u32[]{:S(2)}) collective-permute-start(bf16[4,2,2,2,128,128]{5,4,3,2,1,0:T(8,128)(2,1)} %get-tuple-element.216), channel_id=1, source_target_pairs={{0,2},{1,3},{2,0},{3,1},{4,6},{5,7},{6,4},{7,5},{8,10},{9,11},{10,... | collective-permute-start | bytes 3145736 | tf_op jit(solution)/shard_map/ppermute | solution.py:918
  288.1 26.3 %collective-permute-start.39 = (bf16[3,2,128,256]{3,2,1,0:T(8,128)(2,1)}, bf16[3,2,128,256]{3,2,1,0:T(8,128)(2,1)S(1)}, u32[]{:S(2)}, u32[]{:S(2)}) collective-permute-start(bf16[3,2,128,256]{3,2,1,0:T(8,128)(2,1)} %get-tuple-element.217), channel_id=1, source_target_pairs={{0,8},{4,12},{8,0},{12,4},{16,24},{20,28},{24,16},{28,20},{1,9},{5... | collective-permute-start | bytes 1179656 | tf_op jit(solution)/shard_map/ppermute | solution.py:922
  289.7 31.8 %collective-permute-start.40 = (bf16[3,2,128,256]{3,2,1,0:T(8,128)(2,1)}, bf16[3,2,128,256]{3,2,1,0:T(8,128)(2,1)S(1)}, u32[]{:S(2)}, u32[]{:S(2)}) collective-permute-start(bf16[3,2,128,256]{3,2,1,0:T(8,128)(2,1)} %get-tuple-element.218), channel_id=1, source_target_pairs={{0,2},{1,3},{2,0},{3,1},{4,6},{5,7},{6,4},{7,5},{8,10},{9,11},{10,... | collective-permute-start | bytes 1179656 | tf_op jit(solution)/shard_map/ppermute | solution.py:918
  311.7 38.9 %collective-permute-start.36 = (bf16[4,2,2,2,128,128]{5,4,3,2,1,0:T(8,128)(2,1)}, bf16[4,2,2,2,128,128]{5,4,3,2,1,0:T(8,128)(2,1)}, u32[]{:S(2)}, u32[]{:S(2)}) collective-permute-start(bf16[4,2,2,2,128,128]{5,4,3,2,1,0:T(8,128)(2,1)} %get-tuple-element.226), channel_id=1, source_target_pairs={{0,4},{4,0},{8,12},{12,8},{16,20},{20,16},{24,28},{28,24},{1,5},{5... | collective-permute-start | bytes 3145736 | tf_op jit(solution)/shard_map/ppermute | solution.py:922
  313.1 37.5 %collective-permute-start.42 = (bf16[4,2,2,2,128,128]{5,4,3,2,1,0:T(8,128)(2,1)}, bf16[4,2,2,2,128,128]{5,4,3,2,1,0:T(8,128)(2,1)}, u32[]{:S(2)}, u32[]{:S(2)}) collective-permute-start(bf16[4,2,2,2,128,128]{5,4,3,2,1,0:T(8,128)(2,1)} %get-tuple-element.227), channel_id=1, source_target_pairs={{0,2},{1,3},{2,0},{3,1},{4,6},{5,7},{6,4},{7,5},{8,10},{9,11},{10,... | collective-permute-start | bytes 3145736 | tf_op jit(solution)/shard_map/ppermute | solution.py:918
  325.8 23.5 %collective-permute-start.43 = (bf16[4,2,2,128,128]{4,3,2,1,0:T(8,128)(2,1)}, bf16[4,2,2,128,128]{4,3,2,1,0:T(8,128)(2,1)S(1)}, u32[]{:S(2)}, u32[]{:S(2)}) collective-permute-start(bf16[4,2,2,128,128]{4,3,2,1,0:T(8,128)(2,1)} %get-tuple-element.237), channel_id=1, source_target_pairs={{0,8},{4,12},{8,0},{12,4},{16,24},{20,28},{24,16},{28,20},{1,9},{5... | collective-permute-start | bytes 1572872 | tf_op jit(solution)/shard_map/ppermute | solution.py:922
  327.4 23.2 %collective-permute-start.44 = (bf16[4,2,2,128,128]{4,3,2,1,0:T(8,128)(2,1)}, bf16[4,2,2,128,128]{4,3,2,1,0:T(8,128)(2,1)S(1)}, u32[]{:S(2)}, u32[]{:S(2)}) collective-permute-start(bf16[4,2,2,128,128]{4,3,2,1,0:T(8,128)(2,1)} %get-tuple-element.238), channel_id=1, source_target_pairs={{0,4},{4,0},{8,12},{12,8},{16,20},{20,16},{24,28},{28,24},{1,5},{5... | collective-permute-start | bytes 1572872 | tf_op jit(solution)/shard_map/ppermute | solution.py:922
  328.1 32.2 %collective-permute-start.49 = (bf16[8,128,256]{2,1,0:T(8,128)(2,1)}, bf16[8,128,256]{2,1,0:T(8,128)(2,1)}, u32[]{:S(2)}, u32[]{:S(2)}) collective-permute-start(bf16[8,128,256]{2,1,0:T(8,128)(2,1)} %get-tuple-element.239), channel_id=1, source_target_pairs={{0,16},{4,20},{8,24},{12,28},{16,0},{20,4},{24,8},{28,12},{1,17},{... | collective-permute-start | bytes 1572872 | tf_op jit(solution)/shard_map/ppermute | solution.py:922
  (71 other events, 641.1 us)
Sparse Core Ops, SparseCore 0:
  360.5 57.7 all-gather.2

commit v4 on v3

--- a/solution.py
+++ b/solution.py
@@ -210,7 +210,7 @@
     return jax.ShapeDtypeStruct(shape, dtype)
 
 
-def weight_copies(pieces, order, wbuf, obuf, wsem, osem, columns=(0, 1, 2)):
+def weight_copies(pieces, sc, wbuf, obuf, wsem, osem, columns=(0, 1, 2)):
     groups, outs = [[], [], []], []
     wide = 2 * UNIT
     for index, refs in enumerate(pieces):
@@ -228,9 +228,9 @@
             continue
         rest, = refs
         rows = rest.shape[2]
-        part = wide // 4
-        for quarter in range(4):
-            place = quarter ^ order
+        part = wide // rest.shape[0]
+        for quarter in range(rest.shape[0]):
+            place = quarter ^ (sc[1] if rest.shape[0] == 4 else sc[3])
             for column in columns:
                 low = (columns.index(column) * len(pieces) + index) * wide
                 groups[column].append(
@@ -274,8 +274,8 @@
         wbuf, obuf, att_all, diagonal, wsem, osem, lsem = (next(it) for _ in range(7))
         if last:
             acc, old = next(it), next(it)
-        length, order = sc[0], sc[1]
-        groups, outs = weight_copies(w_refs, order, wbuf, obuf, wsem, osem)
+        length = sc[0]
+        groups, outs = weight_copies(w_refs, sc, wbuf, obuf, wsem, osem)
         for copies in groups + [outs]:
             for copy in copies:
                 copy.start()
@@ -384,9 +384,9 @@
         if last:
             dquery, acc, hat, inv = (next(it) for _ in range(4))
         wsem, osem, ssem, gsem, lsem = (next(it) for _ in range(5))
-        length, order, dp = sc[0], sc[1], sc[2]
-
-        groups, o_copies = weight_copies(w_refs, order, wbuf, obuf, wsem, osem, (0,) if last else ())
+        length, dp = sc[0], sc[2]
+
+        groups, o_copies = weight_copies(w_refs, sc, wbuf, obuf, wsem, osem, (0,) if last else ())
         for copy in o_copies:
             copy.start()
         s_copies = []
@@ -509,7 +509,7 @@
         bufs, sems = [next(it) for _ in jobs], [next(it) for _ in jobs]
         copies = []
         for index, (_, _, _, columns) in enumerate(jobs):
-            groups, _ = weight_copies(w_refs[index], sc[1], bufs[index], None, sems[index], None, columns)
+            groups, _ = weight_copies(w_refs[index], sc, bufs[index], None, sems[index], None, columns)
             copies.append([copy for group in groups for copy in group])
             for copy in copies[-1]:
                 copy.start()
@@ -833,7 +833,7 @@
 
 def combine(jobs, shapes):
     arrays = []
-    for terms, _, _ in jobs:
+    for terms, _, _, _ in jobs:
         for array, _ in terms:
             if not any(array is known for known in arrays):
                 arrays.append(array)
@@ -846,15 +846,15 @@
                 kept.append(len(range(*at.indices(extent))))
         return tuple(kept)
 
-    part_shapes = [part_shape(*terms[0]) for terms, _, _ in jobs]
-    count = sum(len(terms) for terms, _, _ in jobs)
+    part_shapes = [part_shape(*terms[0]) for terms, _, _, _ in jobs]
+    count = sum(len(terms) for terms, _, _, _ in jobs)
 
     def kernel(*refs):
         ins, outs = refs[: len(arrays)], refs[len(arrays) : len(arrays) + len(shapes)]
         rest = refs[len(arrays) + len(shapes) :]
         term_bufs, sum_bufs, isem, osem = rest[:count], rest[count : count + len(jobs)], rest[-2], rest[-1]
         loads, number = [], 0
-        for terms, _, _ in jobs:
+        for terms, _, _, _ in jobs:
             loads.append([])
             for array, index in terms:
                 loads[-1].append(copy_of(ins[position[id(array)]].at[index], term_bufs[number], isem.at[number]))
@@ -863,7 +863,7 @@
             for copy in group:
                 copy.start()
         stores, number = [], 0
-        for job, (terms, out, place) in enumerate(jobs):
+        for job, (terms, out, place, kind) in enumerate(jobs):
             for copy in loads[job]:
                 copy.wait()
             bufs = term_bufs[number : number + len(terms)]
@@ -885,14 +885,23 @@
                 target[index] = total.astype(target.dtype)
                 return carry
 
-            lax.fori_loop(0, size, one, 0)
+            if kind == "range":
+                lax.fori_loop(0, size, one, 0)
+            else:
+                total = bufs[0][0].astype(F32)
+                for buf in bufs[1:]:
+                    total = total + buf[0].astype(F32)
+                sum_bufs[job][...] = jnp.transpose(total) if kind == "turned" else total
             stores.append(copy_of(sum_bufs[job], outs[out].at[place], osem.at[job]))
             stores[-1].start()
         for copy in stores:
             copy.wait()
 
-    scratch = [pltpu.VMEM(part_shapes[job], array.dtype) for job, (terms, _, _) in enumerate(jobs) for array, _ in terms]
-    scratch += [pltpu.VMEM(part_shapes[job], shapes[out].dtype) for job, (_, out, _) in enumerate(jobs)]
+    scratch = [pltpu.VMEM(part_shapes[job], array.dtype) for job, (terms, _, _, _) in enumerate(jobs) for array, _ in terms]
+    for job, (_, out, _, kind) in enumerate(jobs):
+        shape = part_shapes[job]
+        shape = {"range": shape, "plain": shape[1:], "turned": shape[:0:-1]}[kind]
+        scratch.append(pltpu.VMEM(shape, shapes[out].dtype))
     scratch += [pltpu.SemaphoreType.DMA((count,)), pltpu.SemaphoreType.DMA((len(jobs),))]
     return pl.pallas_call(
         kernel,
@@ -942,8 +951,8 @@
 
 
 class Reduction:
-    def __init__(self, sent, portions):
-        self.other = to_sibling(sent)
+    def __init__(self, sent, portions, finish):
+        self.other, self.finish = to_sibling(sent), finish
         self.portions, self.stage, self.sends, self.total = portions, 0, None, None
 
     def begin(self, kept, *earlier):
@@ -975,15 +984,48 @@
                     index.append(1 if name == axis else fixed.get(name, 0 if name in orders[:stage] or (stage > 3 and name == "w") else slice(None)))
                 picked.append((array, tuple(index)))
             if stage < 3:
-                left = 3 - stage + 1 - 1
-                shapes.append(sds((high - low, *(2,) * left, *self.tail), BF16))
-                jobs.append((picked, first_out + number, slice(0, high - low)))
+                shapes.append(sds((high - low, *(2,) * (3 - stage), *self.tail), BF16))
+                jobs.append((picked, first_out + number, slice(0, high - low), "range"))
+            elif stage == 3:
+                if not number:
+                    shapes.append(sds((self.blocks, *self.tail), BF16))
+                jobs.append((picked, first_out, slice(low, high), "range"))
             else:
                 if not number:
-                    shapes.append(sds((self.blocks, *self.tail), BF16 if stage == 3 else F32))
-                jobs.append((picked, first_out, slice(low, high)))
+                    shapes += self.finish[0]
+                for block in range(low, high):
+                    shift = block - low
+                    one = [(a, (slice(index[0].start + shift, index[0].start + shift + 1), *index[1:])) for a, index in picked]
+                    out, place, kind = self.finish[1](block)
+                    jobs.append((one, first_out + out, place, kind))
         self.stage += 1
         return jobs, shapes
+
+
+def attention_finish(counts):
+    stacks = [sds((count, UNIT, 2 * UNIT) if count > 1 else (UNIT, 2 * UNIT), F32) for count in counts]
+
+    def place_of(block):
+        half, matrix = block // 4, block % 4
+        lanes = slice(half * UNIT, (half + 1) * UNIT)
+        if matrix == 3:
+            return len(counts), (lanes, slice(None)), "turned"
+        stack = 0 if matrix < counts[0] else 1
+        if counts[stack] == 1:
+            return stack, (slice(None), lanes), "plain"
+        return stack, (matrix - sum(counts[:stack]), slice(None), lanes), "plain"
+
+    return [*stacks, sds((2 * UNIT, UNIT), F32)], place_of
+
+
+def ffn_finish():
+    def place_of(block):
+        lanes = slice(block // 2 * FFN_PART, (block // 2 + 1) * FFN_PART)
+        if block % 2:
+            return 1, (lanes, slice(None)), "turned"
+        return 0, (slice(None), lanes), "plain"
+
+    return [sds((UNIT, 4 * FFN_PART), F32), sds((4 * FFN_PART, UNIT), F32)], place_of
 
 
 def advance(reductions, *earlier):
@@ -997,7 +1039,7 @@
     for reduction, (low, high) in zip(reductions, bounds):
         reduction.sends = list(results[low:high])
         if reduction.stage == 5:
-            reduction.total = results[low]
+            reduction.total = results[low:high]
     return list(results)
 
 
@@ -1020,50 +1062,52 @@
     dp = lax.axis_index("dp")
     mine = lax.axis_index("tensor")
     order = dp & 3
-    self_scalars = jnp.stack([dec_lengths[0, mine], order, dp, mine]).astype(jnp.int32)
-    cross_scalars = jnp.stack([mem_lengths[0, mine], order, dp, mine]).astype(jnp.int32)
+    inner = (dp >> 1) & 1
+    self_scalars = jnp.stack([dec_lengths[0, mine], order, dp, inner]).astype(jnp.int32)
+    cross_scalars = jnp.stack([mem_lengths[0, mine], order, dp, inner]).astype(jnp.int32)
     gains = [norm_gains[i : i + 1] for i in range(3)]
     biases = [norm_biases[i : i + 1] for i in range(3)]
 
-    def quarter_rows(values):
-        rows = values.shape[-2] // 4
-        return lax.dynamic_slice_in_dim(values, order * rows, rows, values.ndim - 2)
+    def part_rows(values, parts):
+        rows = values.shape[-2] // parts
+        place = order if parts == 4 else inner
+        return lax.dynamic_slice_in_dim(values, place * rows, rows, values.ndim - 2)
 
     def folded(values):
         blocks = values.reshape(values.shape[0], 4, 2 * UNIT)
         return blocks.transpose(1, 0, 2).reshape(1, 4 * values.shape[0], 2 * UNIT)
 
-    self_near = over_y(jnp.concatenate([quarter_rows(self_qkv), folded(quarter_rows(self_out))]))
+    self_near = over_y(jnp.concatenate([part_rows(self_qkv, 4), folded(part_rows(self_out, 4))]))
     cross_near = over_y(
-        jnp.concatenate([quarter_rows(cross_q)[None], quarter_rows(cross_kv), folded(quarter_rows(cross_out))])
-    )
-    ffn_near = over_y(jnp.stack([quarter_rows(ffn_in), quarter_rows(ffn_out)]))
+        jnp.concatenate([part_rows(cross_q, 2)[None], part_rows(cross_kv, 2), folded(part_rows(cross_out, 2))])
+    )
+    ffn_near = over_y(jnp.stack([part_rows(ffn_in, 4), part_rows(ffn_out, 4)]))
     self_own = (self_qkv, self_out)
     self_sib = tuple(to_sibling(w) for w in self_own)
+    self_a = attention_fwd_call(self_scalars, [], [tokens], [self_own, self_sib], None, None)
+    self_near = after(self_near, self_a[4])
     self_side, self_up = over_x(self_near), over_z_near(self_near)
-    self_a = attention_fwd_call(after(self_scalars, self_near), [], [tokens], [self_own, self_sib], None, None)
-    self_side, self_up, cross_near = (after(w, self_a[4]) for w in (self_side, self_up, cross_near))
     self_corner = over_x(self_up)
-    cross_side, cross_up = over_x(cross_near), over_z_near(cross_near)
     self_rest = jnp.stack([after(self_near, cross_near), self_side, self_up, self_corner])
+    cross_up = over_z_near(cross_near)
     self_far = to_sibling(self_rest)
     self_pieces = [self_own, self_sib, (self_rest,), (self_far,)]
     self_b = attention_fwd_call(
-        after(self_scalars, cross_near), [tokens], [tokens], self_pieces[2:], self_a[5], (gains[0], biases[0])
+        self_scalars, [tokens], [tokens], self_pieces[2:], self_a[5], (gains[0], biases[0])
     )
     first_low, first_hat, first_inv = self_b[5:]
     cross_own = (cross_q, cross_kv, cross_out)
     cross_sib = tuple(to_sibling(after(w, self_near)) for w in cross_own)
     ffn_own = (ffn_in, ffn_out)
-    ffn_sib = tuple(to_sibling(after(w, self_near)) for w in ffn_own)
+    ffn_sib = tuple(to_sibling(after(w, first_inv)) for w in ffn_own)
     cross_in = [first_low, memory]
-    cross_corner = over_x(cross_up)
-    cross_rest = jnp.stack([cross_near, cross_side, cross_up, after(cross_corner, self_b[4], ffn_near)])
+    cross_rest = jnp.stack([cross_near, after(cross_up, self_b[4])])
     cross_far = to_sibling(cross_rest)
+    cross_a = attention_fwd_call(after(cross_scalars, ffn_near), [], cross_in, [cross_own, cross_sib], None, None)
     ffn_side, ffn_up = over_x(ffn_near), over_z_near(ffn_near)
-    cross_pieces = [cross_own, cross_sib, (cross_rest,), (cross_far,)]
+    cross_pieces = [cross_own, cross_sib, (cross_rest,), (after(cross_far, cross_a[4]),)]
     cross_b = attention_fwd_call(
-        cross_scalars, [first_hat, gains[0], biases[0]], cross_in, cross_pieces, None, (gains[1], biases[1])
+        cross_scalars, [first_hat, gains[0], biases[0]], cross_in, cross_pieces[2:], cross_a[5], (gains[1], biases[1])
     )
     second_low, second_hat, second_inv = cross_b[5:]
     ffn_side, ffn_up = after(ffn_side, cross_b[4]), after(ffn_up, cross_b[4])
@@ -1086,7 +1130,7 @@
     ffn_d = ffn_bwd_call(
         cross_scalars, third_low, second_low, ffn_pieces[1::2], ffn_saved, plan_of((1, 3)), third_scaled, None
     )
-    ffn_sum = Reduction(ffn_d[1], [(0, 3, "yxz"), (3, 6, "xzy"), (6, 8, "zyx")])
+    ffn_sum = Reduction(ffn_d[1], [(0, 3, "yxz"), (3, 6, "xzy"), (6, 8, "zyx")], ffn_finish())
     ffn_e = ffn_bwd_call(
         cross_scalars, third_low, second_low, ffn_pieces[::2], ffn_saved, plan_of((0, 2)), ffn_d[0],
         (second_hat, second_inv, gains[1]),
@@ -1096,8 +1140,8 @@
     second_back = after(second_back, *advance([ffn_sum]))
 
     cross_e = attention_bwd_call(
-        cross_scalars, second_back, cross_in, cross_pieces[1::2] + cross_pieces[::2], [cross_b[:5]],
-        [(0, 2 * p + h) for p in (1, 3, 0, 2) for h in (0, 1)], second_scaled,
+        cross_scalars, second_back, cross_in, cross_pieces[1::2] + cross_pieces[::2],
+        [cross_a[:5], cross_b[:5]], plan_of((1, 3, 0, 2)), second_scaled,
         (first_hat, first_inv, gains[0]), 2,
     )
     first_back, first_scaled, first_gain, first_bias, memory_part = cross_e[:5]
@@ -1105,7 +1149,7 @@
     norm_sums = jnp.concatenate([jnp.sum(norm_sums, axis=1), jnp.zeros((2, norm_sums.shape[2]), F32)])
     norm_sums = lax.all_gather(norm_sums, ("dp", "tensor"), axis=0)
     sends = advance([ffn_sum], first_gain)
-    cross_sum = Reduction(after(cross_e[5], *sends), [(0, 4, "xzy"), (4, 8, "yxz")])
+    cross_sum = Reduction(after(cross_e[5], *sends), [(0, 4, "xzy"), (4, 8, "zxy")], attention_finish((1, 2)))
     first_back = after(first_back, *sends)
 
     self_saved = [self_a[:5], self_b[:5]]
@@ -1114,7 +1158,7 @@
     )
     cross_sum.begin(cross_e[6], self_d[0])
     sends = advance([cross_sum, ffn_sum], self_d[0])
-    self_sum = Reduction(after(self_d[1], *sends), [(0, 4, "xzy"), (4, 8, "yxz")])
+    self_sum = Reduction(after(self_d[1], *sends), [(0, 4, "yzx"), (4, 8, "xyz")], attention_finish((3,)))
     first_back = after(first_back, *sends)
     self_e = attention_bwd_call(
         self_scalars, first_back, [tokens], self_pieces[::2], self_saved, plan_of((0, 2)), None, None
@@ -1134,22 +1178,13 @@
     norm_total = jnp.sum(after(norm_sums, *sends), axis=0)
     self_sum, cross_sum, ffn_sum = self_sum.total, cross_sum.total, ffn_sum.total
 
-    def matrices(total):
-        return total.reshape(2, 4, UNIT, UNIT).transpose(1, 2, 0, 3).reshape(4, UNIT, 2 * UNIT)
-
-    self_grads, cross_grads = matrices(self_sum), matrices(cross_sum)
-    ffn_grads = ffn_sum.reshape(4, 2, UNIT, FFN_PART).transpose(1, 2, 0, 3).reshape(2, UNIT, -1)
     return (
         out_rows,
         grad_tokens,
         grad_memory,
-        self_grads[:3],
-        self_grads[3].T,
-        cross_grads[0],
-        cross_grads[1:3],
-        cross_grads[3].T,
-        ffn_grads[0],
-        ffn_grads[1].T,
+        *self_sum,
+        *cross_sum,
+        *ffn_sum,
         norm_total[:3],
         norm_total[3:6],
     )

time: 434 us -> 423 us (0.975)
  local copies, waits for them, and re-layouts: 33.9 us -> 19.1 us
  Pallas kernels: 222 us -> 227 us
    slice x10 -> x1, local copies, waits for them, and re-layouts: 9.59 us -> 0.6 us  [sentence_body(): gains = [norm_gains[i:i + 1] for i in range(3)]]
    ppermute x27 -> x25, waiting for transfers between devices: 66.3 us -> 61.5 us  [over_dp(): return lax.ppermute(values, 'dp', swap_pairs(8, mask))]
    pallas_call x3 -> x4, Pallas kernels: 47.9 us -> 51.4 us  [attention_fwd_call(): pl.pallas_call(kernel, out_shape=shapes, in_specs=[SMEM] + [VMEM] * (len(...]
    unnamed x87 -> x86, local copies, waits for them, and re-layouts: 12.3 us -> 9.4 us
    ppermute x27 -> x25, starting transfers between devices: 33 us -> 30.3 us  [over_dp(): return lax.ppermute(values, 'dp', swap_pairs(8, mask))]
  transfers between devices with their start and end apart: 55 -> 53, of which waited for: 23 -> 24; matrix products, arithmetic and copies ran while one was open for 6% -> 4% of each run, Pallas kernels for 41% -> 43%
where the time goes in v4:
time: 423 us; the launch traced here: 419 us
  Pallas kernels  227 us (54%)
  waiting for transfers between devices  102 us (24%)
  starting transfers between devices  47.6 us (11%)
  local copies, waits for them, and re-layouts  19.1 us (5%)
  between operations  15 us (4%)
  other arithmetic  8.64 us (2%)
    pallas_call x3, Pallas kernels, attention_bwd_call(): pl.pallas_call(kernel, out_shape=shapes, in_specs=[SMEM] + [VMEM] * (len(...  63.9 us
    ppermute x25, waiting for transfers between devices, over_dp(): return lax.ppermute(values, 'dp', swap_pairs(8, mask))  61.5 us
    pallas_call x4, Pallas kernels, attention_fwd_call(): pl.pallas_call(kernel, out_shape=shapes, in_specs=[SMEM] + [VMEM] * (len(...  51.4 us
    pallas_call x9, Pallas kernels, combine(): pl.pallas_call(kernel, out_shape=list(shapes), in_specs=[ANY] * len(array...  35.7 us
    pallas_call x2, Pallas kernels, ffn_bwd_call(): pl.pallas_call(kernel, out_shape=shapes, in_specs=specs + [ANY] * len(tai...  33.9 us
    ppermute x25, starting transfers between devices, over_dp(): return lax.ppermute(values, 'dp', swap_pairs(8, mask))  30.3 us
    ppermute x10, waiting for transfers between devices, over_y(): return lax.ppermute(values, 'tensor', swap_pairs(4, 2))  28.3 us
    pallas_call x2, Pallas kernels, ffn_fwd_call(): pl.pallas_call(kernel, out_shape=shapes, in_specs=specs + [ANY] * len(tai...  27 us
  transfers between devices with their start and end apart: 53, of which 24 were waited for; matrix products, arithmetic and copies ran while one was open for 4% of the time, Pallas kernels for 43%

profile of v4, /device:TPU:0, one launch (start us, length us, event | category | flops | bytes accessed | tf_op | source)
XLA Modules:
  0.0 419.2 jit_solution(16908686307831309294)
XLA Ops:
  15.6 11.0 %self_fwd.2 = (bf16[4,512,128]{2,1,0:T(8,128)(2,1)}, bf16[4,512,128]{2,1,0:T(8,128)(2,1)}, bf16[4,512,128]{2,1,0:T(8,128)(2,1)}, bf16[4,512,128]{2,1,0:T(8,128)(...) custom-call(s32[4]{0:T(128)} %add_add_fusion.1.refs_0_, bf16[512,1024]{1,0:T(8,128)(2,1)} %refs_2_.11, ...), custom_call_target="tpu_custom_call" | custom-call | flops 2640000000 | bytes 4194304 | tf_op jit(solution)/shard_map/self_fwd/pallas_call | solution.py:349
  30.2 10.3 %collective-permute-done.5 = bf16[4,256,256]{2,1,0:T(8,128)(2,1)S(1)} collective-permute-done((bf16[4,256,256]{2,1,0:T(8,128)(2,1)}, bf16[4,256,256]{2,1,0:T(8,128)(2,1)S(1)}, u32[]{:S(2)}, u32[]{:S(2)}) %collective-permute-start.5) | collective-permute-done | bytes 524320 | tf_op jit(solution)/shard_map/ppermute | solution.py:931
  42.2 5.6 %collective-permute-done.3 = bf16[4,512,256]{2,1,0:T(8,128)(2,1)} collective-permute-done((bf16[4,512,256]{2,1,0:T(8,128)(2,1)S(1)}, bf16[4,512,256]{2,1,0:T(8,128)(2,1)}, u32[]{:S(2)}, u32[]{:S(2)}) %collective-permute-start.3) | collective-permute-done | bytes 1048608 | tf_op jit(solution)/shard_map/ppermute | solution.py:927
  47.8 5.6 %collective-permute-done.6 = bf16[4,256,256]{2,1,0:T(8,128)(2,1)S(1)} collective-permute-done((bf16[4,256,256]{2,1,0:T(8,128)(2,1)S(1)}, bf16[4,256,256]{2,1,0:T(8,128)(2,1)S(1)}, u32[]{:S(2)}, u32[]{:S(2)}) %collective-permute-start.6) | collective-permute-done | bytes 524320 | tf_op jit(solution)/shard_map/ppermute | solution.py:931
  62.7 13.9 %self_fwd.3 = (bf16[4,512,128]{2,1,0:T(8,128)(2,1)}, bf16[4,512,128]{2,1,0:T(8,128)(2,1)}, bf16[4,512,128]{2,1,0:T(8,128)(2,1)}, bf16[4,512,128]{2,1,0:T(8,128)(...) custom-call(s32[4]{0:T(128)} %add_add_fusion.1.refs_0_, ...), custom_call_target="tpu_custom_call" | custom-call | flops 2640000000 | bytes 4194304 | tf_op jit(solution)/shard_map/self_fwd/pallas_call | solution.py:349
  89.6 5.2 %collective-permute-done.11.refs_8_.refs_10_.refs_13_ = bf16[256,1024]{1,0:T(8,128)(2,1)S(1)} collective-permute-done((bf16[256,1024]{1,0:T(8,128)(2,1)S(1)}, bf16[256,1024]{1,0:T(8,128)(2,1)S(1)}, u32[]{:S(2)}, u32[]{:S(2)}) %collective-permute-start.11) | collective-permute-done | bytes 524320 | tf_op jit(solution)/shard_map/ppermute | solution.py:923
  100.0 11.8 %cross_fwd.2 = (bf16[4,512,128]{2,1,0:T(8,128)(2,1)}, bf16[4,512,128]{2,1,0:T(8,128)(2,1)}, bf16[4,512,128]{2,1,0:T(8,128)(2,1)}, bf16[4,512,128]{2,1,0:T(8,128)...) custom-call(s32[4]{0:T(128)} %add_add_fusion.refs_0_, bf16[512,1024]{1,0:T(8,128)(2,1)} %get-tuple-element.153.refs_1_.refs_2_, ...), custom_call_target="tpu_custom_call" | custom-call | flops 2640000000 | bytes 4194304 | tf_op jit(solution)/shard_map/cross_fwd/pallas_call | solution.py:349
  111.9 14.8 %cross_fwd.3 = (bf16[4,512,128]{2,1,0:T(8,128)(2,1)}, bf16[4,512,128]{2,1,0:T(8,128)(2,1)}, bf16[4,512,128]{2,1,0:T(8,128)(2,1)}, bf16[4,512,128]{2,1,0:T(8,128)...) custom-call(s32[4]{0:T(128)} %add_add_fusion.refs_0_, ...), custom_call_target="tpu_custom_call" | custom-call | flops 2640000000 | bytes 4194304 | tf_op jit(solution)/shard_map/cross_fwd/pallas_call | solution.py:349
  130.8 11.6 %ffn_fwd.2 = (f32[512,1024]{1,0:T(8,128)}, bf16[4,512,512]{2,1,0:T(8,128)(2,1)}, bf16[4,512,512]{2,1,0:T(8,128)(2,1)}) custom-call(s32[4]{0:T(128)} %add_add_fusion.refs_0_, bf16[512,1024]{1,0:T(8,128)(2,1)} %get-tuple-element.164.refs_1_.refs_2_, bf16[1024,1024]{1,0:T(8,128)(2,1)} %refs_7_.3, bf16[1024,1024]{1,0:T(8,128)(2,1)} %refs_8_.2, ...), custom_call_target="tpu_custom_call" | custom-call | flops 13200000000 | bytes 4194304 | tf_op jit(solution)/shard_map/ffn_fwd/pallas_call | solution.py:709
  148.0 15.4 %ffn_fwd.3 = (bf16[512,1024]{1,0:T(8,128)(2,1)}, bf16[512,1024]{1,0:T(8,128)(2,1)}, f32[512,1024]{1,0:T(8,128)}, f32[8,1024]{1,0:T(8,128)}, f32[8,1024]{1,0:T(8,...) custom-call(s32[4]{0:T(128)} %add_add_fusion.refs_0_, ...), custom_call_target="tpu_custom_call" | custom-call | flops 13200000000 | bytes 4194304 | tf_op jit(solution)/shard_map/ffn_fwd/pallas_call | solution.py:709
  163.4 16.4 %ffn_bwd.2 = (f32[512,1024]{1,0:T(8,128)}, bf16[8,2,8,128,256]{4,3,2,1,0:T(8,128)(2,1)}) custom-call(s32[4]{0:T(128)} %add_add_fusion.refs_0_, bf16[512,1024]{1,0:T(8,128)(2,1)} %get-tuple-element.176.refs_1_, bf16[512,1024]{1,0:T(8,128)(2,1)} %get-tuple-element.164.refs_1_.refs_2_, f32[512,1024]{1,0:T(8,128)} %get-tuple-element.178.refs_3_, ...), custom_call_target="tpu_custom_call" | custom-call | flops 18699999232 | bytes 4194304 | tf_op jit(solution)/shard_map/ffn_bwd/pallas_call | solution.py:822
  180.0 17.5 %ffn_bwd.3 = (bf16[512,1024]{1,0:T(8,128)(2,1)}, f32[512,1024]{1,0:T(8,128)}, f32[8,1024]{1,0:T(8,128)}, f32[8,1024]{1,0:T(8,128)}, bf16[8,2,8,128,256]{4,3,2,1,0:T(8,128)(2,1)}) custom-call(s32[4]{0:T(128)} %add_add_fusion.refs_0_, bf16[512,1024]{1,0:T(8,128)(2,1)} %get-tuple-element.176.refs_1_, bf16[512,1024]{1,0:T(8,128)(2,1)} %get-tuple-element.164.refs_1_.refs_2_, ...), custom_call_target="tpu_custom_call" | custom-call | flops 18699999232 | bytes 4194304 | tf_op jit(solution)/shard_map/ffn_bwd/pallas_call | solution.py:822
  197.5 5.2 %combine.9 = (bf16[3,2,2,2,128,256]{5,4,3,2,1,0:T(8,128)(2,1)}, bf16[3,2,2,2,128,256]{5,4,3,2,1,0:T(8,128)(2,1)}, bf16[2,2,2,2,128,256]{5,4,3,2,1,0:T(8,128)(2,1)}) custom-call(bf16[8,2,2,2,2,128,256]{6,5,4,3,2,1,0:T(8,128)(2,1)} %bitcast.42, bf16[8,2,2,2,2,128,256]{6,5,4,3,2,1,0:T(8,128)(2,1)} %bitcast.20.refs_1_.refs_3_.refs_5_.refs_15_), custom_call_target="tpu_custom_call" | custom-call | flops 3300000000 | bytes 4194304 | tf_op jit(solution)/shard_map/combine/pallas_call | solution.py:906
  206.3 32.1 %cross_bwd.1 = (bf16[512,1024]{1,0:T(8,128)(2,1)}, f32[512,1024]{1,0:T(8,128)}, f32[8,1024]{1,0:T(8,128)}, f32[8,1024]{1,0:T(8,128)}, bf16[512,2048]{1,0:T(8,128...) custom-call(s32[4]{0:T(128)} %add_add_fusion.refs_0_, ...), custom_call_target="tpu_custom_call" | custom-call | flops 36960002048 | bytes 4194304 | tf_op jit(solution)/shard_map/cross_bwd/pallas_call | solution.py:487
  248.4 15.9 %self_bwd.2 = (bf16[512,1536]{1,0:T(8,128)(2,1)}, bf16[8,2,8,128,128]{4,3,2,1,0:T(8,128)(2,1)}) custom-call(s32[4]{0:T(128)} %add_add_fusion.1.refs_0_, bf16[512,1024]{1,0:T(8,128)(2,1)} %get-tuple-element.233.refs_1_, bf16[512,1024]{1,0:T(8,128)(2,1)} %refs_2_.11, bf16[3,1024,256]{2,1,0:T(8,128)(2,1)} %collective-permute-done.refs_4_.refs_3_.refs_5_, ...), custom_call_target="tpu_custom_call" | custom-call | flops 18480001024 | bytes 4194304 | tf_op jit(solution)/shard_map/self_bwd/pallas_call | solution.py:487
  267.5 5.1 %combine.11 = (bf16[4,2,2,2,128,128]{5,4,3,2,1,0:T(8,128)(2,1)}, bf16[4,2,2,2,128,128]{5,4,3,2,1,0:T(8,128)(2,1)}, bf16[3,2,128,256]{3,2,1,0:T(8,128)(2,1)}, bf1...) custom-call(bf16[8,2,2,2,2,128,128]{6,5,4,3,2,1,0:T(8,128)(2,1)} %bitcast.47, ...), custom_call_target="tpu_custom_call" | custom-call | flops 3300000000 | bytes 4194304 | tf_op jit(solution)/shard_map/combine/pallas_call | solution.py:906
  277.5 15.9 %self_bwd.3 = (bf16[512,1536]{1,0:T(8,128)(2,1)}, bf16[8,2,8,128,128]{4,3,2,1,0:T(8,128)(2,1)}) custom-call(s32[4]{0:T(128)} %add_add_fusion.1.refs_0_, bf16[512,1024]{1,0:T(8,128)(2,1)} %get-tuple-element.233.refs_1_, bf16[512,1024]{1,0:T(8,128)(2,1)} %refs_2_.11, bf16[3,1024,256]{2,1,0:T(8,128)(2,1)} %refs_8_.3, bf16[256,1024]{1,0:T(8,128)(2,1)} %refs_9_.1, ...), custom_call_target="tpu_custom_call" | custom-call | flops 18480001024 | bytes 4194304 | tf_op jit(solution)/shard_map/self_bwd/pallas_call | solution.py:487
  303.1 7.0 %collective-permute-done.37.refs_8_.refs_18_ = bf16[3,2,128,256]{3,2,1,0:T(8,128)(2,1)S(1)} collective-permute-done((bf16[3,2,128,256]{3,2,1,0:T(8,128)(2,1)}, bf16[3,2,128,256]{3,2,1,0:T(8,128)(2,1)S(1)}, u32[]{:S(2)}, u32[]{:S(2)}) %collective-permute-start.37) | collective-permute-done | bytes 393248 | tf_op jit(solution)/shard_map/ppermute | solution.py:931
  319.2 15.2 %inputs_back.1 = (f32[512,1024]{1,0:T(8,128)}, f32[512,1024]{1,0:T(8,128)}) custom-call(s32[4]{0:T(128)} %add_add_fusion.1.refs_0_, f32[512,1024]{1,0:T(8,128)} %get-tuple-element.241.refs_1_, bf16[512,1536]{1,0:T(8,128)(2,1)} %get-tuple-element.223.refs_2_, bf16[512,1536]{1,0:T(8,128)(2,1)} %get-tuple-element.237.refs_3_, ...), custom_call_target="tpu_custom_call" | custom-call | flops 13200000000 | bytes 4194304 | tf_op jit(solution)/shard_map/inputs_back/pallas_call | solution.py:527
  334.4 7.3 %collective-permute-done.41.refs_7_.refs_9_.refs_11_ = bf16[4,2,2,128,128]{4,3,2,1,0:T(8,128)(2,1)S(1)} collective-permute-done((bf16[4,2,2,128,128]{4,3,2,1,0:T(8,128)(2,1)}, bf16[4,2,2,128,128]{4,3,2,1,0:T(8,128)(2,1)S(1)}, u32[]{:S(2)}, u32[]{:S(2)}) %collective-permute-start.41) | collective-permute-done | bytes 524320 | tf_op jit(solution)/shard_map/ppermute | solution.py:931
  349.9 17.3 %collective-permute-done.45.refs_10_.refs_12_ = bf16[4,2,128,128]{3,2,1,0:T(8,128)(2,1)S(1)} collective-permute-done((bf16[4,2,128,128]{3,2,1,0:T(8,128)(2,1)}, bf16[4,2,128,128]{3,2,1,0:T(8,128)(2,1)S(1)}, u32[]{:S(2)}, u32[]{:S(2)}) %collective-permute-start.45) | collective-permute-done | bytes 262176 | tf_op jit(solution)/shard_map/ppermute | solution.py:927
  373.1 4.5 %combine.15 = (bf16[4,2,128,128]{3,2,1,0:T(8,128)(2,1)}, bf16[4,2,128,128]{3,2,1,0:T(8,128)(2,1)}, bf16[8,128,128]{2,1,0:T(8,128)(2,1)}, f32[128,1024]{1,0:T(8,128)}, f32[1024,128]{1,0:T(8,128)}) custom-call(bf16[8,2,2,2,2,128,128]{6,5,4,3,2,1,0:T(8,128)(2,1)} %bitcast.54, bf16[8,2,2,2,2,128,128]{6,5,4,3,2,1,0:T(8,128)(2,1)} %bitcast.24.refs_1_, ...), custom_call_target="tpu_custom_call" | custom-call | flops 3300000000 | bytes 4194304 | tf_op jit(solution)/shard_map/combine/pallas_call | solution.py:906
  384.6 5.7 %collective-permute-done.49.refs_7_.refs_8_ = bf16[4,2,128,128]{3,2,1,0:T(8,128)(2,1)S(1)} collective-permute-done((bf16[4,2,128,128]{3,2,1,0:T(8,128)(2,1)}, bf16[4,2,128,128]{3,2,1,0:T(8,128)(2,1)S(1)}, u32[]{:S(2)}, u32[]{:S(2)}) %collective-permute-start.49) | collective-permute-done | bytes 262176 | tf_op jit(solution)/shard_map/ppermute | solution.py:931
  397.1 9.8 %collective-permute-done.51.refs_5_ = bf16[8,128,128]{2,1,0:T(8,128)(2,1)S(1)} collective-permute-done((bf16[8,128,128]{2,1,0:T(8,128)(2,1)}, bf16[8,128,128]{2,1,0:T(8,128)(2,1)S(1)}, u32[]{:S(2)}, u32[]{:S(2)}) %collective-permute-start.51) | collective-permute-done | bytes 262176 | tf_op jit(solution)/shard_map/ppermute | solution.py:931
  (217 shorter events, 123.9 us)
Async XLA Ops:
  7.2 402.9 %all-gather.3.cloned.1.call-start = ((), (), s32[]{:S(2)}) async-start(), calls=%async_computation | async-start | bytes 1081344 | tf_op jit(solution)/shard_map/all_gather | solution.py:1150
  13.6 34.1 %collective-permute-start.3 = (bf16[4,512,256]{2,1,0:T(8,128)(2,1)S(1)}, bf16[4,512,256]{2,1,0:T(8,128)(2,1)}, u32[]{:S(2)}, u32[]{:S(2)}) collective-permute-start(bf16[4,512,256]{2,1,0:T(8,128)(2,1)S(1)} %pad_maximum_fusion.2), channel_id=1, source_target_pairs={{0,2},{1,3},{2,0},{3,1},{4,6},{5,7},{6,4},{7,5},{8,10},{9,11},{10,... | collective-permute-start | bytes 3145736 | tf_op jit(solution)/shard_map/ppermute | solution.py:927
  54.8 25.9 %collective-permute-start.12 = (bf16[4,512,256]{2,1,0:T(8,128)(2,1)}, bf16[4,512,256]{2,1,0:T(8,128)(2,1)}, u32[]{:S(2)}, u32[]{:S(2)}) collective-permute-start(bf16[4,512,256]{2,1,0:T(8,128)(2,1)} %collective-permute-done.3), channel_id=1, source_target_pairs={{0,8},{4,12},{8,0},{12,4},{16,24},{20,28},{24,16},{28,20},{1,9},{5... | collective-permute-start | bytes 3145736 | tf_op jit(solution)/shard_map/ppermute | solution.py:931
  58.6 26.4 %collective-permute-start.8 = (bf16[2,256,1024]{2,1,0:T(8,128)(2,1)S(1)}, bf16[2,256,1024]{2,1,0:T(8,128)(2,1)}, u32[]{:S(2)}, u32[]{:S(2)}) collective-permute-start(bf16[2,256,1024]{2,1,0:T(8,128)(2,1)S(1)} %pad_maximum_fusion.3), channel_id=1, source_target_pairs={{0,2},{1,3},{2,0},{3,1},{4,6},{5,7},{6,4},{7,5},{8,10},{9,11},{10,... | collective-permute-start | bytes 3145736 | tf_op jit(solution)/shard_map/ppermute | solution.py:927
  83.9 28.0 %collective-permute-start.13 = (bf16[2,4,512,256]{3,2,1,0:T(8,128)(2,1)}, bf16[2,4,512,256]{3,2,1,0:T(8,128)(2,1)}, u32[]{:S(2)}, u32[]{:S(2)}) collective-permute-start(bf16[2,4,512,256]{3,2,1,0:T(8,128)(2,1)} %pad_maximum_fusion.1.refs_9_.refs_15_.refs_18_), channel_id=1, source_target_pairs={{0,1},{1,0},{2,3},{3,2},{4,5},{5,4},{6,7},{7,6},{8,9},{9,8},{10,11... | collective-permute-start | bytes 6291464 | tf_op jit(solution)/shard_map/ppermute | solution.py:923
  84.5 45.1 %collective-permute-start.14 = (bf16[1024,1024]{1,0:T(8,128)(2,1)}, bf16[1024,1024]{1,0:T(8,128)(2,1)}, u32[]{:S(2)}, u32[]{:S(2)}) collective-permute-start(bf16[1024,1024]{1,0:T(8,128)(2,1)} %refs_7_.3), channel_id=1, source_target_pairs={{0,1},{1,0},{2,3},{3,2},{4,5},{5,4},{6,7},{7,6},{8,9},{9,8},{10,11... | collective-permute-start | bytes 6291464 | tf_op jit(solution)/shard_map/ppermute | solution.py:923
  84.9 45.3 %collective-permute-start.15 = (bf16[1024,1024]{1,0:T(8,128)(2,1)}, bf16[1024,1024]{1,0:T(8,128)(2,1)}, u32[]{:S(2)}, u32[]{:S(2)}) collective-permute-start(bf16[1024,1024]{1,0:T(8,128)(2,1)} %refs_8_.2), channel_id=1, source_target_pairs={{0,1},{1,0},{2,3},{3,2},{4,5},{5,4},{6,7},{7,6},{8,9},{9,8},{10,11... | collective-permute-start | bytes 6291464 | tf_op jit(solution)/shard_map/ppermute | solution.py:923
  94.8 32.0 %collective-permute-start.16 = (bf16[2,256,1024]{2,1,0:T(8,128)(2,1)}, bf16[2,256,1024]{2,1,0:T(8,128)(2,1)}, u32[]{:S(2)}, u32[]{:S(2)}) collective-permute-start(bf16[2,256,1024]{2,1,0:T(8,128)(2,1)} %collective-permute-done.8.refs_9_), channel_id=1, source_target_pairs={{0,4},{4,0},{8,12},{12,8},{16,20},{20,16},{24,28},{28,24},{1,5},{5... | collective-permute-start | bytes 3145736 | tf_op jit(solution)/shard_map/ppermute | solution.py:931
  97.2 31.3 %collective-permute-start.17 = (bf16[2,256,1024]{2,1,0:T(8,128)(2,1)}, bf16[2,256,1024]{2,1,0:T(8,128)(2,1)}, u32[]{:S(2)}, u32[]{:S(2)}) collective-permute-start(bf16[2,256,1024]{2,1,0:T(8,128)(2,1)} %collective-permute-done.8.refs_9_), channel_id=1, source_target_pairs={{0,8},{4,12},{8,0},{12,4},{16,24},{20,28},{24,16},{28,20},{1,9},{5... | collective-permute-start | bytes 3145736 | tf_op jit(solution)/shard_map/ppermute | solution.py:931
  111.9 32.9 %collective-permute-start.20 = (bf16[2,256,1024]{2,1,0:T(8,128)(2,1)}, bf16[2,256,1024]{2,1,0:T(8,128)(2,1)}, u32[]{:S(2)}, u32[]{:S(2)}) collective-permute-start(bf16[2,256,1024]{2,1,0:T(8,128)(2,1)} %collective-permute-done.8.refs_9_), channel_id=1, source_target_pairs={{0,1},{1,0},{2,3},{3,2},{4,5},{5,4},{6,7},{7,6},{8,9},{9,8},{10,11... | collective-permute-start | bytes 3145736 | tf_op jit(solution)/shard_map/ppermute | solution.py:923
  202.7 36.9 %collective-permute-start.26 = (bf16[3,2,2,2,128,256]{5,4,3,2,1,0:T(8,128)(2,1)}, bf16[3,2,2,2,128,256]{5,4,3,2,1,0:T(8,128)(2,1)S(1)}, u32[]{:S(2)}, u32[]{:S(2)}) collective-permute-start(bf16[3,2,2,2,128,256]{5,4,3,2,1,0:T(8,128)(2,1)} %get-tuple-element.189), channel_id=1, source_target_pairs={{0,2},{1,3},{2,0},{3,1},{4,6},{5,7},{6,4},{7,5},{8,10},{9,11},{10,... | collective-permute-start | bytes 4718600 | tf_op jit(solution)/shard_map/ppermute | solution.py:927
  204.3 36.7 %collective-permute-start.27 = (bf16[3,2,2,2,128,256]{5,4,3,2,1,0:T(8,128)(2,1)}, bf16[3,2,2,2,128,256]{5,4,3,2,1,0:T(8,128)(2,1)}, u32[]{:S(2)}, u32[]{:S(2)}) collective-permute-start(bf16[3,2,2,2,128,256]{5,4,3,2,1,0:T(8,128)(2,1)} %get-tuple-element.190), channel_id=1, source_target_pairs={{0,4},{4,0},{8,12},{12,8},{16,20},{20,16},{24,28},{28,24},{1,5},{5... | collective-permute-start | bytes 4718600 | tf_op jit(solution)/shard_map/ppermute | solution.py:931
  205.8 32.6 %collective-permute-start.28 = (bf16[2,2,2,2,128,256]{5,4,3,2,1,0:T(8,128)(2,1)}, bf16[2,2,2,2,128,256]{5,4,3,2,1,0:T(8,128)(2,1)}, u32[]{:S(2)}, u32[]{:S(2)}) collective-permute-start(bf16[2,2,2,2,128,256]{5,4,3,2,1,0:T(8,128)(2,1)} %get-tuple-element.191), channel_id=1, source_target_pairs={{0,8},{4,12},{8,0},{12,4},{16,24},{20,28},{24,16},{28,20},{1,9},{5... | collective-permute-start | bytes 3145736 | tf_op jit(solution)/shard_map/ppermute | solution.py:931
  273.5 26.5 %collective-permute-start.35 = (bf16[4,2,2,2,128,128]{5,4,3,2,1,0:T(8,128)(2,1)}, bf16[4,2,2,2,128,128]{5,4,3,2,1,0:T(8,128)(2,1)S(1)}, u32[]{:S(2)}, u32[]{:S(2)}) collective-permute-start(bf16[4,2,2,2,128,128]{5,4,3,2,1,0:T(8,128)(2,1)} %get-tuple-element.228), channel_id=1, source_target_pairs={{0,4},{4,0},{8,12},{12,8},{16,20},{20,16},{24,28},{28,24},{1,5},{5... | collective-permute-start | bytes 3145736 | tf_op jit(solution)/shard_map/ppermute | solution.py:931
  274.1 27.5 %collective-permute-start.36 = (bf16[4,2,2,2,128,128]{5,4,3,2,1,0:T(8,128)(2,1)}, bf16[4,2,2,2,128,128]{5,4,3,2,1,0:T(8,128)(2,1)}, u32[]{:S(2)}, u32[]{:S(2)}) collective-permute-start(bf16[4,2,2,2,128,128]{5,4,3,2,1,0:T(8,128)(2,1)} %get-tuple-element.229), channel_id=1, source_target_pairs={{0,8},{4,12},{8,0},{12,4},{16,24},{20,28},{24,16},{28,20},{1,9},{5... | collective-permute-start | bytes 3145736 | tf_op jit(solution)/shard_map/ppermute | solution.py:931
  274.6 35.5 %collective-permute-start.37 = (bf16[3,2,128,256]{3,2,1,0:T(8,128)(2,1)}, bf16[3,2,128,256]{3,2,1,0:T(8,128)(2,1)S(1)}, u32[]{:S(2)}, u32[]{:S(2)}) collective-permute-start(bf16[3,2,128,256]{3,2,1,0:T(8,128)(2,1)} %get-tuple-element.230), channel_id=1, source_target_pairs={{0,8},{4,12},{8,0},{12,4},{16,24},{20,28},{24,16},{28,20},{1,9},{5... | collective-permute-start | bytes 1179656 | tf_op jit(solution)/shard_map/ppermute | solution.py:931
  276.1 34.0 %collective-permute-start.38 = (bf16[3,2,128,256]{3,2,1,0:T(8,128)(2,1)}, bf16[3,2,128,256]{3,2,1,0:T(8,128)(2,1)S(1)}, u32[]{:S(2)}, u32[]{:S(2)}) collective-permute-start(bf16[3,2,128,256]{3,2,1,0:T(8,128)(2,1)} %get-tuple-element.231), channel_id=1, source_target_pairs={{0,2},{1,3},{2,0},{3,1},{4,6},{5,7},{6,4},{7,5},{8,10},{9,11},{10,... | collective-permute-start | bytes 1179656 | tf_op jit(solution)/shard_map/ppermute | solution.py:927
  300.0 41.8 %collective-permute-start.34 = (bf16[4,2,2,2,128,128]{5,4,3,2,1,0:T(8,128)(2,1)}, bf16[4,2,2,2,128,128]{5,4,3,2,1,0:T(8,128)(2,1)}, u32[]{:S(2)}, u32[]{:S(2)}) collective-permute-start(bf16[4,2,2,2,128,128]{5,4,3,2,1,0:T(8,128)(2,1)} %get-tuple-element.239), channel_id=1, source_target_pairs={{0,2},{1,3},{2,0},{3,1},{4,6},{5,7},{6,4},{7,5},{8,10},{9,11},{10,... | collective-permute-start | bytes 3145736 | tf_op jit(solution)/shard_map/ppermute | solution.py:927
  301.6 40.2 %collective-permute-start.40 = (bf16[4,2,2,2,128,128]{5,4,3,2,1,0:T(8,128)(2,1)}, bf16[4,2,2,2,128,128]{5,4,3,2,1,0:T(8,128)(2,1)}, u32[]{:S(2)}, u32[]{:S(2)}) collective-permute-start(bf16[4,2,2,2,128,128]{5,4,3,2,1,0:T(8,128)(2,1)} %get-tuple-element.240), channel_id=1, source_target_pairs={{0,4},{4,0},{8,12},{12,8},{16,20},{20,16},{24,28},{28,24},{1,5},{5... | collective-permute-start | bytes 3145736 | tf_op jit(solution)/shard_map/ppermute | solution.py:931
  314.6 27.2 %collective-permute-start.41 = (bf16[4,2,2,128,128]{4,3,2,1,0:T(8,128)(2,1)}, bf16[4,2,2,128,128]{4,3,2,1,0:T(8,128)(2,1)S(1)}, u32[]{:S(2)}, u32[]{:S(2)}) collective-permute-start(bf16[4,2,2,128,128]{4,3,2,1,0:T(8,128)(2,1)} %get-tuple-element.250), channel_id=1, source_target_pairs={{0,8},{4,12},{8,0},{12,4},{16,24},{20,28},{24,16},{28,20},{1,9},{5... | collective-permute-start | bytes 1572872 | tf_op jit(solution)/shard_map/ppermute | solution.py:931
  315.1 26.7 %collective-permute-start.42 = (bf16[4,2,2,128,128]{4,3,2,1,0:T(8,128)(2,1)}, bf16[4,2,2,128,128]{4,3,2,1,0:T(8,128)(2,1)S(1)}, u32[]{:S(2)}, u32[]{:S(2)}) collective-permute-start(bf16[4,2,2,128,128]{4,3,2,1,0:T(8,128)(2,1)} %get-tuple-element.251), channel_id=1, source_target_pairs={{0,4},{4,0},{8,12},{12,8},{16,20},{20,16},{24,28},{28,24},{1,5},{5... | collective-permute-start | bytes 1572872 | tf_op jit(solution)/shard_map/ppermute | solution.py:931
  316.6 33.3 %collective-permute-start.47 = (bf16[8,128,256]{2,1,0:T(8,128)(2,1)}, bf16[8,128,256]{2,1,0:T(8,128)(2,1)}, u32[]{:S(2)}, u32[]{:S(2)}) collective-permute-start(bf16[8,128,256]{2,1,0:T(8,128)(2,1)} %get-tuple-element.252), channel_id=1, source_target_pairs={{0,16},{4,20},{8,24},{12,28},{16,0},{20,4},{24,8},{28,12},{1,17},{... | collective-permute-start | bytes 1572872 | tf_op jit(solution)/shard_map/ppermute | solution.py:931
  346.3 25.1 %collective-permute-start.43 = (bf16[4,2,2,128,128]{4,3,2,1,0:T(8,128)(2,1)}, bf16[4,2,2,128,128]{4,3,2,1,0:T(8,128)(2,1)S(1)}, u32[]{:S(2)}, u32[]{:S(2)}) collective-permute-start(bf16[4,2,2,128,128]{4,3,2,1,0:T(8,128)(2,1)} %get-tuple-element.257), channel_id=1, source_target_pairs={{0,8},{4,12},{8,0},{12,4},{16,24},{20,28},{24,16},{28,20},{1,9},{5... | collective-permute-start | bytes 1572872 | tf_op jit(solution)/shard_map/ppermute | solution.py:931
  346.6 24.8 %collective-permute-start.44 = (bf16[4,2,2,128,128]{4,3,2,1,0:T(8,128)(2,1)}, bf16[4,2,2,128,128]{4,3,2,1,0:T(8,128)(2,1)S(1)}, u32[]{:S(2)}, u32[]{:S(2)}) collective-permute-start(bf16[4,2,2,128,128]{4,3,2,1,0:T(8,128)(2,1)} %get-tuple-element.258), channel_id=1, source_target_pairs={{0,2},{1,3},{2,0},{3,1},{4,6},{5,7},{6,4},{7,5},{8,10},{9,11},{10,... | collective-permute-start | bytes 1572872 | tf_op jit(solution)/shard_map/ppermute | solution.py:927
  (69 other events, 531.4 us)
Sparse Core Ops, SparseCore 0:
  273.6 61.3 all-gather.2

commit v5 on v4

--- a/solution.py
+++ b/solution.py
@@ -1092,18 +1092,17 @@
     cross_up = over_z_near(cross_near)
     self_far = to_sibling(self_rest)
     self_pieces = [self_own, self_sib, (self_rest,), (self_far,)]
+    cross_own, ffn_own = (cross_q, cross_kv, cross_out), (ffn_in, ffn_out)
+    cross_sib = tuple(to_sibling(after(w, self_near)) for w in cross_own)
     self_b = attention_fwd_call(
-        self_scalars, [tokens], [tokens], self_pieces[2:], self_a[5], (gains[0], biases[0])
+        after(self_scalars, *cross_sib), [tokens], [tokens], self_pieces[2:], self_a[5], (gains[0], biases[0])
     )
     first_low, first_hat, first_inv = self_b[5:]
-    cross_own = (cross_q, cross_kv, cross_out)
-    cross_sib = tuple(to_sibling(after(w, self_near)) for w in cross_own)
-    ffn_own = (ffn_in, ffn_out)
-    ffn_sib = tuple(to_sibling(after(w, first_inv)) for w in ffn_own)
     cross_in = [first_low, memory]
     cross_rest = jnp.stack([cross_near, after(cross_up, self_b[4])])
     cross_far = to_sibling(cross_rest)
     cross_a = attention_fwd_call(after(cross_scalars, ffn_near), [], cross_in, [cross_own, cross_sib], None, None)
+    ffn_sib = tuple(to_sibling(after(w, ffn_near)) for w in ffn_own)
     ffn_side, ffn_up = over_x(ffn_near), over_z_near(ffn_near)
     cross_pieces = [cross_own, cross_sib, (cross_rest,), (after(cross_far, cross_a[4]),)]
     cross_b = attention_fwd_call(
@@ -1149,7 +1148,7 @@
     norm_sums = jnp.concatenate([jnp.sum(norm_sums, axis=1), jnp.zeros((2, norm_sums.shape[2]), F32)])
     norm_sums = lax.all_gather(norm_sums, ("dp", "tensor"), axis=0)
     sends = advance([ffn_sum], first_gain)
-    cross_sum = Reduction(after(cross_e[5], *sends), [(0, 4, "xzy"), (4, 8, "zxy")], attention_finish((1, 2)))
+    cross_sum = Reduction(after(cross_e[5], *sends), [(0, 4, "xyz"), (4, 8, "yzx")], attention_finish((1, 2)))
     first_back = after(first_back, *sends)
 
     self_saved = [self_a[:5], self_b[:5]]
@@ -1158,7 +1157,7 @@
     )
     cross_sum.begin(cross_e[6], self_d[0])
     sends = advance([cross_sum, ffn_sum], self_d[0])
-    self_sum = Reduction(after(self_d[1], *sends), [(0, 4, "yzx"), (4, 8, "xyz")], attention_finish((3,)))
+    self_sum = Reduction(after(self_d[1], *sends), [(0, 4, "zxy"), (4, 8, "xyz")], attention_finish((3,)))
     first_back = after(first_back, *sends)
     self_e = attention_bwd_call(
         self_scalars, first_back, [tokens], self_pieces[::2], self_saved, plan_of((0, 2)), None, None
@@ -1173,9 +1172,9 @@
     sends = advance([cross_sum, ffn_sum], *sends)
     sends = advance([self_sum, cross_sum], *sends, grad_tokens)
     sends = advance([self_sum, cross_sum, ffn_sum], *sends)
-    sends = advance([self_sum, cross_sum], *sends)
-    sends = advance([self_sum], *sends)
     norm_total = jnp.sum(after(norm_sums, *sends), axis=0)
+    sends = advance([self_sum, cross_sum], *sends, norm_total)
+    advance([self_sum], *sends)
     self_sum, cross_sum, ffn_sum = self_sum.total, cross_sum.total, ffn_sum.total
 
     return (

time: 423 us -> 414 us (0.979)
    ppermute x25, waiting for transfers between devices: 61.5 us -> 76.4 us  [over_dp(): return lax.ppermute(values, 'dp', swap_pairs(8, mask))]
    ppermute x10, waiting for transfers between devices: 28.3 us -> 16.7 us  [over_y(): return lax.ppermute(values, 'tensor', swap_pairs(4, 2))]
    ppermute x17, waiting for transfers between devices: 11.8 us -> 5.16 us  [to_sibling(): return lax.ppermute(values, 'tensor', swap_pairs(4, 1))]
where the time goes in v5:
time: 414 us; the launch traced here: 411 us
  Pallas kernels  227 us (55%)
  waiting for transfers between devices  98.3 us (24%)
  starting transfers between devices  44.9 us (11%)
  local copies, waits for them, and re-layouts  16.7 us (4%)
  between operations  15.1 us (4%)
  other arithmetic  8.63 us (2%)
    ppermute x25, waiting for transfers between devices, over_dp(): return lax.ppermute(values, 'dp', swap_pairs(8, mask))  76.4 us
    pallas_call x3, Pallas kernels, attention_bwd_call(): pl.pallas_call(kernel, out_shape=shapes, in_specs=[SMEM] + [VMEM] * (len(...  64 us
    pallas_call x4, Pallas kernels, attention_fwd_call(): pl.pallas_call(kernel, out_shape=shapes, in_specs=[SMEM] + [VMEM] * (len(...  51.5 us
    pallas_call x9, Pallas kernels, combine(): pl.pallas_call(kernel, out_shape=list(shapes), in_specs=[ANY] * len(array...  35.7 us
    pallas_call x2, Pallas kernels, ffn_bwd_call(): pl.pallas_call(kernel, out_shape=shapes, in_specs=specs + [ANY] * len(tai...  33.7 us
    ppermute x25, starting transfers between devices, over_dp(): return lax.ppermute(values, 'dp', swap_pairs(8, mask))  27.5 us
    pallas_call x2, Pallas kernels, ffn_fwd_call(): pl.pallas_call(kernel, out_shape=shapes, in_specs=specs + [ANY] * len(tai...  27 us
    ppermute x10, waiting for transfers between devices, over_y(): return lax.ppermute(values, 'tensor', swap_pairs(4, 2))  16.7 us
  transfers between devices with their start and end apart: 53, of which 24 were waited for; matrix products, arithmetic and copies ran while one was open for 4% of the time, Pallas kernels for 43%

profile of v5, /device:TPU:0, one launch (start us, length us, event | category | flops | bytes accessed | tf_op | source)
XLA Modules:
  0.0 410.6 jit_solution(2013682704100754898)
XLA Ops:
  15.7 11.0 %self_fwd.2 = (bf16[4,512,128]{2,1,0:T(8,128)(2,1)}, bf16[4,512,128]{2,1,0:T(8,128)(2,1)}, bf16[4,512,128]{2,1,0:T(8,128)(2,1)}, bf16[4,512,128]{2,1,0:T(8,128)(...) custom-call(s32[4]{0:T(128)} %add_add_fusion.1.refs_0_, bf16[512,1024]{1,0:T(8,128)(2,1)} %refs_2_.11, ...), custom_call_target="tpu_custom_call" | custom-call | flops 2640000000 | bytes 4194304 | tf_op jit(solution)/shard_map/self_fwd/pallas_call | solution.py:349
  30.2 10.3 %collective-permute-done.8 = bf16[4,256,256]{2,1,0:T(8,128)(2,1)S(1)} collective-permute-done((bf16[4,256,256]{2,1,0:T(8,128)(2,1)}, bf16[4,256,256]{2,1,0:T(8,128)(2,1)S(1)}, u32[]{:S(2)}, u32[]{:S(2)}) %collective-permute-start.8) | collective-permute-done | bytes 524320 | tf_op jit(solution)/shard_map/ppermute | solution.py:931
  42.2 5.6 %collective-permute-done.6 = bf16[4,512,256]{2,1,0:T(8,128)(2,1)} collective-permute-done((bf16[4,512,256]{2,1,0:T(8,128)(2,1)S(1)}, bf16[4,512,256]{2,1,0:T(8,128)(2,1)}, u32[]{:S(2)}, u32[]{:S(2)}) %collective-permute-start.6) | collective-permute-done | bytes 1048608 | tf_op jit(solution)/shard_map/ppermute | solution.py:927
  47.8 5.6 %collective-permute-done.9 = bf16[4,256,256]{2,1,0:T(8,128)(2,1)S(1)} collective-permute-done((bf16[4,256,256]{2,1,0:T(8,128)(2,1)S(1)}, bf16[4,256,256]{2,1,0:T(8,128)(2,1)S(1)}, u32[]{:S(2)}, u32[]{:S(2)}) %collective-permute-start.9) | collective-permute-done | bytes 524320 | tf_op jit(solution)/shard_map/ppermute | solution.py:931
  65.2 13.9 %self_fwd.3 = (bf16[4,512,128]{2,1,0:T(8,128)(2,1)}, bf16[4,512,128]{2,1,0:T(8,128)(2,1)}, bf16[4,512,128]{2,1,0:T(8,128)(2,1)}, bf16[4,512,128]{2,1,0:T(8,128)(...) custom-call(s32[4]{0:T(128)} %add_add_fusion.1.refs_0_, ...), custom_call_target="tpu_custom_call" | custom-call | flops 2640000000 | bytes 4194304 | tf_op jit(solution)/shard_map/self_fwd/pallas_call | solution.py:349
  91.4 11.8 %cross_fwd.2 = (bf16[4,512,128]{2,1,0:T(8,128)(2,1)}, bf16[4,512,128]{2,1,0:T(8,128)(2,1)}, bf16[4,512,128]{2,1,0:T(8,128)(2,1)}, bf16[4,512,128]{2,1,0:T(8,128)...) custom-call(s32[4]{0:T(128)} %add_add_fusion.refs_0_, bf16[512,1024]{1,0:T(8,128)(2,1)} %get-tuple-element.158.refs_1_.refs_2_, ...), custom_call_target="tpu_custom_call" | custom-call | flops 2640000000 | bytes 4194304 | tf_op jit(solution)/shard_map/cross_fwd/pallas_call | solution.py:349
  103.3 14.8 %cross_fwd.3 = (bf16[4,512,128]{2,1,0:T(8,128)(2,1)}, bf16[4,512,128]{2,1,0:T(8,128)(2,1)}, bf16[4,512,128]{2,1,0:T(8,128)(2,1)}, bf16[4,512,128]{2,1,0:T(8,128)...) custom-call(s32[4]{0:T(128)} %add_add_fusion.refs_0_, ...), custom_call_target="tpu_custom_call" | custom-call | flops 2640000000 | bytes 4194304 | tf_op jit(solution)/shard_map/cross_fwd/pallas_call | solution.py:349
  122.1 11.6 %ffn_fwd.2 = (f32[512,1024]{1,0:T(8,128)}, bf16[4,512,512]{2,1,0:T(8,128)(2,1)}, bf16[4,512,512]{2,1,0:T(8,128)(2,1)}) custom-call(s32[4]{0:T(128)} %add_add_fusion.refs_0_, bf16[512,1024]{1,0:T(8,128)(2,1)} %get-tuple-element.166.refs_1_.refs_2_, bf16[1024,1024]{1,0:T(8,128)(2,1)} %refs_7_.3, bf16[1024,1024]{1,0:T(8,128)(2,1)} %refs_8_.2, ...), custom_call_target="tpu_custom_call" | custom-call | flops 13200000000 | bytes 4194304 | tf_op jit(solution)/shard_map/ffn_fwd/pallas_call | solution.py:709
  139.3 15.4 %ffn_fwd.3 = (bf16[512,1024]{1,0:T(8,128)(2,1)}, bf16[512,1024]{1,0:T(8,128)(2,1)}, f32[512,1024]{1,0:T(8,128)}, f32[8,1024]{1,0:T(8,128)}, f32[8,1024]{1,0:T(8,...) custom-call(s32[4]{0:T(128)} %add_add_fusion.refs_0_, ...), custom_call_target="tpu_custom_call" | custom-call | flops 13200000000 | bytes 4194304 | tf_op jit(solution)/shard_map/ffn_fwd/pallas_call | solution.py:709
  154.7 16.2 %ffn_bwd.2 = (f32[512,1024]{1,0:T(8,128)}, bf16[8,2,8,128,256]{4,3,2,1,0:T(8,128)(2,1)}) custom-call(s32[4]{0:T(128)} %add_add_fusion.refs_0_, bf16[512,1024]{1,0:T(8,128)(2,1)} %get-tuple-element.177.refs_1_, bf16[512,1024]{1,0:T(8,128)(2,1)} %get-tuple-element.166.refs_1_.refs_2_, f32[512,1024]{1,0:T(8,128)} %get-tuple-element.179.refs_3_, ...), custom_call_target="tpu_custom_call" | custom-call | flops 18699999232 | bytes 4194304 | tf_op jit(solution)/shard_map/ffn_bwd/pallas_call | solution.py:822
  171.2 17.5 %ffn_bwd.3 = (bf16[512,1024]{1,0:T(8,128)(2,1)}, f32[512,1024]{1,0:T(8,128)}, f32[8,1024]{1,0:T(8,128)}, f32[8,1024]{1,0:T(8,128)}, bf16[8,2,8,128,256]{4,3,2,1,0:T(8,128)(2,1)}) custom-call(s32[4]{0:T(128)} %add_add_fusion.refs_0_, bf16[512,1024]{1,0:T(8,128)(2,1)} %get-tuple-element.177.refs_1_, bf16[512,1024]{1,0:T(8,128)(2,1)} %get-tuple-element.166.refs_1_.refs_2_, ...), custom_call_target="tpu_custom_call" | custom-call | flops 18699999232 | bytes 4194304 | tf_op jit(solution)/shard_map/ffn_bwd/pallas_call | solution.py:822
  188.7 5.2 %combine.9 = (bf16[3,2,2,2,128,256]{5,4,3,2,1,0:T(8,128)(2,1)}, bf16[3,2,2,2,128,256]{5,4,3,2,1,0:T(8,128)(2,1)}, bf16[2,2,2,2,128,256]{5,4,3,2,1,0:T(8,128)(2,1)}) custom-call(bf16[8,2,2,2,2,128,256]{6,5,4,3,2,1,0:T(8,128)(2,1)} %bitcast.42, bf16[8,2,2,2,2,128,256]{6,5,4,3,2,1,0:T(8,128)(2,1)} %bitcast.20.refs_1_.refs_3_.refs_5_.refs_15_), custom_call_target="tpu_custom_call" | custom-call | flops 3300000000 | bytes 4194304 | tf_op jit(solution)/shard_map/combine/pallas_call | solution.py:906
  197.5 32.2 %cross_bwd.1 = (bf16[512,1024]{1,0:T(8,128)(2,1)}, f32[512,1024]{1,0:T(8,128)}, f32[8,1024]{1,0:T(8,128)}, f32[8,1024]{1,0:T(8,128)}, bf16[512,2048]{1,0:T(8,128...) custom-call(s32[4]{0:T(128)} %add_add_fusion.refs_0_, ...), custom_call_target="tpu_custom_call" | custom-call | flops 36960002048 | bytes 4194304 | tf_op jit(solution)/shard_map/cross_bwd/pallas_call | solution.py:487
  239.7 16.0 %self_bwd.2 = (bf16[512,1536]{1,0:T(8,128)(2,1)}, bf16[8,2,8,128,128]{4,3,2,1,0:T(8,128)(2,1)}) custom-call(s32[4]{0:T(128)} %add_add_fusion.1.refs_0_, bf16[512,1024]{1,0:T(8,128)(2,1)} %get-tuple-element.235.refs_1_, bf16[512,1024]{1,0:T(8,128)(2,1)} %refs_2_.11, bf16[3,1024,256]{2,1,0:T(8,128)(2,1)} %collective-permute-done.1.refs_4_.refs_3_.refs_5_, ...), custom_call_target="tpu_custom_call" | custom-call | flops 18480001024 | bytes 4194304 | tf_op jit(solution)/shard_map/self_bwd/pallas_call | solution.py:487
  258.6 5.1 %combine.11 = (bf16[4,2,2,2,128,128]{5,4,3,2,1,0:T(8,128)(2,1)}, bf16[4,2,2,2,128,128]{5,4,3,2,1,0:T(8,128)(2,1)}, bf16[3,2,128,256]{3,2,1,0:T(8,128)(2,1)}, bf1...) custom-call(bf16[8,2,2,2,2,128,128]{6,5,4,3,2,1,0:T(8,128)(2,1)} %bitcast.47, ...), custom_call_target="tpu_custom_call" | custom-call | flops 3300000000 | bytes 4194304 | tf_op jit(solution)/shard_map/combine/pallas_call | solution.py:906
  267.7 15.9 %self_bwd.3 = (bf16[512,1536]{1,0:T(8,128)(2,1)}, bf16[8,2,8,128,128]{4,3,2,1,0:T(8,128)(2,1)}) custom-call(s32[4]{0:T(128)} %add_add_fusion.1.refs_0_, bf16[512,1024]{1,0:T(8,128)(2,1)} %get-tuple-element.235.refs_1_, bf16[512,1024]{1,0:T(8,128)(2,1)} %refs_2_.11, bf16[3,1024,256]{2,1,0:T(8,128)(2,1)} %refs_8_.3, bf16[256,1024]{1,0:T(8,128)(2,1)} %refs_9_.1, ...), custom_call_target="tpu_custom_call" | custom-call | flops 18480001024 | bytes 4194304 | tf_op jit(solution)/shard_map/self_bwd/pallas_call | solution.py:487
  293.8 6.1 %collective-permute-done.38.refs_11_.refs_22_ = bf16[3,2,128,256]{3,2,1,0:T(8,128)(2,1)S(1)} collective-permute-done((bf16[3,2,128,256]{3,2,1,0:T(8,128)(2,1)}, bf16[3,2,128,256]{3,2,1,0:T(8,128)(2,1)S(1)}, u32[]{:S(2)}, u32[]{:S(2)}) %collective-permute-start.38) | collective-permute-done | bytes 393248 | tf_op jit(solution)/shard_map/ppermute | solution.py:927
  308.7 15.1 %inputs_back.1 = (f32[512,1024]{1,0:T(8,128)}, f32[512,1024]{1,0:T(8,128)}) custom-call(s32[4]{0:T(128)} %add_add_fusion.1.refs_0_, f32[512,1024]{1,0:T(8,128)} %get-tuple-element.243.refs_1_, bf16[512,1536]{1,0:T(8,128)(2,1)} %get-tuple-element.225.refs_2_, bf16[512,1536]{1,0:T(8,128)(2,1)} %get-tuple-element.239.refs_3_, ...), custom_call_target="tpu_custom_call" | custom-call | flops 13200000000 | bytes 4194304 | tf_op jit(solution)/shard_map/inputs_back/pallas_call | solution.py:527
  323.8 18.3 %collective-permute-done.42.refs_9_.refs_12_.refs_15_ = bf16[4,2,2,128,128]{4,3,2,1,0:T(8,128)(2,1)S(1)} collective-permute-done((bf16[4,2,2,128,128]{4,3,2,1,0:T(8,128)(2,1)}, bf16[4,2,2,128,128]{4,3,2,1,0:T(8,128)(2,1)S(1)}, u32[]{:S(2)}, u32[]{:S(2)}) %collective-permute-start.42) | collective-permute-done | bytes 524320 | tf_op jit(solution)/shard_map/ppermute | solution.py:931
  349.9 5.2 %collective-permute-done.45.refs_10_.refs_12_ = bf16[4,2,128,128]{3,2,1,0:T(8,128)(2,1)S(1)} collective-permute-done((bf16[4,2,128,128]{3,2,1,0:T(8,128)(2,1)}, bf16[4,2,128,128]{3,2,1,0:T(8,128)(2,1)S(1)}, u32[]{:S(2)}, u32[]{:S(2)}) %collective-permute-start.45) | collective-permute-done | bytes 262176 | tf_op jit(solution)/shard_map/ppermute | solution.py:931
  355.1 9.6 %collective-permute-done.46.refs_13_.refs_16_ = bf16[4,2,128,128]{3,2,1,0:T(8,128)(2,1)S(1)} collective-permute-done((bf16[4,2,128,128]{3,2,1,0:T(8,128)(2,1)}, bf16[4,2,128,128]{3,2,1,0:T(8,128)(2,1)S(1)}, u32[]{:S(2)}, u32[]{:S(2)}) %collective-permute-start.46) | collective-permute-done | bytes 262176 | tf_op jit(solution)/shard_map/ppermute | solution.py:931
  366.4 4.5 %combine.15 = (bf16[4,2,128,128]{3,2,1,0:T(8,128)(2,1)}, bf16[4,2,128,128]{3,2,1,0:T(8,128)(2,1)}, bf16[8,128,128]{2,1,0:T(8,128)(2,1)}, f32[128,1024]{1,0:T(8,128)}, f32[1024,128]{1,0:T(8,128)}) custom-call(bf16[8,2,2,2,2,128,128]{6,5,4,3,2,1,0:T(8,128)(2,1)} %bitcast.54, bf16[8,2,2,2,2,128,128]{6,5,4,3,2,1,0:T(8,128)(2,1)} %bitcast.24.refs_1_, ...), custom_call_target="tpu_custom_call" | custom-call | flops 3300000000 | bytes 4194304 | tf_op jit(solution)/shard_map/combine/pallas_call | solution.py:906
  377.5 6.0 %collective-permute-done.49.refs_7_.refs_8_ = bf16[4,2,128,128]{3,2,1,0:T(8,128)(2,1)S(1)} collective-permute-done((bf16[4,2,128,128]{3,2,1,0:T(8,128)(2,1)}, bf16[4,2,128,128]{3,2,1,0:T(8,128)(2,1)S(1)}, u32[]{:S(2)}, u32[]{:S(2)}) %collective-permute-start.49) | collective-permute-done | bytes 262176 | tf_op jit(solution)/shard_map/ppermute | solution.py:931
  389.6 10.7 %collective-permute-done.51.refs_5_ = bf16[8,128,128]{2,1,0:T(8,128)(2,1)S(1)} collective-permute-done((bf16[8,128,128]{2,1,0:T(8,128)(2,1)}, bf16[8,128,128]{2,1,0:T(8,128)(2,1)S(1)}, u32[]{:S(2)}, u32[]{:S(2)}) %collective-permute-start.51) | collective-permute-done | bytes 262176 | tf_op jit(solution)/shard_map/ppermute | solution.py:931
  (215 shorter events, 112.2 us)
Async XLA Ops:
  7.2 368.2 %all-gather.3.cloned.1.call-start = ((), (), s32[]{:S(2)}) async-start(), calls=%async_computation | async-start | bytes 1081344 | tf_op jit(solution)/shard_map/all_gather | solution.py:1149
  13.6 34.1 %collective-permute-start.6 = (bf16[4,512,256]{2,1,0:T(8,128)(2,1)S(1)}, bf16[4,512,256]{2,1,0:T(8,128)(2,1)}, u32[]{:S(2)}, u32[]{:S(2)}) collective-permute-start(bf16[4,512,256]{2,1,0:T(8,128)(2,1)S(1)} %pad_maximum_fusion.2), channel_id=1, source_target_pairs={{0,2},{1,3},{2,0},{3,1},{4,6},{5,7},{6,4},{7,5},{8,10},{9,11},{10,... | collective-permute-start | bytes 3145736 | tf_op jit(solution)/shard_map/ppermute | solution.py:927
  55.5 25.8 %collective-permute-start.12 = (bf16[4,512,256]{2,1,0:T(8,128)(2,1)}, bf16[4,512,256]{2,1,0:T(8,128)(2,1)}, u32[]{:S(2)}, u32[]{:S(2)}) collective-permute-start(bf16[4,512,256]{2,1,0:T(8,128)(2,1)} %collective-permute-done.6), channel_id=1, source_target_pairs={{0,8},{4,12},{8,0},{12,4},{16,24},{20,28},{24,16},{28,20},{1,9},{5... | collective-permute-start | bytes 3145736 | tf_op jit(solution)/shard_map/ppermute | solution.py:931
  61.3 25.3 %collective-permute-start.11 = (bf16[2,256,1024]{2,1,0:T(8,128)(2,1)S(1)}, bf16[2,256,1024]{2,1,0:T(8,128)(2,1)}, u32[]{:S(2)}, u32[]{:S(2)}) collective-permute-start(bf16[2,256,1024]{2,1,0:T(8,128)(2,1)S(1)} %pad_maximum_fusion.3), channel_id=1, source_target_pairs={{0,2},{1,3},{2,0},{3,1},{4,6},{5,7},{6,4},{7,5},{8,10},{9,11},{10,... | collective-permute-start | bytes 3145736 | tf_op jit(solution)/shard_map/ppermute | solution.py:927
  86.7 34.3 %collective-permute-start.14 = (bf16[1024,1024]{1,0:T(8,128)(2,1)}, bf16[1024,1024]{1,0:T(8,128)(2,1)}, u32[]{:S(2)}, u32[]{:S(2)}) collective-permute-start(bf16[1024,1024]{1,0:T(8,128)(2,1)} %refs_7_.3), channel_id=1, source_target_pairs={{0,1},{1,0},{2,3},{3,2},{4,5},{5,4},{6,7},{7,6},{8,9},{9,8},{10,11... | collective-permute-start | bytes 6291464 | tf_op jit(solution)/shard_map/ppermute | solution.py:923
  86.7 34.9 %collective-permute-start.15 = (bf16[1024,1024]{1,0:T(8,128)(2,1)}, bf16[1024,1024]{1,0:T(8,128)(2,1)}, u32[]{:S(2)}, u32[]{:S(2)}) collective-permute-start(bf16[1024,1024]{1,0:T(8,128)(2,1)} %refs_8_.2), channel_id=1, source_target_pairs={{0,1},{1,0},{2,3},{3,2},{4,5},{5,4},{6,7},{7,6},{8,9},{9,8},{10,11... | collective-permute-start | bytes 6291464 | tf_op jit(solution)/shard_map/ppermute | solution.py:923
  87.2 31.0 %collective-permute-start.16 = (bf16[2,256,1024]{2,1,0:T(8,128)(2,1)}, bf16[2,256,1024]{2,1,0:T(8,128)(2,1)}, u32[]{:S(2)}, u32[]{:S(2)}) collective-permute-start(bf16[2,256,1024]{2,1,0:T(8,128)(2,1)} %collective-permute-done.11.refs_9_), channel_id=1, source_target_pairs={{0,4},{4,0},{8,12},{12,8},{16,20},{20,16},{24,28},{28,24},{1,5},{5... | collective-permute-start | bytes 3145736 | tf_op jit(solution)/shard_map/ppermute | solution.py:931
  88.5 31.3 %collective-permute-start.17 = (bf16[2,256,1024]{2,1,0:T(8,128)(2,1)}, bf16[2,256,1024]{2,1,0:T(8,128)(2,1)}, u32[]{:S(2)}, u32[]{:S(2)}) collective-permute-start(bf16[2,256,1024]{2,1,0:T(8,128)(2,1)} %collective-permute-done.11.refs_9_), channel_id=1, source_target_pairs={{0,8},{4,12},{8,0},{12,4},{16,24},{20,28},{24,16},{28,20},{1,9},{5... | collective-permute-start | bytes 3145736 | tf_op jit(solution)/shard_map/ppermute | solution.py:931
  103.2 32.9 %collective-permute-start.20 = (bf16[2,256,1024]{2,1,0:T(8,128)(2,1)}, bf16[2,256,1024]{2,1,0:T(8,128)(2,1)}, u32[]{:S(2)}, u32[]{:S(2)}) collective-permute-start(bf16[2,256,1024]{2,1,0:T(8,128)(2,1)} %collective-permute-done.11.refs_9_), channel_id=1, source_target_pairs={{0,1},{1,0},{2,3},{3,2},{4,5},{5,4},{6,7},{7,6},{8,9},{9,8},{10,11... | collective-permute-start | bytes 3145736 | tf_op jit(solution)/shard_map/ppermute | solution.py:923
  193.9 36.9 %collective-permute-start.26 = (bf16[3,2,2,2,128,256]{5,4,3,2,1,0:T(8,128)(2,1)}, bf16[3,2,2,2,128,256]{5,4,3,2,1,0:T(8,128)(2,1)S(1)}, u32[]{:S(2)}, u32[]{:S(2)}) collective-permute-start(bf16[3,2,2,2,128,256]{5,4,3,2,1,0:T(8,128)(2,1)} %get-tuple-element.190), channel_id=1, source_target_pairs={{0,2},{1,3},{2,0},{3,1},{4,6},{5,7},{6,4},{7,5},{8,10},{9,11},{10,... | collective-permute-start | bytes 4718600 | tf_op jit(solution)/shard_map/ppermute | solution.py:927
  195.5 36.7 %collective-permute-start.27 = (bf16[3,2,2,2,128,256]{5,4,3,2,1,0:T(8,128)(2,1)}, bf16[3,2,2,2,128,256]{5,4,3,2,1,0:T(8,128)(2,1)}, u32[]{:S(2)}, u32[]{:S(2)}) collective-permute-start(bf16[3,2,2,2,128,256]{5,4,3,2,1,0:T(8,128)(2,1)} %get-tuple-element.191), channel_id=1, source_target_pairs={{0,4},{4,0},{8,12},{12,8},{16,20},{20,16},{24,28},{28,24},{1,5},{5... | collective-permute-start | bytes 4718600 | tf_op jit(solution)/shard_map/ppermute | solution.py:931
  197.0 32.6 %collective-permute-start.28 = (bf16[2,2,2,2,128,256]{5,4,3,2,1,0:T(8,128)(2,1)}, bf16[2,2,2,2,128,256]{5,4,3,2,1,0:T(8,128)(2,1)}, u32[]{:S(2)}, u32[]{:S(2)}) collective-permute-start(bf16[2,2,2,2,128,256]{5,4,3,2,1,0:T(8,128)(2,1)} %get-tuple-element.192), channel_id=1, source_target_pairs={{0,8},{4,12},{8,0},{12,4},{16,24},{20,28},{24,16},{28,20},{1,9},{5... | collective-permute-start | bytes 3145736 | tf_op jit(solution)/shard_map/ppermute | solution.py:931
  236.2 21.5 %collective-permute-start.29 = (bf16[8,2,8,128,128]{4,3,2,1,0:T(8,128)(2,1)}, bf16[8,2,8,128,128]{4,3,2,1,0:T(8,128)(2,1)}, u32[]{:S(2)}, u32[]{:S(2)}) collective-permute-start(bf16[8,2,8,128,128]{4,3,2,1,0:T(8,128)(2,1)} %get-tuple-element.216), channel_id=1, source_target_pairs={{0,1},{1,0},{2,3},{3,2},{4,5},{5,4},{6,7},{7,6},{8,9},{9,8},{10,11... | collective-permute-start | bytes 12582920 | tf_op jit(solution)/shard_map/ppermute | solution.py:923
  236.3 20.2 %collective-permute-start.30 = (bf16[3,2,2,128,256]{4,3,2,1,0:T(8,128)(2,1)}, bf16[3,2,2,128,256]{4,3,2,1,0:T(8,128)(2,1)S(1)}, u32[]{:S(2)}, u32[]{:S(2)}) collective-permute-start(bf16[3,2,2,128,256]{4,3,2,1,0:T(8,128)(2,1)} %get-tuple-element.210), channel_id=1, source_target_pairs={{0,4},{4,0},{8,12},{12,8},{16,20},{20,16},{24,28},{28,24},{1,5},{5... | collective-permute-start | bytes 2359304 | tf_op jit(solution)/shard_map/ppermute | solution.py:931
  237.8 19.8 %collective-permute-start.31 = (bf16[3,2,2,128,256]{4,3,2,1,0:T(8,128)(2,1)}, bf16[3,2,2,128,256]{4,3,2,1,0:T(8,128)(2,1)S(1)}, u32[]{:S(2)}, u32[]{:S(2)}) collective-permute-start(bf16[3,2,2,128,256]{4,3,2,1,0:T(8,128)(2,1)} %get-tuple-element.211), channel_id=1, source_target_pairs={{0,8},{4,12},{8,0},{12,4},{16,24},{20,28},{24,16},{28,20},{1,9},{5... | collective-permute-start | bytes 2359304 | tf_op jit(solution)/shard_map/ppermute | solution.py:931
  263.7 19.9 %collective-permute-start.33 = (bf16[8,2,8,128,128]{4,3,2,1,0:T(8,128)(2,1)}, bf16[8,2,8,128,128]{4,3,2,1,0:T(8,128)(2,1)}, u32[]{:S(2)}, u32[]{:S(2)}) collective-permute-start(bf16[8,2,8,128,128]{4,3,2,1,0:T(8,128)(2,1)} %get-tuple-element.238), channel_id=1, source_target_pairs={{0,1},{1,0},{2,3},{3,2},{4,5},{5,4},{6,7},{7,6},{8,9},{9,8},{10,11... | collective-permute-start | bytes 12582920 | tf_op jit(solution)/shard_map/ppermute | solution.py:923
  264.6 26.5 %collective-permute-start.35 = (bf16[4,2,2,2,128,128]{5,4,3,2,1,0:T(8,128)(2,1)}, bf16[4,2,2,2,128,128]{5,4,3,2,1,0:T(8,128)(2,1)S(1)}, u32[]{:S(2)}, u32[]{:S(2)}) collective-permute-start(bf16[4,2,2,2,128,128]{5,4,3,2,1,0:T(8,128)(2,1)} %get-tuple-element.230), channel_id=1, source_target_pairs={{0,4},{4,0},{8,12},{12,8},{16,20},{20,16},{24,28},{28,24},{1,5},{5... | collective-permute-start | bytes 3145736 | tf_op jit(solution)/shard_map/ppermute | solution.py:931
  265.2 27.0 %collective-permute-start.36 = (bf16[4,2,2,2,128,128]{5,4,3,2,1,0:T(8,128)(2,1)}, bf16[4,2,2,2,128,128]{5,4,3,2,1,0:T(8,128)(2,1)}, u32[]{:S(2)}, u32[]{:S(2)}) collective-permute-start(bf16[4,2,2,2,128,128]{5,4,3,2,1,0:T(8,128)(2,1)} %get-tuple-element.231), channel_id=1, source_target_pairs={{0,2},{1,3},{2,0},{3,1},{4,6},{5,7},{6,4},{7,5},{8,10},{9,11},{10,... | collective-permute-start | bytes 3145736 | tf_op jit(solution)/shard_map/ppermute | solution.py:927
  266.6 27.2 %collective-permute-start.37 = (bf16[3,2,128,256]{3,2,1,0:T(8,128)(2,1)}, bf16[3,2,128,256]{3,2,1,0:T(8,128)(2,1)S(1)}, u32[]{:S(2)}, u32[]{:S(2)}) collective-permute-start(bf16[3,2,128,256]{3,2,1,0:T(8,128)(2,1)} %get-tuple-element.232), channel_id=1, source_target_pairs={{0,8},{4,12},{8,0},{12,4},{16,24},{20,28},{24,16},{28,20},{1,9},{5... | collective-permute-start | bytes 1179656 | tf_op jit(solution)/shard_map/ppermute | solution.py:931
  267.0 32.8 %collective-permute-start.38 = (bf16[3,2,128,256]{3,2,1,0:T(8,128)(2,1)}, bf16[3,2,128,256]{3,2,1,0:T(8,128)(2,1)S(1)}, u32[]{:S(2)}, u32[]{:S(2)}) collective-permute-start(bf16[3,2,128,256]{3,2,1,0:T(8,128)(2,1)} %get-tuple-element.233), channel_id=1, source_target_pairs={{0,2},{1,3},{2,0},{3,1},{4,6},{5,7},{6,4},{7,5},{8,10},{9,11},{10,... | collective-permute-start | bytes 1179656 | tf_op jit(solution)/shard_map/ppermute | solution.py:927
  291.1 51.0 %collective-permute-start.34 = (bf16[4,2,2,2,128,128]{5,4,3,2,1,0:T(8,128)(2,1)}, bf16[4,2,2,2,128,128]{5,4,3,2,1,0:T(8,128)(2,1)}, u32[]{:S(2)}, u32[]{:S(2)}) collective-permute-start(bf16[4,2,2,2,128,128]{5,4,3,2,1,0:T(8,128)(2,1)} %get-tuple-element.241), channel_id=1, source_target_pairs={{0,8},{4,12},{8,0},{12,4},{16,24},{20,28},{24,16},{28,20},{1,9},{5... | collective-permute-start | bytes 3145736 | tf_op jit(solution)/shard_map/ppermute | solution.py:931
  292.3 49.8 %collective-permute-start.40 = (bf16[4,2,2,2,128,128]{5,4,3,2,1,0:T(8,128)(2,1)}, bf16[4,2,2,2,128,128]{5,4,3,2,1,0:T(8,128)(2,1)}, u32[]{:S(2)}, u32[]{:S(2)}) collective-permute-start(bf16[4,2,2,2,128,128]{5,4,3,2,1,0:T(8,128)(2,1)} %get-tuple-element.242), channel_id=1, source_target_pairs={{0,4},{4,0},{8,12},{12,8},{16,20},{20,16},{24,28},{28,24},{1,5},{5... | collective-permute-start | bytes 3145736 | tf_op jit(solution)/shard_map/ppermute | solution.py:931
  305.6 36.5 %collective-permute-start.42 = (bf16[4,2,2,128,128]{4,3,2,1,0:T(8,128)(2,1)}, bf16[4,2,2,128,128]{4,3,2,1,0:T(8,128)(2,1)S(1)}, u32[]{:S(2)}, u32[]{:S(2)}) collective-permute-start(bf16[4,2,2,128,128]{4,3,2,1,0:T(8,128)(2,1)} %get-tuple-element.253), channel_id=1, source_target_pairs={{0,8},{4,12},{8,0},{12,4},{16,24},{20,28},{24,16},{28,20},{1,9},{5... | collective-permute-start | bytes 1572872 | tf_op jit(solution)/shard_map/ppermute | solution.py:931
  306.1 43.9 %collective-permute-start.47 = (bf16[8,128,256]{2,1,0:T(8,128)(2,1)}, bf16[8,128,256]{2,1,0:T(8,128)(2,1)}, u32[]{:S(2)}, u32[]{:S(2)}) collective-permute-start(bf16[8,128,256]{2,1,0:T(8,128)(2,1)} %get-tuple-element.254), channel_id=1, source_target_pairs={{0,16},{4,20},{8,24},{12,28},{16,0},{20,4},{24,8},{28,12},{1,17},{... | collective-permute-start | bytes 1572872 | tf_op jit(solution)/shard_map/ppermute | solution.py:931
  (69 other events, 532.5 us)
Sparse Core Ops, SparseCore 0:
  264.7 60.4 all-gather.2

commit v6 on v5

--- a/solution.py
+++ b/solution.py
@@ -1129,7 +1129,7 @@
     ffn_d = ffn_bwd_call(
         cross_scalars, third_low, second_low, ffn_pieces[1::2], ffn_saved, plan_of((1, 3)), third_scaled, None
     )
-    ffn_sum = Reduction(ffn_d[1], [(0, 3, "yxz"), (3, 6, "xzy"), (6, 8, "zyx")], ffn_finish())
+    ffn_sum = Reduction(ffn_d[1], [(0, 3, "yzx"), (3, 6, "xyz"), (6, 8, "zxy")], ffn_finish())
     ffn_e = ffn_bwd_call(
         cross_scalars, third_low, second_low, ffn_pieces[::2], ffn_saved, plan_of((0, 2)), ffn_d[0],
         (second_hat, second_inv, gains[1]),
@@ -1148,7 +1148,7 @@
     norm_sums = jnp.concatenate([jnp.sum(norm_sums, axis=1), jnp.zeros((2, norm_sums.shape[2]), F32)])
     norm_sums = lax.all_gather(norm_sums, ("dp", "tensor"), axis=0)
     sends = advance([ffn_sum], first_gain)
-    cross_sum = Reduction(after(cross_e[5], *sends), [(0, 4, "xyz"), (4, 8, "yzx")], attention_finish((1, 2)))
+    cross_sum = Reduction(after(cross_e[5], *sends), [(0, 4, "zyx"), (4, 8, "yxz")], attention_finish((1, 2)))
     first_back = after(first_back, *sends)
 
     self_saved = [self_a[:5], self_b[:5]]
@@ -1157,7 +1157,7 @@
     )
     cross_sum.begin(cross_e[6], self_d[0])
     sends = advance([cross_sum, ffn_sum], self_d[0])
-    self_sum = Reduction(after(self_d[1], *sends), [(0, 4, "zxy"), (4, 8, "xyz")], attention_finish((3,)))
+    self_sum = Reduction(after(self_d[1], *sends), [(0, 4, "yxz"), (4, 8, "xzy")], attention_finish((3,)))
     first_back = after(first_back, *sends)
     self_e = attention_bwd_call(
         self_scalars, first_back, [tokens], self_pieces[::2], self_saved, plan_of((0, 2)), None, None
@@ -1170,10 +1170,13 @@
         (memory_part, cross_pieces[1::2] + cross_pieces[::2]),
     )
     sends = advance([cross_sum, ffn_sum], *sends)
-    sends = advance([self_sum, cross_sum], *sends, grad_tokens)
-    sends = advance([self_sum, cross_sum, ffn_sum], *sends)
+    sends = advance([self_sum], *sends, grad_tokens)
+    sends = advance([cross_sum, ffn_sum], *sends)
+    sends = advance([self_sum], *sends)
     norm_total = jnp.sum(after(norm_sums, *sends), axis=0)
-    sends = advance([self_sum, cross_sum], *sends, norm_total)
+    sends = advance([cross_sum], *sends, norm_total)
+    sends = advance([self_sum], *sends)
+    sends = advance([cross_sum], *sends)
     advance([self_sum], *sends)
     self_sum, cross_sum, ffn_sum = self_sum.total, cross_sum.total, ffn_sum.total
 

time: 414 us -> 395 us (0.954)
  waiting for transfers between devices: 98.3 us -> 70.2 us
  Pallas kernels: 227 us -> 233 us
    ppermute x25, waiting for transfers between devices: 76.4 us -> 53.5 us  [over_dp(): return lax.ppermute(values, 'dp', swap_pairs(8, mask))]
    pallas_call x9 -> x12, Pallas kernels: 35.7 us -> 41.1 us  [combine(): pl.pallas_call(kernel, out_shape=list(shapes), in_specs=[ANY] * len(array...]
    ppermute x10, waiting for transfers between devices: 16.7 us -> 11.5 us  [over_y(): return lax.ppermute(values, 'tensor', swap_pairs(4, 2))]
    unnamed x86 -> x84, local copies, waits for them, and re-layouts: 8.53 us -> 8.38 us
  transfers between devices with their start and end apart: 53 -> 53, of which waited for: 24 -> 23; matrix products, arithmetic and copies ran while one was open for 4% -> 4% of each run, Pallas kernels for 43% -> 47%
where the time goes in v6:
time: 395 us; the launch traced here: 392 us
  Pallas kernels  233 us (59%)
  waiting for transfers between devices  70.2 us (18%)
  starting transfers between devices  48.7 us (12%)
  local copies, waits for them, and re-layouts  16.6 us (4%)
  between operations  15.1 us (4%)
  other arithmetic  8.63 us (2%)
    pallas_call x3, Pallas kernels, attention_bwd_call(): pl.pallas_call(kernel, out_shape=shapes, in_specs=[SMEM] + [VMEM] * (len(...  64 us
    ppermute x25, waiting for transfers between devices, over_dp(): return lax.ppermute(values, 'dp', swap_pairs(8, mask))  53.5 us
    pallas_call x4, Pallas kernels, attention_fwd_call(): pl.pallas_call(kernel, out_shape=shapes, in_specs=[SMEM] + [VMEM] * (len(...  51.5 us
    pallas_call x12, Pallas kernels, combine(): pl.pallas_call(kernel, out_shape=list(shapes), in_specs=[ANY] * len(array...  41.1 us
    pallas_call x2, Pallas kernels, ffn_bwd_call(): pl.pallas_call(kernel, out_shape=shapes, in_specs=specs + [ANY] * len(tai...  33.8 us
    ppermute x25, starting transfers between devices, over_dp(): return lax.ppermute(values, 'dp', swap_pairs(8, mask))  31.6 us
    pallas_call x2, Pallas kernels, ffn_fwd_call(): pl.pallas_call(kernel, out_shape=shapes, in_specs=specs + [ANY] * len(tai...  27.1 us
    pallas_call x1, Pallas kernels, inputs_back_call(): pl.pallas_call(kernel, out_shape=[sds((rows, depth), F32)] * 2, in_specs=...  15.1 us
  transfers between devices with their start and end apart: 53, of which 23 were waited for; matrix products, arithmetic and copies ran while one was open for 4% of the time, Pallas kernels for 47%

profile of v6, /device:TPU:0, one launch (start us, length us, event | category | flops | bytes accessed | tf_op | source)
XLA Modules:
  0.0 391.8 jit_solution(4769929036066823924)
XLA Ops:
  15.7 11.0 %self_fwd.2 = (bf16[4,512,128]{2,1,0:T(8,128)(2,1)}, bf16[4,512,128]{2,1,0:T(8,128)(2,1)}, bf16[4,512,128]{2,1,0:T(8,128)(2,1)}, bf16[4,512,128]{2,1,0:T(8,128)(...) custom-call(s32[4]{0:T(128)} %add_add_fusion.1.refs_0_, bf16[512,1024]{1,0:T(8,128)(2,1)} %refs_2_.11, ...), custom_call_target="tpu_custom_call" | custom-call | flops 2640000000 | bytes 4194304 | tf_op jit(solution)/shard_map/self_fwd/pallas_call | solution.py:349
  30.2 10.3 %collective-permute-done.8 = bf16[4,256,256]{2,1,0:T(8,128)(2,1)S(1)} collective-permute-done((bf16[4,256,256]{2,1,0:T(8,128)(2,1)}, bf16[4,256,256]{2,1,0:T(8,128)(2,1)S(1)}, u32[]{:S(2)}, u32[]{:S(2)}) %collective-permute-start.8) | collective-permute-done | bytes 524320 | tf_op jit(solution)/shard_map/ppermute | solution.py:931
  42.2 5.6 %collective-permute-done.6 = bf16[4,512,256]{2,1,0:T(8,128)(2,1)} collective-permute-done((bf16[4,512,256]{2,1,0:T(8,128)(2,1)S(1)}, bf16[4,512,256]{2,1,0:T(8,128)(2,1)}, u32[]{:S(2)}, u32[]{:S(2)}) %collective-permute-start.6) | collective-permute-done | bytes 1048608 | tf_op jit(solution)/shard_map/ppermute | solution.py:927
  47.8 5.6 %collective-permute-done.9 = bf16[4,256,256]{2,1,0:T(8,128)(2,1)S(1)} collective-permute-done((bf16[4,256,256]{2,1,0:T(8,128)(2,1)S(1)}, bf16[4,256,256]{2,1,0:T(8,128)(2,1)S(1)}, u32[]{:S(2)}, u32[]{:S(2)}) %collective-permute-start.9) | collective-permute-done | bytes 524320 | tf_op jit(solution)/shard_map/ppermute | solution.py:931
  65.2 13.9 %self_fwd.3 = (bf16[4,512,128]{2,1,0:T(8,128)(2,1)}, bf16[4,512,128]{2,1,0:T(8,128)(2,1)}, bf16[4,512,128]{2,1,0:T(8,128)(2,1)}, bf16[4,512,128]{2,1,0:T(8,128)(...) custom-call(s32[4]{0:T(128)} %add_add_fusion.1.refs_0_, ...), custom_call_target="tpu_custom_call" | custom-call | flops 2640000000 | bytes 4194304 | tf_op jit(solution)/shard_map/self_fwd/pallas_call | solution.py:349
  91.4 11.8 %cross_fwd.2 = (bf16[4,512,128]{2,1,0:T(8,128)(2,1)}, bf16[4,512,128]{2,1,0:T(8,128)(2,1)}, bf16[4,512,128]{2,1,0:T(8,128)(2,1)}, bf16[4,512,128]{2,1,0:T(8,128)...) custom-call(s32[4]{0:T(128)} %add_add_fusion.refs_0_, bf16[512,1024]{1,0:T(8,128)(2,1)} %get-tuple-element.156.refs_1_.refs_2_, ...), custom_call_target="tpu_custom_call" | custom-call | flops 2640000000 | bytes 4194304 | tf_op jit(solution)/shard_map/cross_fwd/pallas_call | solution.py:349
  103.3 14.8 %cross_fwd.3 = (bf16[4,512,128]{2,1,0:T(8,128)(2,1)}, bf16[4,512,128]{2,1,0:T(8,128)(2,1)}, bf16[4,512,128]{2,1,0:T(8,128)(2,1)}, bf16[4,512,128]{2,1,0:T(8,128)...) custom-call(s32[4]{0:T(128)} %add_add_fusion.refs_0_, ...), custom_call_target="tpu_custom_call" | custom-call | flops 2640000000 | bytes 4194304 | tf_op jit(solution)/shard_map/cross_fwd/pallas_call | solution.py:349
  122.1 11.6 %ffn_fwd.2 = (f32[512,1024]{1,0:T(8,128)}, bf16[4,512,512]{2,1,0:T(8,128)(2,1)}, bf16[4,512,512]{2,1,0:T(8,128)(2,1)}) custom-call(s32[4]{0:T(128)} %add_add_fusion.refs_0_, bf16[512,1024]{1,0:T(8,128)(2,1)} %get-tuple-element.164.refs_1_.refs_2_, bf16[1024,1024]{1,0:T(8,128)(2,1)} %refs_7_.3, bf16[1024,1024]{1,0:T(8,128)(2,1)} %refs_8_.2, ...), custom_call_target="tpu_custom_call" | custom-call | flops 13200000000 | bytes 4194304 | tf_op jit(solution)/shard_map/ffn_fwd/pallas_call | solution.py:709
  139.3 15.5 %ffn_fwd.3 = (bf16[512,1024]{1,0:T(8,128)(2,1)}, bf16[512,1024]{1,0:T(8,128)(2,1)}, f32[512,1024]{1,0:T(8,128)}, f32[8,1024]{1,0:T(8,128)}, f32[8,1024]{1,0:T(8,...) custom-call(s32[4]{0:T(128)} %add_add_fusion.refs_0_, ...), custom_call_target="tpu_custom_call" | custom-call | flops 13200000000 | bytes 4194304 | tf_op jit(solution)/shard_map/ffn_fwd/pallas_call | solution.py:709
  154.7 16.3 %ffn_bwd.2 = (f32[512,1024]{1,0:T(8,128)}, bf16[8,2,8,128,256]{4,3,2,1,0:T(8,128)(2,1)}) custom-call(s32[4]{0:T(128)} %add_add_fusion.refs_0_, bf16[512,1024]{1,0:T(8,128)(2,1)} %get-tuple-element.175.refs_1_, bf16[512,1024]{1,0:T(8,128)(2,1)} %get-tuple-element.164.refs_1_.refs_2_, f32[512,1024]{1,0:T(8,128)} %get-tuple-element.177.refs_3_, ...), custom_call_target="tpu_custom_call" | custom-call | flops 18699999232 | bytes 4194304 | tf_op jit(solution)/shard_map/ffn_bwd/pallas_call | solution.py:822
  171.3 17.5 %ffn_bwd.3 = (bf16[512,1024]{1,0:T(8,128)(2,1)}, f32[512,1024]{1,0:T(8,128)}, f32[8,1024]{1,0:T(8,128)}, f32[8,1024]{1,0:T(8,128)}, bf16[8,2,8,128,256]{4,3,2,1,0:T(8,128)(2,1)}) custom-call(s32[4]{0:T(128)} %add_add_fusion.refs_0_, bf16[512,1024]{1,0:T(8,128)(2,1)} %get-tuple-element.175.refs_1_, bf16[512,1024]{1,0:T(8,128)(2,1)} %get-tuple-element.164.refs_1_.refs_2_, ...), custom_call_target="tpu_custom_call" | custom-call | flops 18699999232 | bytes 4194304 | tf_op jit(solution)/shard_map/ffn_bwd/pallas_call | solution.py:822
  188.8 5.2 %combine.12 = (bf16[3,2,2,2,128,256]{5,4,3,2,1,0:T(8,128)(2,1)}, bf16[3,2,2,2,128,256]{5,4,3,2,1,0:T(8,128)(2,1)}, bf16[2,2,2,2,128,256]{5,4,3,2,1,0:T(8,128)(2,1)}) custom-call(bf16[8,2,2,2,2,128,256]{6,5,4,3,2,1,0:T(8,128)(2,1)} %bitcast.42, bf16[8,2,2,2,2,128,256]{6,5,4,3,2,1,0:T(8,128)(2,1)} %bitcast.20.refs_1_.refs_3_.refs_5_.refs_7_), custom_call_target="tpu_custom_call" | custom-call | flops 3300000000 | bytes 4194304 | tf_op jit(solution)/shard_map/combine/pallas_call | solution.py:906
  197.6 32.2 %cross_bwd.1 = (bf16[512,1024]{1,0:T(8,128)(2,1)}, f32[512,1024]{1,0:T(8,128)}, f32[8,1024]{1,0:T(8,128)}, f32[8,1024]{1,0:T(8,128)}, bf16[512,2048]{1,0:T(8,128...) custom-call(s32[4]{0:T(128)} %add_add_fusion.refs_0_, ...), custom_call_target="tpu_custom_call" | custom-call | flops 36960002048 | bytes 4194304 | tf_op jit(solution)/shard_map/cross_bwd/pallas_call | solution.py:487
  232.3 4.0 %combine.13 = (bf16[3,2,2,128,256]{4,3,2,1,0:T(8,128)(2,1)}, bf16[3,2,2,128,256]{4,3,2,1,0:T(8,128)(2,1)}, bf16[2,2,2,128,256]{4,3,2,1,0:T(8,128)(2,1)}) custom-call(bf16[8,2,2,2,2,128,256]{6,5,4,3,2,1,0:T(8,128)(2,1)} %bitcast.43, bf16[8,2,2,2,2,128,256]{6,5,4,3,2,1,0:T(8,128)(2,1)} %bitcast.20.refs_1_.refs_3_.refs_5_.refs_7_, ...), custom_call_target="tpu_custom_call" | custom-call | flops 3300000000 | bytes 4194304 | tf_op jit(solution)/shard_map/combine/pallas_call | solution.py:906
  239.8 16.0 %self_bwd.2 = (bf16[512,1536]{1,0:T(8,128)(2,1)}, bf16[8,2,8,128,128]{4,3,2,1,0:T(8,128)(2,1)}) custom-call(s32[4]{0:T(128)} %add_add_fusion.1.refs_0_, bf16[512,1024]{1,0:T(8,128)(2,1)} %get-tuple-element.233.refs_1_, bf16[512,1024]{1,0:T(8,128)(2,1)} %refs_2_.11, bf16[3,1024,256]{2,1,0:T(8,128)(2,1)} %collective-permute-done.1.refs_4_.refs_3_.refs_5_, ...), custom_call_target="tpu_custom_call" | custom-call | flops 18480001024 | bytes 4194304 | tf_op jit(solution)/shard_map/self_bwd/pallas_call | solution.py:487
  257.8 5.1 %combine.14 = (bf16[4,2,2,2,128,128]{5,4,3,2,1,0:T(8,128)(2,1)}, bf16[4,2,2,2,128,128]{5,4,3,2,1,0:T(8,128)(2,1)}, bf16[3,2,128,256]{3,2,1,0:T(8,128)(2,1)}, bf1...) custom-call(bf16[8,2,2,2,2,128,128]{6,5,4,3,2,1,0:T(8,128)(2,1)} %bitcast.47, ...), custom_call_target="tpu_custom_call" | custom-call | flops 3300000000 | bytes 4194304 | tf_op jit(solution)/shard_map/combine/pallas_call | solution.py:906
  268.7 15.9 %self_bwd.3 = (bf16[512,1536]{1,0:T(8,128)(2,1)}, bf16[8,2,8,128,128]{4,3,2,1,0:T(8,128)(2,1)}) custom-call(s32[4]{0:T(128)} %add_add_fusion.1.refs_0_, bf16[512,1024]{1,0:T(8,128)(2,1)} %get-tuple-element.233.refs_1_, bf16[512,1024]{1,0:T(8,128)(2,1)} %refs_2_.11, bf16[3,1024,256]{2,1,0:T(8,128)(2,1)} %refs_8_.3, bf16[256,1024]{1,0:T(8,128)(2,1)} %refs_9_.1, ...), custom_call_target="tpu_custom_call" | custom-call | flops 18480001024 | bytes 4194304 | tf_op jit(solution)/shard_map/self_bwd/pallas_call | solution.py:487
  285.4 4.1 %combine.15 = (bf16[4,2,2,2,128,128]{5,4,3,2,1,0:T(8,128)(2,1)}, bf16[4,2,2,2,128,128]{5,4,3,2,1,0:T(8,128)(2,1)}) custom-call(bf16[8,2,2,2,2,128,128]{6,5,4,3,2,1,0:T(8,128)(2,1)} %bitcast.52, bf16[8,2,2,2,2,128,128]{6,5,4,3,2,1,0:T(8,128)(2,1)} %bitcast.24.refs_1_), custom_call_target="tpu_custom_call" | custom-call | flops 3300000000 | bytes 4194304 | tf_op jit(solution)/shard_map/combine/pallas_call | solution.py:906
  293.5 6.3 %collective-permute-done.38.refs_11_.refs_14_ = bf16[3,2,128,256]{3,2,1,0:T(8,128)(2,1)S(1)} collective-permute-done((bf16[3,2,128,256]{3,2,1,0:T(8,128)(2,1)}, bf16[3,2,128,256]{3,2,1,0:T(8,128)(2,1)S(1)}, u32[]{:S(2)}, u32[]{:S(2)}) %collective-permute-start.38) | collective-permute-done | bytes 393248 | tf_op jit(solution)/shard_map/ppermute | solution.py:931
  300.6 3.6 combine.16
  310.0 15.1 %inputs_back.1 = (f32[512,1024]{1,0:T(8,128)}, f32[512,1024]{1,0:T(8,128)}) custom-call(s32[4]{0:T(128)} %add_add_fusion.1.refs_0_, f32[512,1024]{1,0:T(8,128)} %get-tuple-element.241.refs_1_, bf16[512,1536]{1,0:T(8,128)(2,1)} %get-tuple-element.223.refs_2_, bf16[512,1536]{1,0:T(8,128)(2,1)} %get-tuple-element.237.refs_3_, ...), custom_call_target="tpu_custom_call" | custom-call | flops 13200000000 | bytes 4194304 | tf_op jit(solution)/shard_map/inputs_back/pallas_call | solution.py:527
  335.1 3.8 combine.18
  341.5 4.9 %collective-permute-done.45.refs_5_.refs_6_.refs_7_ = bf16[4,2,2,128,128]{4,3,2,1,0:T(8,128)(2,1)} collective-permute-done((bf16[4,2,2,128,128]{4,3,2,1,0:T(8,128)(2,1)}, bf16[4,2,2,128,128]{4,3,2,1,0:T(8,128)(2,1)}, u32[]{:S(2)}, u32[]{:S(2)}) %collective-permute-start.45) | collective-permute-done | bytes 524320 | tf_op jit(solution)/shard_map/ppermute | solution.py:931
  363.7 12.8 %collective-permute-done.51.refs_5_ = bf16[8,128,128]{2,1,0:T(8,128)(2,1)S(1)} collective-permute-done((bf16[8,128,128]{2,1,0:T(8,128)(2,1)}, bf16[8,128,128]{2,1,0:T(8,128)(2,1)S(1)}, u32[]{:S(2)}, u32[]{:S(2)}) %collective-permute-start.51) | collective-permute-done | bytes 262176 | tf_op jit(solution)/shard_map/ppermute | solution.py:931
  (216 shorter events, 113.8 us)
Async XLA Ops:
  7.2 342.9 %all-gather.3.cloned.1.call-start = ((), (), s32[]{:S(2)}) async-start(), calls=%async_computation | async-start | bytes 1081344 | tf_op jit(solution)/shard_map/all_gather | solution.py:1149
  13.6 34.1 %collective-permute-start.6 = (bf16[4,512,256]{2,1,0:T(8,128)(2,1)S(1)}, bf16[4,512,256]{2,1,0:T(8,128)(2,1)}, u32[]{:S(2)}, u32[]{:S(2)}) collective-permute-start(bf16[4,512,256]{2,1,0:T(8,128)(2,1)S(1)} %pad_maximum_fusion.2), channel_id=1, source_target_pairs={{0,2},{1,3},{2,0},{3,1},{4,6},{5,7},{6,4},{7,5},{8,10},{9,11},{10,... | collective-permute-start | bytes 3145736 | tf_op jit(solution)/shard_map/ppermute | solution.py:927
  55.5 25.8 %collective-permute-start.12 = (bf16[4,512,256]{2,1,0:T(8,128)(2,1)}, bf16[4,512,256]{2,1,0:T(8,128)(2,1)}, u32[]{:S(2)}, u32[]{:S(2)}) collective-permute-start(bf16[4,512,256]{2,1,0:T(8,128)(2,1)} %collective-permute-done.6), channel_id=1, source_target_pairs={{0,8},{4,12},{8,0},{12,4},{16,24},{20,28},{24,16},{28,20},{1,9},{5... | collective-permute-start | bytes 3145736 | tf_op jit(solution)/shard_map/ppermute | solution.py:931
  61.4 25.3 %collective-permute-start.11 = (bf16[2,256,1024]{2,1,0:T(8,128)(2,1)S(1)}, bf16[2,256,1024]{2,1,0:T(8,128)(2,1)}, u32[]{:S(2)}, u32[]{:S(2)}) collective-permute-start(bf16[2,256,1024]{2,1,0:T(8,128)(2,1)S(1)} %pad_maximum_fusion.3), channel_id=1, source_target_pairs={{0,2},{1,3},{2,0},{3,1},{4,6},{5,7},{6,4},{7,5},{8,10},{9,11},{10,... | collective-permute-start | bytes 3145736 | tf_op jit(solution)/shard_map/ppermute | solution.py:927
  86.7 34.3 %collective-permute-start.14 = (bf16[1024,1024]{1,0:T(8,128)(2,1)}, bf16[1024,1024]{1,0:T(8,128)(2,1)}, u32[]{:S(2)}, u32[]{:S(2)}) collective-permute-start(bf16[1024,1024]{1,0:T(8,128)(2,1)} %refs_7_.3), channel_id=1, source_target_pairs={{0,1},{1,0},{2,3},{3,2},{4,5},{5,4},{6,7},{7,6},{8,9},{9,8},{10,11... | collective-permute-start | bytes 6291464 | tf_op jit(solution)/shard_map/ppermute | solution.py:923
  86.7 34.9 %collective-permute-start.15 = (bf16[1024,1024]{1,0:T(8,128)(2,1)}, bf16[1024,1024]{1,0:T(8,128)(2,1)}, u32[]{:S(2)}, u32[]{:S(2)}) collective-permute-start(bf16[1024,1024]{1,0:T(8,128)(2,1)} %refs_8_.2), channel_id=1, source_target_pairs={{0,1},{1,0},{2,3},{3,2},{4,5},{5,4},{6,7},{7,6},{8,9},{9,8},{10,11... | collective-permute-start | bytes 6291464 | tf_op jit(solution)/shard_map/ppermute | solution.py:923
  87.2 30.9 %collective-permute-start.16 = (bf16[2,256,1024]{2,1,0:T(8,128)(2,1)}, bf16[2,256,1024]{2,1,0:T(8,128)(2,1)}, u32[]{:S(2)}, u32[]{:S(2)}) collective-permute-start(bf16[2,256,1024]{2,1,0:T(8,128)(2,1)} %collective-permute-done.11.refs_9_), channel_id=1, source_target_pairs={{0,4},{4,0},{8,12},{12,8},{16,20},{20,16},{24,28},{28,24},{1,5},{5... | collective-permute-start | bytes 3145736 | tf_op jit(solution)/shard_map/ppermute | solution.py:931
  88.5 31.3 %collective-permute-start.17 = (bf16[2,256,1024]{2,1,0:T(8,128)(2,1)}, bf16[2,256,1024]{2,1,0:T(8,128)(2,1)}, u32[]{:S(2)}, u32[]{:S(2)}) collective-permute-start(bf16[2,256,1024]{2,1,0:T(8,128)(2,1)} %collective-permute-done.11.refs_9_), channel_id=1, source_target_pairs={{0,8},{4,12},{8,0},{12,4},{16,24},{20,28},{24,16},{28,20},{1,9},{5... | collective-permute-start | bytes 3145736 | tf_op jit(solution)/shard_map/ppermute | solution.py:931
  103.2 32.9 %collective-permute-start.20 = (bf16[2,256,1024]{2,1,0:T(8,128)(2,1)}, bf16[2,256,1024]{2,1,0:T(8,128)(2,1)}, u32[]{:S(2)}, u32[]{:S(2)}) collective-permute-start(bf16[2,256,1024]{2,1,0:T(8,128)(2,1)} %collective-permute-done.11.refs_9_), channel_id=1, source_target_pairs={{0,1},{1,0},{2,3},{3,2},{4,5},{5,4},{6,7},{7,6},{8,9},{9,8},{10,11... | collective-permute-start | bytes 3145736 | tf_op jit(solution)/shard_map/ppermute | solution.py:923
  194.0 36.9 %collective-permute-start.26 = (bf16[3,2,2,2,128,256]{5,4,3,2,1,0:T(8,128)(2,1)}, bf16[3,2,2,2,128,256]{5,4,3,2,1,0:T(8,128)(2,1)S(1)}, u32[]{:S(2)}, u32[]{:S(2)}) collective-permute-start(bf16[3,2,2,2,128,256]{5,4,3,2,1,0:T(8,128)(2,1)} %get-tuple-element.188), channel_id=1, source_target_pairs={{0,2},{1,3},{2,0},{3,1},{4,6},{5,7},{6,4},{7,5},{8,10},{9,11},{10,... | collective-permute-start | bytes 4718600 | tf_op jit(solution)/shard_map/ppermute | solution.py:927
  195.6 36.7 %collective-permute-start.27 = (bf16[3,2,2,2,128,256]{5,4,3,2,1,0:T(8,128)(2,1)}, bf16[3,2,2,2,128,256]{5,4,3,2,1,0:T(8,128)(2,1)}, u32[]{:S(2)}, u32[]{:S(2)}) collective-permute-start(bf16[3,2,2,2,128,256]{5,4,3,2,1,0:T(8,128)(2,1)} %get-tuple-element.189), channel_id=1, source_target_pairs={{0,4},{4,0},{8,12},{12,8},{16,20},{20,16},{24,28},{28,24},{1,5},{5... | collective-permute-start | bytes 4718600 | tf_op jit(solution)/shard_map/ppermute | solution.py:931
  197.1 32.6 %collective-permute-start.28 = (bf16[2,2,2,2,128,256]{5,4,3,2,1,0:T(8,128)(2,1)}, bf16[2,2,2,2,128,256]{5,4,3,2,1,0:T(8,128)(2,1)}, u32[]{:S(2)}, u32[]{:S(2)}) collective-permute-start(bf16[2,2,2,2,128,256]{5,4,3,2,1,0:T(8,128)(2,1)} %get-tuple-element.190), channel_id=1, source_target_pairs={{0,8},{4,12},{8,0},{12,4},{16,24},{20,28},{24,16},{28,20},{1,9},{5... | collective-permute-start | bytes 3145736 | tf_op jit(solution)/shard_map/ppermute | solution.py:931
  236.3 20.4 %collective-permute-start.29 = (bf16[8,2,8,128,128]{4,3,2,1,0:T(8,128)(2,1)}, bf16[8,2,8,128,128]{4,3,2,1,0:T(8,128)(2,1)}, u32[]{:S(2)}, u32[]{:S(2)}) collective-permute-start(bf16[8,2,8,128,128]{4,3,2,1,0:T(8,128)(2,1)} %get-tuple-element.214), channel_id=1, source_target_pairs={{0,1},{1,0},{2,3},{3,2},{4,5},{5,4},{6,7},{7,6},{8,9},{9,8},{10,11... | collective-permute-start | bytes 12582920 | tf_op jit(solution)/shard_map/ppermute | solution.py:923
  262.9 21.7 %collective-permute-start.33 = (bf16[8,2,8,128,128]{4,3,2,1,0:T(8,128)(2,1)}, bf16[8,2,8,128,128]{4,3,2,1,0:T(8,128)(2,1)}, u32[]{:S(2)}, u32[]{:S(2)}) collective-permute-start(bf16[8,2,8,128,128]{4,3,2,1,0:T(8,128)(2,1)} %get-tuple-element.236), channel_id=1, source_target_pairs={{0,1},{1,0},{2,3},{3,2},{4,5},{5,4},{6,7},{7,6},{8,9},{9,8},{10,11... | collective-permute-start | bytes 12582920 | tf_op jit(solution)/shard_map/ppermute | solution.py:923
  263.8 26.9 %collective-permute-start.35 = (bf16[4,2,2,2,128,128]{5,4,3,2,1,0:T(8,128)(2,1)}, bf16[4,2,2,2,128,128]{5,4,3,2,1,0:T(8,128)(2,1)S(1)}, u32[]{:S(2)}, u32[]{:S(2)}) collective-permute-start(bf16[4,2,2,2,128,128]{5,4,3,2,1,0:T(8,128)(2,1)} %get-tuple-element.228), channel_id=1, source_target_pairs={{0,8},{4,12},{8,0},{12,4},{16,24},{20,28},{24,16},{28,20},{1,9},{5... | collective-permute-start | bytes 3145736 | tf_op jit(solution)/shard_map/ppermute | solution.py:931
  265.3 26.7 %collective-permute-start.36 = (bf16[4,2,2,2,128,128]{5,4,3,2,1,0:T(8,128)(2,1)}, bf16[4,2,2,2,128,128]{5,4,3,2,1,0:T(8,128)(2,1)}, u32[]{:S(2)}, u32[]{:S(2)}) collective-permute-start(bf16[4,2,2,2,128,128]{5,4,3,2,1,0:T(8,128)(2,1)} %get-tuple-element.229), channel_id=1, source_target_pairs={{0,2},{1,3},{2,0},{3,1},{4,6},{5,7},{6,4},{7,5},{8,10},{9,11},{10,... | collective-permute-start | bytes 3145736 | tf_op jit(solution)/shard_map/ppermute | solution.py:927
  266.7 26.9 %collective-permute-start.37 = (bf16[3,2,128,256]{3,2,1,0:T(8,128)(2,1)}, bf16[3,2,128,256]{3,2,1,0:T(8,128)(2,1)S(1)}, u32[]{:S(2)}, u32[]{:S(2)}) collective-permute-start(bf16[3,2,128,256]{3,2,1,0:T(8,128)(2,1)} %get-tuple-element.230), channel_id=1, source_target_pairs={{0,4},{4,0},{8,12},{12,8},{16,20},{20,16},{24,28},{28,24},{1,5},{5... | collective-permute-start | bytes 1179656 | tf_op jit(solution)/shard_map/ppermute | solution.py:931
  268.2 31.7 %collective-permute-start.38 = (bf16[3,2,128,256]{3,2,1,0:T(8,128)(2,1)}, bf16[3,2,128,256]{3,2,1,0:T(8,128)(2,1)S(1)}, u32[]{:S(2)}, u32[]{:S(2)}) collective-permute-start(bf16[3,2,128,256]{3,2,1,0:T(8,128)(2,1)} %get-tuple-element.231), channel_id=1, source_target_pairs={{0,8},{4,12},{8,0},{12,4},{16,24},{20,28},{24,16},{28,20},{1,9},{5... | collective-permute-start | bytes 1179656 | tf_op jit(solution)/shard_map/ppermute | solution.py:931
  290.7 34.5 %collective-permute-start.34 = (bf16[4,2,2,2,128,128]{5,4,3,2,1,0:T(8,128)(2,1)}, bf16[4,2,2,2,128,128]{5,4,3,2,1,0:T(8,128)(2,1)}, u32[]{:S(2)}, u32[]{:S(2)}) collective-permute-start(bf16[4,2,2,2,128,128]{5,4,3,2,1,0:T(8,128)(2,1)} %get-tuple-element.239), channel_id=1, source_target_pairs={{0,2},{1,3},{2,0},{3,1},{4,6},{5,7},{6,4},{7,5},{8,10},{9,11},{10,... | collective-permute-start | bytes 3145736 | tf_op jit(solution)/shard_map/ppermute | solution.py:927
  292.0 33.1 %collective-permute-start.40 = (bf16[4,2,2,2,128,128]{5,4,3,2,1,0:T(8,128)(2,1)}, bf16[4,2,2,2,128,128]{5,4,3,2,1,0:T(8,128)(2,1)}, u32[]{:S(2)}, u32[]{:S(2)}) collective-permute-start(bf16[4,2,2,2,128,128]{5,4,3,2,1,0:T(8,128)(2,1)} %get-tuple-element.240), channel_id=1, source_target_pairs={{0,4},{4,0},{8,12},{12,8},{16,20},{20,16},{24,28},{28,24},{1,5},{5... | collective-permute-start | bytes 3145736 | tf_op jit(solution)/shard_map/ppermute | solution.py:931
  304.2 28.4 %collective-permute-start.42 = (bf16[4,2,2,128,128]{4,3,2,1,0:T(8,128)(2,1)}, bf16[4,2,2,128,128]{4,3,2,1,0:T(8,128)(2,1)S(1)}, u32[]{:S(2)}, u32[]{:S(2)}) collective-permute-start(bf16[4,2,2,128,128]{4,3,2,1,0:T(8,128)(2,1)} %get-tuple-element.250), channel_id=1, source_target_pairs={{0,2},{1,3},{2,0},{3,1},{4,6},{5,7},{6,4},{7,5},{8,10},{9,11},{10,... | collective-permute-start | bytes 1572872 | tf_op jit(solution)/shard_map/ppermute | solution.py:927
  305.8 26.9 %collective-permute-start.43 = (bf16[4,2,2,128,128]{4,3,2,1,0:T(8,128)(2,1)}, bf16[4,2,2,128,128]{4,3,2,1,0:T(8,128)(2,1)S(1)}, u32[]{:S(2)}, u32[]{:S(2)}) collective-permute-start(bf16[4,2,2,128,128]{4,3,2,1,0:T(8,128)(2,1)} %get-tuple-element.251), channel_id=1, source_target_pairs={{0,4},{4,0},{8,12},{12,8},{16,20},{20,16},{24,28},{28,24},{1,5},{5... | collective-permute-start | bytes 1572872 | tf_op jit(solution)/shard_map/ppermute | solution.py:931
  307.3 27.8 %collective-permute-start.44 = (bf16[8,128,256]{2,1,0:T(8,128)(2,1)}, bf16[8,128,256]{2,1,0:T(8,128)(2,1)}, u32[]{:S(2)}, u32[]{:S(2)}) collective-permute-start(bf16[8,128,256]{2,1,0:T(8,128)(2,1)} %get-tuple-element.252), channel_id=1, source_target_pairs={{0,16},{4,20},{8,24},{12,28},{16,0},{20,4},{24,8},{28,12},{1,17},{... | collective-permute-start | bytes 1572872 | tf_op jit(solution)/shard_map/ppermute | solution.py:931
  355.0 21.5 %collective-permute-start.51 = (bf16[8,128,128]{2,1,0:T(8,128)(2,1)}, bf16[8,128,128]{2,1,0:T(8,128)(2,1)S(1)}, u32[]{:S(2)}, u32[]{:S(2)}) collective-permute-start(bf16[8,128,128]{2,1,0:T(8,128)(2,1)} %combine.20), channel_id=1, source_target_pairs={{0,16},{4,20},{8,24},{12,28},{16,0},{20,4},{24,8},{28,12},{1,17},{... | collective-permute-start | bytes 786440 | tf_op jit(solution)/shard_map/ppermute | solution.py:931
  (68 other events, 518.7 us)
Sparse Core Ops, SparseCore 0:
  263.9 63.1 all-gather.2

commit v7 on v6

--- a/solution.py
+++ b/solution.py
@@ -180,12 +180,16 @@
     return jnp.sum(values.reshape(values.shape[0] // 8, 8, values.shape[1]), axis=0)
 
 
-def each_chunk(rows, body):
+def each_chunk(rows, body, results):
     def step(index, carry):
-        body(pl.ds(pl.multiple_of(index * ROW_CHUNK, ROW_CHUNK), ROW_CHUNK))
+        at = pl.ds(pl.multiple_of(index * ROW_CHUNK, ROW_CHUNK), ROW_CHUNK)
+        body(at)
+        for buffer, out, sem in results:
+            copy_of(buffer.at[at, :], out.at[at, :], sem).start()
         return carry
 
     lax.fori_loop(0, rows // ROW_CHUNK, step, 0)
+    return [copy_of(*result) for result in results]
 
 
 def store_shards(target, weight, dp):
@@ -215,7 +219,7 @@
     wide = 2 * UNIT
     for index, refs in enumerate(pieces):
         at = slice(index * wide, (index + 1) * wide)
-        if len(refs) > 1:
+        if len(refs[-1].shape) == 2:
             column = 0
             for ref in refs[:-1]:
                 for source in [ref] if len(ref.shape) == 2 else [ref.at[c] for c in range(ref.shape[0])]:
@@ -226,16 +230,16 @@
             if obuf is not None:
                 outs.append(copy_of(refs[-1], obuf.at[at, :], osem.at[index, 0]))
             continue
-        rest, = refs
-        rows = rest.shape[2]
-        part = wide // rest.shape[0]
-        for quarter in range(rest.shape[0]):
-            place = quarter ^ (sc[1] if rest.shape[0] == 4 else sc[3])
+        parts = [refs[0].at[n] for n in range(refs[0].shape[0])] if len(refs[0].shape) == 4 else refs
+        rows = parts[0].shape[1]
+        part = wide // len(parts)
+        for quarter, ref in enumerate(parts):
+            place = quarter ^ (sc[1] if len(parts) == 4 else sc[3])
             for column in columns:
                 low = (columns.index(column) * len(pieces) + index) * wide
                 groups[column].append(
                     copy_of(
-                        rest.at[quarter, column],
+                        ref.at[column],
                         wbuf.at[pl.ds(pl.multiple_of(place * rows, rows), rows), low : low + wide],
                         wsem.at[column, index, quarter],
                     )
@@ -243,7 +247,7 @@
             for block in range(4 if obuf is not None else 0):
                 outs.append(
                     copy_of(
-                        rest.at[quarter, 3, block * part : (block + 1) * part, :],
+                        ref.at[3, block * part : (block + 1) * part, :],
                         obuf.at[pl.ds(pl.multiple_of(index * wide + place * part, part), part), block * wide : (block + 1) * wide],
                         osem.at[index, 4 * quarter + block],
                     )
@@ -266,15 +270,16 @@
         res_in = next(it) if last else None
         part_in = next(it) if has_partial else None
         w_refs = [[next(it) for _ in piece] for piece in pieces]
-        q_ref, k_ref, v_ref, att_ref, lse_ref = (next(it) for _ in range(5))
-        if last:
-            low_ref, hat_ref, inv_ref = next(it), next(it), next(it)
+        unit_outs, lse_ref = [next(it) for _ in range(4)], next(it)
+        if last:
+            norm_outs = [next(it) for _ in range(3)]
         else:
             sum_ref = next(it)
-        wbuf, obuf, att_all, diagonal, wsem, osem, lsem = (next(it) for _ in range(7))
-        if last:
-            acc, old = next(it), next(it)
-        length = sc[0]
+        wbuf, obuf, att_all, diagonal, wsem, osem, lsem, usem = (next(it) for _ in range(8))
+        q_ref, k_ref, v_ref, att_ref = (next(it) for _ in range(4))
+        if last:
+            acc, old, low_ref, hat_ref, inv_ref = (next(it) for _ in range(5))
+        length = sc[0] if causal else sc[4]
         groups, outs = weight_copies(w_refs, sc, wbuf, obuf, wsem, osem)
         for copies in groups + [outs]:
             for copy in copies:
@@ -299,6 +304,10 @@
             for index in range(number):
                 result[index] = proj[:, index * UNIT : (index + 1) * UNIT]
 
+        flushes = [copy_of(*pair, usem.at[index]) for index, pair in enumerate(zip((q_ref, k_ref, v_ref, att_ref), unit_outs))]
+        for copy in flushes[:3]:
+            copy.start()
+
         def step(u, carry):
             attended = attend_unit(q_ref[u], k_ref[u], v_ref[u], length, causal, diagonal, lse_ref.at[u])
             att_ref[u] = attended
@@ -306,6 +315,7 @@
             return carry
 
         lax.fori_loop(0, number, step, 0)
+        flushes[3].start()
         for copy in outs + late:
             copy.wait()
         if has_partial:
@@ -322,7 +332,10 @@
                 hat_ref[at, :] = hat
                 inv_ref[at, :] = jnp.broadcast_to(inverse, (ROW_CHUNK, 128))
 
-            each_chunk(rows, chunk)
+            triples = zip((low_ref, hat_ref, inv_ref), norm_outs)
+            flushes += each_chunk(rows, chunk, [(*pair, usem.at[4 + index]) for index, pair in enumerate(triples)])
+        for copy in flushes:
+            copy.wait()
 
     unit_rows = sds((number, rows, UNIT), BF16)
     shapes = [unit_rows] * 4 + [sds((number, 2, rows), F32)]
@@ -343,14 +356,17 @@
         pltpu.SemaphoreType.DMA((3, len(pieces), 4)),
         pltpu.SemaphoreType.DMA((len(pieces), 16)),
         pltpu.SemaphoreType.DMA((2,)),
+        pltpu.SemaphoreType.DMA((7,)),
     ]
+    scratch += [pltpu.VMEM((number, rows, UNIT), BF16)] * 4
     if last:
         scratch += [pltpu.VMEM((rows, depth), F32), pltpu.VMEM((rows, depth), residual[0].dtype)]
+        scratch += [pltpu.VMEM((rows, depth), BF16), pltpu.VMEM((rows, depth), F32), pltpu.VMEM((rows, 128), F32)]
     return pl.pallas_call(
         kernel,
         out_shape=shapes,
         in_specs=[SMEM] + [VMEM] * (len(args) - 1) + [ANY] * len(tail),
-        out_specs=[VMEM] * len(shapes),
+        out_specs=[ANY] * 4 + [VMEM] + ([ANY] * 3 if last else [VMEM]),
         scratch_shapes=scratch,
         compiler_params=params(),
         cost_estimate=cost_of(0.6 * number),
@@ -382,9 +398,9 @@
         wbuf, obuf, sbuf, lbuf, att_all, grad_all = (next(it) for _ in range(6))
         stage, diagonal = next(it), next(it)
         if last:
-            dquery, acc, hat, inv = (next(it) for _ in range(4))
+            dquery, acc, hat, inv, low_buf, scaled_buf, nsem = (next(it) for _ in range(7))
         wsem, osem, ssem, gsem, lsem = (next(it) for _ in range(5))
-        length, dp = sc[0], sc[2]
+        length, dp = sc[0] if causal else sc[4], sc[2]
 
         groups, o_copies = weight_copies(w_refs, sc, wbuf, obuf, wsem, osem, (0,) if last else ())
         for copy in o_copies:
@@ -449,7 +465,9 @@
             copy.wait()
         if last:
             acc[...] += dot_nt(dquery[...], wbuf[...])
-            norm_back_rows(acc, hat, inv, gain_ref, low_ref, scaled_ref, gsum_ref, bsum_ref, rows)
+            g_copies += norm_back_rows(
+                acc, hat, inv, gain_ref, low_buf, scaled_buf, (low_ref, scaled_ref), nsem, gsum_ref, bsum_ref, rows
+            )
         for copy in g_copies:
             copy.wait()
 
@@ -458,7 +476,7 @@
     if last:
         shapes += [sds((rows, depth), BF16), big, sds((8, depth), F32), sds((8, depth), F32)]
     shapes.append(sds((rows, (3 - skip) * wide), BF16))
-    specs_out = [VMEM] * len(shapes) + [ANY] * results
+    specs_out = ([ANY] * 2 + [VMEM] * 3 if last else [VMEM]) + [ANY] * results
     shapes += [sds((8, number // 2 // results, 8, UNIT, UNIT), BF16)] * results
     args = [scalars, grad_low, *others] + ([norm[2]] if last else [])
     tail = [norm[0], norm[1], carried] if last else []
@@ -477,6 +495,7 @@
     ]
     if last:
         scratch += [pltpu.VMEM((rows, wide), BF16), pltpu.VMEM((rows, depth), F32), pltpu.VMEM((rows, depth), F32), pltpu.VMEM((rows, 128), F32)]
+        scratch += [pltpu.VMEM((rows, depth), BF16), pltpu.VMEM((rows, depth), F32), pltpu.SemaphoreType.DMA((2,))]
     scratch += [
         pltpu.SemaphoreType.DMA((3, len(pieces), 4)),
         pltpu.SemaphoreType.DMA((len(pieces), 16)),
@@ -537,19 +556,20 @@
     )(*args, *tail)
 
 
-def norm_back_rows(acc, hat, inv, gain_ref, low_ref, scaled_ref, gsum_ref, bsum_ref, rows):
+def norm_back_rows(acc, hat, inv, gain_ref, low_buf, scaled_buf, outs, sems, gsum_ref, bsum_ref, rows):
     gsum_ref[...] = jnp.zeros_like(gsum_ref)
     bsum_ref[...] = jnp.zeros_like(bsum_ref)
 
     def chunk(at):
         gradient, normed = acc[at, :], hat[at, :]
         grad_in = norm_back_chunk(gradient, normed, inv[at, :1], gain_ref[...])
-        low_ref[at, :] = grad_in.astype(BF16)
-        scaled_ref[at, :] = RESIDUAL_ALPHA * grad_in
+        low_buf[at, :] = grad_in.astype(BF16)
+        scaled_buf[at, :] = RESIDUAL_ALPHA * grad_in
         gsum_ref[...] += fold_rows(gradient * normed)
         bsum_ref[...] += fold_rows(gradient)
 
-    each_chunk(rows, chunk)
+    pairs = zip((low_buf, scaled_buf), outs)
+    return each_chunk(rows, chunk, [(*pair, sems.at[index]) for index, pair in enumerate(pairs)])
 
 
 GELU_SCALE = 0.7978845608028654
@@ -605,13 +625,14 @@
         part_in = next(it) if has_partial else None
         w_refs = [[next(it) for _ in piece] for piece in pieces]
         if last:
-            out_ref, low_ref, scaled_ref, gsum_ref, bsum_ref = (next(it) for _ in range(5))
+            norm_outs = [next(it) for _ in range(3)]
+            gsum_ref, bsum_ref = next(it), next(it)
         else:
             sum_ref = next(it)
         act_ref, slope_ref = next(it), next(it)
         ubuf, dbuf, abuf, sbuf, pbuf, psem = (next(it) for _ in range(6))
         if last:
-            acc, hat, cot, lsem = (next(it) for _ in range(4))
+            acc, hat, cot, lsem, out_ref, low_ref, scaled_ref, nsem = (next(it) for _ in range(8))
         wsem, gsem = next(it), next(it)
         target = acc if last else sum_ref
 
@@ -674,7 +695,8 @@
                 gsum_ref[...] += fold_rows(gradient * xhat)
                 bsum_ref[...] += fold_rows(gradient)
 
-            each_chunk(rows, chunk)
+            triples = zip((out_ref, low_ref, scaled_ref), norm_outs)
+            saves += each_chunk(rows, chunk, [(*pair, nsem.at[index]) for index, pair in enumerate(triples)])
         for copy in saves:
             copy.wait()
 
@@ -683,7 +705,7 @@
         shapes = [low, low, big, sds((8, depth), F32), sds((8, depth), F32)]
     else:
         shapes = [big]
-    specs_out = [VMEM] * len(shapes) + [ANY, ANY]
+    specs_out = ([ANY] * 3 + [VMEM] * 2 if last else [VMEM]) + [ANY, ANY]
     shapes += [sds((number, rows, FFN_UNIT), BF16)] * 2
     args = [scalars, inputs]
     if last:
@@ -704,6 +726,10 @@
             pltpu.VMEM((rows, depth), F32),
             pltpu.VMEM((rows, depth), BF16),
             pltpu.SemaphoreType.DMA((2,)),
+            pltpu.VMEM((rows, depth), BF16),
+            pltpu.VMEM((rows, depth), BF16),
+            pltpu.VMEM((rows, depth), F32),
+            pltpu.SemaphoreType.DMA((3,)),
         ]
     scratch += [pltpu.SemaphoreType.DMA((2, len(pieces), 4)), pltpu.SemaphoreType.DMA((2, number))]
     return pl.pallas_call(
@@ -738,7 +764,7 @@
         g_ref = next(it)
         ubuf, dbuf, abuf, sbuf, gbuf, stage, psem = (next(it) for _ in range(7))
         if last:
-            acc, hat, inv, lsem = (next(it) for _ in range(4))
+            acc, hat, inv, lsem, low_buf, scaled_buf, nsem = (next(it) for _ in range(7))
         wsem, ssem, gsem = next(it), next(it), next(it)
         order, dp = sc[1], sc[2]
         target = acc if last else sum_ref
@@ -789,13 +815,15 @@
         if last:
             for copy in late:
                 copy.wait()
-            norm_back_rows(acc, hat, inv, gain_ref, low_ref, scaled_ref, gsum_ref, bsum_ref, rows)
+            g_copies += norm_back_rows(
+                acc, hat, inv, gain_ref, low_buf, scaled_buf, (low_ref, scaled_ref), nsem, gsum_ref, bsum_ref, rows
+            )
         for copy in g_copies:
             copy.wait()
 
     big, low = sds((rows, depth), F32), sds((rows, depth), BF16)
     shapes = [low, big, sds((8, depth), F32), sds((8, depth), F32)] if last else [big]
-    specs_out = [VMEM] * len(shapes) + [ANY]
+    specs_out = ([ANY] * 2 + [VMEM] * 2 if last else [VMEM]) + [ANY]
     shapes.append(sds((8, number // 2, 8, UNIT, FFN_PART), BF16))
     args = [scalars, grad_low, inputs] + ([norm[2]] if last else [])
     specs = [SMEM] + [VMEM] * (len(args) - 1)
@@ -816,6 +844,9 @@
             pltpu.VMEM((rows, depth), F32),
             pltpu.VMEM((rows, depth), F32),
             pltpu.VMEM((rows, 128), F32),
+            pltpu.SemaphoreType.DMA((2,)),
+            pltpu.VMEM((rows, depth), BF16),
+            pltpu.VMEM((rows, depth), F32),
             pltpu.SemaphoreType.DMA((2,)),
         ]
     scratch += [pltpu.SemaphoreType.DMA((2, len(pieces), 4)), pltpu.SemaphoreType.DMA((2, number)), pltpu.SemaphoreType.DMA]
@@ -1063,8 +1094,7 @@
     mine = lax.axis_index("tensor")
     order = dp & 3
     inner = (dp >> 1) & 1
-    self_scalars = jnp.stack([dec_lengths[0, mine], order, dp, inner]).astype(jnp.int32)
-    cross_scalars = jnp.stack([mem_lengths[0, mine], order, dp, inner]).astype(jnp.int32)
+    scalars = jnp.stack([dec_lengths[0, mine], order, dp, inner, mem_lengths[0, mine]]).astype(jnp.int32)
     gains = [norm_gains[i : i + 1] for i in range(3)]
     biases = [norm_biases[i : i + 1] for i in range(3)]
 
@@ -1084,40 +1114,40 @@
     ffn_near = over_y(jnp.stack([part_rows(ffn_in, 4), part_rows(ffn_out, 4)]))
     self_own = (self_qkv, self_out)
     self_sib = tuple(to_sibling(w) for w in self_own)
-    self_a = attention_fwd_call(self_scalars, [], [tokens], [self_own, self_sib], None, None)
+    self_a = attention_fwd_call(scalars, [], [tokens], [self_own, self_sib], None, None)
     self_near = after(self_near, self_a[4])
     self_side, self_up = over_x(self_near), over_z_near(self_near)
     self_corner = over_x(self_up)
-    self_rest = jnp.stack([after(self_near, cross_near), self_side, self_up, self_corner])
+    cross_own, ffn_own = (cross_q, cross_kv, cross_out), (ffn_in, ffn_out)
+    cross_sib = tuple(to_sibling(w) for w in cross_own)
     cross_up = over_z_near(cross_near)
-    self_far = to_sibling(self_rest)
-    self_pieces = [self_own, self_sib, (self_rest,), (self_far,)]
-    cross_own, ffn_own = (cross_q, cross_kv, cross_out), (ffn_in, ffn_out)
-    cross_sib = tuple(to_sibling(after(w, self_near)) for w in cross_own)
+    self_rest = (self_near, self_side, self_up, after(self_corner, cross_near, *cross_sib))
+    self_far = tuple(to_sibling(w) for w in self_rest)
+    self_pieces = [self_own, self_sib, self_rest, self_far]
     self_b = attention_fwd_call(
-        after(self_scalars, *cross_sib), [tokens], [tokens], self_pieces[2:], self_a[5], (gains[0], biases[0])
+        scalars, [tokens], [tokens], self_pieces[2:], self_a[5], (gains[0], biases[0])
     )
     first_low, first_hat, first_inv = self_b[5:]
     cross_in = [first_low, memory]
     cross_rest = jnp.stack([cross_near, after(cross_up, self_b[4])])
     cross_far = to_sibling(cross_rest)
-    cross_a = attention_fwd_call(after(cross_scalars, ffn_near), [], cross_in, [cross_own, cross_sib], None, None)
+    cross_a = attention_fwd_call(after(scalars, ffn_near), [], cross_in, [cross_own, cross_sib], None, None)
     ffn_sib = tuple(to_sibling(after(w, ffn_near)) for w in ffn_own)
     ffn_side, ffn_up = over_x(ffn_near), over_z_near(ffn_near)
     cross_pieces = [cross_own, cross_sib, (cross_rest,), (after(cross_far, cross_a[4]),)]
     cross_b = attention_fwd_call(
-        cross_scalars, [first_hat, gains[0], biases[0]], cross_in, cross_pieces[2:], cross_a[5], (gains[1], biases[1])
+        scalars, [first_hat, gains[0], biases[0]], cross_in, cross_pieces[2:], cross_a[5], (gains[1], biases[1])
     )
     second_low, second_hat, second_inv = cross_b[5:]
     ffn_side, ffn_up = after(ffn_side, cross_b[4]), after(ffn_up, cross_b[4])
     up_corner, down_corner = over_x(ffn_up[:1]), over_z_near(ffn_side[1:])
     ffn_pieces = [ffn_own, ffn_sib]
-    ffn_a = ffn_fwd_call(cross_scalars, second_low, ffn_pieces, None, None)
+    ffn_a = ffn_fwd_call(scalars, second_low, ffn_pieces, None, None)
     up_corner, down_corner = after(up_corner, ffn_a[0]), after(down_corner, ffn_a[0])
     ffn_rest = (ffn_near, ffn_side, ffn_up, up_corner, down_corner)
     ffn_pieces += [ffn_rest, tuple(to_sibling(w) for w in ffn_rest)]
     ffn_b = ffn_fwd_call(
-        cross_scalars, second_low, ffn_pieces[2:], ffn_a[0],
+        scalars, second_low, ffn_pieces[2:], ffn_a[0],
         (second_hat, gains[1], biases[1], cotangent, gains[2], biases[2]),
     )
     out_rows, third_low, third_scaled, third_gain, third_bias = ffn_b[:5]
@@ -1127,11 +1157,11 @@
 
     ffn_saved = [ffn_a[1:3], ffn_b[5:7]]
     ffn_d = ffn_bwd_call(
-        cross_scalars, third_low, second_low, ffn_pieces[1::2], ffn_saved, plan_of((1, 3)), third_scaled, None
+        scalars, third_low, second_low, ffn_pieces[1::2], ffn_saved, plan_of((1, 3)), third_scaled, None
     )
     ffn_sum = Reduction(ffn_d[1], [(0, 3, "yzx"), (3, 6, "xyz"), (6, 8, "zxy")], ffn_finish())
     ffn_e = ffn_bwd_call(
-        cross_scalars, third_low, second_low, ffn_pieces[::2], ffn_saved, plan_of((0, 2)), ffn_d[0],
+        scalars, third_low, second_low, ffn_pieces[::2], ffn_saved, plan_of((0, 2)), ffn_d[0],
         (second_hat, second_inv, gains[1]),
     )
     second_back, second_scaled, second_gain, second_bias = ffn_e[:4]
@@ -1139,7 +1169,7 @@
     second_back = after(second_back, *advance([ffn_sum]))
 
     cross_e = attention_bwd_call(
-        cross_scalars, second_back, cross_in, cross_pieces[1::2] + cross_pieces[::2],
+        scalars, second_back, cross_in, cross_pieces[1::2] + cross_pieces[::2],
         [cross_a[:5], cross_b[:5]], plan_of((1, 3, 0, 2)), second_scaled,
         (first_hat, first_inv, gains[0]), 2,
     )
@@ -1153,19 +1183,19 @@
 
     self_saved = [self_a[:5], self_b[:5]]
     self_d = attention_bwd_call(
-        self_scalars, first_back, [tokens], self_pieces[1::2], self_saved, plan_of((1, 3)), None, None
+        scalars, first_back, [tokens], self_pieces[1::2], self_saved, plan_of((1, 3)), None, None
     )
     cross_sum.begin(cross_e[6], self_d[0])
     sends = advance([cross_sum, ffn_sum], self_d[0])
     self_sum = Reduction(after(self_d[1], *sends), [(0, 4, "yxz"), (4, 8, "xzy")], attention_finish((3,)))
     first_back = after(first_back, *sends)
     self_e = attention_bwd_call(
-        self_scalars, first_back, [tokens], self_pieces[::2], self_saved, plan_of((0, 2)), None, None
+        scalars, first_back, [tokens], self_pieces[::2], self_saved, plan_of((0, 2)), None, None
     )
     self_sum.begin(self_e[1], self_e[0])
     sends = advance([self_sum])
     grad_tokens, grad_memory = inputs_back_call(
-        self_scalars, after(first_scaled, *sends),
+        scalars, after(first_scaled, *sends),
         [(self_d[0], self_pieces[1::2]), (self_e[0], self_pieces[::2])],
         (memory_part, cross_pieces[1::2] + cross_pieces[::2]),
     )

time: 395 us -> 387 us (0.980)
  other arithmetic: 8.63 us -> 4.63 us
    another operation x3 -> x0, other arithmetic: 3.98 us -> none  [the longest x1 1.42 us: sentence_body(): jnp.stack([after(self_near, cross_near), self_side, self_up, self_corner])]
  transfers between devices with their start and end apart: 53 -> 56, of which waited for: 23 -> 22; matrix products, arithmetic and copies ran while one was open for 4% -> 4% of each run, Pallas kernels for 47% -> 47%
where the time goes in v7:
time: 387 us; the launch traced here: 384 us
  Pallas kernels  230 us (59%)
  waiting for transfers between devices  66.4 us (17%)
  starting transfers between devices  49.7 us (13%)
  local copies, waits for them, and re-layouts  17.8 us (5%)
  between operations  15.1 us (4%)
  other arithmetic  4.63 us (1%)
    pallas_call x3, Pallas kernels, attention_bwd_call(): pl.pallas_call(kernel, out_shape=shapes, in_specs=[SMEM] + [VMEM] * (len(...  64.1 us
    ppermute x25, waiting for transfers between devices, over_dp(): return lax.ppermute(values, 'dp', swap_pairs(8, mask))  50.5 us
    pallas_call x4, Pallas kernels, attention_fwd_call(): pl.pallas_call(kernel, out_shape=shapes, in_specs=[SMEM] + [VMEM] * (len(...  50.1 us
    pallas_call x12, Pallas kernels, combine(): pl.pallas_call(kernel, out_shape=list(shapes), in_specs=[ANY] * len(array...  41.1 us
    pallas_call x2, Pallas kernels, ffn_bwd_call(): pl.pallas_call(kernel, out_shape=shapes, in_specs=specs + [ANY] * len(tai...  33.6 us
    ppermute x25, starting transfers between devices, over_dp(): return lax.ppermute(values, 'dp', swap_pairs(8, mask))  32.4 us
    pallas_call x2, Pallas kernels, ffn_fwd_call(): pl.pallas_call(kernel, out_shape=shapes, in_specs=specs + [ANY] * len(tai...  26 us
    pallas_call x1, Pallas kernels, inputs_back_call(): pl.pallas_call(kernel, out_shape=[sds((rows, depth), F32)] * 2, in_specs=...  15.1 us
  transfers between devices with their start and end apart: 56, of which 22 were waited for; matrix products, arithmetic and copies ran while one was open for 4% of the time, Pallas kernels for 47%

profile of v7, /device:TPU:0, one launch (start us, length us, event | category | flops | bytes accessed | tf_op | source)
XLA Modules:
  0.0 383.6 jit_solution(8957206850517422970)
XLA Ops:
  16.9 11.1 %self_fwd.2 = (bf16[4,512,128]{2,1,0:T(8,128)(2,1)}, bf16[4,512,128]{2,1,0:T(8,128)(2,1)}, bf16[4,512,128]{2,1,0:T(8,128)(2,1)}, bf16[4,512,128]{2,1,0:T(8,128)(...) custom-call(s32[5]{0:T(128)} %stack.54.refs_0_, bf16[512,1024]{1,0:T(8,128)(2,1)} %refs_2_.11, ...), custom_call_target="tpu_custom_call" | custom-call | flops 2640000000 | bytes 4194304 | tf_op jit(solution)/shard_map/self_fwd/pallas_call | solution.py:365
  31.6 10.8 %collective-permute-done.4.refs_8_.refs_7_.refs_15_ = bf16[4,256,256]{2,1,0:T(8,128)(2,1)S(1)} collective-permute-done((bf16[4,256,256]{2,1,0:T(8,128)(2,1)}, bf16[4,256,256]{2,1,0:T(8,128)(2,1)S(1)}, u32[]{:S(2)}, u32[]{:S(2)}) %collective-permute-start.4) | collective-permute-done | bytes 524320 | tf_op jit(solution)/shard_map/ppermute | solution.py:962
  44.1 3.7 collective-permute-done.6
  51.5 4.4 %collective-permute-done.5.refs_9_.refs_8_.refs_16_ = bf16[4,256,256]{2,1,0:T(8,128)(2,1)S(1)} collective-permute-done((bf16[4,256,256]{2,1,0:T(8,128)(2,1)S(1)}, bf16[4,256,256]{2,1,0:T(8,128)(2,1)S(1)}, u32[]{:S(2)}, u32[]{:S(2)}) %collective-permute-start.5) | collective-permute-done | bytes 524320 | tf_op jit(solution)/shard_map/ppermute | solution.py:962
  59.4 13.0 %self_fwd.3 = (bf16[4,512,128]{2,1,0:T(8,128)(2,1)}, bf16[4,512,128]{2,1,0:T(8,128)(2,1)}, bf16[4,512,128]{2,1,0:T(8,128)(2,1)}, bf16[4,512,128]{2,1,0:T(8,128)(...) custom-call(s32[5]{0:T(128)} %stack.54.refs_0_, ...), custom_call_target="tpu_custom_call" | custom-call | flops 2640000000 | bytes 4194304 | tf_op jit(solution)/shard_map/self_fwd/pallas_call | solution.py:365
  75.8 6.0 %collective-permute-done.14.refs_9_ = bf16[2,256,1024]{2,1,0:T(8,128)(2,1)} collective-permute-done((bf16[2,256,1024]{2,1,0:T(8,128)(2,1)S(1)}, bf16[2,256,1024]{2,1,0:T(8,128)(2,1)}, u32[]{:S(2)}, u32[]{:S(2)}) %collective-permute-start.14) | collective-permute-done | bytes 1048608 | tf_op jit(solution)/shard_map/ppermute | solution.py:958
  85.2 11.9 %cross_fwd.2 = (bf16[4,512,128]{2,1,0:T(8,128)(2,1)}, bf16[4,512,128]{2,1,0:T(8,128)(2,1)}, bf16[4,512,128]{2,1,0:T(8,128)(2,1)}, bf16[4,512,128]{2,1,0:T(8,128)...) custom-call(s32[5]{0:T(128)} %stack.54.refs_0_, bf16[512,1024]{1,0:T(8,128)(2,1)} %get-tuple-element.148.refs_1_.refs_2_, ...), custom_call_target="tpu_custom_call" | custom-call | flops 2640000000 | bytes 4194304 | tf_op jit(solution)/shard_map/cross_fwd/pallas_call | solution.py:365
  97.2 14.0 %cross_fwd.3 = (bf16[4,512,128]{2,1,0:T(8,128)(2,1)}, bf16[4,512,128]{2,1,0:T(8,128)(2,1)}, bf16[4,512,128]{2,1,0:T(8,128)(2,1)}, bf16[4,512,128]{2,1,0:T(8,128)...) custom-call(s32[5]{0:T(128)} %stack.54.refs_0_, ...), custom_call_target="tpu_custom_call" | custom-call | flops 2640000000 | bytes 4194304 | tf_op jit(solution)/shard_map/cross_fwd/pallas_call | solution.py:365
  115.3 11.6 %ffn_fwd.2 = (f32[512,1024]{1,0:T(8,128)}, bf16[4,512,512]{2,1,0:T(8,128)(2,1)}, bf16[4,512,512]{2,1,0:T(8,128)(2,1)}) custom-call(s32[5]{0:T(128)} %stack.54.refs_0_, bf16[512,1024]{1,0:T(8,128)(2,1)} %get-tuple-element.156.refs_1_.refs_2_, bf16[1024,1024]{1,0:T(8,128)(2,1)} %refs_7_.3, bf16[1024,1024]{1,0:T(8,128)(2,1)} %refs_8_.1, ...), custom_call_target="tpu_custom_call" | custom-call | flops 13200000000 | bytes 4194304 | tf_op jit(solution)/shard_map/ffn_fwd/pallas_call | solution.py:735
  132.4 14.4 %ffn_fwd.3 = (bf16[512,1024]{1,0:T(8,128)(2,1)}, bf16[512,1024]{1,0:T(8,128)(2,1)}, f32[512,1024]{1,0:T(8,128)}, f32[8,1024]{1,0:T(8,128)}, f32[8,1024]{1,0:T(8,...) custom-call(s32[5]{0:T(128)} %stack.54.refs_0_, bf16[512,1024]{1,0:T(8,128)(2,1)} %get-tuple-element.156.refs_1_.refs_2_, ...), custom_call_target="tpu_custom_call" | custom-call | flops 13200000000 | bytes 4194304 | tf_op jit(solution)/shard_map/ffn_fwd/pallas_call | solution.py:735
  146.7 16.4 %ffn_bwd.2 = (f32[512,1024]{1,0:T(8,128)}, bf16[8,2,8,128,256]{4,3,2,1,0:T(8,128)(2,1)}) custom-call(s32[5]{0:T(128)} %stack.54.refs_0_, bf16[512,1024]{1,0:T(8,128)(2,1)} %get-tuple-element.167.refs_1_, bf16[512,1024]{1,0:T(8,128)(2,1)} %get-tuple-element.156.refs_1_.refs_2_, f32[512,1024]{1,0:T(8,128)} %get-tuple-element.169.refs_3_, ...), custom_call_target="tpu_custom_call" | custom-call | flops 18699999232 | bytes 4194304 | tf_op jit(solution)/shard_map/ffn_bwd/pallas_call | solution.py:853
  163.3 17.2 %ffn_bwd.3 = (bf16[512,1024]{1,0:T(8,128)(2,1)}, f32[512,1024]{1,0:T(8,128)}, f32[8,1024]{1,0:T(8,128)}, f32[8,1024]{1,0:T(8,128)}, bf16[8,2,8,128,256]{4,3,2,1,0:T(8,128)(2,1)}) custom-call(s32[5]{0:T(128)} %stack.54.refs_0_, bf16[512,1024]{1,0:T(8,128)(2,1)} %get-tuple-element.167.refs_1_, bf16[512,1024]{1,0:T(8,128)(2,1)} %get-tuple-element.156.refs_1_.refs_2_, ...), custom_call_target="tpu_custom_call" | custom-call | flops 18699999232 | bytes 4194304 | tf_op jit(solution)/shard_map/ffn_bwd/pallas_call | solution.py:853
  180.5 5.3 %combine.12 = (bf16[3,2,2,2,128,256]{5,4,3,2,1,0:T(8,128)(2,1)}, bf16[3,2,2,2,128,256]{5,4,3,2,1,0:T(8,128)(2,1)}, bf16[2,2,2,2,128,256]{5,4,3,2,1,0:T(8,128)(2,1)}) custom-call(bf16[8,2,2,2,2,128,256]{6,5,4,3,2,1,0:T(8,128)(2,1)} %bitcast.38, bf16[8,2,2,2,2,128,256]{6,5,4,3,2,1,0:T(8,128)(2,1)} %bitcast.16.refs_1_.refs_3_.refs_5_.refs_7_), custom_call_target="tpu_custom_call" | custom-call | flops 3300000000 | bytes 4194304 | tf_op jit(solution)/shard_map/combine/pallas_call | solution.py:937
  189.6 32.2 %cross_bwd.1 = (bf16[512,1024]{1,0:T(8,128)(2,1)}, f32[512,1024]{1,0:T(8,128)}, f32[8,1024]{1,0:T(8,128)}, f32[8,1024]{1,0:T(8,128)}, bf16[512,2048]{1,0:T(8,128...) custom-call(s32[5]{0:T(128)} %stack.54.refs_0_, ...), custom_call_target="tpu_custom_call" | custom-call | flops 36960002048 | bytes 4194304 | tf_op jit(solution)/shard_map/cross_bwd/pallas_call | solution.py:506
  224.2 4.0 %combine.13 = (bf16[3,2,2,128,256]{4,3,2,1,0:T(8,128)(2,1)}, bf16[3,2,2,128,256]{4,3,2,1,0:T(8,128)(2,1)}, bf16[2,2,2,128,256]{4,3,2,1,0:T(8,128)(2,1)}) custom-call(bf16[8,2,2,2,2,128,256]{6,5,4,3,2,1,0:T(8,128)(2,1)} %bitcast.39, bf16[8,2,2,2,2,128,256]{6,5,4,3,2,1,0:T(8,128)(2,1)} %bitcast.16.refs_1_.refs_3_.refs_5_.refs_7_, ...), custom_call_target="tpu_custom_call" | custom-call | flops 3300000000 | bytes 4194304 | tf_op jit(solution)/shard_map/combine/pallas_call | solution.py:937
  231.8 16.0 %self_bwd.2 = (bf16[512,1536]{1,0:T(8,128)(2,1)}, bf16[8,2,8,128,128]{4,3,2,1,0:T(8,128)(2,1)}) custom-call(s32[5]{0:T(128)} %stack.54.refs_0_, bf16[512,1024]{1,0:T(8,128)(2,1)} %get-tuple-element.225.refs_1_, bf16[512,1024]{1,0:T(8,128)(2,1)} %refs_2_.11, bf16[3,1024,256]{2,1,0:T(8,128)(2,1)} %collective-permute-done.refs_4_.refs_3_.refs_5_, ...), custom_call_target="tpu_custom_call" | custom-call | flops 18480001024 | bytes 4194304 | tf_op jit(solution)/shard_map/self_bwd/pallas_call | solution.py:506
  249.8 5.1 %combine.14 = (bf16[4,2,2,2,128,128]{5,4,3,2,1,0:T(8,128)(2,1)}, bf16[4,2,2,2,128,128]{5,4,3,2,1,0:T(8,128)(2,1)}, bf16[3,2,128,256]{3,2,1,0:T(8,128)(2,1)}, bf1...) custom-call(bf16[8,2,2,2,2,128,128]{6,5,4,3,2,1,0:T(8,128)(2,1)} %bitcast.43, ...), custom_call_target="tpu_custom_call" | custom-call | flops 3300000000 | bytes 4194304 | tf_op jit(solution)/shard_map/combine/pallas_call | solution.py:937
  260.7 15.9 %self_bwd.3 = (bf16[512,1536]{1,0:T(8,128)(2,1)}, bf16[8,2,8,128,128]{4,3,2,1,0:T(8,128)(2,1)}) custom-call(s32[5]{0:T(128)} %stack.54.refs_0_, bf16[512,1024]{1,0:T(8,128)(2,1)} %get-tuple-element.225.refs_1_, bf16[512,1024]{1,0:T(8,128)(2,1)} %refs_2_.11, bf16[3,1024,256]{2,1,0:T(8,128)(2,1)} %refs_11_.1, bf16[256,1024]{1,0:T(8,128)(2,1)} %refs_12_.3, ...), custom_call_target="tpu_custom_call" | custom-call | flops 18480001024 | bytes 4194304 | tf_op jit(solution)/shard_map/self_bwd/pallas_call | solution.py:506
  277.4 4.1 %combine.15 = (bf16[4,2,2,2,128,128]{5,4,3,2,1,0:T(8,128)(2,1)}, bf16[4,2,2,2,128,128]{5,4,3,2,1,0:T(8,128)(2,1)}) custom-call(bf16[8,2,2,2,2,128,128]{6,5,4,3,2,1,0:T(8,128)(2,1)} %bitcast.48, bf16[8,2,2,2,2,128,128]{6,5,4,3,2,1,0:T(8,128)(2,1)} %bitcast.20.refs_1_), custom_call_target="tpu_custom_call" | custom-call | flops 3300000000 | bytes 4194304 | tf_op jit(solution)/shard_map/combine/pallas_call | solution.py:937
  285.5 6.4 %collective-permute-done.41.refs_11_.refs_14_ = bf16[3,2,128,256]{3,2,1,0:T(8,128)(2,1)S(1)} collective-permute-done((bf16[3,2,128,256]{3,2,1,0:T(8,128)(2,1)}, bf16[3,2,128,256]{3,2,1,0:T(8,128)(2,1)S(1)}, u32[]{:S(2)}, u32[]{:S(2)}) %collective-permute-start.41) | collective-permute-done | bytes 393248 | tf_op jit(solution)/shard_map/ppermute | solution.py:962
  301.9 15.1 %inputs_back.1 = (f32[512,1024]{1,0:T(8,128)}, f32[512,1024]{1,0:T(8,128)}) custom-call(s32[5]{0:T(128)} %stack.54.refs_0_, f32[512,1024]{1,0:T(8,128)} %get-tuple-element.233.refs_1_, bf16[512,1536]{1,0:T(8,128)(2,1)} %get-tuple-element.215.refs_2_, bf16[512,1536]{1,0:T(8,128)(2,1)} %get-tuple-element.229.refs_3_, ...), custom_call_target="tpu_custom_call" | custom-call | flops 13200000000 | bytes 4194304 | tf_op jit(solution)/shard_map/inputs_back/pallas_call | solution.py:546
  327.0 3.8 %combine.18 = (bf16[4,2,128,128]{3,2,1,0:T(8,128)(2,1)}, bf16[4,2,128,128]{3,2,1,0:T(8,128)(2,1)}, f32[128,1024]{1,0:T(8,128)}, f32[1024,128]{1,0:T(8,128)}) custom-call(bf16[8,2,2,2,2,128,128]{6,5,4,3,2,1,0:T(8,128)(2,1)} %bitcast.45, bf16[8,2,2,2,2,128,128]{6,5,4,3,2,1,0:T(8,128)(2,1)} %bitcast.18.refs_1_, bf16[4,2,2,2,128,128]{5,4,3,2,1,0:T(8,128)(2,1)} %copy-done.1, ...), custom_call_target="tpu_custom_call" | custom-call | flops 3300000000 | bytes 4194304 | tf_op jit(solution)/shard_map/combine/pallas_call | solution.py:937
  333.3 5.0 %collective-permute-done.48.refs_5_.refs_6_.refs_7_ = bf16[4,2,2,128,128]{4,3,2,1,0:T(8,128)(2,1)} collective-permute-done((bf16[4,2,2,128,128]{4,3,2,1,0:T(8,128)(2,1)}, bf16[4,2,2,128,128]{4,3,2,1,0:T(8,128)(2,1)}, u32[]{:S(2)}, u32[]{:S(2)}) %collective-permute-start.48) | collective-permute-done | bytes 524320 | tf_op jit(solution)/shard_map/ppermute | solution.py:962
  355.7 12.7 %collective-permute-done.54.refs_5_ = bf16[8,128,128]{2,1,0:T(8,128)(2,1)S(1)} collective-permute-done((bf16[8,128,128]{2,1,0:T(8,128)(2,1)}, bf16[8,128,128]{2,1,0:T(8,128)(2,1)S(1)}, u32[]{:S(2)}, u32[]{:S(2)}) %collective-permute-start.54) | collective-permute-done | bytes 262176 | tf_op jit(solution)/shard_map/ppermute | solution.py:962
  (220 shorter events, 108.4 us)
Async XLA Ops:
  7.2 334.7 %all-gather.3.cloned.1.call-start = ((), (), s32[]{:S(2)}) async-start(), calls=%async_computation | async-start | bytes 1081344 | tf_op jit(solution)/shard_map/all_gather | solution.py:1179
  13.7 34.1 %collective-permute-start.6 = (bf16[4,512,256]{2,1,0:T(8,128)(2,1)S(1)}, bf16[4,512,256]{2,1,0:T(8,128)(2,1)}, u32[]{:S(2)}, u32[]{:S(2)}) collective-permute-start(bf16[4,512,256]{2,1,0:T(8,128)(2,1)S(1)} %pad_maximum_fusion.1), channel_id=1, source_target_pairs={{0,2},{1,3},{2,0},{3,1},{4,6},{5,7},{6,4},{7,5},{8,10},{9,11},{10,... | collective-permute-start | bytes 3145736 | tf_op jit(solution)/shard_map/ppermute | solution.py:958
  16.5 34.4 %collective-permute-start.8 = (bf16[2,1024,256]{2,1,0:T(8,128)(2,1)}, bf16[2,1024,256]{2,1,0:T(8,128)(2,1)}, u32[]{:S(2)}, u32[]{:S(2)}) collective-permute-start(bf16[2,1024,256]{2,1,0:T(8,128)(2,1)} %refs_22_.1), channel_id=1, source_target_pairs={{0,1},{1,0},{2,3},{3,2},{4,5},{5,4},{6,7},{7,6},{8,9},{9,8},{10,11... | collective-permute-start | bytes 3145736 | tf_op jit(solution)/shard_map/ppermute | solution.py:954
  47.9 24.9 %collective-permute-start.15 = (bf16[4,512,256]{2,1,0:T(8,128)(2,1)}, bf16[4,512,256]{2,1,0:T(8,128)(2,1)}, u32[]{:S(2)}, u32[]{:S(2)}) collective-permute-start(bf16[4,512,256]{2,1,0:T(8,128)(2,1)} %collective-permute-done.6), channel_id=1, source_target_pairs={{0,8},{4,12},{8,0},{12,4},{16,24},{20,28},{24,16},{28,20},{1,9},{5... | collective-permute-start | bytes 3145736 | tf_op jit(solution)/shard_map/ppermute | solution.py:962
  56.1 25.7 %collective-permute-start.14 = (bf16[2,256,1024]{2,1,0:T(8,128)(2,1)S(1)}, bf16[2,256,1024]{2,1,0:T(8,128)(2,1)}, u32[]{:S(2)}, u32[]{:S(2)}) collective-permute-start(bf16[2,256,1024]{2,1,0:T(8,128)(2,1)S(1)} %pad_maximum_fusion.2), channel_id=1, source_target_pairs={{0,2},{1,3},{2,0},{3,1},{4,6},{5,7},{6,4},{7,5},{8,10},{9,11},{10,... | collective-permute-start | bytes 3145736 | tf_op jit(solution)/shard_map/ppermute | solution.py:958
  81.8 32.2 %collective-permute-start.17 = (bf16[1024,1024]{1,0:T(8,128)(2,1)}, bf16[1024,1024]{1,0:T(8,128)(2,1)}, u32[]{:S(2)}, u32[]{:S(2)}) collective-permute-start(bf16[1024,1024]{1,0:T(8,128)(2,1)} %refs_7_.3), channel_id=1, source_target_pairs={{0,1},{1,0},{2,3},{3,2},{4,5},{5,4},{6,7},{7,6},{8,9},{9,8},{10,11... | collective-permute-start | bytes 6291464 | tf_op jit(solution)/shard_map/ppermute | solution.py:954
  81.8 32.8 %collective-permute-start.18 = (bf16[1024,1024]{1,0:T(8,128)(2,1)}, bf16[1024,1024]{1,0:T(8,128)(2,1)}, u32[]{:S(2)}, u32[]{:S(2)}) collective-permute-start(bf16[1024,1024]{1,0:T(8,128)(2,1)} %refs_8_.1), channel_id=1, source_target_pairs={{0,1},{1,0},{2,3},{3,2},{4,5},{5,4},{6,7},{7,6},{8,9},{9,8},{10,11... | collective-permute-start | bytes 6291464 | tf_op jit(solution)/shard_map/ppermute | solution.py:954
  82.3 28.9 %collective-permute-start.19 = (bf16[2,256,1024]{2,1,0:T(8,128)(2,1)}, bf16[2,256,1024]{2,1,0:T(8,128)(2,1)}, u32[]{:S(2)}, u32[]{:S(2)}) collective-permute-start(bf16[2,256,1024]{2,1,0:T(8,128)(2,1)} %collective-permute-done.14.refs_9_), channel_id=1, source_target_pairs={{0,4},{4,0},{8,12},{12,8},{16,20},{20,16},{24,28},{28,24},{1,5},{5... | collective-permute-start | bytes 3145736 | tf_op jit(solution)/shard_map/ppermute | solution.py:962
  83.8 29.0 %collective-permute-start.20 = (bf16[2,256,1024]{2,1,0:T(8,128)(2,1)}, bf16[2,256,1024]{2,1,0:T(8,128)(2,1)}, u32[]{:S(2)}, u32[]{:S(2)}) collective-permute-start(bf16[2,256,1024]{2,1,0:T(8,128)(2,1)} %collective-permute-done.14.refs_9_), channel_id=1, source_target_pairs={{0,8},{4,12},{8,0},{12,4},{16,24},{20,28},{24,16},{28,20},{1,9},{5... | collective-permute-start | bytes 3145736 | tf_op jit(solution)/shard_map/ppermute | solution.py:962
  97.1 32.1 %collective-permute-start.23 = (bf16[2,256,1024]{2,1,0:T(8,128)(2,1)}, bf16[2,256,1024]{2,1,0:T(8,128)(2,1)}, u32[]{:S(2)}, u32[]{:S(2)}) collective-permute-start(bf16[2,256,1024]{2,1,0:T(8,128)(2,1)} %collective-permute-done.14.refs_9_), channel_id=1, source_target_pairs={{0,1},{1,0},{2,3},{3,2},{4,5},{5,4},{6,7},{7,6},{8,9},{9,8},{10,11... | collective-permute-start | bytes 3145736 | tf_op jit(solution)/shard_map/ppermute | solution.py:954
  185.9 37.0 %collective-permute-start.29 = (bf16[3,2,2,2,128,256]{5,4,3,2,1,0:T(8,128)(2,1)}, bf16[3,2,2,2,128,256]{5,4,3,2,1,0:T(8,128)(2,1)S(1)}, u32[]{:S(2)}, u32[]{:S(2)}) collective-permute-start(bf16[3,2,2,2,128,256]{5,4,3,2,1,0:T(8,128)(2,1)} %get-tuple-element.180), channel_id=1, source_target_pairs={{0,2},{1,3},{2,0},{3,1},{4,6},{5,7},{6,4},{7,5},{8,10},{9,11},{10,... | collective-permute-start | bytes 4718600 | tf_op jit(solution)/shard_map/ppermute | solution.py:958
  187.5 36.7 %collective-permute-start.30 = (bf16[3,2,2,2,128,256]{5,4,3,2,1,0:T(8,128)(2,1)}, bf16[3,2,2,2,128,256]{5,4,3,2,1,0:T(8,128)(2,1)}, u32[]{:S(2)}, u32[]{:S(2)}) collective-permute-start(bf16[3,2,2,2,128,256]{5,4,3,2,1,0:T(8,128)(2,1)} %get-tuple-element.181), channel_id=1, source_target_pairs={{0,4},{4,0},{8,12},{12,8},{16,20},{20,16},{24,28},{28,24},{1,5},{5... | collective-permute-start | bytes 4718600 | tf_op jit(solution)/shard_map/ppermute | solution.py:962
  189.0 32.9 %collective-permute-start.31 = (bf16[2,2,2,2,128,256]{5,4,3,2,1,0:T(8,128)(2,1)}, bf16[2,2,2,2,128,256]{5,4,3,2,1,0:T(8,128)(2,1)}, u32[]{:S(2)}, u32[]{:S(2)}) collective-permute-start(bf16[2,2,2,2,128,256]{5,4,3,2,1,0:T(8,128)(2,1)} %get-tuple-element.182), channel_id=1, source_target_pairs={{0,8},{4,12},{8,0},{12,4},{16,24},{20,28},{24,16},{28,20},{1,9},{5... | collective-permute-start | bytes 3145736 | tf_op jit(solution)/shard_map/ppermute | solution.py:962
  254.9 21.8 %collective-permute-start.36 = (bf16[8,2,8,128,128]{4,3,2,1,0:T(8,128)(2,1)}, bf16[8,2,8,128,128]{4,3,2,1,0:T(8,128)(2,1)}, u32[]{:S(2)}, u32[]{:S(2)}) collective-permute-start(bf16[8,2,8,128,128]{4,3,2,1,0:T(8,128)(2,1)} %get-tuple-element.228), channel_id=1, source_target_pairs={{0,1},{1,0},{2,3},{3,2},{4,5},{5,4},{6,7},{7,6},{8,9},{9,8},{10,11... | collective-permute-start | bytes 12582920 | tf_op jit(solution)/shard_map/ppermute | solution.py:954
  255.8 26.9 %collective-permute-start.38 = (bf16[4,2,2,2,128,128]{5,4,3,2,1,0:T(8,128)(2,1)}, bf16[4,2,2,2,128,128]{5,4,3,2,1,0:T(8,128)(2,1)S(1)}, u32[]{:S(2)}, u32[]{:S(2)}) collective-permute-start(bf16[4,2,2,2,128,128]{5,4,3,2,1,0:T(8,128)(2,1)} %get-tuple-element.220), channel_id=1, source_target_pairs={{0,8},{4,12},{8,0},{12,4},{16,24},{20,28},{24,16},{28,20},{1,9},{5... | collective-permute-start | bytes 3145736 | tf_op jit(solution)/shard_map/ppermute | solution.py:962
  257.3 26.8 %collective-permute-start.39 = (bf16[4,2,2,2,128,128]{5,4,3,2,1,0:T(8,128)(2,1)}, bf16[4,2,2,2,128,128]{5,4,3,2,1,0:T(8,128)(2,1)}, u32[]{:S(2)}, u32[]{:S(2)}) collective-permute-start(bf16[4,2,2,2,128,128]{5,4,3,2,1,0:T(8,128)(2,1)} %get-tuple-element.221), channel_id=1, source_target_pairs={{0,2},{1,3},{2,0},{3,1},{4,6},{5,7},{6,4},{7,5},{8,10},{9,11},{10,... | collective-permute-start | bytes 3145736 | tf_op jit(solution)/shard_map/ppermute | solution.py:958
  258.6 26.9 %collective-permute-start.40 = (bf16[3,2,128,256]{3,2,1,0:T(8,128)(2,1)}, bf16[3,2,128,256]{3,2,1,0:T(8,128)(2,1)S(1)}, u32[]{:S(2)}, u32[]{:S(2)}) collective-permute-start(bf16[3,2,128,256]{3,2,1,0:T(8,128)(2,1)} %get-tuple-element.222), channel_id=1, source_target_pairs={{0,4},{4,0},{8,12},{12,8},{16,20},{20,16},{24,28},{28,24},{1,5},{5... | collective-permute-start | bytes 1179656 | tf_op jit(solution)/shard_map/ppermute | solution.py:962
  260.0 31.9 %collective-permute-start.41 = (bf16[3,2,128,256]{3,2,1,0:T(8,128)(2,1)}, bf16[3,2,128,256]{3,2,1,0:T(8,128)(2,1)S(1)}, u32[]{:S(2)}, u32[]{:S(2)}) collective-permute-start(bf16[3,2,128,256]{3,2,1,0:T(8,128)(2,1)} %get-tuple-element.223), channel_id=1, source_target_pairs={{0,8},{4,12},{8,0},{12,4},{16,24},{20,28},{24,16},{28,20},{1,9},{5... | collective-permute-start | bytes 1179656 | tf_op jit(solution)/shard_map/ppermute | solution.py:962
  282.7 34.3 %collective-permute-start.37 = (bf16[4,2,2,2,128,128]{5,4,3,2,1,0:T(8,128)(2,1)}, bf16[4,2,2,2,128,128]{5,4,3,2,1,0:T(8,128)(2,1)}, u32[]{:S(2)}, u32[]{:S(2)}) collective-permute-start(bf16[4,2,2,2,128,128]{5,4,3,2,1,0:T(8,128)(2,1)} %get-tuple-element.231), channel_id=1, source_target_pairs={{0,2},{1,3},{2,0},{3,1},{4,6},{5,7},{6,4},{7,5},{8,10},{9,11},{10,... | collective-permute-start | bytes 3145736 | tf_op jit(solution)/shard_map/ppermute | solution.py:958
  284.0 33.0 %collective-permute-start.43 = (bf16[4,2,2,2,128,128]{5,4,3,2,1,0:T(8,128)(2,1)}, bf16[4,2,2,2,128,128]{5,4,3,2,1,0:T(8,128)(2,1)}, u32[]{:S(2)}, u32[]{:S(2)}) collective-permute-start(bf16[4,2,2,2,128,128]{5,4,3,2,1,0:T(8,128)(2,1)} %get-tuple-element.232), channel_id=1, source_target_pairs={{0,4},{4,0},{8,12},{12,8},{16,20},{20,16},{24,28},{28,24},{1,5},{5... | collective-permute-start | bytes 3145736 | tf_op jit(solution)/shard_map/ppermute | solution.py:962
  296.2 28.3 %collective-permute-start.45 = (bf16[4,2,2,128,128]{4,3,2,1,0:T(8,128)(2,1)}, bf16[4,2,2,128,128]{4,3,2,1,0:T(8,128)(2,1)S(1)}, u32[]{:S(2)}, u32[]{:S(2)}) collective-permute-start(bf16[4,2,2,128,128]{4,3,2,1,0:T(8,128)(2,1)} %get-tuple-element.242), channel_id=1, source_target_pairs={{0,2},{1,3},{2,0},{3,1},{4,6},{5,7},{6,4},{7,5},{8,10},{9,11},{10,... | collective-permute-start | bytes 1572872 | tf_op jit(solution)/shard_map/ppermute | solution.py:958
  297.6 26.9 %collective-permute-start.46 = (bf16[4,2,2,128,128]{4,3,2,1,0:T(8,128)(2,1)}, bf16[4,2,2,128,128]{4,3,2,1,0:T(8,128)(2,1)S(1)}, u32[]{:S(2)}, u32[]{:S(2)}) collective-permute-start(bf16[4,2,2,128,128]{4,3,2,1,0:T(8,128)(2,1)} %get-tuple-element.243), channel_id=1, source_target_pairs={{0,4},{4,0},{8,12},{12,8},{16,20},{20,16},{24,28},{28,24},{1,5},{5... | collective-permute-start | bytes 1572872 | tf_op jit(solution)/shard_map/ppermute | solution.py:962
  299.2 27.8 %collective-permute-start.47 = (bf16[8,128,256]{2,1,0:T(8,128)(2,1)}, bf16[8,128,256]{2,1,0:T(8,128)(2,1)}, u32[]{:S(2)}, u32[]{:S(2)}) collective-permute-start(bf16[8,128,256]{2,1,0:T(8,128)(2,1)} %get-tuple-element.244), channel_id=1, source_target_pairs={{0,16},{4,20},{8,24},{12,28},{16,0},{20,4},{24,8},{28,12},{1,17},{... | collective-permute-start | bytes 1572872 | tf_op jit(solution)/shard_map/ppermute | solution.py:962
  346.8 21.5 %collective-permute-start.54 = (bf16[8,128,128]{2,1,0:T(8,128)(2,1)}, bf16[8,128,128]{2,1,0:T(8,128)(2,1)S(1)}, u32[]{:S(2)}, u32[]{:S(2)}) collective-permute-start(bf16[8,128,128]{2,1,0:T(8,128)(2,1)} %combine.20), channel_id=1, source_target_pairs={{0,16},{4,20},{8,24},{12,28},{16,0},{20,4},{24,8},{28,12},{1,17},{... | collective-permute-start | bytes 786440 | tf_op jit(solution)/shard_map/ppermute | solution.py:962
  (71 other events, 619.9 us)
Sparse Core Ops, SparseCore 0:
  255.9 62.9 all-gather.2
